TPU v7x, 128 devices: a whole 4x4x4 slice. The times are simulated.
128 devices in a mesh: section: 2 (over core), head: 4 (over x), tok: 16 (over z, y).
Axes of the slice: x: 4, y: 4, z: 4, core: 2. Of those that a mesh axis runs over, the one named last changes fastest.
Arguments:
- hidden: bfloat16 [16, 384, 3072], P('tok'), may hold values from -6 to 6
- latent: float32 [16, 384, 64], P('tok', ('section', 'head')), may hold values from -6 to 6
- w_qkv: bfloat16 [2, 3072, 3, 3072], P(None, None, None, ('section', 'head')), may hold values from -0.109375 to 0.109375
- w_out: bfloat16 [2, 3072, 3072], P(None, ('section', 'head')), may hold values from -0.109375 to 0.109375
- w_final: bfloat16 [3072, 64], replicated, may hold values from -0.109375 to 0.109375
- qk_gain: float32 [2, 2, 128], replicated, may hold values from 0.5 to 2.5
- modulation: float32 [2, 3, 3072], replicated, may hold values from -3 to 3
- stale_kv: bfloat16 [2, 2, 16, 384, 3072], P(None, None, 'tok', None, ('section', 'head')), may hold values from -60 to 60
- request_patches: int32 [4], replicated, may hold values from 1 to 8, 16 in all
- patch_order: int32 [16], replicated, may hold values from 0 to 15, each once
- step_index: int32 [1], replicated, may hold values from 0 to 27
Outputs:
- layer_out: bfloat16 [2, 16, 384, 3072], P(None, 'tok', ('section', 'head'))
- latent_next: float32 [16, 384, 64], P('tok', ('section', 'head'))
- denoised: float32 [16, 384, 64], P('tok', ('section', 'head'))
Inputs may be any that keep to these rules, and one draw needn't show every extreme that they name: `request_patches`: the lengths sum to 16; the longest is exactly 8. `patch_order`: each patch appears once.
All inputs are finite; a program needn't handle non-finite values.
Results may differ from a plain program's by a relative error of at most 0.03.
Values may be sent and summed in bfloat16 or wider, within the bound.
A program may use at most 192 MiB of HBM per device.

v0:
```python
import functools
import math

import jax
import jax.numpy as jnp
from jax import lax
from jax.experimental import pallas as pl
from jax.experimental.pallas import tpu as pltpu
from jax.sharding import PartitionSpec as P

STEPS = 28


norm_eps = 1e-06
time_shift = 3.0
rope_base = 10000.0


def layer_norm(inputs):
    average = jnp.mean(inputs, axis=-1, keepdims=True)
    centred = inputs - average
    variance = jnp.mean(centred * centred, axis=-1, keepdims=True)
    return centred * lax.rsqrt(variance + norm_eps)


def rms_norm(inputs, gains):
    return inputs * lax.rsqrt(jnp.mean(inputs * inputs, axis=-1, keepdims=True) + norm_eps) * gains


def rotate(inputs, positions):
    half_dim = inputs.shape[-1] // 2
    frequency = rope_base ** (-2.0 * jnp.arange(half_dim, dtype=jnp.float32) / inputs.shape[-1])
    angles = positions[..., None, None] * frequency
    pairs = inputs.reshape(inputs.shape[:-1] + (half_dim, 2))
    even_lane = pairs[..., 0]
    odd_lane = pairs[..., 1]
    cosine = jnp.cos(angles)
    sine = jnp.sin(angles)
    turned = jnp.stack(
        [even_lane * cosine - odd_lane * sine, even_lane * sine + odd_lane * cosine], axis=-1
    )
    return turned.reshape(inputs.shape)


def slot_layout(request_patches, patch_order):
    request_ends = jnp.cumsum(request_patches)
    starts = request_ends - request_patches
    request_of = jnp.sum((request_ends[None, :] <= patch_order[:, None]).astype(jnp.int32), axis=1)
    chosen = request_of[:, None] == jnp.arange(request_patches.shape[0], dtype=jnp.int32)[None, :]
    first_patch = jnp.sum(jnp.where(chosen, starts[None, :], 0), axis=1)
    return (request_of, patch_order - first_patch)


def project(inputs, layer_mod, weight, gains, positions, head_dim):
    normed = (layer_norm(inputs.astype(jnp.float32)) * (1.0 + layer_mod[1]) + layer_mod[0]).astype(
        jnp.bfloat16
    )
    rows = inputs.shape[0]
    column_count = weight.shape[2]
    heads = column_count // head_dim
    pieces = [
        jnp.dot(normed, weight[:, part, :], preferred_element_type=jnp.float32).reshape(
            rows, heads, head_dim
        )
        for part in range(3)
    ]
    queries = rotate(rms_norm(pieces[0], gains[0]), positions).astype(jnp.bfloat16)
    keys_fresh = rotate(rms_norm(pieces[1], gains[1]), positions).astype(jnp.bfloat16)
    values_fresh = pieces[2].astype(jnp.bfloat16)
    return (
        queries.reshape(rows, column_count),
        keys_fresh.reshape(rows, column_count),
        values_fresh.reshape(rows, column_count),
    )


def attention_kernel(
    head_dim, fetch_ref, allow_ref, q_ref, kf_ref, vf_ref, ks_ref, vs_ref, o_ref, m_sc, l_sc, acc_sc
):
    slot = pl.program_id(0)
    heads = q_ref.shape[1] // head_dim
    scaling = 1.0 / math.sqrt(head_dim)
    contract = (((1,), (1,)), ((), ()))

    @pl.when(slot == 0)
    def _fresh():
        for h in range(heads):
            lanes = slice(h * head_dim, (h + 1) * head_dim)
            scores = (
                lax.dot_general(
                    q_ref[:, lanes], kf_ref[:, lanes], contract, preferred_element_type=jnp.float32
                )
                * scaling
            )
            row_max = jnp.max(scores, axis=1, keepdims=True)
            weights = jnp.exp(scores - row_max)
            m_sc[h] = row_max
            l_sc[h] = jnp.sum(weights, axis=1, keepdims=True)
            acc_sc[h] = jnp.dot(
                weights.astype(jnp.bfloat16), vf_ref[:, lanes], preferred_element_type=jnp.float32
            )

    @pl.when(allow_ref[slot] != 0)
    def _stale():
        for h in range(heads):
            lanes = slice(h * head_dim, (h + 1) * head_dim)
            scores = (
                lax.dot_general(
                    q_ref[:, lanes], ks_ref[:, lanes], contract, preferred_element_type=jnp.float32
                )
                * scaling
            )
            old_max = m_sc[h]
            new_max = jnp.maximum(old_max, jnp.max(scores, axis=1, keepdims=True))
            factor = jnp.exp(old_max - new_max)
            weights = jnp.exp(scores - new_max)
            l_sc[h] = l_sc[h] * factor + jnp.sum(weights, axis=1, keepdims=True)
            acc_sc[h] = acc_sc[h] * factor + jnp.dot(
                weights.astype(jnp.bfloat16), vs_ref[:, lanes], preferred_element_type=jnp.float32
            )
            m_sc[h] = new_max

    @pl.when(slot == pl.num_programs(0) - 1)
    def _finish():
        for h in range(heads):
            lanes = slice(h * head_dim, (h + 1) * head_dim)
            o_ref[:, lanes] = (acc_sc[h] / l_sc[h]).astype(o_ref.dtype)


def attend(queries, keys_fresh, values_fresh, stale_all, layer_idx, fetch, allow, head_dim):
    rows, features = queries.shape
    slot_total = stale_all.shape[2]
    heads = features // head_dim
    whole = pl.BlockSpec((rows, features), lambda j, f, a: (0, 0))
    key_spec = pl.BlockSpec(
        (None, None, None, rows, features), lambda j, f, a: (layer_idx, 0, f[j], 0, 0)
    )
    value_spec = pl.BlockSpec(
        (None, None, None, rows, features), lambda j, f, a: (layer_idx, 1, f[j], 0, 0)
    )
    return pl.pallas_call(
        functools.partial(attention_kernel, head_dim),
        out_shape=jax.ShapeDtypeStruct((rows, features), jnp.bfloat16),
        grid_spec=pltpu.PrefetchScalarGridSpec(
            num_scalar_prefetch=2,
            grid=(slot_total,),
            in_specs=[whole, whole, whole, key_spec, value_spec],
            out_specs=whole,
            scratch_shapes=[
                pltpu.VMEM((heads, rows, 1), jnp.float32),
                pltpu.VMEM((heads, rows, 1), jnp.float32),
                pltpu.VMEM((heads, rows, head_dim), jnp.float32),
            ],
        ),
        compiler_params=pltpu.CompilerParams(dimension_semantics=("arbitrary",)),
    )(fetch, allow, queries, keys_fresh, values_fresh, stale_all, stale_all)


def noise_level(position):
    time_left = 1.0 - position.astype(jnp.float32) / STEPS
    return time_shift * time_left / (1.0 + (time_shift - 1.0) * time_left)


def shards(
    hidden,
    latent,
    w_qkv,
    w_out,
    w_final,
    qk_gain,
    modulation,
    stale_kv,
    request_patches,
    patch_order,
    step_index,
):
    section_count = lax.axis_size("section")
    head_count = lax.axis_size("head")
    group_count = section_count * head_count
    section_index = lax.axis_index("section")
    head_index = lax.axis_index("head")
    tok_index = lax.axis_index("tok")
    group_index = section_index * head_count + head_index
    patch_len = hidden.shape[1]
    width = hidden.shape[2]
    head_dim = qk_gain.shape[-1]
    own_rows = patch_len // group_count
    layer_count = w_qkv.shape[0]
    request_of, offsets = slot_layout(request_patches, patch_order)
    slot_total = request_of.shape[0]
    my_request = request_of[tok_index]
    my_offset = offsets[tok_index]
    positions = (my_offset * patch_len + jnp.arange(patch_len, dtype=jnp.int32)).astype(jnp.float32)
    slot_ids = jnp.arange(slot_total, dtype=jnp.int32)
    allowed = (request_of == my_request) & (slot_ids != tok_index)
    marked = jnp.where(allowed, slot_ids, -1)
    running = lax.cummax(marked, axis=0)
    first_allowed = jnp.argmax(allowed).astype(jnp.int32)
    fetch = jnp.where(running >= 0, running, first_allowed).astype(jnp.int32)
    allow = allowed.astype(jnp.int32)
    stale_all = lax.all_gather(stale_kv, "tok", axis=2, tiled=True)
    current_full = hidden[0]
    own_input = lax.dynamic_slice_in_dim(current_full, group_index * own_rows, own_rows, 0)
    outputs = []
    for layer_idx in range(layer_count):
        queries, keys_fresh, values_fresh = project(
            current_full,
            modulation[layer_idx],
            w_qkv[layer_idx],
            qk_gain[layer_idx],
            positions,
            head_dim,
        )
        attended = attend(
            queries, keys_fresh, values_fresh, stale_all, layer_idx, fetch, allow, head_dim
        )
        partial = jnp.dot(attended, w_out[layer_idx], preferred_element_type=jnp.float32).astype(
            jnp.bfloat16
        )
        summed = lax.psum_scatter(
            partial, ("section", "head"), scatter_dimension=0, tiled=True
        ).astype(jnp.float32)
        gate = modulation[layer_idx, 2]
        own_out = (own_input.astype(jnp.float32) + gate * summed).astype(jnp.bfloat16)
        if layer_idx + 1 < layer_count:
            current_full = lax.all_gather(own_out, ("section", "head"), axis=0, tiled=True)
        own_input = own_out
        outputs.append(own_out)
    last_own = outputs[-1]
    layer_out = jnp.stack(outputs)[:, None]
    normed = layer_norm(last_own.astype(jnp.float32)).astype(jnp.bfloat16)
    velocity = jnp.dot(normed, w_final, preferred_element_type=jnp.float32)[None]
    level_now = noise_level(step_index[0])
    level_next = noise_level(step_index[0] + 1)
    return (layer_out, latent + (level_next - level_now) * velocity, latent - level_now * velocity)


def solution(mesh):
    placed = (
        P("tok", None, None),
        P("tok", ("section", "head"), None),
        P(None, None, None, ("section", "head")),
        P(None, ("section", "head"), None),
        P(),
        P(),
        P(),
        P(None, None, "tok", None, ("section", "head")),
        P(),
        P(),
        P(),
    )
    return jax.shard_map(
        shards,
        mesh=mesh,
        in_specs=placed,
        out_specs=(
            P(None, "tok", ("section", "head"), None),
            P("tok", ("section", "head"), None),
            P("tok", ("section", "head"), None),
        ),
        check_vma=False,
    )
```

profile of v0, /device:TPU:8, one launch (start us, length us, event | category | flops | bytes accessed | tf_op | source)
XLA Modules:
  0.0 332.2 jit_solution(10988061354399205398)
XLA Ops:
  11.7 6.1 %slice_bitcast_fusion.1 = (bf16[3072,3,384]{2,0,1:T(8,128)(2,1)S(1)}, bf16[3072,3,384]{2,0,1:T(8,128)(2,1)S(1)}) fusion(bf16[2,3072,3,384]{3,1,2,0:T(8,128)(2,1)} %param.13), kind=kLoop, calls=%fused_computation.1 | loop fusion | bytes 28311552 | tf_op jit(solution)/shard_map/squeeze | solution.py:209
  17.8 5.3 %slice_bitcast_fusion.2 = (bf16[384,3072]{0,1:T(8,128)(2,1)}, bf16[384,3072]{0,1:T(8,128)(2,1)}, bf16[384,3072]{0,1:T(8,128)(2,1)}, bf16[384,3072]{0,1:T(8,128)(...) fusion(bf16[3072,3,384]{2,0,1:T(8,128)(2,1)S(1)} %get-tuple-element.17, ...), kind=kLoop, calls=%fused_computation.24 | loop fusion | bytes 28311552 | tf_op jit(solution)/shard_map/dot_general | solution.py:62
  23.1 4.5 %copy.48 = bf16[384,3072]{1,0:T(8,128)(2,1)} copy(bf16[384,3072]{0,1:T(8,128)(2,1)} %get-tuple-element.59) | data formatting | bytes 4718592 | tf_op jit(solution)/shard_map/dot_general | solution.py:62
  31.8 1.4 multiply_reduce_fusion.2
  34.2 1.4 reshape.400
  36.3 4.3 %copy.47 = bf16[384,3072]{1,0:T(8,128)(2,1)} copy(bf16[384,3072]{0,1:T(8,128)(2,1)} %get-tuple-element.58) | data formatting | bytes 4718592 | tf_op jit(solution)/shard_map/dot_general | solution.py:62
  40.7 3.8 %multiply_reduce_fusion.3 = (f32[384,3]{0,1:T(4,128)S(1)}, f32[384,3,128]{0,2,1:T(8,128)S(1)}) fusion(bf16[384,3072,1]{1,0,2:T(8,128)(2,1)} %copy-done.7, bf16[3,128,3072]{2,1,0:T(8,128)(2,1)} %bitcast.134), kind=kOutput, calls=%fused_computation.53 | convolution fusion | flops 906263424 | bytes 5313024 | tf_op jit(solution)/shard_map/dot_general | solution.py:62
  45.5 2.2 reshape.399
  48.8 3.3 %subtract_convert_fusion.2 = (bf16[384,3,64,1]{0,3,2,1:T(2,128)(2,1)}, bf16[384,3,64,1]{0,3,2,1:T(2,128)(2,1)}, bf16[384,3,64,1]{0,3,2,1:T(2,128)(2,1)S(1)}, bf16[384,3,64,1]{0,3,2,1:T(2,128)(2,1)S(1)}) fusion(f32[384,3,64,2]{0,3,2,1:T(2,128)S(1)} %reshape.400, f32[384,64]{0,1:T(8,128)S(1)} %get-tuple-element.45, f32[384,64]{0,1:T(8,128)S(1)} %get-tuple-element.44, ...), kind=kLoop, calls=%fused_computation.66 | loop fusion | flops 1179648 | bytes 1966080 | tf_op jit(solution)/shard_map/convert.5
  53.8 1.7 pad_maximum_fusion.1
  56.5 4.4 %copy.49 = bf16[384,3072]{1,0:T(8,128)(2,1)} copy(bf16[384,3072]{0,1:T(8,128)(2,1)} %get-tuple-element.60) | data formatting | bytes 4718592 | tf_op jit(solution)/shard_map/dot_general | solution.py:62
  60.9 3.8 %convolution_convert_fusion.3 = bf16[384,3,128]{0,2,1:T(8,128)(2,1)S(1)} fusion(bf16[384,3072,1]{1,0,2:T(8,128)(2,1)} %copy-done.7, bf16[3,128,3072]{2,1,0:T(8,128)(2,1)} %bitcast.135), kind=kOutput, calls=%fused_computation.35 | convolution fusion | flops 906117120 | bytes 5013504 | tf_op jit(solution)/shard_map/dot_general | solution.py:62
  69.3 65.3 %all-gather.3.cloned.1.call-done.ks_ref.vs_ref = bf16[2,2,16,384,384]{4,3,2,1,0:T(8,128)(2,1)} async-done(((bf16[2,2,1,384,384]{4,3,2,1,0:T(8,128)(2,1)}), bf16[2,2,16,384,384]{4,3,2,1,0:T(8,128)(2,1)}) %all-gather.3.cloned.1.call-update) | async-done | bytes 18874384 | tf_op jit(solution)/shard_map/all_gather | solution.py:201
  134.6 23.2 %shard_map.130 = bf16[384,384]{1,0:T(8,128)(2,1)} custom-call(s32[16]{0:T(128)} %compare_select_fusion.fetch_ref, s32[16]{0:T(128)} %fusion.29.allow_ref, bf16[384,384]{1,0:T(8,128)(2,1)} %copy.50.q_ref, bf16[384,384]{1,0:T(8,128)(2,1)} %copy.51.kf_ref, bf16[384,384]{1,0:T(8,128)(2,1)} %copy.52.vf_ref, ...), custom_call_target="tpu_custom_call" | custom-call | tf_op jit(solution)/shard_map/pallas_call | solution.py:141
  157.8 4.6 %convolution_convert_fusion.1 = bf16[384,3072]{1,0:T(8,128)(2,1)} fusion(bf16[384,384]{1,0:T(8,128)(2,1)} %shard_map.130, bf16[2,384,3072]{2,1,0:T(8,128)(2,1)} %param.14), kind=kOutput, calls=%fused_computation.21 | convolution fusion | flops 907149312 | bytes 5013504 | tf_op jit(solution)/shard_map/dot_general | solution.py:217
  162.5 38.5 %reduce-scatter.3.cloned.1.call-done = bf16[48,3072]{1,0:T(8,128)(2,1)} async-done(((bf16[384,3072]{1,0:T(8,128)(2,1)}), bf16[48,3072]{1,0:T(8,128)(2,1)}) %reduce-scatter.3.cloned.1.call-update) | async-done | bytes 294928 | tf_op jit(solution)/shard_map/reduce_scatter | solution.py:220
  201.0 1.7 fusion.23
  202.8 4.3 %copy.54 = bf16[384,3072]{1,0:T(8,128)(2,1)} copy(bf16[384,3072]{0,1:T(8,128)(2,1)} %get-tuple-element.19) | data formatting | bytes 4718592 | tf_op jit(solution)/shard_map/dot_general | solution.py:62
  207.2 4.5 %copy.53 = bf16[384,3072]{1,0:T(8,128)(2,1)} copy(bf16[384,3072]{0,1:T(8,128)(2,1)} %get-tuple-element.20) | data formatting | bytes 4718592 | tf_op jit(solution)/shard_map/dot_general | solution.py:62
  211.6 2.6 copy.55
  214.3 14.7 %all-gather.5.cloned.1.call-done = bf16[384,3072]{1,0:T(8,128)(2,1)} async-done(((bf16[48,3072]{1,0:T(8,128)(2,1)}), bf16[384,3072]{1,0:T(8,128)(2,1)}) %all-gather.5.cloned.1.call-update) | async-done | bytes 2359312 | tf_op jit(solution)/shard_map/all_gather | solution.py:226
  228.9 2.2 convert_reduce_fusion.1
  232.1 2.4 multiply_reduce_fusion
  235.4 1.4 reshape.403
  236.9 3.3 multiply_reduce_fusion.1
  241.1 2.2 reshape.402
  243.3 3.3 %subtract_convert_fusion = (bf16[384,3,64,1]{0,3,2,1:T(2,128)(2,1)}, bf16[384,3,64,1]{0,3,2,1:T(2,128)(2,1)}, bf16[384,3,64,1]{0,3,2,1:T(2,128)(2,1)S(1)}, bf16[384,3,64,1]{0,3,2,1:T(2,128)(2,1)S(1)}) fusion(f32[384,3,64,2]{0,3,2,1:T(2,128)S(1)} %reshape.403, f32[384,64]{0,1:T(8,128)S(1)} %get-tuple-element.45, f32[384,64]{0,1:T(8,128)S(1)} %get-tuple-element.44, ...), kind=kLoop, calls=%fused_computation.62 | loop fusion | flops 1179648 | bytes 1966080 | tf_op jit(solution)/shard_map/convert.1
  248.3 1.7 pad_maximum_fusion.3
  251.1 3.2 convolution_convert_fusion.2
  255.2 23.2 %shard_map.131 = bf16[384,384]{1,0:T(8,128)(2,1)} custom-call(s32[16]{0:T(128)} %compare_select_fusion.fetch_ref, s32[16]{0:T(128)} %fusion.29.allow_ref, bf16[384,384]{1,0:T(8,128)(2,1)} %copy.56.q_ref, bf16[384,384]{1,0:T(8,128)(2,1)} %copy.57.kf_ref, bf16[384,384]{1,0:T(8,128)(2,1)} %copy.58.vf_ref, ...), custom_call_target="tpu_custom_call" | custom-call | tf_op jit(solution)/shard_map/pallas_call | solution.py:141
  278.4 4.6 %convolution_convert_fusion = bf16[384,3072]{1,0:T(8,128)(2,1)} fusion(bf16[384,384]{1,0:T(8,128)(2,1)} %shard_map.131, bf16[2,384,3072]{2,1,0:T(8,128)(2,1)} %param.14), kind=kOutput, calls=%fused_computation.20 | convolution fusion | flops 907149312 | bytes 5013504 | tf_op jit(solution)/shard_map/dot_general | solution.py:217
  283.8 38.6 %reduce-scatter.5.cloned.1.call-done = bf16[48,3072]{1,0:T(8,128)(2,1)} async-done(((bf16[384,3072]{1,0:T(8,128)(2,1)}), bf16[48,3072]{1,0:T(8,128)(2,1)}) %reduce-scatter.5.cloned.1.call-update) | async-done | bytes 294928 | tf_op jit(solution)/shard_map/reduce_scatter | solution.py:220
  (105 shorter events, 28.8 us)
Async XLA Ops:
  7.2 317.6 %copy-start = (bf16[3072,64]{0,1:T(8,128)(2,1)S(1)}, bf16[3072,64]{0,1:T(8,128)(2,1)}, u32[]{:S(2)}) copy-start(bf16[3072,64]{0,1:T(8,128)(2,1)} %param.15) | copy-start | bytes 1179652
  7.2 127.5 %all-gather.3.cloned.1.call-start = ((), (), s32[]{:S(2)}) async-start(), calls=%async_computation.2 | async-start | bytes 20054016 | tf_op jit(solution)/shard_map/all_gather | solution.py:201
  7.9 193.1 %reduce-scatter.3.cloned.1.call-start = ((), (), s32[]{:S(2)}) async-start(), calls=%async_computation.3 | async-start | bytes 2654208 | tf_op jit(solution)/shard_map/reduce_scatter | solution.py:220
  23.1 4.5 %copy-start.15 = (f32[2,2,128]{2,1,0:T(2,128)S(1)}, f32[2,2,128]{2,1,0:T(2,128)}, u32[]{:S(2)}) copy-start(f32[2,2,128]{2,1,0:T(2,128)} %param.16) | copy-start | bytes 6148
  23.1 5.1 %copy-start.1 = (bf16[1,384,3072]{2,1,0:T(8,128)(2,1)S(1)}, bf16[1,384,3072]{2,1,0:T(8,128)(2,1)}, u32[]{:S(2)}) copy-start(bf16[1,384,3072]{2,1,0:T(8,128)(2,1)} %param.11) | copy-start | bytes 7077892
  28.2 1.2 copy-start.8
  30.0 1.7 copy-start.5
  31.2 2.0 copy-start.7
  33.2 2.4 copy-start.20
  33.2 2.5 copy-start.21
  60.9 7.3 %copy-start.18 = (s32[16]{0:T(128)S(1)}, s32[16]{0:T(128)}, u32[]{:S(2)}) copy-start(s32[16]{0:T(128)} %reduce.19) | copy-start | bytes 196
  162.4 38.6 %copy-start.9 = (f32[1,1,3072]{2,0,1:T(1,128)S(1)}, f32[1,1,3072]{2,0,1:T(1,128)}, u32[]{:S(2)}) copy-start(f32[1,1,3072]{2,0,1:T(1,128)} %get-tuple-element.39) | copy-start | bytes 36868
  162.4 66.5 %all-gather.5.cloned.1.call-start = ((), (), s32[]{:S(2)}) async-start(), calls=%async_computation.4 | async-start | bytes 2654208 | tf_op jit(solution)/shard_map/all_gather | solution.py:226
  202.8 119.6 %reduce-scatter.5.cloned.1.call-start = ((), (), s32[]{:S(2)}) async-start(), calls=%async_computation.5 | async-start | bytes 2654208 | tf_op jit(solution)/shard_map/reduce_scatter | solution.py:220
  207.2 4.5 %copy-start.2 = (bf16[384,3072]{0,1:T(8,128)(2,1)S(1)}, bf16[384,3072]{0,1:T(8,128)(2,1)}, u32[]{:S(2)}) copy-start(bf16[384,3072]{0,1:T(8,128)(2,1)} %get-tuple-element.18) | copy-start | bytes 7077892
  228.9 2.4 copy-start.3
  228.9 3.1 copy-start.6
  228.9 3.2 copy-start.10
  232.1 2.4 copy-start.16
  232.1 2.4 copy-start.14
  236.9 3.3 copy-start.13
  246.6 4.4 %copy-start.11 = (f32[1,1,3072]{2,0,1:T(1,128)S(1)}, f32[1,1,3072]{2,0,1:T(1,128)}, u32[]{:S(2)}) copy-start(f32[1,1,3072]{2,0,1:T(1,128)} %get-tuple-element.40) | copy-start | bytes 36868
  246.6 4.4 %copy-start.12 = (f32[1,1,3072]{2,0,1:T(1,128)S(1)}, f32[1,1,3072]{2,0,1:T(1,128)}, u32[]{:S(2)}) copy-start(f32[1,1,3072]{2,0,1:T(1,128)} %get-tuple-element.41) | copy-start | bytes 36868
  246.6 4.4 %copy-start.17 = (f32[384]{0:T(512)S(1)}, f32[384]{0:T(512)}, u32[]{:S(2)}) copy-start(f32[384]{0:T(512)} %copy-done.16) | copy-start | bytes 4612
  283.0 39.4 %copy-start.4 = (bf16[48,3072]{1,0:T(8,128)(2,1)S(1)}, bf16[48,3072]{1,0:T(8,128)(2,1)}, u32[]{:S(2)}) copy-start(bf16[48,3072]{1,0:T(8,128)(2,1)} %fusion.23) | copy-start | bytes 884740
  283.0 41.7 %copy-start.19 = (f32[1,48,64]{2,1,0:T(8,128)S(1)}, f32[1,48,64]{2,1,0:T(8,128)}, u32[]{:S(2)}) copy-start(f32[1,48,64]{2,1,0:T(8,128)} %param.12) | copy-start | bytes 36868
Sparse Core Ops, SparseCore 0:
  10.2 124.4 all-gather.2
  162.5 38.4 reduce-scatter.2
  202.9 25.9 all-gather.4
  283.2 39.2 reduce-scatter.4
where the time goes:
time: 335 us; the launch traced here: 332 us
  waiting for transfers between devices  158 us (47%)
  local copies, waits for them, and re-layouts  51.9 us (15%)
  Pallas kernels  46.4 us (14%)
  other arithmetic  32.4 us (10%)
  matrix products  28 us (8%)
  between operations  15.5 us (5%)
    reduce_scatter x2, waiting for transfers between devices, shards(): lax.psum_scatter(partial, ('section', 'head'), scatter_dimension=0, tiled...  77.1 us
    all_gather x1, waiting for transfers between devices, shards(): stale_all = lax.all_gather(stale_kv, 'tok', axis=2, tiled=True)  65.3 us
    pallas_call x2, Pallas kernels, attend(): pl.pallas_call(functools.partial(attention_kernel, head_dim), out_shape=j...  46.4 us
    dot_general x7, local copies, waits for them, and re-layouts, project(): jnp.dot(normed, weight[:, part, :], preferred_element_type=jnp.float32)  30 us
    dot_general x6, matrix products, project(): jnp.dot(normed, weight[:, part, :], preferred_element_type=jnp.float32)  17.9 us
    all_gather x1, waiting for transfers between devices, shards(): lax.all_gather(own_out, ('section', 'head'), axis=0, tiled=True)  14.7 us
    dot_general x2, matrix products, shards(): jnp.dot(attended, w_out[layer_idx], preferred_element_type=jnp.float32)  9.17 us
    another operation x5, other arithmetic  8.24 us
  transfers between devices with their start and end apart: 4, of which 4 were waited for; matrix products, arithmetic and copies ran while one was open for 21% of the time, Pallas kernels for 0%

commit v1 on v0

--- a/solution.py
+++ b/solution.py
@@ -127,16 +127,16 @@
             o_ref[:, lanes] = (acc_sc[h] / l_sc[h]).astype(o_ref.dtype)
 
 
-def attend(queries, keys_fresh, values_fresh, stale_all, layer_idx, fetch, allow, head_dim):
+def attend(queries, keys_fresh, values_fresh, stale, fetch, allow, head_dim):
     rows, features = queries.shape
-    slot_total = stale_all.shape[2]
+    slot_total = stale.shape[1]
     heads = features // head_dim
     whole = pl.BlockSpec((rows, features), lambda j, f, a: (0, 0))
     key_spec = pl.BlockSpec(
-        (None, None, None, rows, features), lambda j, f, a: (layer_idx, 0, f[j], 0, 0)
+        (None, None, rows, features), lambda j, f, a: (0, f[j], 0, 0)
     )
     value_spec = pl.BlockSpec(
-        (None, None, None, rows, features), lambda j, f, a: (layer_idx, 1, f[j], 0, 0)
+        (None, None, rows, features), lambda j, f, a: (1, f[j], 0, 0)
     )
     return pl.pallas_call(
         functools.partial(attention_kernel, head_dim),
@@ -153,7 +153,154 @@
             ],
         ),
         compiler_params=pltpu.CompilerParams(dimension_semantics=("arbitrary",)),
-    )(fetch, allow, queries, keys_fresh, values_fresh, stale_all, stale_all)
+    )(fetch, allow, queries, keys_fresh, values_fresh, stale, stale)
+
+
+def exchange_kernel(head_count, own_rows, gather, part_ref, own_ref, gate_ref, *rest):
+    if gather:
+        (out_ref, full_ref, near, far, mid, acc, far_in, spread,
+         s1_send, s1_recv, s2_send, s2_recv, g1_send, g1_recv, g2_send, g2_recv) = rest
+    else:
+        (out_ref, near, far, mid, acc, s1_send, s1_recv, s2_send, s2_recv) = rest
+    mesh_ids = pl.DeviceIdType.MESH
+    section = lax.axis_index("section")
+    head = lax.axis_index("head")
+    tok = lax.axis_index("tok")
+    other = 1 - section
+    half = head_count * own_rows
+
+    barrier = pltpu.get_barrier_semaphore()
+    pl.semaphore_signal(barrier, inc=1, device_id=(other, head, tok), device_id_type=mesh_ids)
+    for h in range(head_count):
+        @pl.when(h != head)
+        def _greet():
+            pl.semaphore_signal(barrier, inc=1, device_id=(section, h, tok), device_id_type=mesh_ids)
+    pl.semaphore_wait(barrier, head_count)
+
+    first = pltpu.make_async_remote_copy(
+        src_ref=part_ref.at[pl.ds(pl.multiple_of(other * half, own_rows), half)],
+        dst_ref=near,
+        send_sem=s1_send,
+        recv_sem=s1_recv,
+        device_id=(other, head, tok),
+        device_id_type=mesh_ids,
+    )
+    first.start()
+    first.wait()
+    base = pl.multiple_of(section * half, own_rows)
+    for h in range(head_count):
+        rows = pl.ds(pl.multiple_of(base + h * own_rows, own_rows), own_rows)
+        mid[h] = (
+            part_ref[rows, :].astype(jnp.float32)
+            + near[h * own_rows:(h + 1) * own_rows, :].astype(jnp.float32)
+        ).astype(mid.dtype)
+
+    def far_copy(h, slot):
+        return pltpu.make_async_remote_copy(
+            src_ref=mid.at[h],
+            dst_ref=far.at[slot],
+            send_sem=s2_send.at[h],
+            recv_sem=s2_recv.at[slot],
+            device_id=(section, h, tok),
+            device_id_type=mesh_ids,
+        )
+
+    for h in range(head_count):
+        @pl.when(h != head)
+        def _send():
+            far_copy(h, head).start()
+    mine = pl.ds(pl.multiple_of(base + head * own_rows, own_rows), own_rows)
+    near_mine = pl.ds(pl.multiple_of(head * own_rows, own_rows), own_rows)
+    acc[...] = part_ref[mine, :].astype(jnp.float32) + near[near_mine, :].astype(jnp.float32)
+    for h in range(head_count):
+        @pl.when(h != head)
+        def _wait():
+            far_copy(h, h).wait()
+            acc[...] += far[h].astype(jnp.float32)
+    if not gather:
+        out_ref[...] = acc[...]
+        return
+    spread[head] = (own_ref[...].astype(jnp.float32) + gate_ref[...] * acc[...]).astype(spread.dtype)
+    out_ref[...] = spread[head]
+
+    def share_copy(h, slot):
+        return pltpu.make_async_remote_copy(
+            src_ref=spread.at[head],
+            dst_ref=far_in.at[slot],
+            send_sem=g1_send.at[h],
+            recv_sem=g1_recv.at[slot],
+            device_id=(section, h, tok),
+            device_id_type=mesh_ids,
+        )
+
+    for h in range(head_count):
+        @pl.when(h != head)
+        def _share():
+            share_copy(h, head).start()
+    for h in range(head_count):
+        @pl.when(h != head)
+        def _collect():
+            share_copy(h, h).wait()
+            spread[h] = far_in[h]
+    last = pltpu.make_async_remote_copy(
+        src_ref=spread,
+        dst_ref=full_ref.at[section],
+        send_sem=g2_send,
+        recv_sem=g2_recv,
+        device_id=(other, head, tok),
+        device_id_type=mesh_ids,
+    )
+    last.start()
+    full_ref[section] = spread[...]
+    last.wait()
+
+
+def exchange(partial, own_input, gate, layer_idx, gather, head_count, own_rows):
+    rows, width = partial.shape
+    half = head_count * own_rows
+    vmem = pl.BlockSpec(memory_space=pltpu.VMEM)
+    scratch = [
+        pltpu.VMEM((half, width), partial.dtype),
+        pltpu.VMEM((head_count, own_rows, width), partial.dtype),
+        pltpu.VMEM((head_count, own_rows, width), partial.dtype),
+        pltpu.VMEM((own_rows, width), jnp.float32),
+    ]
+    if gather:
+        out_shape = (
+            jax.ShapeDtypeStruct((own_rows, width), jnp.bfloat16),
+            jax.ShapeDtypeStruct((rows // half, head_count, own_rows, width), jnp.bfloat16),
+        )
+        out_specs = (vmem, vmem)
+        scratch += [
+            pltpu.VMEM((head_count, own_rows, width), jnp.bfloat16),
+            pltpu.VMEM((head_count, own_rows, width), jnp.bfloat16),
+        ]
+    else:
+        out_shape = jax.ShapeDtypeStruct((own_rows, width), jnp.float32)
+        out_specs = vmem
+    scratch += [
+        pltpu.SemaphoreType.DMA(()),
+        pltpu.SemaphoreType.DMA(()),
+        pltpu.SemaphoreType.DMA((head_count,)),
+        pltpu.SemaphoreType.DMA((head_count,)),
+    ]
+    if gather:
+        scratch += [
+            pltpu.SemaphoreType.DMA((head_count,)),
+            pltpu.SemaphoreType.DMA((head_count,)),
+            pltpu.SemaphoreType.DMA(()),
+            pltpu.SemaphoreType.DMA(()),
+        ]
+    return pl.pallas_call(
+        functools.partial(exchange_kernel, head_count, own_rows, gather),
+        out_shape=out_shape,
+        in_specs=[vmem, vmem, vmem],
+        out_specs=out_specs,
+        scratch_shapes=scratch,
+        compiler_params=pltpu.CompilerParams(
+            collective_id=layer_idx, has_side_effects=True, vmem_limit_bytes=48 * 1024 * 1024
+        ),
+    )(partial, own_input, gate.reshape(1, width))
 
 
 def noise_level(position):
@@ -198,7 +345,9 @@
     first_allowed = jnp.argmax(allowed).astype(jnp.int32)
     fetch = jnp.where(running >= 0, running, first_allowed).astype(jnp.int32)
     allow = allowed.astype(jnp.int32)
-    stale_all = lax.all_gather(stale_kv, "tok", axis=2, tiled=True)
+    stale_layers = [
+        lax.all_gather(stale_kv[layer], "tok", axis=1, tiled=True) for layer in range(layer_count)
+    ]
     current_full = hidden[0]
     own_input = lax.dynamic_slice_in_dim(current_full, group_index * own_rows, own_rows, 0)
     outputs = []
@@ -212,18 +361,20 @@
             head_dim,
         )
         attended = attend(
-            queries, keys_fresh, values_fresh, stale_all, layer_idx, fetch, allow, head_dim
+            queries, keys_fresh, values_fresh, stale_layers[layer_idx], fetch, allow, head_dim
         )
         partial = jnp.dot(attended, w_out[layer_idx], preferred_element_type=jnp.float32).astype(
             jnp.bfloat16
         )
-        summed = lax.psum_scatter(
-            partial, ("section", "head"), scatter_dimension=0, tiled=True
-        ).astype(jnp.float32)
         gate = modulation[layer_idx, 2]
-        own_out = (own_input.astype(jnp.float32) + gate * summed).astype(jnp.bfloat16)
         if layer_idx + 1 < layer_count:
-            current_full = lax.all_gather(own_out, ("section", "head"), axis=0, tiled=True)
+            own_out, gathered = exchange(
+                partial, own_input, gate, layer_idx, True, head_count, own_rows
+            )
+            current_full = gathered.reshape(patch_len, width)
+        else:
+            summed = exchange(partial, own_input, gate, layer_idx, False, head_count, own_rows)
+            own_out = (own_input.astype(jnp.float32) + gate * summed).astype(jnp.bfloat16)
         own_input = own_out
         outputs.append(own_out)
     last_own = outputs[-1]

time: 335 us -> 229 us (0.68)
  waiting for transfers between devices: 158 us -> 6.9 us
  Pallas kernels: 46.4 us -> 105 us
  other arithmetic: 32.4 us -> 22.2 us
    reduce_scatter x2 -> x0, waiting for transfers between devices: 77.1 us -> none  [shards(): lax.psum_scatter(partial, ('section', 'head'), scatter_dimension=0, tiled...]
    all_gather x2, waiting for transfers between devices: 80 us -> 6.19 us  [shards(): lax.all_gather(stale_kv[layer], 'tok', axis=1, tiled=True)]
    pallas_call x0 -> x2, Pallas kernels: none -> 59.2 us  [exchange(): pl.pallas_call(functools.partial(exchange_kernel, head_count, own_rows, g...]
  transfers between devices with their start and end apart: 4 -> 2, of which waited for: 4 -> 1; matrix products, arithmetic and copies ran while one was open for 21% -> 40% of each run, Pallas kernels for 0% -> 27%
where the time goes in v1:
time: 229 us; the launch traced here: 227 us
  Pallas kernels  105 us (46%)
  local copies, waits for them, and re-layouts  52.6 us (23%)
  matrix products  24.7 us (11%)
  other arithmetic  22.2 us (10%)
  between operations  15.8 us (7%)
  waiting for transfers between devices  6.9 us (3%)
    pallas_call x2, Pallas kernels, exchange(): pl.pallas_call(functools.partial(exchange_kernel, head_count, own_rows, g...  59.2 us
    pallas_call x2, Pallas kernels, attend(): pl.pallas_call(functools.partial(attention_kernel, head_dim), out_shape=j...  45.9 us
    dot_general x7, local copies, waits for them, and re-layouts, project(): jnp.dot(normed, weight[:, part, :], preferred_element_type=jnp.float32)  31.2 us
    dot_general x6, matrix products, project(): jnp.dot(normed, weight[:, part, :], preferred_element_type=jnp.float32)  17.4 us
    dot_general x2, matrix products, shards(): jnp.dot(attended, w_out[layer_idx], preferred_element_type=jnp.float32)  6.37 us
    all_gather x2, waiting for transfers between devices, shards(): lax.all_gather(stale_kv[layer], 'tok', axis=1, tiled=True)  6.19 us
    squeeze x1, local copies, waits for them, and re-layouts, shards(): w_qkv[layer_idx]  6.09 us
    another operation x5, other arithmetic  5.25 us
  transfers between devices with their start and end apart: 2, of which 1 were waited for; matrix products, arithmetic and copies ran while one was open for 40% of the time, Pallas kernels for 27%

profile of v1, /device:TPU:8, one launch (start us, length us, event | category | flops | bytes accessed | tf_op | source)
XLA Modules:
  0.0 227.4 jit_solution(7369477883438638276)
XLA Ops:
  7.2 2.4 %fusion.28 = (bf16[1,2,1,384,384]{4,3,2,1,0:T(8,128)(2,1)}, bf16[1,2,1,384,384]{4,3,2,1,0:T(8,128)(2,1)}) fusion(bf16[2,2,1,384,384]{4,3,2,1,0:T(8,128)(2,1)} %param.18), kind=kLoop, calls=%fused_computation.101 | loop fusion | bytes 2359296 | tf_op jit(solution)/shard_map/slice | solution.py:349
  11.1 6.1 %slice_bitcast_fusion = (bf16[3072,3,384]{2,0,1:T(8,128)(2,1)S(1)}, bf16[3072,3,384]{2,0,1:T(8,128)(2,1)S(1)}) fusion(bf16[2,3072,3,384]{3,1,2,0:T(8,128)(2,1)} %param.13), kind=kLoop, calls=%fused_computation | loop fusion | bytes 28311552 | tf_op jit(solution)/shard_map/squeeze | solution.py:358
  17.2 5.2 %slice_bitcast_fusion.2 = (bf16[384,3072]{0,1:T(8,128)(2,1)}, bf16[384,3072]{0,1:T(8,128)(2,1)}, bf16[384,3072]{0,1:T(8,128)(2,1)}, bf16[384,3072]{0,1:T(8,128)(...) fusion(bf16[3072,3,384]{2,0,1:T(8,128)(2,1)S(1)} %get-tuple-element.20, ...), kind=kLoop, calls=%fused_computation.23 | loop fusion | bytes 28311552 | tf_op jit(solution)/shard_map/dot_general | solution.py:62
  22.4 4.5 %copy.47 = bf16[384,3072]{1,0:T(8,128)(2,1)} copy(bf16[384,3072]{0,1:T(8,128)(2,1)} %get-tuple-element.65) | data formatting | bytes 4718592 | tf_op jit(solution)/shard_map/dot_general | solution.py:62
  28.1 1.2 fusion.13
  29.9 1.4 multiply_reduce_fusion.3
  32.2 1.4 reshape.471
  33.6 4.3 %copy.48 = bf16[384,3072]{1,0:T(8,128)(2,1)} copy(bf16[384,3072]{0,1:T(8,128)(2,1)} %get-tuple-element.66) | data formatting | bytes 4718592 | tf_op jit(solution)/shard_map/dot_general | solution.py:62
  37.9 3.8 %multiply_reduce_fusion.2 = (f32[384,3]{0,1:T(4,128)S(1)}, f32[384,3,128]{0,2,1:T(8,128)S(1)}) fusion(bf16[384,3072,1]{1,0,2:T(8,128)(2,1)} %copy-done.6, bf16[3,128,3072]{2,1,0:T(8,128)(2,1)} %bitcast.142), kind=kOutput, calls=%fused_computation.48 | convolution fusion | flops 906263424 | bytes 5313024 | tf_op jit(solution)/shard_map/dot_general | solution.py:62
  42.7 2.2 reshape.472
  47.6 3.4 %subtract_convert_fusion.2 = (bf16[384,3,64,1]{0,3,2,1:T(2,128)(2,1)S(1)}, bf16[384,3,64,1]{0,3,2,1:T(2,128)(2,1)S(1)}, bf16[384,3,64,1]{0,3,2,1:T(2,128)(2,1)}, bf16[384,3,64,1]{0,3,2,1:T(2,128)(2,1)}) fusion(f32[384,3,64,2]{0,3,2,1:T(2,128)} %reshape.472, f32[384,64]{0,1:T(8,128)S(1)} %get-tuple-element.52, f32[384,64]{0,1:T(8,128)S(1)} %get-tuple-element.51, ...), kind=kLoop, calls=%fused_computation.64 | loop fusion | flops 1179648 | bytes 1966080 | tf_op jit(solution)/shard_map/convert.4
  52.7 1.7 pad_maximum_fusion
  56.3 4.3 %copy.49 = bf16[384,3072]{1,0:T(8,128)(2,1)} copy(bf16[384,3072]{0,1:T(8,128)(2,1)} %get-tuple-element.67) | data formatting | bytes 4718592 | tf_op jit(solution)/shard_map/dot_general | solution.py:62
  60.6 3.9 %convolution_convert_fusion.3 = bf16[384,3,128]{0,2,1:T(8,128)(2,1)S(1)} fusion(bf16[384,3072,1]{1,0,2:T(8,128)(2,1)} %copy-done.6, bf16[3,128,3072]{2,1,0:T(8,128)(2,1)} %bitcast.143), kind=kOutput, calls=%fused_computation.34 | convolution fusion | flops 906117120 | bytes 5013504 | tf_op jit(solution)/shard_map/dot_general | solution.py:62
  65.4 4.3 %copy.55 = bf16[384,3072]{1,0:T(8,128)(2,1)} copy(bf16[384,3072]{0,1:T(8,128)(2,1)} %get-tuple-element.22) | data formatting | bytes 4718592 | tf_op jit(solution)/shard_map/dot_general | solution.py:62
  69.7 4.4 %copy.53 = bf16[384,3072]{1,0:T(8,128)(2,1)} copy(bf16[384,3072]{0,1:T(8,128)(2,1)} %get-tuple-element.24) | data formatting | bytes 4718592 | tf_op jit(solution)/shard_map/dot_general | solution.py:62
  74.1 4.3 %copy.54 = bf16[384,3072]{1,0:T(8,128)(2,1)} copy(bf16[384,3072]{0,1:T(8,128)(2,1)} %get-tuple-element.23) | data formatting | bytes 4718592 | tf_op jit(solution)/shard_map/dot_general | solution.py:62
  78.5 1.2 fusion.27.allow_ref
  79.7 1.3 iota_reduce_fusion
  81.0 1.1 compare_select_fusion.fetch_ref
  82.1 6.2 %all-gather.5.cloned.1.call-done = bf16[1,2,16,384,384]{4,3,2,1,0:T(8,128)(2,1)} async-done(((bf16[1,2,1,384,384]{4,3,2,1,0:T(8,128)(2,1)}), bf16[1,2,16,384,384]{4,3,2,1,0:T(8,128)(2,1)}) %all-gather.5.cloned.1.call-update) | async-done | bytes 9437200 | tf_op jit(solution)/shard_map/all_gather | solution.py:349
  88.3 23.0 %shard_map.130 = bf16[384,384]{1,0:T(8,128)(2,1)} custom-call(s32[16]{0:T(128)} %compare_select_fusion.fetch_ref, s32[16]{0:T(128)} %fusion.27.allow_ref, bf16[384,384]{1,0:T(8,128)(2,1)} %copy.50.q_ref, bf16[384,384]{1,0:T(8,128)(2,1)} %copy.51.kf_ref, bf16[384,384]{1,0:T(8,128)(2,1)} %copy.52.vf_ref, bf16[2,16,384,384]{3,2,1,0:T(8,128)(2,1)} %bitcast.132, ...), custom_call_target="tpu_custom_call" | custom-call | tf_op jit(solution)/shard_map/pallas_call | solution.py:141
  111.2 3.2 %convolution_convert_fusion.1.part_ref = bf16[384,3072]{1,0:T(8,128)(2,1)S(1)} fusion(bf16[384,384]{1,0:T(8,128)(2,1)} %shard_map.130, bf16[2,384,3072]{2,1,0:T(8,128)(2,1)} %param.14), kind=kOutput, calls=%fused_computation.21 | convolution fusion | flops 907149312 | bytes 5013504 | tf_op jit(solution)/shard_map/dot_general | solution.py:366
  114.5 39.1 %shard_map.131 = (bf16[48,3072]{1,0:T(8,128)(2,1)S(1)}, bf16[2,4,48,3072]{3,2,1,0:T(8,128)(2,1)S(1)}) custom-call(bf16[384,3072]{1,0:T(8,128)(2,1)S(1)} %convolution_convert_fusion.1.part_ref, bf16[48,3072]{1,0:T(8,128)(2,1)S(1)} %dynamic-slice_bitcast_fusion.own_ref, f32[1,3072]{1,0:T(1,128)S(1)} %get-tuple-element.44.gate_ref), custom_call_target="tpu_custom_call" | custom-call | tf_op jit(solution)/shard_map/pallas_call | solution.py:294
  154.7 1.2 fusion.5
  156.4 1.4 convolution_convert_fusion.2
  158.7 3.1 %multiply_reduce_fusion.1 = (f32[384,3]{0,1:T(4,128)S(1)}, f32[384,3,128]{0,2,1:T(8,128)S(1)}) fusion(bf16[384,3072,1]{1,0,2:T(8,128)(2,1)} %bitcast.140, bf16[3,128,3072]{2,1,0:T(8,128)(2,1)S(1)} %bitcast.136), kind=kOutput, calls=%fused_computation.46 | convolution fusion | flops 906263424 | bytes 5313024 | tf_op jit(solution)/shard_map/dot_general | solution.py:62
  162.3 3.8 %multiply_reduce_fusion = (f32[384,3]{0,1:T(4,128)S(1)}, f32[384,3,128]{0,2,1:T(8,128)S(1)}) fusion(bf16[384,3072,1]{1,0,2:T(8,128)(2,1)} %bitcast.141, bf16[3,128,3072]{2,1,0:T(8,128)(2,1)} %bitcast.135), kind=kOutput, calls=%fused_computation.44 | convolution fusion | flops 906263424 | bytes 5313024 | tf_op jit(solution)/shard_map/dot_general | solution.py:62
  167.0 1.6 subtract_convert_fusion
  172.0 23.0 %shard_map.132 = bf16[384,384]{1,0:T(8,128)(2,1)} custom-call(s32[16]{0:T(128)} %compare_select_fusion.fetch_ref, s32[16]{0:T(128)} %fusion.27.allow_ref, bf16[384,384]{1,0:T(8,128)(2,1)} %copy.56.q_ref, bf16[384,384]{1,0:T(8,128)(2,1)} %copy.57.kf_ref, bf16[384,384]{1,0:T(8,128)(2,1)} %copy.58.vf_ref, bf16[2,16,384,384]{3,2,1,0:T(8,128)(2,1)} %bitcast.130, ...), custom_call_target="tpu_custom_call" | custom-call | tf_op jit(solution)/shard_map/pallas_call | solution.py:141
  194.9 3.2 %convolution_convert_fusion.part_ref = bf16[384,3072]{1,0:T(8,128)(2,1)S(1)} fusion(bf16[384,384]{1,0:T(8,128)(2,1)} %shard_map.132, bf16[2,384,3072]{2,1,0:T(8,128)(2,1)} %param.14), kind=kOutput, calls=%fused_computation.20 | convolution fusion | flops 907149312 | bytes 5013504 | tf_op jit(solution)/shard_map/dot_general | solution.py:366
  198.1 20.1 %shard_map.133 = f32[48,3072]{1,0:T(8,128)S(1)} custom-call(bf16[384,3072]{1,0:T(8,128)(2,1)S(1)} %convolution_convert_fusion.part_ref, bf16[48,3072]{1,0:T(8,128)(2,1)S(1)} %get-tuple-element.7.own_ref, f32[1,3072]{1,0:T(1,128)S(1)} %get-tuple-element.43.gate_ref), custom_call_target="tpu_custom_call" | custom-call | tf_op jit(solution)/shard_map/pallas_call | solution.py:294
  (87 shorter events, 20.4 us)
Async XLA Ops:
  7.2 212.5 %copy-start = (bf16[3072,64]{0,1:T(8,128)(2,1)S(1)}, bf16[3072,64]{0,1:T(8,128)(2,1)}, u32[]{:S(2)}) copy-start(bf16[3072,64]{0,1:T(8,128)(2,1)} %param.15) | copy-start | bytes 1179652
  7.2 81.1 %all-gather.5.cloned.1.call-start = ((), (), s32[]{:S(2)}) async-start(), calls=%async_computation | async-start | bytes 10027008 | tf_op jit(solution)/shard_map/all_gather | solution.py:349
  9.7 162.3 %all-gather.7.cloned.1.call-start = ((), (), s32[]{:S(2)}) async-start(), calls=%async_computation.1 | async-start | bytes 10027008 | tf_op jit(solution)/shard_map/all_gather | solution.py:349
  22.4 4.5 %copy-start.10 = (f32[2,2,128]{2,1,0:T(2,128)S(1)}, f32[2,2,128]{2,1,0:T(2,128)}, u32[]{:S(2)}) copy-start(f32[2,2,128]{2,1,0:T(2,128)} %param.16) | copy-start | bytes 6148
  22.4 4.5 %copy-start.1 = (bf16[1,384,3072]{2,1,0:T(8,128)(2,1)S(1)}, bf16[1,384,3072]{2,1,0:T(8,128)(2,1)}, u32[]{:S(2)}) copy-start(bf16[1,384,3072]{2,1,0:T(8,128)(2,1)} %param.11) | copy-start | bytes 7077892
  26.9 1.2 copy-start.9
  28.1 1.7 copy-start.4
  29.4 1.9 copy-start.6
  41.7 3.2 %copy-start.12 = (s32[4]{0:T(128)S(1)}, s32[4]{0:T(128)}, u32[]{:S(2)}) copy-start(s32[4]{0:T(128)} %param.19) | copy-start | bytes 52
  41.7 3.4 %copy-start.13 = (s32[16]{0:T(128)S(1)}, s32[16]{0:T(128)}, u32[]{:S(2)}) copy-start(s32[16]{0:T(128)} %param.20) | copy-start | bytes 196
  47.6 3.4 %copy-start.7 = (f32[384,64]{0,1:T(8,128)}, f32[384,64]{0,1:T(8,128)S(1)}, u32[]{:S(2)}) copy-start(f32[384,64]{0,1:T(8,128)S(1)} %get-tuple-element.52) | copy-start | bytes 294916
  154.7 1.7 copy-start.3
  155.9 1.9 copy-start.5
  156.4 2.3 %copy-start.2 = (bf16[384,3072]{1,0:T(8,128)(2,1)S(1)}, bf16[384,3072]{1,0:T(8,128)(2,1)}, u32[]{:S(2)}) copy-start(bf16[384,3072]{1,0:T(8,128)(2,1)} %copy.53) | copy-start | bytes 7077892
  166.1 0.9 copy-start.8
  198.1 21.5 %copy-start.11 = (f32[1,48,64]{2,1,0:T(8,128)S(1)}, f32[1,48,64]{2,1,0:T(8,128)}, u32[]{:S(2)}) copy-start(f32[1,48,64]{2,1,0:T(8,128)} %param.12) | copy-start | bytes 36868
Sparse Core Ops, SparseCore 0:
  10.2 78.0 all-gather.4
  90.4 75.2 all-gather.6

commit v2 on v1

--- a/solution.py
+++ b/solution.py
@@ -129,14 +129,14 @@
 
 def attend(queries, keys_fresh, values_fresh, stale, fetch, allow, head_dim):
     rows, features = queries.shape
-    slot_total = stale.shape[1]
+    slot_total = stale.shape[0]
     heads = features // head_dim
     whole = pl.BlockSpec((rows, features), lambda j, f, a: (0, 0))
     key_spec = pl.BlockSpec(
-        (None, None, rows, features), lambda j, f, a: (0, f[j], 0, 0)
+        (None, None, rows, features), lambda j, f, a: (f[j], 0, 0, 0)
     )
     value_spec = pl.BlockSpec(
-        (None, None, rows, features), lambda j, f, a: (1, f[j], 0, 0)
+        (None, None, rows, features), lambda j, f, a: (f[j], 1, 0, 0)
     )
     return pl.pallas_call(
         functools.partial(attention_kernel, head_dim),
@@ -346,7 +346,8 @@
     fetch = jnp.where(running >= 0, running, first_allowed).astype(jnp.int32)
     allow = allowed.astype(jnp.int32)
     stale_layers = [
-        lax.all_gather(stale_kv[layer], "tok", axis=1, tiled=True) for layer in range(layer_count)
+        lax.all_gather(jnp.swapaxes(stale_kv[layer], 0, 1), "tok", axis=0, tiled=True)
+        for layer in range(layer_count)
     ]
     current_full = hidden[0]
     own_input = lax.dynamic_slice_in_dim(current_full, group_index * own_rows, own_rows, 0)

time: 229 us -> 229 us (level)
  the two profiles are of different devices: /device:TPU:8 before, /device:TPU:48 now
where the time goes in v2:
time: 229 us; the launch traced here: 228 us
  Pallas kernels  107 us (47%)
  local copies, waits for them, and re-layouts  52.6 us (23%)
  matrix products  24.7 us (11%)
  other arithmetic  22.2 us (10%)
  between operations  15.8 us (7%)
  waiting for transfers between devices  5 us (2%)
    pallas_call x2, Pallas kernels, exchange(): pl.pallas_call(functools.partial(exchange_kernel, head_count, own_rows, g...  59.3 us
    pallas_call x2, Pallas kernels, attend(): pl.pallas_call(functools.partial(attention_kernel, head_dim), out_shape=j...  47.9 us
    dot_general x7, local copies, waits for them, and re-layouts, project(): jnp.dot(normed, weight[:, part, :], preferred_element_type=jnp.float32)  31.3 us
    dot_general x6, matrix products, project(): jnp.dot(normed, weight[:, part, :], preferred_element_type=jnp.float32)  17.4 us
    dot_general x2, matrix products, shards(): jnp.dot(attended, w_out[layer_idx], preferred_element_type=jnp.float32)  6.35 us
    squeeze x1, local copies, waits for them, and re-layouts, shards(): w_qkv[layer_idx]  6.09 us
    another operation x5, other arithmetic  5.25 us
  transfers between devices with their start and end apart: 2, of which 1 were waited for; matrix products, arithmetic and copies ran while one was open for 40% of the time, Pallas kernels for 28%

profile of v2, /device:TPU:48, one launch (start us, length us, event | category | flops | bytes accessed | tf_op | source)
XLA Modules:
  0.0 227.5 jit_solution(16255225035841252397)
XLA Ops:
  7.2 2.4 %fusion.28 = (bf16[1,2,1,384,384]{4,3,2,1,0:T(8,128)(2,1)}, bf16[1,2,1,384,384]{4,3,2,1,0:T(8,128)(2,1)}) fusion(bf16[2,2,1,384,384]{4,3,2,1,0:T(8,128)(2,1)} %param.18), kind=kLoop, calls=%fused_computation.101 | loop fusion | bytes 2359296 | tf_op jit(solution)/shard_map/slice | solution.py:349
  11.1 6.1 %slice_bitcast_fusion = (bf16[3072,3,384]{2,0,1:T(8,128)(2,1)S(1)}, bf16[3072,3,384]{2,0,1:T(8,128)(2,1)S(1)}) fusion(bf16[2,3072,3,384]{3,1,2,0:T(8,128)(2,1)} %param.13), kind=kLoop, calls=%fused_computation | loop fusion | bytes 28311552 | tf_op jit(solution)/shard_map/squeeze | solution.py:359
  17.2 5.2 %slice_bitcast_fusion.2 = (bf16[384,3072]{0,1:T(8,128)(2,1)}, bf16[384,3072]{0,1:T(8,128)(2,1)}, bf16[384,3072]{0,1:T(8,128)(2,1)}, bf16[384,3072]{0,1:T(8,128)(...) fusion(bf16[3072,3,384]{2,0,1:T(8,128)(2,1)S(1)} %get-tuple-element.23, ...), kind=kLoop, calls=%fused_computation.23 | loop fusion | bytes 28311552 | tf_op jit(solution)/shard_map/dot_general | solution.py:62
  22.4 4.5 %copy.65 = bf16[384,3072]{1,0:T(8,128)(2,1)} copy(bf16[384,3072]{0,1:T(8,128)(2,1)} %get-tuple-element.68) | data formatting | bytes 4718592 | tf_op jit(solution)/shard_map/dot_general | solution.py:62
  28.2 1.2 fusion.13
  29.9 1.4 multiply_reduce_fusion.3
  32.2 1.4 reshape.471
  33.6 4.3 %copy.66 = bf16[384,3072]{1,0:T(8,128)(2,1)} copy(bf16[384,3072]{0,1:T(8,128)(2,1)} %get-tuple-element.69) | data formatting | bytes 4718592 | tf_op jit(solution)/shard_map/dot_general | solution.py:62
  37.9 3.8 %multiply_reduce_fusion.2 = (f32[384,3]{0,1:T(4,128)S(1)}, f32[384,3,128]{0,2,1:T(8,128)S(1)}) fusion(bf16[384,3072,1]{1,0,2:T(8,128)(2,1)} %copy-done.6, bf16[3,128,3072]{2,1,0:T(8,128)(2,1)} %bitcast.142), kind=kOutput, calls=%fused_computation.48 | convolution fusion | flops 906263424 | bytes 5313024 | tf_op jit(solution)/shard_map/dot_general | solution.py:62
  42.7 2.2 reshape.472
  47.6 3.4 %subtract_convert_fusion.2 = (bf16[384,3,64,1]{0,3,2,1:T(2,128)(2,1)S(1)}, bf16[384,3,64,1]{0,3,2,1:T(2,128)(2,1)S(1)}, bf16[384,3,64,1]{0,3,2,1:T(2,128)(2,1)}, bf16[384,3,64,1]{0,3,2,1:T(2,128)(2,1)}) fusion(f32[384,3,64,2]{0,3,2,1:T(2,128)} %reshape.472, f32[384,64]{0,1:T(8,128)S(1)} %get-tuple-element.55, f32[384,64]{0,1:T(8,128)S(1)} %get-tuple-element.54, ...), kind=kLoop, calls=%fused_computation.64 | loop fusion | flops 1179648 | bytes 1966080 | tf_op jit(solution)/shard_map/convert.4
  52.7 1.7 pad_maximum_fusion
  56.3 4.3 %copy.67 = bf16[384,3072]{1,0:T(8,128)(2,1)} copy(bf16[384,3072]{0,1:T(8,128)(2,1)} %get-tuple-element.70) | data formatting | bytes 4718592 | tf_op jit(solution)/shard_map/dot_general | solution.py:62
  60.6 3.9 %convolution_convert_fusion.3 = bf16[384,3,128]{0,2,1:T(8,128)(2,1)S(1)} fusion(bf16[384,3072,1]{1,0,2:T(8,128)(2,1)} %copy-done.6, bf16[3,128,3072]{2,1,0:T(8,128)(2,1)} %bitcast.143), kind=kOutput, calls=%fused_computation.34 | convolution fusion | flops 906117120 | bytes 5013504 | tf_op jit(solution)/shard_map/dot_general | solution.py:62
  65.4 4.3 %copy.73 = bf16[384,3072]{1,0:T(8,128)(2,1)} copy(bf16[384,3072]{0,1:T(8,128)(2,1)} %get-tuple-element.25) | data formatting | bytes 4718592 | tf_op jit(solution)/shard_map/dot_general | solution.py:62
  69.8 4.3 %copy.71 = bf16[384,3072]{1,0:T(8,128)(2,1)} copy(bf16[384,3072]{0,1:T(8,128)(2,1)} %get-tuple-element.27) | data formatting | bytes 4718592 | tf_op jit(solution)/shard_map/dot_general | solution.py:62
  74.1 4.3 %copy.72 = bf16[384,3072]{1,0:T(8,128)(2,1)} copy(bf16[384,3072]{0,1:T(8,128)(2,1)} %get-tuple-element.26) | data formatting | bytes 4718592 | tf_op jit(solution)/shard_map/dot_general | solution.py:62
  78.5 1.2 fusion.27.allow_ref
  79.8 1.3 iota_reduce_fusion
  81.0 1.1 compare_select_fusion.fetch_ref
  82.1 4.3 %all-gather.5.cloned.1.call-done = bf16[16,2,1,384,384]{4,3,2,1,0:T(8,128)(2,1)} async-done(((bf16[1,2,1,384,384]{4,3,2,1,0:T(8,128)(2,1)}), bf16[16,2,1,384,384]{4,3,2,1,0:T(8,128)(2,1)}) %all-gather.5.cloned.1.call-update) | async-done | bytes 9437200 | tf_op jit(solution)/shard_map/all_gather | solution.py:349
  86.4 24.0 %shard_map.130 = bf16[384,384]{1,0:T(8,128)(2,1)} custom-call(s32[16]{0:T(128)} %compare_select_fusion.fetch_ref, s32[16]{0:T(128)} %fusion.27.allow_ref, bf16[384,384]{1,0:T(8,128)(2,1)} %copy.68.q_ref, bf16[384,384]{1,0:T(8,128)(2,1)} %copy.69.kf_ref, bf16[384,384]{1,0:T(8,128)(2,1)} %copy.70.vf_ref, bf16[16,2,384,384]{3,2,1,0:T(8,128)(2,1)} %bitcast.132, ...), custom_call_target="tpu_custom_call" | custom-call | tf_op jit(solution)/shard_map/pallas_call | solution.py:141
  110.4 3.2 %convolution_convert_fusion.1.part_ref = bf16[384,3072]{1,0:T(8,128)(2,1)S(1)} fusion(bf16[384,384]{1,0:T(8,128)(2,1)} %shard_map.130, bf16[2,384,3072]{2,1,0:T(8,128)(2,1)} %param.14), kind=kOutput, calls=%fused_computation.21 | convolution fusion | flops 907149312 | bytes 5013504 | tf_op jit(solution)/shard_map/dot_general | solution.py:367
  113.6 39.1 %shard_map.131 = (bf16[48,3072]{1,0:T(8,128)(2,1)S(1)}, bf16[2,4,48,3072]{3,2,1,0:T(8,128)(2,1)S(1)}) custom-call(bf16[384,3072]{1,0:T(8,128)(2,1)S(1)} %convolution_convert_fusion.1.part_ref, bf16[48,3072]{1,0:T(8,128)(2,1)S(1)} %dynamic-slice_bitcast_fusion.own_ref, f32[1,3072]{1,0:T(1,128)S(1)} %get-tuple-element.47.gate_ref), custom_call_target="tpu_custom_call" | custom-call | tf_op jit(solution)/shard_map/pallas_call | solution.py:294
  153.9 1.2 fusion.5
  155.6 1.4 convolution_convert_fusion.2
  157.9 3.1 %multiply_reduce_fusion.1 = (f32[384,3]{0,1:T(4,128)S(1)}, f32[384,3,128]{0,2,1:T(8,128)S(1)}) fusion(bf16[384,3072,1]{1,0,2:T(8,128)(2,1)} %bitcast.140, bf16[3,128,3072]{2,1,0:T(8,128)(2,1)S(1)} %bitcast.136), kind=kOutput, calls=%fused_computation.46 | convolution fusion | flops 906263424 | bytes 5313024 | tf_op jit(solution)/shard_map/dot_general | solution.py:62
  161.5 3.8 %multiply_reduce_fusion = (f32[384,3]{0,1:T(4,128)S(1)}, f32[384,3,128]{0,2,1:T(8,128)S(1)}) fusion(bf16[384,3072,1]{1,0,2:T(8,128)(2,1)} %bitcast.141, bf16[3,128,3072]{2,1,0:T(8,128)(2,1)} %bitcast.135), kind=kOutput, calls=%fused_computation.44 | convolution fusion | flops 906263424 | bytes 5313024 | tf_op jit(solution)/shard_map/dot_general | solution.py:62
  166.2 1.6 subtract_convert_fusion
  171.1 23.9 %shard_map.132 = bf16[384,384]{1,0:T(8,128)(2,1)} custom-call(s32[16]{0:T(128)} %compare_select_fusion.fetch_ref, s32[16]{0:T(128)} %fusion.27.allow_ref, bf16[384,384]{1,0:T(8,128)(2,1)} %copy.74.q_ref, bf16[384,384]{1,0:T(8,128)(2,1)} %copy.75.kf_ref, bf16[384,384]{1,0:T(8,128)(2,1)} %copy.76.vf_ref, bf16[16,2,384,384]{3,2,1,0:T(8,128)(2,1)} %bitcast.130, ...), custom_call_target="tpu_custom_call" | custom-call | tf_op jit(solution)/shard_map/pallas_call | solution.py:141
  195.1 3.2 %convolution_convert_fusion.part_ref = bf16[384,3072]{1,0:T(8,128)(2,1)S(1)} fusion(bf16[384,384]{1,0:T(8,128)(2,1)} %shard_map.132, bf16[2,384,3072]{2,1,0:T(8,128)(2,1)} %param.14), kind=kOutput, calls=%fused_computation.20 | convolution fusion | flops 907149312 | bytes 5013504 | tf_op jit(solution)/shard_map/dot_general | solution.py:367
  198.2 20.1 %shard_map.133 = f32[48,3072]{1,0:T(8,128)S(1)} custom-call(bf16[384,3072]{1,0:T(8,128)(2,1)S(1)} %convolution_convert_fusion.part_ref, bf16[48,3072]{1,0:T(8,128)(2,1)S(1)} %get-tuple-element.7.own_ref, f32[1,3072]{1,0:T(1,128)S(1)} %get-tuple-element.46.gate_ref), custom_call_target="tpu_custom_call" | custom-call | tf_op jit(solution)/shard_map/pallas_call | solution.py:294
  (87 shorter events, 20.4 us)
Async XLA Ops:
  7.2 212.6 %copy-start = (bf16[3072,64]{0,1:T(8,128)(2,1)S(1)}, bf16[3072,64]{0,1:T(8,128)(2,1)}, u32[]{:S(2)}) copy-start(bf16[3072,64]{0,1:T(8,128)(2,1)} %param.15) | copy-start | bytes 1179652
  7.2 79.2 %all-gather.5.cloned.1.call-start = ((), (), s32[]{:S(2)}) async-start(), calls=%async_computation | async-start | bytes 10027008 | tf_op jit(solution)/shard_map/all_gather | solution.py:349
  9.7 161.5 %all-gather.7.cloned.1.call-start = ((), (), s32[]{:S(2)}) async-start(), calls=%async_computation.1 | async-start | bytes 10027008 | tf_op jit(solution)/shard_map/all_gather | solution.py:349
  22.4 4.5 %copy-start.10 = (f32[2,2,128]{2,1,0:T(2,128)S(1)}, f32[2,2,128]{2,1,0:T(2,128)}, u32[]{:S(2)}) copy-start(f32[2,2,128]{2,1,0:T(2,128)} %param.16) | copy-start | bytes 6148
  22.4 4.5 %copy-start.1 = (bf16[1,384,3072]{2,1,0:T(8,128)(2,1)S(1)}, bf16[1,384,3072]{2,1,0:T(8,128)(2,1)}, u32[]{:S(2)}) copy-start(bf16[1,384,3072]{2,1,0:T(8,128)(2,1)} %param.11) | copy-start | bytes 7077892
  26.9 1.2 copy-start.9
  28.1 1.7 copy-start.4
  29.4 1.9 copy-start.6
  41.7 3.2 %copy-start.12 = (s32[4]{0:T(128)S(1)}, s32[4]{0:T(128)}, u32[]{:S(2)}) copy-start(s32[4]{0:T(128)} %param.19) | copy-start | bytes 52
  41.7 3.4 %copy-start.13 = (s32[16]{0:T(128)S(1)}, s32[16]{0:T(128)}, u32[]{:S(2)}) copy-start(s32[16]{0:T(128)} %param.20) | copy-start | bytes 196
  47.6 3.4 %copy-start.7 = (f32[384,64]{0,1:T(8,128)}, f32[384,64]{0,1:T(8,128)S(1)}, u32[]{:S(2)}) copy-start(f32[384,64]{0,1:T(8,128)S(1)} %get-tuple-element.55) | copy-start | bytes 294916
  153.9 1.7 copy-start.3
  155.1 1.9 copy-start.5
  155.6 2.3 %copy-start.2 = (bf16[384,3072]{1,0:T(8,128)(2,1)S(1)}, bf16[384,3072]{1,0:T(8,128)(2,1)}, u32[]{:S(2)}) copy-start(bf16[384,3072]{1,0:T(8,128)(2,1)} %copy.71) | copy-start | bytes 7077892
  165.3 0.9 copy-start.8
  198.2 21.5 %copy-start.11 = (f32[1,48,64]{2,1,0:T(8,128)S(1)}, f32[1,48,64]{2,1,0:T(8,128)}, u32[]{:S(2)}) copy-start(f32[1,48,64]{2,1,0:T(8,128)} %param.12) | copy-start | bytes 36868
Sparse Core Ops, SparseCore 0:
  10.2 76.2 all-gather.4
  88.6 75.2 all-gather.6

commit v3 on v2

--- a/solution.py
+++ b/solution.py
@@ -82,10 +82,14 @@
     scaling = 1.0 / math.sqrt(head_dim)
     contract = (((1,), (1,)), ((), ()))
 
+    def lanes_of(h):
+        return pl.ds(pl.multiple_of(h * head_dim, head_dim), head_dim)
+
     @pl.when(slot == 0)
     def _fresh():
-        for h in range(heads):
-            lanes = slice(h * head_dim, (h + 1) * head_dim)
+        @pl.loop(0, heads)
+        def _head(h):
+            lanes = lanes_of(h)
             scores = (
                 lax.dot_general(
                     q_ref[:, lanes], kf_ref[:, lanes], contract, preferred_element_type=jnp.float32
@@ -102,8 +106,9 @@
 
     @pl.when(allow_ref[slot] != 0)
     def _stale():
-        for h in range(heads):
-            lanes = slice(h * head_dim, (h + 1) * head_dim)
+        @pl.loop(0, heads)
+        def _head(h):
+            lanes = lanes_of(h)
             scores = (
                 lax.dot_general(
                     q_ref[:, lanes], ks_ref[:, lanes], contract, preferred_element_type=jnp.float32
@@ -122,9 +127,9 @@
 
     @pl.when(slot == pl.num_programs(0) - 1)
     def _finish():
-        for h in range(heads):
-            lanes = slice(h * head_dim, (h + 1) * head_dim)
-            o_ref[:, lanes] = (acc_sc[h] / l_sc[h]).astype(o_ref.dtype)
+        @pl.loop(0, heads)
+        def _head(h):
+            o_ref[:, lanes_of(h)] = (acc_sc[h] / l_sc[h]).astype(o_ref.dtype)
 
 
 def attend(queries, keys_fresh, values_fresh, stale, fetch, allow, head_dim):

time: 229 us -> 233 us (1.017)
  the two profiles are of different devices: /device:TPU:48 before, /device:TPU:8 now
where the time goes in v3:
time: 233 us; the launch traced here: 230 us
  Pallas kernels  108 us (46%)
  local copies, waits for them, and re-layouts  52.6 us (23%)
  matrix products  24.6 us (11%)
  other arithmetic  22.2 us (10%)
  between operations  15.8 us (7%)
  waiting for transfers between devices  6.9 us (3%)
    pallas_call x2, Pallas kernels, exchange(): pl.pallas_call(functools.partial(exchange_kernel, head_count, own_rows, g...  59.2 us
    pallas_call x2, Pallas kernels, attend(): pl.pallas_call(functools.partial(attention_kernel, head_dim), out_shape=j...  49 us
    dot_general x7, local copies, waits for them, and re-layouts, project(): jnp.dot(normed, weight[:, part, :], preferred_element_type=jnp.float32)  31.2 us
    dot_general x6, matrix products, project(): jnp.dot(normed, weight[:, part, :], preferred_element_type=jnp.float32)  17.4 us
    dot_general x2, matrix products, shards(): jnp.dot(attended, w_out[layer_idx], preferred_element_type=jnp.float32)  6.32 us
    all_gather x2, waiting for transfers between devices, shards(): lax.all_gather(jnp.swapaxes(stale_kv[layer], 0, 1), 'tok', axis=0, tiled=...  6.19 us
    squeeze x1, local copies, waits for them, and re-layouts, shards(): w_qkv[layer_idx]  6.09 us
    another operation x5, other arithmetic  5.25 us
  transfers between devices with their start and end apart: 2, of which 1 were waited for; matrix products, arithmetic and copies ran while one was open for 39% of the time, Pallas kernels for 28%

profile of v3, /device:TPU:8, one launch (start us, length us, event | category | flops | bytes accessed | tf_op | source)
XLA Modules:
  0.0 230.4 jit_solution(5235980039360544644)
XLA Ops:
  7.2 2.4 %fusion.28 = (bf16[1,2,1,384,384]{4,3,2,1,0:T(8,128)(2,1)}, bf16[1,2,1,384,384]{4,3,2,1,0:T(8,128)(2,1)}) fusion(bf16[2,2,1,384,384]{4,3,2,1,0:T(8,128)(2,1)} %param.18), kind=kLoop, calls=%fused_computation.101 | loop fusion | bytes 2359296 | tf_op jit(solution)/shard_map/slice | solution.py:354
  11.1 6.1 %slice_bitcast_fusion = (bf16[3072,3,384]{2,0,1:T(8,128)(2,1)S(1)}, bf16[3072,3,384]{2,0,1:T(8,128)(2,1)S(1)}) fusion(bf16[2,3072,3,384]{3,1,2,0:T(8,128)(2,1)} %param.13), kind=kLoop, calls=%fused_computation | loop fusion | bytes 28311552 | tf_op jit(solution)/shard_map/squeeze | solution.py:364
  17.2 5.2 %slice_bitcast_fusion.2 = (bf16[384,3072]{0,1:T(8,128)(2,1)}, bf16[384,3072]{0,1:T(8,128)(2,1)}, bf16[384,3072]{0,1:T(8,128)(2,1)}, bf16[384,3072]{0,1:T(8,128)(...) fusion(bf16[3072,3,384]{2,0,1:T(8,128)(2,1)S(1)} %get-tuple-element.23, ...), kind=kLoop, calls=%fused_computation.23 | loop fusion | bytes 28311552 | tf_op jit(solution)/shard_map/dot_general | solution.py:62
  22.4 4.5 %copy.65 = bf16[384,3072]{1,0:T(8,128)(2,1)} copy(bf16[384,3072]{0,1:T(8,128)(2,1)} %get-tuple-element.68) | data formatting | bytes 4718592 | tf_op jit(solution)/shard_map/dot_general | solution.py:62
  28.1 1.2 fusion.13
  29.8 1.4 multiply_reduce_fusion.3
  32.2 1.4 reshape.471
  33.6 4.3 %copy.66 = bf16[384,3072]{1,0:T(8,128)(2,1)} copy(bf16[384,3072]{0,1:T(8,128)(2,1)} %get-tuple-element.69) | data formatting | bytes 4718592 | tf_op jit(solution)/shard_map/dot_general | solution.py:62
  37.9 3.8 %multiply_reduce_fusion.2 = (f32[384,3]{0,1:T(4,128)S(1)}, f32[384,3,128]{0,2,1:T(8,128)S(1)}) fusion(bf16[384,3072,1]{1,0,2:T(8,128)(2,1)} %copy-done.6, bf16[3,128,3072]{2,1,0:T(8,128)(2,1)} %bitcast.142), kind=kOutput, calls=%fused_computation.48 | convolution fusion | flops 906263424 | bytes 5313024 | tf_op jit(solution)/shard_map/dot_general | solution.py:62
  42.7 2.2 reshape.472
  47.6 3.4 %subtract_convert_fusion.2 = (bf16[384,3,64,1]{0,3,2,1:T(2,128)(2,1)S(1)}, bf16[384,3,64,1]{0,3,2,1:T(2,128)(2,1)S(1)}, bf16[384,3,64,1]{0,3,2,1:T(2,128)(2,1)}, bf16[384,3,64,1]{0,3,2,1:T(2,128)(2,1)}) fusion(f32[384,3,64,2]{0,3,2,1:T(2,128)} %reshape.472, f32[384,64]{0,1:T(8,128)S(1)} %get-tuple-element.55, f32[384,64]{0,1:T(8,128)S(1)} %get-tuple-element.54, ...), kind=kLoop, calls=%fused_computation.64 | loop fusion | flops 1179648 | bytes 1966080 | tf_op jit(solution)/shard_map/convert.4
  52.7 1.7 pad_maximum_fusion
  56.3 4.3 %copy.67 = bf16[384,3072]{1,0:T(8,128)(2,1)} copy(bf16[384,3072]{0,1:T(8,128)(2,1)} %get-tuple-element.70) | data formatting | bytes 4718592 | tf_op jit(solution)/shard_map/dot_general | solution.py:62
  60.6 3.9 %convolution_convert_fusion.3 = bf16[384,3,128]{0,2,1:T(8,128)(2,1)S(1)} fusion(bf16[384,3072,1]{1,0,2:T(8,128)(2,1)} %copy-done.6, bf16[3,128,3072]{2,1,0:T(8,128)(2,1)} %bitcast.143), kind=kOutput, calls=%fused_computation.34 | convolution fusion | flops 906117120 | bytes 5013504 | tf_op jit(solution)/shard_map/dot_general | solution.py:62
  65.4 4.3 %copy.73 = bf16[384,3072]{1,0:T(8,128)(2,1)} copy(bf16[384,3072]{0,1:T(8,128)(2,1)} %get-tuple-element.25) | data formatting | bytes 4718592 | tf_op jit(solution)/shard_map/dot_general | solution.py:62
  69.7 4.4 %copy.71 = bf16[384,3072]{1,0:T(8,128)(2,1)} copy(bf16[384,3072]{0,1:T(8,128)(2,1)} %get-tuple-element.27) | data formatting | bytes 4718592 | tf_op jit(solution)/shard_map/dot_general | solution.py:62
  74.1 4.3 %copy.72 = bf16[384,3072]{1,0:T(8,128)(2,1)} copy(bf16[384,3072]{0,1:T(8,128)(2,1)} %get-tuple-element.26) | data formatting | bytes 4718592 | tf_op jit(solution)/shard_map/dot_general | solution.py:62
  78.5 1.2 fusion.27.allow_ref
  79.7 1.3 iota_reduce_fusion
  81.0 1.1 compare_select_fusion.fetch_ref
  82.1 6.2 %all-gather.5.cloned.1.call-done = bf16[16,2,1,384,384]{4,3,2,1,0:T(8,128)(2,1)} async-done(((bf16[1,2,1,384,384]{4,3,2,1,0:T(8,128)(2,1)}), bf16[16,2,1,384,384]{4,3,2,1,0:T(8,128)(2,1)}) %all-gather.5.cloned.1.call-update) | async-done | bytes 9437200 | tf_op jit(solution)/shard_map/all_gather | solution.py:354
  88.3 24.5 %shard_map.130 = bf16[384,384]{1,0:T(8,128)(2,1)} custom-call(s32[16]{0:T(128)} %compare_select_fusion.fetch_ref, s32[16]{0:T(128)} %fusion.27.allow_ref, bf16[384,384]{1,0:T(8,128)(2,1)} %copy.68.q_ref, bf16[384,384]{1,0:T(8,128)(2,1)} %copy.69.kf_ref, bf16[384,384]{1,0:T(8,128)(2,1)} %copy.70.vf_ref, bf16[16,2,384,384]{3,2,1,0:T(8,128)(2,1)} %bitcast.132, ...), custom_call_target="tpu_custom_call" | custom-call | tf_op jit(solution)/shard_map/pallas_call | solution.py:146
  112.8 3.2 %convolution_convert_fusion.1.part_ref = bf16[384,3072]{1,0:T(8,128)(2,1)S(1)} fusion(bf16[384,384]{1,0:T(8,128)(2,1)} %shard_map.130, bf16[2,384,3072]{2,1,0:T(8,128)(2,1)} %param.14), kind=kOutput, calls=%fused_computation.21 | convolution fusion | flops 907149312 | bytes 5013504 | tf_op jit(solution)/shard_map/dot_general | solution.py:372
  116.0 39.1 %shard_map.131 = (bf16[48,3072]{1,0:T(8,128)(2,1)S(1)}, bf16[2,4,48,3072]{3,2,1,0:T(8,128)(2,1)S(1)}) custom-call(bf16[384,3072]{1,0:T(8,128)(2,1)S(1)} %convolution_convert_fusion.1.part_ref, bf16[48,3072]{1,0:T(8,128)(2,1)S(1)} %dynamic-slice_bitcast_fusion.own_ref, f32[1,3072]{1,0:T(1,128)S(1)} %get-tuple-element.47.gate_ref), custom_call_target="tpu_custom_call" | custom-call | tf_op jit(solution)/shard_map/pallas_call | solution.py:299
  156.2 1.2 fusion.5
  157.9 1.4 convolution_convert_fusion.2
  160.2 3.1 %multiply_reduce_fusion.1 = (f32[384,3]{0,1:T(4,128)S(1)}, f32[384,3,128]{0,2,1:T(8,128)S(1)}) fusion(bf16[384,3072,1]{1,0,2:T(8,128)(2,1)} %bitcast.140, bf16[3,128,3072]{2,1,0:T(8,128)(2,1)S(1)} %bitcast.136), kind=kOutput, calls=%fused_computation.46 | convolution fusion | flops 906263424 | bytes 5313024 | tf_op jit(solution)/shard_map/dot_general | solution.py:62
  163.8 3.8 %multiply_reduce_fusion = (f32[384,3]{0,1:T(4,128)S(1)}, f32[384,3,128]{0,2,1:T(8,128)S(1)}) fusion(bf16[384,3072,1]{1,0,2:T(8,128)(2,1)} %bitcast.141, bf16[3,128,3072]{2,1,0:T(8,128)(2,1)} %bitcast.135), kind=kOutput, calls=%fused_computation.44 | convolution fusion | flops 906263424 | bytes 5313024 | tf_op jit(solution)/shard_map/dot_general | solution.py:62
  168.5 1.6 subtract_convert_fusion
  173.4 24.5 %shard_map.132 = bf16[384,384]{1,0:T(8,128)(2,1)} custom-call(s32[16]{0:T(128)} %compare_select_fusion.fetch_ref, s32[16]{0:T(128)} %fusion.27.allow_ref, bf16[384,384]{1,0:T(8,128)(2,1)} %copy.74.q_ref, bf16[384,384]{1,0:T(8,128)(2,1)} %copy.75.kf_ref, bf16[384,384]{1,0:T(8,128)(2,1)} %copy.76.vf_ref, bf16[16,2,384,384]{3,2,1,0:T(8,128)(2,1)} %bitcast.130, ...), custom_call_target="tpu_custom_call" | custom-call | tf_op jit(solution)/shard_map/pallas_call | solution.py:146
  198.0 3.2 %convolution_convert_fusion.part_ref = bf16[384,3072]{1,0:T(8,128)(2,1)S(1)} fusion(bf16[384,384]{1,0:T(8,128)(2,1)} %shard_map.132, bf16[2,384,3072]{2,1,0:T(8,128)(2,1)} %param.14), kind=kOutput, calls=%fused_computation.20 | convolution fusion | flops 907149312 | bytes 5013504 | tf_op jit(solution)/shard_map/dot_general | solution.py:372
  201.1 20.1 %shard_map.133 = f32[48,3072]{1,0:T(8,128)S(1)} custom-call(bf16[384,3072]{1,0:T(8,128)(2,1)S(1)} %convolution_convert_fusion.part_ref, bf16[48,3072]{1,0:T(8,128)(2,1)S(1)} %get-tuple-element.7.own_ref, f32[1,3072]{1,0:T(1,128)S(1)} %get-tuple-element.46.gate_ref), custom_call_target="tpu_custom_call" | custom-call | tf_op jit(solution)/shard_map/pallas_call | solution.py:299
  (87 shorter events, 20.4 us)
Async XLA Ops:
  7.2 215.5 %copy-start = (bf16[3072,64]{0,1:T(8,128)(2,1)S(1)}, bf16[3072,64]{0,1:T(8,128)(2,1)}, u32[]{:S(2)}) copy-start(bf16[3072,64]{0,1:T(8,128)(2,1)} %param.15) | copy-start | bytes 1179652
  7.2 81.1 %all-gather.5.cloned.1.call-start = ((), (), s32[]{:S(2)}) async-start(), calls=%async_computation | async-start | bytes 10027008 | tf_op jit(solution)/shard_map/all_gather | solution.py:354
  9.7 163.8 %all-gather.7.cloned.1.call-start = ((), (), s32[]{:S(2)}) async-start(), calls=%async_computation.1 | async-start | bytes 10027008 | tf_op jit(solution)/shard_map/all_gather | solution.py:354
  22.4 4.5 %copy-start.10 = (f32[2,2,128]{2,1,0:T(2,128)S(1)}, f32[2,2,128]{2,1,0:T(2,128)}, u32[]{:S(2)}) copy-start(f32[2,2,128]{2,1,0:T(2,128)} %param.16) | copy-start | bytes 6148
  22.4 4.5 %copy-start.1 = (bf16[1,384,3072]{2,1,0:T(8,128)(2,1)S(1)}, bf16[1,384,3072]{2,1,0:T(8,128)(2,1)}, u32[]{:S(2)}) copy-start(bf16[1,384,3072]{2,1,0:T(8,128)(2,1)} %param.11) | copy-start | bytes 7077892
  26.9 1.2 copy-start.9
  28.1 1.7 copy-start.4
  29.4 1.9 copy-start.6
  41.7 3.2 %copy-start.12 = (s32[4]{0:T(128)S(1)}, s32[4]{0:T(128)}, u32[]{:S(2)}) copy-start(s32[4]{0:T(128)} %param.19) | copy-start | bytes 52
  41.7 3.4 %copy-start.13 = (s32[16]{0:T(128)S(1)}, s32[16]{0:T(128)}, u32[]{:S(2)}) copy-start(s32[16]{0:T(128)} %param.20) | copy-start | bytes 196
  47.6 3.4 %copy-start.7 = (f32[384,64]{0,1:T(8,128)}, f32[384,64]{0,1:T(8,128)S(1)}, u32[]{:S(2)}) copy-start(f32[384,64]{0,1:T(8,128)S(1)} %get-tuple-element.55) | copy-start | bytes 294916
  156.2 1.7 copy-start.3
  157.4 1.9 copy-start.5
  157.9 2.3 %copy-start.2 = (bf16[384,3072]{1,0:T(8,128)(2,1)S(1)}, bf16[384,3072]{1,0:T(8,128)(2,1)}, u32[]{:S(2)}) copy-start(bf16[384,3072]{1,0:T(8,128)(2,1)} %copy.71) | copy-start | bytes 7077892
  167.6 0.9 copy-start.8
  201.1 21.5 %copy-start.11 = (f32[1,48,64]{2,1,0:T(8,128)S(1)}, f32[1,48,64]{2,1,0:T(8,128)}, u32[]{:S(2)}) copy-start(f32[1,48,64]{2,1,0:T(8,128)} %param.12) | copy-start | bytes 36868
Sparse Core Ops, SparseCore 0:
  10.2 78.0 all-gather.4
  90.4 75.1 all-gather.6

commit v4 on v2

--- a/solution.py
+++ b/solution.py
@@ -158,7 +158,7 @@
 
 def exchange_kernel(head_count, own_rows, gather, part_ref, own_ref, gate_ref, *rest):
     if gather:
-        (out_ref, full_ref, near, far, mid, acc, far_in, spread,
+        (out_ref, full_ref, near, far, mid, acc,
          s1_send, s1_recv, s2_send, s2_recv, g1_send, g1_recv, g2_send, g2_recv) = rest
     else:
         (out_ref, near, far, mid, acc, s1_send, s1_recv, s2_send, s2_recv) = rest
@@ -177,23 +177,15 @@
             pl.semaphore_signal(barrier, inc=1, device_id=(section, h, tok), device_id_type=mesh_ids)
     pl.semaphore_wait(barrier, head_count)
 
-    first = pltpu.make_async_remote_copy(
-        src_ref=part_ref.at[pl.ds(pl.multiple_of(other * half, own_rows), half)],
-        dst_ref=near,
-        send_sem=s1_send,
-        recv_sem=s1_recv,
-        device_id=(other, head, tok),
-        device_id_type=mesh_ids,
-    )
-    first.start()
-    first.wait()
-    base = pl.multiple_of(section * half, own_rows)
-    for h in range(head_count):
-        rows = pl.ds(pl.multiple_of(base + h * own_rows, own_rows), own_rows)
-        mid[h] = (
-            part_ref[rows, :].astype(jnp.float32)
-            + near[h * own_rows:(h + 1) * own_rows, :].astype(jnp.float32)
-        ).astype(mid.dtype)
+    def near_copy(h):
+        return pltpu.make_async_remote_copy(
+            src_ref=part_ref.at[pl.ds(pl.multiple_of(other * half + h * own_rows, own_rows), own_rows)],
+            dst_ref=near.at[h],
+            send_sem=s1_send.at[h],
+            recv_sem=s1_recv.at[h],
+            device_id=(other, head, tok),
+            device_id_type=mesh_ids,
+        )
 
     def far_copy(h, slot):
         return pltpu.make_async_remote_copy(
@@ -206,12 +198,21 @@
         )
 
     for h in range(head_count):
+        near_copy(h).start()
+    base = pl.multiple_of(section * half, own_rows)
+    for h in range(head_count):
+        near_copy(h).wait()
+
         @pl.when(h != head)
         def _send():
+            rows = pl.ds(pl.multiple_of(base + h * own_rows, own_rows), own_rows)
+            mid[h] = (part_ref[rows, :].astype(jnp.float32) + near[h].astype(jnp.float32)).astype(
+                mid.dtype
+            )
             far_copy(h, head).start()
+
     mine = pl.ds(pl.multiple_of(base + head * own_rows, own_rows), own_rows)
-    near_mine = pl.ds(pl.multiple_of(head * own_rows, own_rows), own_rows)
-    acc[...] = part_ref[mine, :].astype(jnp.float32) + near[near_mine, :].astype(jnp.float32)
+    acc[...] = part_ref[mine, :].astype(jnp.float32) + near[head].astype(jnp.float32)
     for h in range(head_count):
         @pl.when(h != head)
         def _wait():
@@ -220,39 +221,45 @@
     if not gather:
         out_ref[...] = acc[...]
         return
-    spread[head] = (own_ref[...].astype(jnp.float32) + gate_ref[...] * acc[...]).astype(spread.dtype)
-    out_ref[...] = spread[head]
+    result = (own_ref[...].astype(jnp.float32) + gate_ref[...] * acc[...]).astype(full_ref.dtype)
+    full_ref[section, head] = result
+    out_ref[...] = result
 
     def share_copy(h, slot):
         return pltpu.make_async_remote_copy(
-            src_ref=spread.at[head],
-            dst_ref=far_in.at[slot],
+            src_ref=full_ref.at[section, head],
+            dst_ref=full_ref.at[section, slot],
             send_sem=g1_send.at[h],
             recv_sem=g1_recv.at[slot],
             device_id=(section, h, tok),
             device_id_type=mesh_ids,
         )
 
+    def pass_copy(h):
+        return pltpu.make_async_remote_copy(
+            src_ref=full_ref.at[section, h],
+            dst_ref=full_ref.at[section, h],
+            send_sem=g2_send.at[h],
+            recv_sem=g2_recv.at[h],
+            device_id=(other, head, tok),
+            device_id_type=mesh_ids,
+        )
+
     for h in range(head_count):
         @pl.when(h != head)
         def _share():
             share_copy(h, head).start()
     for h in range(head_count):
+        @pl.when(h == head)
+        def _own():
+            pass_copy(h).start()
+    for h in range(head_count):
         @pl.when(h != head)
         def _collect():
             share_copy(h, h).wait()
-            spread[h] = far_in[h]
-    last = pltpu.make_async_remote_copy(
-        src_ref=spread,
-        dst_ref=full_ref.at[section],
-        send_sem=g2_send,
-        recv_sem=g2_recv,
-        device_id=(other, head, tok),
-        device_id_type=mesh_ids,
-    )
-    last.start()
-    full_ref[section] = spread[...]
-    last.wait()
+            pass_copy(h).start()
+    for h in range(head_count):
+        pass_copy(h).wait()
 
 
 def exchange(partial, own_input, gate, layer_idx, gather, head_count, own_rows):
@@ -260,7 +267,7 @@
     half = head_count * own_rows
     vmem = pl.BlockSpec(memory_space=pltpu.VMEM)
     scratch = [
-        pltpu.VMEM((half, width), partial.dtype),
+        pltpu.VMEM((head_count, own_rows, width), partial.dtype),
         pltpu.VMEM((head_count, own_rows, width), partial.dtype),
         pltpu.VMEM((head_count, own_rows, width), partial.dtype),
         pltpu.VMEM((own_rows, width), jnp.float32),
@@ -271,26 +278,11 @@
             jax.ShapeDtypeStruct((rows // half, head_count, own_rows, width), jnp.bfloat16),
         )
         out_specs = (vmem, vmem)
-        scratch += [
-            pltpu.VMEM((head_count, own_rows, width), jnp.bfloat16),
-            pltpu.VMEM((head_count, own_rows, width), jnp.bfloat16),
-        ]
     else:
         out_shape = jax.ShapeDtypeStruct((own_rows, width), jnp.float32)
         out_specs = vmem
-    scratch += [
-        pltpu.SemaphoreType.DMA(()),
-        pltpu.SemaphoreType.DMA(()),
-        pltpu.SemaphoreType.DMA((head_count,)),
-        pltpu.SemaphoreType.DMA((head_count,)),
-    ]
-    if gather:
-        scratch += [
-            pltpu.SemaphoreType.DMA((head_count,)),
-            pltpu.SemaphoreType.DMA((head_count,)),
-            pltpu.SemaphoreType.DMA(()),
-            pltpu.SemaphoreType.DMA(()),
-        ]
+    semaphore_sets = 4 if gather else 2
+    scratch += [pltpu.SemaphoreType.DMA((head_count,))] * (2 * semaphore_sets)
     return pl.pallas_call(
         functools.partial(exchange_kernel, head_count, own_rows, gather),
         out_shape=out_shape,

time: 229 us -> 228 us (level)
  the two profiles are of different devices: /device:TPU:48 before, /device:TPU:22 now
where the time goes in v4:
time: 228 us; the launch traced here: 227 us
  Pallas kernels  105 us (46%)
  local copies, waits for them, and re-layouts  52.6 us (23%)
  matrix products  24.6 us (11%)
  other arithmetic  22.2 us (10%)
  between operations  15.8 us (7%)
  waiting for transfers between devices  6.7 us (3%)
    pallas_call x2, Pallas kernels, exchange(): pl.pallas_call(functools.partial(exchange_kernel, head_count, own_rows, g...  56.7 us
    pallas_call x2, Pallas kernels, attend(): pl.pallas_call(functools.partial(attention_kernel, head_dim), out_shape=j...  47.9 us
    dot_general x7, local copies, waits for them, and re-layouts, project(): jnp.dot(normed, weight[:, part, :], preferred_element_type=jnp.float32)  31.2 us
    dot_general x6, matrix products, project(): jnp.dot(normed, weight[:, part, :], preferred_element_type=jnp.float32)  17.4 us
    dot_general x2, matrix products, shards(): jnp.dot(attended, w_out[layer_idx], preferred_element_type=jnp.float32)  6.33 us
    squeeze x1, local copies, waits for them, and re-layouts, shards(): w_qkv[layer_idx]  6.09 us
    all_gather x2, waiting for transfers between devices, shards(): lax.all_gather(jnp.swapaxes(stale_kv[layer], 0, 1), 'tok', axis=0, tiled=...  5.99 us
    another operation x5, other arithmetic  5.25 us
  transfers between devices with their start and end apart: 2, of which 1 were waited for; matrix products, arithmetic and copies ran while one was open for 40% of the time, Pallas kernels for 26%

profile of v4, /device:TPU:22, one launch (start us, length us, event | category | flops | bytes accessed | tf_op | source)
XLA Modules:
  0.0 226.6 jit_solution(11471437072606980803)
XLA Ops:
  7.2 2.4 %fusion.28 = (bf16[1,2,1,384,384]{4,3,2,1,0:T(8,128)(2,1)}, bf16[1,2,1,384,384]{4,3,2,1,0:T(8,128)(2,1)}) fusion(bf16[2,2,1,384,384]{4,3,2,1,0:T(8,128)(2,1)} %param.18), kind=kLoop, calls=%fused_computation.101 | loop fusion | bytes 2359296 | tf_op jit(solution)/shard_map/slice | solution.py:341
  11.1 6.1 %slice_bitcast_fusion = (bf16[3072,3,384]{2,0,1:T(8,128)(2,1)S(1)}, bf16[3072,3,384]{2,0,1:T(8,128)(2,1)S(1)}) fusion(bf16[2,3072,3,384]{3,1,2,0:T(8,128)(2,1)} %param.13), kind=kLoop, calls=%fused_computation | loop fusion | bytes 28311552 | tf_op jit(solution)/shard_map/squeeze | solution.py:351
  17.2 5.2 %slice_bitcast_fusion.2 = (bf16[384,3072]{0,1:T(8,128)(2,1)}, bf16[384,3072]{0,1:T(8,128)(2,1)}, bf16[384,3072]{0,1:T(8,128)(2,1)}, bf16[384,3072]{0,1:T(8,128)(...) fusion(bf16[3072,3,384]{2,0,1:T(8,128)(2,1)S(1)} %get-tuple-element.23, ...), kind=kLoop, calls=%fused_computation.23 | loop fusion | bytes 28311552 | tf_op jit(solution)/shard_map/dot_general | solution.py:62
  22.4 4.5 %copy.65 = bf16[384,3072]{1,0:T(8,128)(2,1)} copy(bf16[384,3072]{0,1:T(8,128)(2,1)} %get-tuple-element.68) | data formatting | bytes 4718592 | tf_op jit(solution)/shard_map/dot_general | solution.py:62
  28.1 1.2 fusion.13
  29.8 1.4 multiply_reduce_fusion.3
  32.2 1.4 reshape.471
  33.6 4.3 %copy.66 = bf16[384,3072]{1,0:T(8,128)(2,1)} copy(bf16[384,3072]{0,1:T(8,128)(2,1)} %get-tuple-element.69) | data formatting | bytes 4718592 | tf_op jit(solution)/shard_map/dot_general | solution.py:62
  37.9 3.8 %multiply_reduce_fusion.2 = (f32[384,3]{0,1:T(4,128)S(1)}, f32[384,3,128]{0,2,1:T(8,128)S(1)}) fusion(bf16[384,3072,1]{1,0,2:T(8,128)(2,1)} %copy-done.6, bf16[3,128,3072]{2,1,0:T(8,128)(2,1)} %bitcast.142), kind=kOutput, calls=%fused_computation.48 | convolution fusion | flops 906263424 | bytes 5313024 | tf_op jit(solution)/shard_map/dot_general | solution.py:62
  42.7 2.2 reshape.472
  47.6 3.4 %subtract_convert_fusion.2 = (bf16[384,3,64,1]{0,3,2,1:T(2,128)(2,1)S(1)}, bf16[384,3,64,1]{0,3,2,1:T(2,128)(2,1)S(1)}, bf16[384,3,64,1]{0,3,2,1:T(2,128)(2,1)}, bf16[384,3,64,1]{0,3,2,1:T(2,128)(2,1)}) fusion(f32[384,3,64,2]{0,3,2,1:T(2,128)} %reshape.472, f32[384,64]{0,1:T(8,128)S(1)} %get-tuple-element.55, f32[384,64]{0,1:T(8,128)S(1)} %get-tuple-element.54, ...), kind=kLoop, calls=%fused_computation.64 | loop fusion | flops 1179648 | bytes 1966080 | tf_op jit(solution)/shard_map/convert.4
  52.7 1.7 pad_maximum_fusion
  56.3 4.3 %copy.67 = bf16[384,3072]{1,0:T(8,128)(2,1)} copy(bf16[384,3072]{0,1:T(8,128)(2,1)} %get-tuple-element.70) | data formatting | bytes 4718592 | tf_op jit(solution)/shard_map/dot_general | solution.py:62
  60.6 3.9 %convolution_convert_fusion.3 = bf16[384,3,128]{0,2,1:T(8,128)(2,1)S(1)} fusion(bf16[384,3072,1]{1,0,2:T(8,128)(2,1)} %copy-done.6, bf16[3,128,3072]{2,1,0:T(8,128)(2,1)} %bitcast.143), kind=kOutput, calls=%fused_computation.34 | convolution fusion | flops 906117120 | bytes 5013504 | tf_op jit(solution)/shard_map/dot_general | solution.py:62
  65.4 4.3 %copy.73 = bf16[384,3072]{1,0:T(8,128)(2,1)} copy(bf16[384,3072]{0,1:T(8,128)(2,1)} %get-tuple-element.25) | data formatting | bytes 4718592 | tf_op jit(solution)/shard_map/dot_general | solution.py:62
  69.7 4.4 %copy.71 = bf16[384,3072]{1,0:T(8,128)(2,1)} copy(bf16[384,3072]{0,1:T(8,128)(2,1)} %get-tuple-element.27) | data formatting | bytes 4718592 | tf_op jit(solution)/shard_map/dot_general | solution.py:62
  74.0 4.3 %copy.72 = bf16[384,3072]{1,0:T(8,128)(2,1)} copy(bf16[384,3072]{0,1:T(8,128)(2,1)} %get-tuple-element.26) | data formatting | bytes 4718592 | tf_op jit(solution)/shard_map/dot_general | solution.py:62
  78.4 1.2 fusion.27.allow_ref
  79.7 1.3 iota_reduce_fusion
  81.0 1.1 compare_select_fusion.fetch_ref
  82.1 6.0 %all-gather.5.cloned.1.call-done = bf16[16,2,1,384,384]{4,3,2,1,0:T(8,128)(2,1)} async-done(((bf16[1,2,1,384,384]{4,3,2,1,0:T(8,128)(2,1)}), bf16[16,2,1,384,384]{4,3,2,1,0:T(8,128)(2,1)}) %all-gather.5.cloned.1.call-update) | async-done | bytes 9437200 | tf_op jit(solution)/shard_map/all_gather | solution.py:341
  88.1 23.9 %shard_map.130 = bf16[384,384]{1,0:T(8,128)(2,1)} custom-call(s32[16]{0:T(128)} %compare_select_fusion.fetch_ref, s32[16]{0:T(128)} %fusion.27.allow_ref, bf16[384,384]{1,0:T(8,128)(2,1)} %copy.68.q_ref, bf16[384,384]{1,0:T(8,128)(2,1)} %copy.69.kf_ref, bf16[384,384]{1,0:T(8,128)(2,1)} %copy.70.vf_ref, bf16[16,2,384,384]{3,2,1,0:T(8,128)(2,1)} %bitcast.132, ...), custom_call_target="tpu_custom_call" | custom-call | tf_op jit(solution)/shard_map/pallas_call | solution.py:141
  112.0 3.2 %convolution_convert_fusion.1.part_ref = bf16[384,3072]{1,0:T(8,128)(2,1)S(1)} fusion(bf16[384,384]{1,0:T(8,128)(2,1)} %shard_map.130, bf16[2,384,3072]{2,1,0:T(8,128)(2,1)} %param.14), kind=kOutput, calls=%fused_computation.21 | convolution fusion | flops 907149312 | bytes 5013504 | tf_op jit(solution)/shard_map/dot_general | solution.py:359
  115.2 36.0 %shard_map.131 = (bf16[48,3072]{1,0:T(8,128)(2,1)S(1)}, bf16[2,4,48,3072]{3,2,1,0:T(8,128)(2,1)S(1)}) custom-call(bf16[384,3072]{1,0:T(8,128)(2,1)S(1)} %convolution_convert_fusion.1.part_ref, bf16[48,3072]{1,0:T(8,128)(2,1)S(1)} %dynamic-slice_bitcast_fusion.own_ref, f32[1,3072]{1,0:T(1,128)S(1)} %get-tuple-element.47.gate_ref), custom_call_target="tpu_custom_call" | custom-call | tf_op jit(solution)/shard_map/pallas_call | solution.py:286
  152.4 1.2 fusion.5
  154.1 1.4 convolution_convert_fusion.2
  156.4 3.1 %multiply_reduce_fusion.1 = (f32[384,3]{0,1:T(4,128)S(1)}, f32[384,3,128]{0,2,1:T(8,128)S(1)}) fusion(bf16[384,3072,1]{1,0,2:T(8,128)(2,1)} %bitcast.140, bf16[3,128,3072]{2,1,0:T(8,128)(2,1)S(1)} %bitcast.136), kind=kOutput, calls=%fused_computation.46 | convolution fusion | flops 906263424 | bytes 5313024 | tf_op jit(solution)/shard_map/dot_general | solution.py:62
  160.0 3.8 %multiply_reduce_fusion = (f32[384,3]{0,1:T(4,128)S(1)}, f32[384,3,128]{0,2,1:T(8,128)S(1)}) fusion(bf16[384,3072,1]{1,0,2:T(8,128)(2,1)} %bitcast.141, bf16[3,128,3072]{2,1,0:T(8,128)(2,1)} %bitcast.135), kind=kOutput, calls=%fused_computation.44 | convolution fusion | flops 906263424 | bytes 5313024 | tf_op jit(solution)/shard_map/dot_general | solution.py:62
  164.6 1.6 subtract_convert_fusion
  169.6 23.9 %shard_map.132 = bf16[384,384]{1,0:T(8,128)(2,1)} custom-call(s32[16]{0:T(128)} %compare_select_fusion.fetch_ref, s32[16]{0:T(128)} %fusion.27.allow_ref, bf16[384,384]{1,0:T(8,128)(2,1)} %copy.74.q_ref, bf16[384,384]{1,0:T(8,128)(2,1)} %copy.75.kf_ref, bf16[384,384]{1,0:T(8,128)(2,1)} %copy.76.vf_ref, bf16[16,2,384,384]{3,2,1,0:T(8,128)(2,1)} %bitcast.130, ...), custom_call_target="tpu_custom_call" | custom-call | tf_op jit(solution)/shard_map/pallas_call | solution.py:141
  193.5 3.2 %convolution_convert_fusion.part_ref = bf16[384,3072]{1,0:T(8,128)(2,1)S(1)} fusion(bf16[384,384]{1,0:T(8,128)(2,1)} %shard_map.132, bf16[2,384,3072]{2,1,0:T(8,128)(2,1)} %param.14), kind=kOutput, calls=%fused_computation.20 | convolution fusion | flops 907149312 | bytes 5013504 | tf_op jit(solution)/shard_map/dot_general | solution.py:359
  196.7 20.7 %shard_map.133 = f32[48,3072]{1,0:T(8,128)S(1)} custom-call(bf16[384,3072]{1,0:T(8,128)(2,1)S(1)} %convolution_convert_fusion.part_ref, bf16[48,3072]{1,0:T(8,128)(2,1)S(1)} %get-tuple-element.7.own_ref, f32[1,3072]{1,0:T(1,128)S(1)} %get-tuple-element.46.gate_ref), custom_call_target="tpu_custom_call" | custom-call | tf_op jit(solution)/shard_map/pallas_call | solution.py:286
  (87 shorter events, 20.4 us)
Async XLA Ops:
  7.2 211.7 %copy-start = (bf16[3072,64]{0,1:T(8,128)(2,1)S(1)}, bf16[3072,64]{0,1:T(8,128)(2,1)}, u32[]{:S(2)}) copy-start(bf16[3072,64]{0,1:T(8,128)(2,1)} %param.15) | copy-start | bytes 1179652
  7.2 80.9 %all-gather.5.cloned.1.call-start = ((), (), s32[]{:S(2)}) async-start(), calls=%async_computation | async-start | bytes 10027008 | tf_op jit(solution)/shard_map/all_gather | solution.py:341
  9.7 159.9 %all-gather.7.cloned.1.call-start = ((), (), s32[]{:S(2)}) async-start(), calls=%async_computation.1 | async-start | bytes 10027008 | tf_op jit(solution)/shard_map/all_gather | solution.py:341
  22.4 4.5 %copy-start.10 = (f32[2,2,128]{2,1,0:T(2,128)S(1)}, f32[2,2,128]{2,1,0:T(2,128)}, u32[]{:S(2)}) copy-start(f32[2,2,128]{2,1,0:T(2,128)} %param.16) | copy-start | bytes 6148
  22.4 4.5 %copy-start.1 = (bf16[1,384,3072]{2,1,0:T(8,128)(2,1)S(1)}, bf16[1,384,3072]{2,1,0:T(8,128)(2,1)}, u32[]{:S(2)}) copy-start(bf16[1,384,3072]{2,1,0:T(8,128)(2,1)} %param.11) | copy-start | bytes 7077892
  26.9 1.2 copy-start.9
  28.1 1.7 copy-start.4
  29.4 1.9 copy-start.6
  41.7 3.2 %copy-start.12 = (s32[4]{0:T(128)S(1)}, s32[4]{0:T(128)}, u32[]{:S(2)}) copy-start(s32[4]{0:T(128)} %param.19) | copy-start | bytes 52
  41.7 3.4 %copy-start.13 = (s32[16]{0:T(128)S(1)}, s32[16]{0:T(128)}, u32[]{:S(2)}) copy-start(s32[16]{0:T(128)} %param.20) | copy-start | bytes 196
  47.6 3.4 %copy-start.7 = (f32[384,64]{0,1:T(8,128)}, f32[384,64]{0,1:T(8,128)S(1)}, u32[]{:S(2)}) copy-start(f32[384,64]{0,1:T(8,128)S(1)} %get-tuple-element.55) | copy-start | bytes 294916
  152.4 1.7 copy-start.3
  153.6 1.9 copy-start.5
  154.0 2.3 %copy-start.2 = (bf16[384,3072]{1,0:T(8,128)(2,1)S(1)}, bf16[384,3072]{1,0:T(8,128)(2,1)}, u32[]{:S(2)}) copy-start(bf16[384,3072]{1,0:T(8,128)(2,1)} %copy.71) | copy-start | bytes 7077892
  163.7 0.9 copy-start.8
  196.7 22.1 %copy-start.11 = (f32[1,48,64]{2,1,0:T(8,128)S(1)}, f32[1,48,64]{2,1,0:T(8,128)}, u32[]{:S(2)}) copy-start(f32[1,48,64]{2,1,0:T(8,128)} %param.12) | copy-start | bytes 36868
Sparse Core Ops, SparseCore 0:
  10.2 77.8 all-gather.4
  90.2 75.2 all-gather.6

commit v5 on v4

--- a/solution.py
+++ b/solution.py
@@ -156,18 +156,24 @@
     )(fetch, allow, queries, keys_fresh, values_fresh, stale, stale)
 
 
-def exchange_kernel(head_count, own_rows, gather, part_ref, own_ref, gate_ref, *rest):
+def exchange_kernel(head_count, own_rows, split, gather, part_ref, own_ref, gate_ref, *rest):
     if gather:
-        (out_ref, full_ref, near, far, mid, acc,
-         s1_send, s1_recv, s2_send, s2_recv, g1_send, g1_recv, g2_send, g2_recv) = rest
+        (out_ref, full_ref, near, mid, land_a, land_b, sums_a, sums_b, acc,
+         s1_send, s1_recv, r_send, r_recv, a_send, a_recv, g2_send, g2_recv) = rest
     else:
-        (out_ref, near, far, mid, acc, s1_send, s1_recv, s2_send, s2_recv) = rest
+        (out_ref, near, mid, land_a, land_b, sums_a, sums_b, acc,
+         s1_send, s1_recv, r_send, r_recv) = rest
     mesh_ids = pl.DeviceIdType.MESH
     section = lax.axis_index("section")
     head = lax.axis_index("head")
     tok = lax.axis_index("tok")
     other = 1 - section
     half = head_count * own_rows
+    up = lax.rem(head + 1, head_count)
+    down = lax.rem(head + head_count - 1, head_count)
+    opposite = lax.rem(head + 2, head_count)
+    low = pl.ds(0, split)
+    high = pl.ds(split, own_rows - split)
 
     barrier = pltpu.get_barrier_semaphore()
     pl.semaphore_signal(barrier, inc=1, device_id=(other, head, tok), device_id_type=mesh_ids)
@@ -187,13 +193,13 @@
             device_id_type=mesh_ids,
         )
 
-    def far_copy(h, slot):
+    def ring(kind, src, dst, target, send_sem, recv_sem):
         return pltpu.make_async_remote_copy(
-            src_ref=mid.at[h],
-            dst_ref=far.at[slot],
-            send_sem=s2_send.at[h],
-            recv_sem=s2_recv.at[slot],
-            device_id=(section, h, tok),
+            src_ref=src,
+            dst_ref=dst,
+            send_sem=send_sem.at[kind],
+            recv_sem=recv_sem.at[kind],
+            device_id=(section, target, tok),
             device_id_type=mesh_ids,
         )
 
@@ -204,36 +210,50 @@
         near_copy(h).wait()
 
         @pl.when(h != head)
-        def _send():
+        def _pair():
             rows = pl.ds(pl.multiple_of(base + h * own_rows, own_rows), own_rows)
             mid[h] = (part_ref[rows, :].astype(jnp.float32) + near[h].astype(jnp.float32)).astype(
                 mid.dtype
             )
-            far_copy(h, head).start()
-
+
+    pass_a = ring(0, mid.at[opposite, low], land_a.at[0], up, r_send, r_recv)
+    pass_b = ring(1, mid.at[opposite, high], land_b.at[0], down, r_send, r_recv)
+    direct_a = ring(2, mid.at[down, low], land_a.at[1], down, r_send, r_recv)
+    direct_b = ring(3, mid.at[up, high], land_b.at[1], up, r_send, r_recv)
+    pass_a.start()
+    pass_b.start()
+    direct_a.start()
+    direct_b.start()
     mine = pl.ds(pl.multiple_of(base + head * own_rows, own_rows), own_rows)
     acc[...] = part_ref[mine, :].astype(jnp.float32) + near[head].astype(jnp.float32)
-    for h in range(head_count):
-        @pl.when(h != head)
-        def _wait():
-            far_copy(h, h).wait()
-            acc[...] += far[h].astype(jnp.float32)
+    pass_a.wait()
+    sums_a[...] = (mid[up, low].astype(jnp.float32) + land_a[0].astype(jnp.float32)).astype(
+        sums_a.dtype
+    )
+    joined_a = ring(4, sums_a, land_a.at[2], up, r_send, r_recv)
+    joined_a.start()
+    pass_b.wait()
+    sums_b[...] = (mid[down, high].astype(jnp.float32) + land_b[0].astype(jnp.float32)).astype(
+        sums_b.dtype
+    )
+    joined_b = ring(5, sums_b, land_b.at[2], down, r_send, r_recv)
+    joined_b.start()
+    direct_a.wait()
+    direct_b.wait()
+    joined_a.wait()
+    joined_b.wait()
+    acc[low, :] += (
+        land_a[1].astype(jnp.float32) + land_a[2].astype(jnp.float32)
+    )
+    acc[high, :] += (
+        land_b[1].astype(jnp.float32) + land_b[2].astype(jnp.float32)
+    )
     if not gather:
         out_ref[...] = acc[...]
         return
     result = (own_ref[...].astype(jnp.float32) + gate_ref[...] * acc[...]).astype(full_ref.dtype)
     full_ref[section, head] = result
     out_ref[...] = result
-
-    def share_copy(h, slot):
-        return pltpu.make_async_remote_copy(
-            src_ref=full_ref.at[section, head],
-            dst_ref=full_ref.at[section, slot],
-            send_sem=g1_send.at[h],
-            recv_sem=g1_recv.at[slot],
-            device_id=(section, h, tok),
-            device_id_type=mesh_ids,
-        )
 
     def pass_copy(h):
         return pltpu.make_async_remote_copy(
@@ -245,32 +265,49 @@
             device_id_type=mesh_ids,
         )
 
-    for h in range(head_count):
-        @pl.when(h != head)
-        def _share():
-            share_copy(h, head).start()
-    for h in range(head_count):
-        @pl.when(h == head)
-        def _own():
-            pass_copy(h).start()
-    for h in range(head_count):
-        @pl.when(h != head)
-        def _collect():
-            share_copy(h, h).wait()
-            pass_copy(h).start()
-    for h in range(head_count):
-        pass_copy(h).wait()
+    to_up = ring(0, full_ref.at[section, head], full_ref.at[section, head], up, a_send, a_recv)
+    to_down = ring(1, full_ref.at[section, head], full_ref.at[section, head], down, a_send, a_recv)
+    to_up.start()
+    to_down.start()
+    pass_copy(head).start()
+    to_up.wait()
+    onward_a = ring(
+        2, full_ref.at[section, down, low], full_ref.at[section, down, low], up, a_send, a_recv
+    )
+    onward_a.start()
+    pass_copy(down).start()
+    to_down.wait()
+    onward_b = ring(
+        3, full_ref.at[section, up, high], full_ref.at[section, up, high], down, a_send, a_recv
+    )
+    onward_b.start()
+    pass_copy(up).start()
+    onward_a.wait()
+    onward_b.wait()
+    pass_copy(opposite).start()
+    pass_copy(head).wait()
+    pass_copy(down).wait()
+    pass_copy(up).wait()
+    pass_copy(opposite).wait()
 
 
 def exchange(partial, own_input, gate, layer_idx, gather, head_count, own_rows):
     rows, width = partial.shape
     half = head_count * own_rows
+    split = (own_rows * 2 // 3) // 16 * 16
     vmem = pl.BlockSpec(memory_space=pltpu.VMEM)
     scratch = [
         pltpu.VMEM((head_count, own_rows, width), partial.dtype),
         pltpu.VMEM((head_count, own_rows, width), partial.dtype),
-        pltpu.VMEM((head_count, own_rows, width), partial.dtype),
+        pltpu.VMEM((3, split, width), partial.dtype),
+        pltpu.VMEM((3, own_rows - split, width), partial.dtype),
+        pltpu.VMEM((split, width), partial.dtype),
+        pltpu.VMEM((own_rows - split, width), partial.dtype),
         pltpu.VMEM((own_rows, width), jnp.float32),
+        pltpu.SemaphoreType.DMA((head_count,)),
+        pltpu.SemaphoreType.DMA((head_count,)),
+        pltpu.SemaphoreType.DMA((6,)),
+        pltpu.SemaphoreType.DMA((6,)),
     ]
     if gather:
         out_shape = (
@@ -278,13 +315,12 @@
             jax.ShapeDtypeStruct((rows // half, head_count, own_rows, width), jnp.bfloat16),
         )
         out_specs = (vmem, vmem)
+        scratch += [pltpu.SemaphoreType.DMA((head_count,))] * 4
     else:
         out_shape = jax.ShapeDtypeStruct((own_rows, width), jnp.float32)
         out_specs = vmem
-    semaphore_sets = 4 if gather else 2
-    scratch += [pltpu.SemaphoreType.DMA((head_count,))] * (2 * semaphore_sets)
     return pl.pallas_call(
-        functools.partial(exchange_kernel, head_count, own_rows, gather),
+        functools.partial(exchange_kernel, head_count, own_rows, split, gather),
         out_shape=out_shape,
         in_specs=[vmem, vmem, vmem],
         out_specs=out_specs,

time: 228 us -> 223 us (0.978)
  the two profiles are of different devices: /device:TPU:22 before, /device:TPU:8 now
where the time goes in v5:
time: 223 us; the launch traced here: 221 us
  Pallas kernels  98.5 us (44%)
  local copies, waits for them, and re-layouts  52.6 us (24%)
  matrix products  24.7 us (11%)
  other arithmetic  22.2 us (10%)
  between operations  15.8 us (7%)
  waiting for transfers between devices  6.9 us (3%)
    pallas_call x2, Pallas kernels, exchange(): pl.pallas_call(functools.partial(exchange_kernel, head_count, own_rows, s...  50.6 us
    pallas_call x2, Pallas kernels, attend(): pl.pallas_call(functools.partial(attention_kernel, head_dim), out_shape=j...  47.9 us
    dot_general x7, local copies, waits for them, and re-layouts, project(): jnp.dot(normed, weight[:, part, :], preferred_element_type=jnp.float32)  31.2 us
    dot_general x6, matrix products, project(): jnp.dot(normed, weight[:, part, :], preferred_element_type=jnp.float32)  17.4 us
    dot_general x2, matrix products, shards(): jnp.dot(attended, w_out[layer_idx], preferred_element_type=jnp.float32)  6.34 us
    all_gather x2, waiting for transfers between devices, shards(): lax.all_gather(jnp.swapaxes(stale_kv[layer], 0, 1), 'tok', axis=0, tiled=...  6.19 us
    squeeze x1, local copies, waits for them, and re-layouts, shards(): w_qkv[layer_idx]  6.09 us
    another operation x5, other arithmetic  5.25 us
  transfers between devices with their start and end apart: 2, of which 1 were waited for; matrix products, arithmetic and copies ran while one was open for 41% of the time, Pallas kernels for 25%

profile of v5, /device:TPU:8, one launch (start us, length us, event | category | flops | bytes accessed | tf_op | source)
XLA Modules:
  0.0 220.8 jit_solution(11058348114790572746)
XLA Ops:
  7.2 2.4 %fusion.28 = (bf16[1,2,1,384,384]{4,3,2,1,0:T(8,128)(2,1)}, bf16[1,2,1,384,384]{4,3,2,1,0:T(8,128)(2,1)}) fusion(bf16[2,2,1,384,384]{4,3,2,1,0:T(8,128)(2,1)} %param.18), kind=kLoop, calls=%fused_computation.101 | loop fusion | bytes 2359296 | tf_op jit(solution)/shard_map/slice | solution.py:377
  11.1 6.1 %slice_bitcast_fusion = (bf16[3072,3,384]{2,0,1:T(8,128)(2,1)S(1)}, bf16[3072,3,384]{2,0,1:T(8,128)(2,1)S(1)}) fusion(bf16[2,3072,3,384]{3,1,2,0:T(8,128)(2,1)} %param.13), kind=kLoop, calls=%fused_computation | loop fusion | bytes 28311552 | tf_op jit(solution)/shard_map/squeeze | solution.py:387
  17.2 5.2 %slice_bitcast_fusion.2 = (bf16[384,3072]{0,1:T(8,128)(2,1)}, bf16[384,3072]{0,1:T(8,128)(2,1)}, bf16[384,3072]{0,1:T(8,128)(2,1)}, bf16[384,3072]{0,1:T(8,128)(...) fusion(bf16[3072,3,384]{2,0,1:T(8,128)(2,1)S(1)} %get-tuple-element.23, ...), kind=kLoop, calls=%fused_computation.23 | loop fusion | bytes 28311552 | tf_op jit(solution)/shard_map/dot_general | solution.py:62
  22.4 4.5 %copy.65 = bf16[384,3072]{1,0:T(8,128)(2,1)} copy(bf16[384,3072]{0,1:T(8,128)(2,1)} %get-tuple-element.68) | data formatting | bytes 4718592 | tf_op jit(solution)/shard_map/dot_general | solution.py:62
  28.1 1.2 fusion.13
  29.8 1.4 multiply_reduce_fusion.3
  32.2 1.4 reshape.471
  33.6 4.3 %copy.66 = bf16[384,3072]{1,0:T(8,128)(2,1)} copy(bf16[384,3072]{0,1:T(8,128)(2,1)} %get-tuple-element.69) | data formatting | bytes 4718592 | tf_op jit(solution)/shard_map/dot_general | solution.py:62
  37.9 3.8 %multiply_reduce_fusion.2 = (f32[384,3]{0,1:T(4,128)S(1)}, f32[384,3,128]{0,2,1:T(8,128)S(1)}) fusion(bf16[384,3072,1]{1,0,2:T(8,128)(2,1)} %copy-done.6, bf16[3,128,3072]{2,1,0:T(8,128)(2,1)} %bitcast.142), kind=kOutput, calls=%fused_computation.48 | convolution fusion | flops 906263424 | bytes 5313024 | tf_op jit(solution)/shard_map/dot_general | solution.py:62
  42.7 2.2 %reshape.472 = f32[384,3,64,2]{0,3,2,1:T(2,128)} reshape(f32[384,3,128]{0,2,1:T(8,128)} %multiply_multiply_fusion.2) | data formatting | bytes 1179648 | tf_op jit(solution)/shard_map/reshape | solution.py:34
  47.6 3.4 %subtract_convert_fusion.2 = (bf16[384,3,64,1]{0,3,2,1:T(2,128)(2,1)S(1)}, bf16[384,3,64,1]{0,3,2,1:T(2,128)(2,1)S(1)}, bf16[384,3,64,1]{0,3,2,1:T(2,128)(2,1)}, bf16[384,3,64,1]{0,3,2,1:T(2,128)(2,1)}) fusion(f32[384,3,64,2]{0,3,2,1:T(2,128)} %reshape.472, f32[384,64]{0,1:T(8,128)S(1)} %get-tuple-element.55, f32[384,64]{0,1:T(8,128)S(1)} %get-tuple-element.54, ...), kind=kLoop, calls=%fused_computation.64 | loop fusion | flops 1179648 | bytes 1966080 | tf_op jit(solution)/shard_map/convert.4
  52.7 1.7 pad_maximum_fusion
  56.3 4.3 %copy.67 = bf16[384,3072]{1,0:T(8,128)(2,1)} copy(bf16[384,3072]{0,1:T(8,128)(2,1)} %get-tuple-element.70) | data formatting | bytes 4718592 | tf_op jit(solution)/shard_map/dot_general | solution.py:62
  60.6 3.9 %convolution_convert_fusion.3 = bf16[384,3,128]{0,2,1:T(8,128)(2,1)S(1)} fusion(bf16[384,3072,1]{1,0,2:T(8,128)(2,1)} %copy-done.6, bf16[3,128,3072]{2,1,0:T(8,128)(2,1)} %bitcast.143), kind=kOutput, calls=%fused_computation.34 | convolution fusion | flops 906117120 | bytes 5013504 | tf_op jit(solution)/shard_map/dot_general | solution.py:62
  65.4 4.3 %copy.73 = bf16[384,3072]{1,0:T(8,128)(2,1)} copy(bf16[384,3072]{0,1:T(8,128)(2,1)} %get-tuple-element.25) | data formatting | bytes 4718592 | tf_op jit(solution)/shard_map/dot_general | solution.py:62
  69.7 4.4 %copy.71 = bf16[384,3072]{1,0:T(8,128)(2,1)} copy(bf16[384,3072]{0,1:T(8,128)(2,1)} %get-tuple-element.27) | data formatting | bytes 4718592 | tf_op jit(solution)/shard_map/dot_general | solution.py:62
  74.1 4.3 %copy.72 = bf16[384,3072]{1,0:T(8,128)(2,1)} copy(bf16[384,3072]{0,1:T(8,128)(2,1)} %get-tuple-element.26) | data formatting | bytes 4718592 | tf_op jit(solution)/shard_map/dot_general | solution.py:62
  78.5 1.2 fusion.27.allow_ref
  79.7 1.3 iota_reduce_fusion
  81.0 1.1 compare_select_fusion.fetch_ref
  82.1 6.2 %all-gather.5.cloned.1.call-done = bf16[16,2,1,384,384]{4,3,2,1,0:T(8,128)(2,1)} async-done(((bf16[1,2,1,384,384]{4,3,2,1,0:T(8,128)(2,1)}), bf16[16,2,1,384,384]{4,3,2,1,0:T(8,128)(2,1)}) %all-gather.5.cloned.1.call-update) | async-done | bytes 9437200 | tf_op jit(solution)/shard_map/all_gather | solution.py:377
  88.3 23.9 %shard_map.130 = bf16[384,384]{1,0:T(8,128)(2,1)} custom-call(s32[16]{0:T(128)} %compare_select_fusion.fetch_ref, s32[16]{0:T(128)} %fusion.27.allow_ref, bf16[384,384]{1,0:T(8,128)(2,1)} %copy.68.q_ref, bf16[384,384]{1,0:T(8,128)(2,1)} %copy.69.kf_ref, bf16[384,384]{1,0:T(8,128)(2,1)} %copy.70.vf_ref, bf16[16,2,384,384]{3,2,1,0:T(8,128)(2,1)} %bitcast.132, ...), custom_call_target="tpu_custom_call" | custom-call | tf_op jit(solution)/shard_map/pallas_call | solution.py:141
  112.2 3.2 %convolution_convert_fusion.1.part_ref = bf16[384,3072]{1,0:T(8,128)(2,1)S(1)} fusion(bf16[384,384]{1,0:T(8,128)(2,1)} %shard_map.130, bf16[2,384,3072]{2,1,0:T(8,128)(2,1)} %param.14), kind=kOutput, calls=%fused_computation.21 | convolution fusion | flops 907149312 | bytes 5013504 | tf_op jit(solution)/shard_map/dot_general | solution.py:395
  115.4 32.3 %shard_map.131 = (bf16[48,3072]{1,0:T(8,128)(2,1)S(1)}, bf16[2,4,48,3072]{3,2,1,0:T(8,128)(2,1)S(1)}) custom-call(bf16[384,3072]{1,0:T(8,128)(2,1)S(1)} %convolution_convert_fusion.1.part_ref, bf16[48,3072]{1,0:T(8,128)(2,1)S(1)} %dynamic-slice_bitcast_fusion.own_ref, f32[1,3072]{1,0:T(1,128)S(1)} %get-tuple-element.47.gate_ref), custom_call_target="tpu_custom_call" | custom-call | tf_op jit(solution)/shard_map/pallas_call | solution.py:322
  148.8 1.2 fusion.5
  150.5 1.4 convolution_convert_fusion.2
  152.8 3.1 %multiply_reduce_fusion.1 = (f32[384,3]{0,1:T(4,128)S(1)}, f32[384,3,128]{0,2,1:T(8,128)S(1)}) fusion(bf16[384,3072,1]{1,0,2:T(8,128)(2,1)} %bitcast.140, bf16[3,128,3072]{2,1,0:T(8,128)(2,1)S(1)} %bitcast.136), kind=kOutput, calls=%fused_computation.46 | convolution fusion | flops 906263424 | bytes 5313024 | tf_op jit(solution)/shard_map/dot_general | solution.py:62
  156.5 3.8 %multiply_reduce_fusion = (f32[384,3]{0,1:T(4,128)S(1)}, f32[384,3,128]{0,2,1:T(8,128)S(1)}) fusion(bf16[384,3072,1]{1,0,2:T(8,128)(2,1)} %bitcast.141, bf16[3,128,3072]{2,1,0:T(8,128)(2,1)} %bitcast.135), kind=kOutput, calls=%fused_computation.44 | convolution fusion | flops 906263424 | bytes 5313024 | tf_op jit(solution)/shard_map/dot_general | solution.py:62
  161.1 1.6 subtract_convert_fusion
  166.1 23.9 %shard_map.132 = bf16[384,384]{1,0:T(8,128)(2,1)} custom-call(s32[16]{0:T(128)} %compare_select_fusion.fetch_ref, s32[16]{0:T(128)} %fusion.27.allow_ref, bf16[384,384]{1,0:T(8,128)(2,1)} %copy.74.q_ref, bf16[384,384]{1,0:T(8,128)(2,1)} %copy.75.kf_ref, bf16[384,384]{1,0:T(8,128)(2,1)} %copy.76.vf_ref, bf16[16,2,384,384]{3,2,1,0:T(8,128)(2,1)} %bitcast.130, ...), custom_call_target="tpu_custom_call" | custom-call | tf_op jit(solution)/shard_map/pallas_call | solution.py:141
  190.0 3.2 %convolution_convert_fusion.part_ref = bf16[384,3072]{1,0:T(8,128)(2,1)S(1)} fusion(bf16[384,384]{1,0:T(8,128)(2,1)} %shard_map.132, bf16[2,384,3072]{2,1,0:T(8,128)(2,1)} %param.14), kind=kOutput, calls=%fused_computation.20 | convolution fusion | flops 907149312 | bytes 5013504 | tf_op jit(solution)/shard_map/dot_general | solution.py:395
  193.2 18.4 %shard_map.133 = f32[48,3072]{1,0:T(8,128)S(1)} custom-call(bf16[384,3072]{1,0:T(8,128)(2,1)S(1)} %convolution_convert_fusion.part_ref, bf16[48,3072]{1,0:T(8,128)(2,1)S(1)} %get-tuple-element.7.own_ref, f32[1,3072]{1,0:T(1,128)S(1)} %get-tuple-element.46.gate_ref), custom_call_target="tpu_custom_call" | custom-call | tf_op jit(solution)/shard_map/pallas_call | solution.py:322
  (87 shorter events, 20.4 us)
Async XLA Ops:
  7.2 205.8 %copy-start = (bf16[3072,64]{0,1:T(8,128)(2,1)S(1)}, bf16[3072,64]{0,1:T(8,128)(2,1)}, u32[]{:S(2)}) copy-start(bf16[3072,64]{0,1:T(8,128)(2,1)} %param.15) | copy-start | bytes 1179652
  7.2 81.1 %all-gather.5.cloned.1.call-start = ((), (), s32[]{:S(2)}) async-start(), calls=%async_computation | async-start | bytes 10027008 | tf_op jit(solution)/shard_map/all_gather | solution.py:377
  9.7 156.4 %all-gather.7.cloned.1.call-start = ((), (), s32[]{:S(2)}) async-start(), calls=%async_computation.1 | async-start | bytes 10027008 | tf_op jit(solution)/shard_map/all_gather | solution.py:377
  22.4 4.5 %copy-start.10 = (f32[2,2,128]{2,1,0:T(2,128)S(1)}, f32[2,2,128]{2,1,0:T(2,128)}, u32[]{:S(2)}) copy-start(f32[2,2,128]{2,1,0:T(2,128)} %param.16) | copy-start | bytes 6148
  22.4 4.5 %copy-start.1 = (bf16[1,384,3072]{2,1,0:T(8,128)(2,1)S(1)}, bf16[1,384,3072]{2,1,0:T(8,128)(2,1)}, u32[]{:S(2)}) copy-start(bf16[1,384,3072]{2,1,0:T(8,128)(2,1)} %param.11) | copy-start | bytes 7077892
  26.9 1.2 copy-start.9
  28.1 1.7 copy-start.4
  29.4 1.9 copy-start.6
  41.7 3.2 %copy-start.12 = (s32[4]{0:T(128)S(1)}, s32[4]{0:T(128)}, u32[]{:S(2)}) copy-start(s32[4]{0:T(128)} %param.19) | copy-start | bytes 52
  41.7 3.4 %copy-start.13 = (s32[16]{0:T(128)S(1)}, s32[16]{0:T(128)}, u32[]{:S(2)}) copy-start(s32[16]{0:T(128)} %param.20) | copy-start | bytes 196
  47.6 3.4 %copy-start.7 = (f32[384,64]{0,1:T(8,128)}, f32[384,64]{0,1:T(8,128)S(1)}, u32[]{:S(2)}) copy-start(f32[384,64]{0,1:T(8,128)S(1)} %get-tuple-element.55) | copy-start | bytes 294916
  148.8 1.7 copy-start.3
  150.0 1.9 copy-start.5
  150.5 2.3 %copy-start.2 = (bf16[384,3072]{1,0:T(8,128)(2,1)S(1)}, bf16[384,3072]{1,0:T(8,128)(2,1)}, u32[]{:S(2)}) copy-start(bf16[384,3072]{1,0:T(8,128)(2,1)} %copy.71) | copy-start | bytes 7077892
  160.3 0.9 copy-start.8
  193.2 19.8 %copy-start.11 = (f32[1,48,64]{2,1,0:T(8,128)S(1)}, f32[1,48,64]{2,1,0:T(8,128)}, u32[]{:S(2)}) copy-start(f32[1,48,64]{2,1,0:T(8,128)} %param.12) | copy-start | bytes 36868
Sparse Core Ops, SparseCore 0:
  10.2 78.0 all-gather.4
  90.4 75.2 all-gather.6

commit v6 on v5

--- a/solution.py
+++ b/solution.py
@@ -75,29 +75,28 @@
 
 
 def attention_kernel(
-    head_dim, fetch_ref, allow_ref, q_ref, kf_ref, vf_ref, ks_ref, vs_ref, o_ref, m_sc, l_sc, acc_sc
+    head_dim, fetch_ref, allow_ref, q_ref, kf_ref, vf_ref, ks_ref, vs_ref, o_ref, qt_sc, m_sc, l_sc, acc_sc
 ):
     slot = pl.program_id(0)
     heads = q_ref.shape[1] // head_dim
     scaling = 1.0 / math.sqrt(head_dim)
-    contract = (((1,), (1,)), ((), ()))
+    by_key = (((0,), (0,)), ((), ()))
 
     @pl.when(slot == 0)
     def _fresh():
         for h in range(heads):
             lanes = slice(h * head_dim, (h + 1) * head_dim)
+            qt_sc[h] = q_ref[:, lanes].T
             scores = (
-                lax.dot_general(
-                    q_ref[:, lanes], kf_ref[:, lanes], contract, preferred_element_type=jnp.float32
-                )
-                * scaling
-            )
-            row_max = jnp.max(scores, axis=1, keepdims=True)
-            weights = jnp.exp(scores - row_max)
-            m_sc[h] = row_max
-            l_sc[h] = jnp.sum(weights, axis=1, keepdims=True)
-            acc_sc[h] = jnp.dot(
-                weights.astype(jnp.bfloat16), vf_ref[:, lanes], preferred_element_type=jnp.float32
+                jnp.dot(kf_ref[:, lanes], qt_sc[h], preferred_element_type=jnp.float32) * scaling
+            )
+            col_max = jnp.max(scores, axis=0, keepdims=True)
+            weights = jnp.exp(scores - col_max)
+            m_sc[h] = col_max
+            l_sc[h] = jnp.sum(weights, axis=0, keepdims=True)
+            acc_sc[h] = lax.dot_general(
+                vf_ref[:, lanes], weights.astype(jnp.bfloat16), by_key,
+                preferred_element_type=jnp.float32,
             )
 
     @pl.when(allow_ref[slot] != 0)
@@ -105,18 +104,16 @@
         for h in range(heads):
             lanes = slice(h * head_dim, (h + 1) * head_dim)
             scores = (
-                lax.dot_general(
-                    q_ref[:, lanes], ks_ref[:, lanes], contract, preferred_element_type=jnp.float32
-                )
-                * scaling
+                jnp.dot(ks_ref[:, lanes], qt_sc[h], preferred_element_type=jnp.float32) * scaling
             )
             old_max = m_sc[h]
-            new_max = jnp.maximum(old_max, jnp.max(scores, axis=1, keepdims=True))
+            new_max = jnp.maximum(old_max, jnp.max(scores, axis=0, keepdims=True))
             factor = jnp.exp(old_max - new_max)
             weights = jnp.exp(scores - new_max)
-            l_sc[h] = l_sc[h] * factor + jnp.sum(weights, axis=1, keepdims=True)
-            acc_sc[h] = acc_sc[h] * factor + jnp.dot(
-                weights.astype(jnp.bfloat16), vs_ref[:, lanes], preferred_element_type=jnp.float32
+            l_sc[h] = l_sc[h] * factor + jnp.sum(weights, axis=0, keepdims=True)
+            acc_sc[h] = acc_sc[h] * factor + lax.dot_general(
+                vs_ref[:, lanes], weights.astype(jnp.bfloat16), by_key,
+                preferred_element_type=jnp.float32,
             )
             m_sc[h] = new_max
 
@@ -124,7 +121,7 @@
     def _finish():
         for h in range(heads):
             lanes = slice(h * head_dim, (h + 1) * head_dim)
-            o_ref[:, lanes] = (acc_sc[h] / l_sc[h]).astype(o_ref.dtype)
+            o_ref[:, lanes] = (acc_sc[h] / l_sc[h]).T.astype(o_ref.dtype)
 
 
 def attend(queries, keys_fresh, values_fresh, stale, fetch, allow, head_dim):
@@ -147,9 +144,10 @@
             in_specs=[whole, whole, whole, key_spec, value_spec],
             out_specs=whole,
             scratch_shapes=[
-                pltpu.VMEM((heads, rows, 1), jnp.float32),
-                pltpu.VMEM((heads, rows, 1), jnp.float32),
-                pltpu.VMEM((heads, rows, head_dim), jnp.float32),
+                pltpu.VMEM((heads, head_dim, rows), jnp.bfloat16),
+                pltpu.VMEM((heads, 1, rows), jnp.float32),
+                pltpu.VMEM((heads, 1, rows), jnp.float32),
+                pltpu.VMEM((heads, head_dim, rows), jnp.float32),
             ],
         ),
         compiler_params=pltpu.CompilerParams(dimension_semantics=("arbitrary",)),

time: 223 us -> 216 us (0.969)
  the two profiles are of different devices: /device:TPU:8 before, /device:TPU:1 now
where the time goes in v6:
time: 216 us; the launch traced here: 215 us
  Pallas kernels  85.9 us (40%)
  local copies, waits for them, and re-layouts  52.6 us (24%)
  matrix products  25 us (12%)
  other arithmetic  22.3 us (10%)
  between operations  15.8 us (7%)
  waiting for transfers between devices  13.1 us (6%)
    pallas_call x2, Pallas kernels, exchange(): pl.pallas_call(functools.partial(exchange_kernel, head_count, own_rows, s...  51.2 us
    pallas_call x2, Pallas kernels, attend(): pl.pallas_call(functools.partial(attention_kernel, head_dim), out_shape=j...  34.7 us
    dot_general x7, local copies, waits for them, and re-layouts, project(): jnp.dot(normed, weight[:, part, :], preferred_element_type=jnp.float32)  31.3 us
    dot_general x6, matrix products, project(): jnp.dot(normed, weight[:, part, :], preferred_element_type=jnp.float32)  17.7 us
    all_gather x2, waiting for transfers between devices, shards(): lax.all_gather(jnp.swapaxes(stale_kv[layer], 0, 1), 'tok', axis=0, tiled=...  12.3 us
    dot_general x2, matrix products, shards(): jnp.dot(attended, w_out[layer_idx], preferred_element_type=jnp.float32)  6.36 us
    squeeze x1, local copies, waits for them, and re-layouts, shards(): w_qkv[layer_idx]  6.09 us
    another operation x5, other arithmetic  5.42 us
  transfers between devices with their start and end apart: 2, of which 2 were waited for; matrix products, arithmetic and copies ran while one was open for 42% of the time, Pallas kernels for 23%

profile of v6, /device:TPU:1, one launch (start us, length us, event | category | flops | bytes accessed | tf_op | source)
XLA Modules:
  0.0 214.7 jit_solution(9678935774076060643)
XLA Ops:
  7.2 2.4 %fusion.28 = (bf16[1,2,1,384,384]{4,3,2,1,0:T(8,128)(2,1)}, bf16[1,2,1,384,384]{4,3,2,1,0:T(8,128)(2,1)}) fusion(bf16[2,2,1,384,384]{4,3,2,1,0:T(8,128)(2,1)} %param.18), kind=kLoop, calls=%fused_computation.101 | loop fusion | bytes 2359296 | tf_op jit(solution)/shard_map/slice | solution.py:375
  11.1 6.1 %slice_bitcast_fusion = (bf16[3072,3,384]{2,0,1:T(8,128)(2,1)S(1)}, bf16[3072,3,384]{2,0,1:T(8,128)(2,1)S(1)}) fusion(bf16[2,3072,3,384]{3,1,2,0:T(8,128)(2,1)} %param.13), kind=kLoop, calls=%fused_computation | loop fusion | bytes 28311552 | tf_op jit(solution)/shard_map/squeeze | solution.py:385
  17.2 5.2 %slice_bitcast_fusion.2 = (bf16[384,3072]{0,1:T(8,128)(2,1)}, bf16[384,3072]{0,1:T(8,128)(2,1)}, bf16[384,3072]{0,1:T(8,128)(2,1)}, bf16[384,3072]{0,1:T(8,128)(...) fusion(bf16[3072,3,384]{2,0,1:T(8,128)(2,1)S(1)} %get-tuple-element.23, ...), kind=kLoop, calls=%fused_computation.23 | loop fusion | bytes 28311552 | tf_op jit(solution)/shard_map/dot_general | solution.py:62
  22.4 4.5 %copy.65 = bf16[384,3072]{1,0:T(8,128)(2,1)} copy(bf16[384,3072]{0,1:T(8,128)(2,1)} %get-tuple-element.68) | data formatting | bytes 4718592 | tf_op jit(solution)/shard_map/dot_general | solution.py:62
  28.2 1.2 fusion.13
  29.9 1.4 multiply_reduce_fusion.3
  32.2 1.4 reshape.471
  33.7 4.3 %copy.66 = bf16[384,3072]{1,0:T(8,128)(2,1)} copy(bf16[384,3072]{0,1:T(8,128)(2,1)} %get-tuple-element.69) | data formatting | bytes 4718592 | tf_op jit(solution)/shard_map/dot_general | solution.py:62
  38.0 3.8 %multiply_reduce_fusion.2 = (f32[384,3]{0,1:T(4,128)S(1)}, f32[384,3,128]{0,2,1:T(8,128)S(1)}) fusion(bf16[384,3072,1]{1,0,2:T(8,128)(2,1)} %copy-done.6, bf16[3,128,3072]{2,1,0:T(8,128)(2,1)} %bitcast.142), kind=kOutput, calls=%fused_computation.48 | convolution fusion | flops 906263424 | bytes 5313024 | tf_op jit(solution)/shard_map/dot_general | solution.py:62
  42.7 2.2 %reshape.472 = f32[384,3,64,2]{0,3,2,1:T(2,128)} reshape(f32[384,3,128]{0,2,1:T(8,128)} %multiply_multiply_fusion.2) | data formatting | bytes 1179648 | tf_op jit(solution)/shard_map/reshape | solution.py:34
  47.6 3.5 %subtract_convert_fusion.2 = (bf16[384,3,64,1]{0,3,2,1:T(2,128)(2,1)S(1)}, bf16[384,3,64,1]{0,3,2,1:T(2,128)(2,1)S(1)}, bf16[384,3,64,1]{0,3,2,1:T(2,128)(2,1)}, bf16[384,3,64,1]{0,3,2,1:T(2,128)(2,1)}) fusion(f32[384,3,64,2]{0,3,2,1:T(2,128)} %reshape.472, f32[384,64]{0,1:T(8,128)S(1)} %get-tuple-element.55, f32[384,64]{0,1:T(8,128)S(1)} %get-tuple-element.54, ...), kind=kLoop, calls=%fused_computation.64 | loop fusion | flops 1179648 | bytes 1966080 | tf_op jit(solution)/shard_map/convert.4
  52.9 1.7 pad_maximum_fusion
  56.5 4.3 %copy.67 = bf16[384,3072]{1,0:T(8,128)(2,1)} copy(bf16[384,3072]{0,1:T(8,128)(2,1)} %get-tuple-element.70) | data formatting | bytes 4718592 | tf_op jit(solution)/shard_map/dot_general | solution.py:62
  60.8 4.0 %convolution_convert_fusion.3 = bf16[384,3,128]{0,2,1:T(8,128)(2,1)S(1)} fusion(bf16[384,3072,1]{1,0,2:T(8,128)(2,1)} %copy-done.6, bf16[3,128,3072]{2,1,0:T(8,128)(2,1)} %bitcast.143), kind=kOutput, calls=%fused_computation.34 | convolution fusion | flops 906117120 | bytes 5013504 | tf_op jit(solution)/shard_map/dot_general | solution.py:62
  65.7 4.3 %copy.73 = bf16[384,3072]{1,0:T(8,128)(2,1)} copy(bf16[384,3072]{0,1:T(8,128)(2,1)} %get-tuple-element.25) | data formatting | bytes 4718592 | tf_op jit(solution)/shard_map/dot_general | solution.py:62
  70.0 4.3 %copy.71 = bf16[384,3072]{1,0:T(8,128)(2,1)} copy(bf16[384,3072]{0,1:T(8,128)(2,1)} %get-tuple-element.27) | data formatting | bytes 4718592 | tf_op jit(solution)/shard_map/dot_general | solution.py:62
  74.3 4.3 %copy.72 = bf16[384,3072]{1,0:T(8,128)(2,1)} copy(bf16[384,3072]{0,1:T(8,128)(2,1)} %get-tuple-element.26) | data formatting | bytes 4718592 | tf_op jit(solution)/shard_map/dot_general | solution.py:62
  78.7 1.2 fusion.27.allow_ref
  80.0 1.3 iota_reduce_fusion
  82.4 6.8 %all-gather.5.cloned.1.call-done = bf16[16,2,1,384,384]{4,3,2,1,0:T(8,128)(2,1)} async-done(((bf16[1,2,1,384,384]{4,3,2,1,0:T(8,128)(2,1)}), bf16[16,2,1,384,384]{4,3,2,1,0:T(8,128)(2,1)}) %all-gather.5.cloned.1.call-update) | async-done | bytes 9437200 | tf_op jit(solution)/shard_map/all_gather | solution.py:375
  89.2 17.4 %shard_map.130 = bf16[384,384]{1,0:T(8,128)(2,1)} custom-call(s32[16]{0:T(128)} %compare_select_fusion.fetch_ref, s32[16]{0:T(128)} %fusion.27.allow_ref, bf16[384,384]{1,0:T(8,128)(2,1)} %copy.68.q_ref, bf16[384,384]{1,0:T(8,128)(2,1)} %copy.69.kf_ref, bf16[384,384]{1,0:T(8,128)(2,1)} %copy.70.vf_ref, bf16[16,2,384,384]{3,2,1,0:T(8,128)(2,1)} %bitcast.132, ...), custom_call_target="tpu_custom_call" | custom-call | tf_op jit(solution)/shard_map/pallas_call | solution.py:138
  106.6 3.2 %convolution_convert_fusion.1.part_ref = bf16[384,3072]{1,0:T(8,128)(2,1)S(1)} fusion(bf16[384,384]{1,0:T(8,128)(2,1)} %shard_map.130, bf16[2,384,3072]{2,1,0:T(8,128)(2,1)} %param.14), kind=kOutput, calls=%fused_computation.21 | convolution fusion | flops 907149312 | bytes 5013504 | tf_op jit(solution)/shard_map/dot_general | solution.py:393
  109.8 32.6 %shard_map.131 = (bf16[48,3072]{1,0:T(8,128)(2,1)S(1)}, bf16[2,4,48,3072]{3,2,1,0:T(8,128)(2,1)S(1)}) custom-call(bf16[384,3072]{1,0:T(8,128)(2,1)S(1)} %convolution_convert_fusion.1.part_ref, bf16[48,3072]{1,0:T(8,128)(2,1)S(1)} %dynamic-slice_bitcast_fusion.own_ref, f32[1,3072]{1,0:T(1,128)S(1)} %get-tuple-element.47.gate_ref), custom_call_target="tpu_custom_call" | custom-call | tf_op jit(solution)/shard_map/pallas_call | solution.py:320
  143.6 1.2 fusion.5
  145.3 1.4 convolution_convert_fusion.2
  147.6 3.2 %multiply_reduce_fusion.1 = (f32[384,3]{0,1:T(4,128)S(1)}, f32[384,3,128]{0,2,1:T(8,128)S(1)}) fusion(bf16[384,3072,1]{1,0,2:T(8,128)(2,1)} %bitcast.140, bf16[3,128,3072]{2,1,0:T(8,128)(2,1)S(1)} %bitcast.136), kind=kOutput, calls=%fused_computation.46 | convolution fusion | flops 906263424 | bytes 5313024 | tf_op jit(solution)/shard_map/dot_general | solution.py:62
  151.3 3.9 %multiply_reduce_fusion = (f32[384,3]{0,1:T(4,128)S(1)}, f32[384,3,128]{0,2,1:T(8,128)S(1)}) fusion(bf16[384,3072,1]{1,0,2:T(8,128)(2,1)} %bitcast.141, bf16[3,128,3072]{2,1,0:T(8,128)(2,1)} %bitcast.135), kind=kOutput, calls=%fused_computation.44 | convolution fusion | flops 906263424 | bytes 5313024 | tf_op jit(solution)/shard_map/dot_general | solution.py:62
  156.1 1.6 subtract_convert_fusion
  161.1 5.5 %all-gather.7.cloned.1.call-done = bf16[16,2,1,384,384]{4,3,2,1,0:T(8,128)(2,1)} async-done(((bf16[1,2,1,384,384]{4,3,2,1,0:T(8,128)(2,1)}), bf16[16,2,1,384,384]{4,3,2,1,0:T(8,128)(2,1)}) %all-gather.7.cloned.1.call-update) | async-done | bytes 9437200 | tf_op jit(solution)/shard_map/all_gather | solution.py:375
  166.6 17.3 %shard_map.132 = bf16[384,384]{1,0:T(8,128)(2,1)} custom-call(s32[16]{0:T(128)} %compare_select_fusion.fetch_ref, s32[16]{0:T(128)} %fusion.27.allow_ref, bf16[384,384]{1,0:T(8,128)(2,1)} %copy.74.q_ref, bf16[384,384]{1,0:T(8,128)(2,1)} %copy.75.kf_ref, bf16[384,384]{1,0:T(8,128)(2,1)} %copy.76.vf_ref, bf16[16,2,384,384]{3,2,1,0:T(8,128)(2,1)} %bitcast.130, ...), custom_call_target="tpu_custom_call" | custom-call | tf_op jit(solution)/shard_map/pallas_call | solution.py:138
  183.9 3.2 %convolution_convert_fusion.part_ref = bf16[384,3072]{1,0:T(8,128)(2,1)S(1)} fusion(bf16[384,384]{1,0:T(8,128)(2,1)} %shard_map.132, bf16[2,384,3072]{2,1,0:T(8,128)(2,1)} %param.14), kind=kOutput, calls=%fused_computation.20 | convolution fusion | flops 907149312 | bytes 5013504 | tf_op jit(solution)/shard_map/dot_general | solution.py:393
  187.1 18.5 %shard_map.133 = f32[48,3072]{1,0:T(8,128)S(1)} custom-call(bf16[384,3072]{1,0:T(8,128)(2,1)S(1)} %convolution_convert_fusion.part_ref, bf16[48,3072]{1,0:T(8,128)(2,1)S(1)} %get-tuple-element.7.own_ref, f32[1,3072]{1,0:T(1,128)S(1)} %get-tuple-element.46.gate_ref), custom_call_target="tpu_custom_call" | custom-call | tf_op jit(solution)/shard_map/pallas_call | solution.py:320
  (87 shorter events, 21.4 us)
Async XLA Ops:
  7.2 199.8 %copy-start = (bf16[3072,64]{0,1:T(8,128)(2,1)S(1)}, bf16[3072,64]{0,1:T(8,128)(2,1)}, u32[]{:S(2)}) copy-start(bf16[3072,64]{0,1:T(8,128)(2,1)} %param.15) | copy-start | bytes 1179652
  7.2 82.0 %all-gather.5.cloned.1.call-start = ((), (), s32[]{:S(2)}) async-start(), calls=%async_computation | async-start | bytes 10027008 | tf_op jit(solution)/shard_map/all_gather | solution.py:375
  9.7 156.9 %all-gather.7.cloned.1.call-start = ((), (), s32[]{:S(2)}) async-start(), calls=%async_computation.1 | async-start | bytes 10027008 | tf_op jit(solution)/shard_map/all_gather | solution.py:375
  22.4 4.5 %copy-start.10 = (f32[2,2,128]{2,1,0:T(2,128)S(1)}, f32[2,2,128]{2,1,0:T(2,128)}, u32[]{:S(2)}) copy-start(f32[2,2,128]{2,1,0:T(2,128)} %param.16) | copy-start | bytes 6148
  22.4 4.5 %copy-start.1 = (bf16[1,384,3072]{2,1,0:T(8,128)(2,1)S(1)}, bf16[1,384,3072]{2,1,0:T(8,128)(2,1)}, u32[]{:S(2)}) copy-start(bf16[1,384,3072]{2,1,0:T(8,128)(2,1)} %param.11) | copy-start | bytes 7077892
  26.9 1.2 copy-start.9
  28.2 1.7 copy-start.4
  29.4 1.8 copy-start.6
  41.8 3.2 %copy-start.12 = (s32[4]{0:T(128)S(1)}, s32[4]{0:T(128)}, u32[]{:S(2)}) copy-start(s32[4]{0:T(128)} %param.19) | copy-start | bytes 52
  41.8 3.4 %copy-start.13 = (s32[16]{0:T(128)S(1)}, s32[16]{0:T(128)}, u32[]{:S(2)}) copy-start(s32[16]{0:T(128)} %param.20) | copy-start | bytes 196
  47.6 3.5 %copy-start.7 = (f32[384,64]{0,1:T(8,128)}, f32[384,64]{0,1:T(8,128)S(1)}, u32[]{:S(2)}) copy-start(f32[384,64]{0,1:T(8,128)S(1)} %get-tuple-element.55) | copy-start | bytes 294916
  143.6 1.7 copy-start.3
  144.8 1.9 copy-start.5
  145.3 2.3 %copy-start.2 = (bf16[384,3072]{1,0:T(8,128)(2,1)S(1)}, bf16[384,3072]{1,0:T(8,128)(2,1)}, u32[]{:S(2)}) copy-start(bf16[384,3072]{1,0:T(8,128)(2,1)} %copy.71) | copy-start | bytes 7077892
  155.2 0.9 copy-start.8
  187.1 19.9 %copy-start.11 = (f32[1,48,64]{2,1,0:T(8,128)S(1)}, f32[1,48,64]{2,1,0:T(8,128)}, u32[]{:S(2)}) copy-start(f32[1,48,64]{2,1,0:T(8,128)} %param.12) | copy-start | bytes 36868
Sparse Core Ops, SparseCore 0:
  10.2 78.9 all-gather.4
  91.3 75.1 all-gather.6

commit v7 on v6

--- a/solution.py
+++ b/solution.py
@@ -156,22 +156,23 @@
 
 def exchange_kernel(head_count, own_rows, split, gather, part_ref, own_ref, gate_ref, *rest):
     if gather:
-        (out_ref, full_ref, near, mid, land_a, land_b, sums_a, sums_b, acc,
-         s1_send, s1_recv, r_send, r_recv, a_send, a_recv, g2_send, g2_recv) = rest
+        (out_ref, full_ref, land_a, land_b, sums_a, sums_b, acc,
+         r_send, r_recv, a_send, a_recv, g2_send, g2_recv) = rest
     else:
-        (out_ref, near, mid, land_a, land_b, sums_a, sums_b, acc,
-         s1_send, s1_recv, r_send, r_recv) = rest
+        (out_ref, land_a, land_b, sums_a, sums_b, acc, r_send, r_recv) = rest
     mesh_ids = pl.DeviceIdType.MESH
     section = lax.axis_index("section")
     head = lax.axis_index("head")
     tok = lax.axis_index("tok")
     other = 1 - section
-    half = head_count * own_rows
     up = lax.rem(head + 1, head_count)
     down = lax.rem(head + head_count - 1, head_count)
     opposite = lax.rem(head + 2, head_count)
     low = pl.ds(0, split)
     high = pl.ds(split, own_rows - split)
+
+    def rows_of(block, offset, count):
+        return pl.ds(pl.multiple_of(block * own_rows + offset, 16), count)
 
     barrier = pltpu.get_barrier_semaphore()
     pl.semaphore_signal(barrier, inc=1, device_id=(other, head, tok), device_id_type=mesh_ids)
@@ -180,16 +181,6 @@
         def _greet():
             pl.semaphore_signal(barrier, inc=1, device_id=(section, h, tok), device_id_type=mesh_ids)
     pl.semaphore_wait(barrier, head_count)
-
-    def near_copy(h):
-        return pltpu.make_async_remote_copy(
-            src_ref=part_ref.at[pl.ds(pl.multiple_of(other * half + h * own_rows, own_rows), own_rows)],
-            dst_ref=near.at[h],
-            send_sem=s1_send.at[h],
-            recv_sem=s1_recv.at[h],
-            device_id=(other, head, tok),
-            device_id_type=mesh_ids,
-        )
 
     def ring(kind, src, dst, target, send_sem, recv_sem):
         return pltpu.make_async_remote_copy(
@@ -201,51 +192,36 @@
             device_id_type=mesh_ids,
         )
 
-    for h in range(head_count):
-        near_copy(h).start()
-    base = pl.multiple_of(section * half, own_rows)
-    for h in range(head_count):
-        near_copy(h).wait()
-
-        @pl.when(h != head)
-        def _pair():
-            rows = pl.ds(pl.multiple_of(base + h * own_rows, own_rows), own_rows)
-            mid[h] = (part_ref[rows, :].astype(jnp.float32) + near[h].astype(jnp.float32)).astype(
-                mid.dtype
-            )
-
-    pass_a = ring(0, mid.at[opposite, low], land_a.at[0], up, r_send, r_recv)
-    pass_b = ring(1, mid.at[opposite, high], land_b.at[0], down, r_send, r_recv)
-    direct_a = ring(2, mid.at[down, low], land_a.at[1], down, r_send, r_recv)
-    direct_b = ring(3, mid.at[up, high], land_b.at[1], up, r_send, r_recv)
+    low_count = split
+    high_count = own_rows - split
+    pass_a = ring(0, part_ref.at[rows_of(opposite, 0, low_count)], land_a.at[0], up, r_send, r_recv)
+    pass_b = ring(1, part_ref.at[rows_of(opposite, split, high_count)], land_b.at[0], down, r_send, r_recv)
+    direct_a = ring(2, part_ref.at[rows_of(down, 0, low_count)], land_a.at[1], down, r_send, r_recv)
+    direct_b = ring(3, part_ref.at[rows_of(up, split, high_count)], land_b.at[1], up, r_send, r_recv)
     pass_a.start()
     pass_b.start()
     direct_a.start()
     direct_b.start()
-    mine = pl.ds(pl.multiple_of(base + head * own_rows, own_rows), own_rows)
-    acc[...] = part_ref[mine, :].astype(jnp.float32) + near[head].astype(jnp.float32)
+    acc[...] = part_ref[rows_of(head, 0, own_rows), :].astype(jnp.float32)
     pass_a.wait()
-    sums_a[...] = (mid[up, low].astype(jnp.float32) + land_a[0].astype(jnp.float32)).astype(
-        sums_a.dtype
-    )
+    sums_a[...] = (
+        part_ref[rows_of(up, 0, low_count), :].astype(jnp.float32) + land_a[0].astype(jnp.float32)
+    ).astype(sums_a.dtype)
     joined_a = ring(4, sums_a, land_a.at[2], up, r_send, r_recv)
     joined_a.start()
     pass_b.wait()
-    sums_b[...] = (mid[down, high].astype(jnp.float32) + land_b[0].astype(jnp.float32)).astype(
-        sums_b.dtype
-    )
+    sums_b[...] = (
+        part_ref[rows_of(down, split, high_count), :].astype(jnp.float32)
+        + land_b[0].astype(jnp.float32)
+    ).astype(sums_b.dtype)
     joined_b = ring(5, sums_b, land_b.at[2], down, r_send, r_recv)
     joined_b.start()
     direct_a.wait()
     direct_b.wait()
     joined_a.wait()
     joined_b.wait()
-    acc[low, :] += (
-        land_a[1].astype(jnp.float32) + land_a[2].astype(jnp.float32)
-    )
-    acc[high, :] += (
-        land_b[1].astype(jnp.float32) + land_b[2].astype(jnp.float32)
-    )
+    acc[low, :] += land_a[1].astype(jnp.float32) + land_a[2].astype(jnp.float32)
+    acc[high, :] += land_b[1].astype(jnp.float32) + land_b[2].astype(jnp.float32)
     if not gather:
         out_ref[...] = acc[...]
         return
@@ -291,26 +267,21 @@
 
 def exchange(partial, own_input, gate, layer_idx, gather, head_count, own_rows):
     rows, width = partial.shape
-    half = head_count * own_rows
     split = (own_rows * 2 // 3) // 16 * 16
     vmem = pl.BlockSpec(memory_space=pltpu.VMEM)
     scratch = [
-        pltpu.VMEM((head_count, own_rows, width), partial.dtype),
-        pltpu.VMEM((head_count, own_rows, width), partial.dtype),
         pltpu.VMEM((3, split, width), partial.dtype),
         pltpu.VMEM((3, own_rows - split, width), partial.dtype),
         pltpu.VMEM((split, width), partial.dtype),
         pltpu.VMEM((own_rows - split, width), partial.dtype),
         pltpu.VMEM((own_rows, width), jnp.float32),
-        pltpu.SemaphoreType.DMA((head_count,)),
-        pltpu.SemaphoreType.DMA((head_count,)),
         pltpu.SemaphoreType.DMA((6,)),
         pltpu.SemaphoreType.DMA((6,)),
     ]
     if gather:
         out_shape = (
             jax.ShapeDtypeStruct((own_rows, width), jnp.bfloat16),
-            jax.ShapeDtypeStruct((rows // half, head_count, own_rows, width), jnp.bfloat16),
+            jax.ShapeDtypeStruct((2, head_count, own_rows, width), jnp.bfloat16),
         )
         out_specs = (vmem, vmem)
         scratch += [pltpu.SemaphoreType.DMA((head_count,))] * 4
@@ -376,6 +347,7 @@
         for layer in range(layer_count)
     ]
     current_full = hidden[0]
+    w_partner = lax.ppermute(w_out, "section", perm=[(0, 1), (1, 0)])
     own_input = lax.dynamic_slice_in_dim(current_full, group_index * own_rows, own_rows, 0)
     outputs = []
     for layer_idx in range(layer_count):
@@ -390,9 +362,14 @@
         attended = attend(
             queries, keys_fresh, values_fresh, stale_layers[layer_idx], fetch, allow, head_dim
         )
-        partial = jnp.dot(attended, w_out[layer_idx], preferred_element_type=jnp.float32).astype(
-            jnp.bfloat16
-        )
+        half_rows = patch_len // section_count
+        mine = lax.dynamic_slice_in_dim(attended, section_index * half_rows, half_rows, 0)
+        theirs = lax.dynamic_slice_in_dim(attended, (1 - section_index) * half_rows, half_rows, 0)
+        swapped = lax.ppermute(theirs, "section", perm=[(0, 1), (1, 0)])
+        partial = (
+            jnp.dot(mine, w_out[layer_idx], preferred_element_type=jnp.float32)
+            + jnp.dot(swapped, w_partner[layer_idx], preferred_element_type=jnp.float32)
+        ).astype(jnp.bfloat16)
         gate = modulation[layer_idx, 2]
         if layer_idx + 1 < layer_count:
             own_out, gathered = exchange(

time: 216 us -> 216 us (level)
  the two profiles are of different devices: /device:TPU:1 before, /device:TPU:8 now
where the time goes in v7:
time: 216 us; the launch traced here: 213 us
  Pallas kernels  78.2 us (36%)
  local copies, waits for them, and re-layouts  54.4 us (25%)
  matrix products  28.5 us (13%)
  other arithmetic  22.2 us (10%)
  between operations  15.9 us (7%)
  waiting for transfers between devices  13.7 us (6%)
    pallas_call x2, Pallas kernels, exchange(): pl.pallas_call(functools.partial(exchange_kernel, head_count, own_rows, s...  45.4 us
    pallas_call x2, Pallas kernels, attend(): pl.pallas_call(functools.partial(attention_kernel, head_dim), out_shape=j...  32.8 us
    dot_general x7, local copies, waits for them, and re-layouts, project(): jnp.dot(normed, weight[:, part, :], preferred_element_type=jnp.float32)  31.2 us
    dot_general x6, matrix products, project(): jnp.dot(normed, weight[:, part, :], preferred_element_type=jnp.float32)  17.4 us
    all_gather x2, waiting for transfers between devices, shards(): lax.all_gather(jnp.swapaxes(stale_kv[layer], 0, 1), 'tok', axis=0, tiled=...  13 us
    squeeze x1, local copies, waits for them, and re-layouts, shards(): w_qkv[layer_idx]  6.09 us
    another operation x5, other arithmetic  5.26 us
    dot_general x2, matrix products, shards(): jnp.dot(mine, w_out[layer_idx], preferred_element_type=jnp.float32)  5.13 us
  transfers between devices with their start and end apart: 5, of which 2 were waited for; matrix products, arithmetic and copies ran while one was open for 45% of the time, Pallas kernels for 21%

profile of v7, /device:TPU:8, one launch (start us, length us, event | category | flops | bytes accessed | tf_op | source)
XLA Modules:
  0.0 213.3 jit_solution(2079553122696587486)
XLA Ops:
  7.2 2.4 %fusion.36 = (bf16[1,2,1,384,384]{4,3,2,1,0:T(8,128)(2,1)}, bf16[1,2,1,384,384]{4,3,2,1,0:T(8,128)(2,1)}) fusion(bf16[2,2,1,384,384]{4,3,2,1,0:T(8,128)(2,1)} %param.18), kind=kLoop, calls=%fused_computation.113 | loop fusion | bytes 2359296 | tf_op jit(solution)/shard_map/slice | solution.py:346
  11.2 6.1 %slice_bitcast_fusion = (bf16[3072,3,384]{2,0,1:T(8,128)(2,1)S(1)}, bf16[3072,3,384]{2,0,1:T(8,128)(2,1)S(1)}) fusion(bf16[2,3072,3,384]{3,1,2,0:T(8,128)(2,1)} %param.13), kind=kLoop, calls=%fused_computation | loop fusion | bytes 28311552 | tf_op jit(solution)/shard_map/squeeze | solution.py:357
  17.3 5.2 %slice_bitcast_fusion.4 = (bf16[384,3072]{0,1:T(8,128)(2,1)}, bf16[384,3072]{0,1:T(8,128)(2,1)}, bf16[384,3072]{0,1:T(8,128)(2,1)}, bf16[384,3072]{0,1:T(8,128)(...) fusion(bf16[3072,3,384]{2,0,1:T(8,128)(2,1)S(1)} %get-tuple-element.23, ...), kind=kLoop, calls=%fused_computation.26 | loop fusion | bytes 28311552 | tf_op jit(solution)/shard_map/dot_general | solution.py:62
  22.5 4.4 %copy.65 = bf16[384,3072]{1,0:T(8,128)(2,1)} copy(bf16[384,3072]{0,1:T(8,128)(2,1)} %get-tuple-element.68) | data formatting | bytes 4718592 | tf_op jit(solution)/shard_map/dot_general | solution.py:62
  28.3 1.3 fusion.15
  30.0 1.4 multiply_reduce_fusion.3
  32.3 1.4 reshape.471
  33.8 4.3 %copy.66 = bf16[384,3072]{1,0:T(8,128)(2,1)} copy(bf16[384,3072]{0,1:T(8,128)(2,1)} %get-tuple-element.69) | data formatting | bytes 4718592 | tf_op jit(solution)/shard_map/dot_general | solution.py:62
  38.0 3.8 %multiply_reduce_fusion.2 = (f32[384,3]{0,1:T(4,128)S(1)}, f32[384,3,128]{0,2,1:T(8,128)S(1)}) fusion(bf16[384,3072,1]{1,0,2:T(8,128)(2,1)} %copy-done.6, bf16[3,128,3072]{2,1,0:T(8,128)(2,1)} %bitcast.148), kind=kOutput, calls=%fused_computation.54 | convolution fusion | flops 906263424 | bytes 5313024 | tf_op jit(solution)/shard_map/dot_general | solution.py:62
  42.8 2.2 %reshape.472 = f32[384,3,64,2]{0,3,2,1:T(2,128)} reshape(f32[384,3,128]{0,2,1:T(8,128)} %multiply_multiply_fusion.2) | data formatting | bytes 1179648 | tf_op jit(solution)/shard_map/reshape | solution.py:34
  47.7 3.4 %subtract_convert_fusion.2 = (bf16[384,3,64,1]{0,3,2,1:T(2,128)(2,1)S(1)}, bf16[384,3,64,1]{0,3,2,1:T(2,128)(2,1)S(1)}, bf16[384,3,64,1]{0,3,2,1:T(2,128)(2,1)}, bf16[384,3,64,1]{0,3,2,1:T(2,128)(2,1)}) fusion(f32[384,3,64,2]{0,3,2,1:T(2,128)} %reshape.472, f32[384,64]{0,1:T(8,128)S(1)} %get-tuple-element.55, f32[384,64]{0,1:T(8,128)S(1)} %get-tuple-element.54, ...), kind=kLoop, calls=%fused_computation.70 | loop fusion | flops 1179648 | bytes 1966080 | tf_op jit(solution)/shard_map/convert.4
  52.8 1.7 pad_maximum_fusion
  56.4 4.3 %copy.67 = bf16[384,3072]{1,0:T(8,128)(2,1)} copy(bf16[384,3072]{0,1:T(8,128)(2,1)} %get-tuple-element.70) | data formatting | bytes 4718592 | tf_op jit(solution)/shard_map/dot_general | solution.py:62
  60.7 3.9 %convolution_convert_fusion.1 = bf16[384,3,128]{0,2,1:T(8,128)(2,1)S(1)} fusion(bf16[384,3072,1]{1,0,2:T(8,128)(2,1)} %copy-done.6, bf16[3,128,3072]{2,1,0:T(8,128)(2,1)} %bitcast.149), kind=kOutput, calls=%fused_computation.40 | convolution fusion | flops 906117120 | bytes 5013504 | tf_op jit(solution)/shard_map/dot_general | solution.py:62
  65.5 4.3 %copy.73 = bf16[384,3072]{1,0:T(8,128)(2,1)} copy(bf16[384,3072]{0,1:T(8,128)(2,1)} %get-tuple-element.25) | data formatting | bytes 4718592 | tf_op jit(solution)/shard_map/dot_general | solution.py:62
  69.8 4.4 %copy.71 = bf16[384,3072]{1,0:T(8,128)(2,1)} copy(bf16[384,3072]{0,1:T(8,128)(2,1)} %get-tuple-element.27) | data formatting | bytes 4718592 | tf_op jit(solution)/shard_map/dot_general | solution.py:62
  74.2 4.3 %copy.72 = bf16[384,3072]{1,0:T(8,128)(2,1)} copy(bf16[384,3072]{0,1:T(8,128)(2,1)} %get-tuple-element.26) | data formatting | bytes 4718592 | tf_op jit(solution)/shard_map/dot_general | solution.py:62
  79.7 1.3 iota_reduce_fusion
  82.1 6.1 %all-gather.5.cloned.1.call-done = bf16[16,2,1,384,384]{4,3,2,1,0:T(8,128)(2,1)} async-done(((bf16[1,2,1,384,384]{4,3,2,1,0:T(8,128)(2,1)}), bf16[16,2,1,384,384]{4,3,2,1,0:T(8,128)(2,1)}) %all-gather.5.cloned.1.call-update) | async-done | bytes 9437200 | tf_op jit(solution)/shard_map/all_gather | solution.py:346
  88.2 16.4 %shard_map.130 = bf16[384,384]{1,0:T(8,128)(2,1)} custom-call(s32[16]{0:T(128)} %compare_select_fusion.fetch_ref, s32[16]{0:T(128)} %fusion.35.allow_ref, bf16[384,384]{1,0:T(8,128)(2,1)} %copy.68.q_ref, bf16[384,384]{1,0:T(8,128)(2,1)} %copy.69.kf_ref, bf16[384,384]{1,0:T(8,128)(2,1)} %copy.70.vf_ref, bf16[16,2,384,384]{3,2,1,0:T(8,128)(2,1)} %bitcast.138, ...), custom_call_target="tpu_custom_call" | custom-call | tf_op jit(solution)/shard_map/pallas_call | solution.py:138
  105.6 2.6 %fusion.18 = f32[192,3072]{1,0:T(8,128)S(1)} fusion(bf16[2,384,3072]{2,1,0:T(8,128)(2,1)} %param.14, bf16[384,384]{1,0:T(8,128)(2,1)} %shard_map.130, s32[]{:T(128)S(6)} %select_n.42), kind=kOutput, calls=%fused_computation.35 | convolution fusion | flops 452984832 | bytes 4866052 | tf_op jit(solution)/shard_map/dot_general | solution.py:370
  108.2 2.6 %fusion.13.part_ref = bf16[192,3072]{1,0:T(8,128)(2,1)S(1)} fusion(f32[192,3072]{1,0:T(8,128)S(1)} %fusion.18, bf16[192,384]{1,0:T(8,128)(2,1)S(1)} %collective-permute-done, bf16[2,384,3072]{2,1,0:T(8,128)(2,1)} %collective-permute-done.1), kind=kOutput, calls=%fused_computation.22 | convolution fusion | flops 454164480 | bytes 6045696 | tf_op jit(solution)/shard_map/dot_general | solution.py:371
  110.8 29.4 %shard_map.131 = (bf16[48,3072]{1,0:T(8,128)(2,1)S(1)}, bf16[2,4,48,3072]{3,2,1,0:T(8,128)(2,1)S(1)}) custom-call(bf16[192,3072]{1,0:T(8,128)(2,1)S(1)} %fusion.13.part_ref, bf16[48,3072]{1,0:T(8,128)(2,1)S(1)} %dynamic-slice_bitcast_fusion.own_ref, f32[1,3072]{1,0:T(1,128)S(1)} %get-tuple-element.47.gate_ref), custom_call_target="tpu_custom_call" | custom-call | tf_op jit(solution)/shard_map/pallas_call | solution.py:291
  143.1 1.4 convolution_convert_fusion
  145.4 3.1 %multiply_reduce_fusion.1 = (f32[384,3]{0,1:T(4,128)S(1)}, f32[384,3,128]{0,2,1:T(8,128)S(1)}) fusion(bf16[384,3072,1]{1,0,2:T(8,128)(2,1)} %bitcast.146, bf16[3,128,3072]{2,1,0:T(8,128)(2,1)S(1)} %bitcast.142), kind=kOutput, calls=%fused_computation.52 | convolution fusion | flops 906263424 | bytes 5313024 | tf_op jit(solution)/shard_map/dot_general | solution.py:62
  149.0 3.9 %multiply_reduce_fusion = (f32[384,3]{0,1:T(4,128)S(1)}, f32[384,3,128]{0,2,1:T(8,128)S(1)}) fusion(bf16[384,3072,1]{1,0,2:T(8,128)(2,1)} %bitcast.147, bf16[3,128,3072]{2,1,0:T(8,128)(2,1)} %bitcast.141), kind=kOutput, calls=%fused_computation.50 | convolution fusion | flops 906263424 | bytes 5313024 | tf_op jit(solution)/shard_map/dot_general | solution.py:62
  153.7 1.6 subtract_convert_fusion
  158.7 6.9 %all-gather.7.cloned.1.call-done = bf16[16,2,1,384,384]{4,3,2,1,0:T(8,128)(2,1)} async-done(((bf16[1,2,1,384,384]{4,3,2,1,0:T(8,128)(2,1)}), bf16[16,2,1,384,384]{4,3,2,1,0:T(8,128)(2,1)}) %all-gather.7.cloned.1.call-update) | async-done | bytes 9437200 | tf_op jit(solution)/shard_map/all_gather | solution.py:346
  165.6 16.4 %shard_map.132 = bf16[384,384]{1,0:T(8,128)(2,1)} custom-call(s32[16]{0:T(128)} %compare_select_fusion.fetch_ref, s32[16]{0:T(128)} %fusion.35.allow_ref, bf16[384,384]{1,0:T(8,128)(2,1)} %copy.74.q_ref, bf16[384,384]{1,0:T(8,128)(2,1)} %copy.75.kf_ref, bf16[384,384]{1,0:T(8,128)(2,1)} %copy.76.vf_ref, bf16[16,2,384,384]{3,2,1,0:T(8,128)(2,1)} %bitcast.136, ...), custom_call_target="tpu_custom_call" | custom-call | tf_op jit(solution)/shard_map/pallas_call | solution.py:138
  183.0 2.5 %fusion.16 = f32[192,3072]{1,0:T(8,128)S(1)} fusion(bf16[2,384,3072]{2,1,0:T(8,128)(2,1)} %param.14, bf16[384,384]{1,0:T(8,128)(2,1)} %shard_map.132, s32[]{:T(128)S(6)} %select_n.42), kind=kOutput, calls=%fused_computation.33 | convolution fusion | flops 452984832 | bytes 4866052 | tf_op jit(solution)/shard_map/dot_general | solution.py:370
  185.6 2.5 %fusion.14.part_ref = bf16[192,3072]{1,0:T(8,128)(2,1)S(1)} fusion(f32[192,3072]{1,0:T(8,128)S(1)} %fusion.16, bf16[192,384]{1,0:T(8,128)(2,1)S(1)} %collective-permute-done.2, bf16[2,384,3072]{2,1,0:T(8,128)(2,1)} %collective-permute-done.1), kind=kOutput, calls=%fused_computation.23 | convolution fusion | flops 454164480 | bytes 6045696 | tf_op jit(solution)/shard_map/dot_general | solution.py:371
  188.1 16.1 %shard_map.133 = f32[48,3072]{1,0:T(8,128)S(1)} custom-call(bf16[192,3072]{1,0:T(8,128)(2,1)S(1)} %fusion.14.part_ref, bf16[48,3072]{1,0:T(8,128)(2,1)S(1)} %get-tuple-element.7.own_ref, f32[1,3072]{1,0:T(1,128)S(1)} %get-tuple-element.46.gate_ref), custom_call_target="tpu_custom_call" | custom-call | tf_op jit(solution)/shard_map/pallas_call | solution.py:291
  (97 shorter events, 26.0 us)
Async XLA Ops:
  7.2 198.3 %copy-start = (bf16[3072,64]{0,1:T(8,128)(2,1)S(1)}, bf16[3072,64]{0,1:T(8,128)(2,1)}, u32[]{:S(2)}) copy-start(bf16[3072,64]{0,1:T(8,128)(2,1)} %param.15) | copy-start | bytes 1179652
  7.2 81.0 %all-gather.5.cloned.1.call-start = ((), (), s32[]{:S(2)}) async-start(), calls=%async_computation | async-start | bytes 10027008 | tf_op jit(solution)/shard_map/all_gather | solution.py:346
  9.7 155.9 %all-gather.7.cloned.1.call-start = ((), (), s32[]{:S(2)}) async-start(), calls=%async_computation.1 | async-start | bytes 10027008 | tf_op jit(solution)/shard_map/all_gather | solution.py:346
  10.4 97.8 %collective-permute-start.1 = (bf16[2,384,3072]{2,1,0:T(8,128)(2,1)}, bf16[2,384,3072]{2,1,0:T(8,128)(2,1)}, u32[]{:S(2)}, u32[]{:S(2)}) collective-permute-start(bf16[2,384,3072]{2,1,0:T(8,128)(2,1)} %param.14), channel_id=1, source_target_pairs={{0,64},{64,0},{1,65},{65,1},{2,66},{66,2},{3,67},{67,3},{4,68},{68... | collective-permute-start | bytes 14155784 | tf_op jit(solution)/shard_map/ppermute | solution.py:350
  22.5 4.4 %copy-start.10 = (f32[2,2,128]{2,1,0:T(2,128)S(1)}, f32[2,2,128]{2,1,0:T(2,128)}, u32[]{:S(2)}) copy-start(f32[2,2,128]{2,1,0:T(2,128)} %param.16) | copy-start | bytes 6148
  22.5 4.4 %copy-start.1 = (bf16[1,384,3072]{2,1,0:T(8,128)(2,1)S(1)}, bf16[1,384,3072]{2,1,0:T(8,128)(2,1)}, u32[]{:S(2)}) copy-start(bf16[1,384,3072]{2,1,0:T(8,128)(2,1)} %param.11) | copy-start | bytes 7077892
  27.0 1.2 copy-start.9
  28.2 1.7 copy-start.4
  29.5 1.9 copy-start.6
  41.8 3.2 %copy-start.12 = (s32[4]{0:T(128)S(1)}, s32[4]{0:T(128)}, u32[]{:S(2)}) copy-start(s32[4]{0:T(128)} %param.19) | copy-start | bytes 52
  41.9 3.4 %copy-start.13 = (s32[16]{0:T(128)S(1)}, s32[16]{0:T(128)}, u32[]{:S(2)}) copy-start(s32[16]{0:T(128)} %param.20) | copy-start | bytes 196
  47.7 3.4 %copy-start.7 = (f32[384,64]{0,1:T(8,128)}, f32[384,64]{0,1:T(8,128)S(1)}, u32[]{:S(2)}) copy-start(f32[384,64]{0,1:T(8,128)S(1)} %get-tuple-element.55) | copy-start | bytes 294916
  105.5 2.7 %collective-permute-start = (bf16[192,384]{1,0:T(8,128)(2,1)S(1)}, bf16[192,384]{1,0:T(8,128)(2,1)S(1)}, u32[]{:S(2)}, u32[]{:S(2)}) collective-permute-start(bf16[192,384]{1,0:T(8,128)(2,1)S(1)} %constant_dynamic-slice_fusion.1), channel_id=1, source_target_pairs={{0,64},{64,0},{1,65},{65,1},{2,66},{66,2},{3,67},{67,3},{4,68},{68... | collective-permute-start | bytes 442376 | tf_op jit(solution)/shard_map/ppermute | solution.py:368
  141.3 1.8 copy-start.3
  142.6 1.9 copy-start.5
  143.1 2.3 %copy-start.2 = (bf16[384,3072]{1,0:T(8,128)(2,1)S(1)}, bf16[384,3072]{1,0:T(8,128)(2,1)}, u32[]{:S(2)}) copy-start(bf16[384,3072]{1,0:T(8,128)(2,1)} %copy.71) | copy-start | bytes 7077892
  152.8 0.9 copy-start.8
  182.9 2.6 %collective-permute-start.2 = (bf16[192,384]{1,0:T(8,128)(2,1)S(1)}, bf16[192,384]{1,0:T(8,128)(2,1)S(1)}, u32[]{:S(2)}, u32[]{:S(2)}) collective-permute-start(bf16[192,384]{1,0:T(8,128)(2,1)S(1)} %constant_dynamic-slice_fusion), channel_id=1, source_target_pairs={{0,64},{64,0},{1,65},{65,1},{2,66},{66,2},{3,67},{67,3},{4,68},{68... | collective-permute-start | bytes 442376 | tf_op jit(solution)/shard_map/ppermute | solution.py:368
  188.1 17.4 %copy-start.11 = (f32[1,48,64]{2,1,0:T(8,128)S(1)}, f32[1,48,64]{2,1,0:T(8,128)}, u32[]{:S(2)}) copy-start(f32[1,48,64]{2,1,0:T(8,128)} %param.12) | copy-start | bytes 36868
Sparse Core Ops, SparseCore 0:
  10.2 77.9 all-gather.4
  90.3 75.2 all-gather.6

commit v8 on v7

--- a/solution.py
+++ b/solution.py
@@ -9,6 +9,7 @@
 from jax.sharding import PartitionSpec as P
 
 STEPS = 28
+MOST = 8
 
 
 norm_eps = 1e-06
@@ -126,7 +127,7 @@
 
 def attend(queries, keys_fresh, values_fresh, stale, fetch, allow, head_dim):
     rows, features = queries.shape
-    slot_total = stale.shape[0]
+    slot_total = fetch.shape[0]
     heads = features // head_dim
     whole = pl.BlockSpec((rows, features), lambda j, f, a: (0, 0))
     key_spec = pl.BlockSpec(
@@ -337,11 +338,14 @@
     positions = (my_offset * patch_len + jnp.arange(patch_len, dtype=jnp.int32)).astype(jnp.float32)
     slot_ids = jnp.arange(slot_total, dtype=jnp.int32)
     allowed = (request_of == my_request) & (slot_ids != tok_index)
-    marked = jnp.where(allowed, slot_ids, -1)
-    running = lax.cummax(marked, axis=0)
-    first_allowed = jnp.argmax(allowed).astype(jnp.int32)
-    fetch = jnp.where(running >= 0, running, first_allowed).astype(jnp.int32)
-    allow = allowed.astype(jnp.int32)
+    rank = jnp.cumsum(allowed.astype(jnp.int32)) - 1
+    count = jnp.sum(allowed.astype(jnp.int32))
+    step_ids = jnp.arange(MOST - 1, dtype=jnp.int32)
+    picked = allowed[None, :] & (rank[None, :] == step_ids[:, None])
+    compact = jnp.sum(jnp.where(picked, slot_ids[None, :], 0), axis=1)
+    last_pick = jnp.sum(jnp.where(allowed & (rank == count - 1), slot_ids, 0))
+    fetch = jnp.where(step_ids < count, compact, last_pick).astype(jnp.int32)
+    allow = (step_ids < count).astype(jnp.int32)
     stale_layers = [
         lax.all_gather(jnp.swapaxes(stale_kv[layer], 0, 1), "tok", axis=0, tiled=True)
         for layer in range(layer_count)

time: 216 us -> 212 us (0.981)
  Pallas kernels: 78.2 us -> 73.2 us
    pallas_call x2, Pallas kernels: 32.8 us -> 27.8 us  [attend(): pl.pallas_call(functools.partial(attention_kernel, head_dim), out_shape=j...]
    another operation x6 -> x4, other arithmetic: 6.55 us -> 5.14 us
  transfers between devices with their start and end apart: 5 -> 5, of which waited for: 2 -> 2; matrix products, arithmetic and copies ran while one was open for 45% -> 46% of each run, Pallas kernels for 21% -> 21%
where the time goes in v8:
time: 212 us; the launch traced here: 211 us
  Pallas kernels  73.2 us (35%)
  local copies, waits for them, and re-layouts  54.4 us (26%)
  matrix products  28.6 us (13%)
  other arithmetic  23.7 us (11%)
  between operations  16.5 us (8%)
  waiting for transfers between devices  14 us (7%)
    pallas_call x2, Pallas kernels, exchange(): pl.pallas_call(functools.partial(exchange_kernel, head_count, own_rows, s...  45.4 us
    dot_general x7, local copies, waits for them, and re-layouts, project(): jnp.dot(normed, weight[:, part, :], preferred_element_type=jnp.float32)  31.2 us
    pallas_call x2, Pallas kernels, attend(): pl.pallas_call(functools.partial(attention_kernel, head_dim), out_shape=j...  27.8 us
    dot_general x6, matrix products, project(): jnp.dot(normed, weight[:, part, :], preferred_element_type=jnp.float32)  17.5 us
    all_gather x2, waiting for transfers between devices, shards(): lax.all_gather(jnp.swapaxes(stale_kv[layer], 0, 1), 'tok', axis=0, tiled=...  13.3 us
    squeeze x1, local copies, waits for them, and re-layouts, shards(): w_qkv[layer_idx]  6.09 us
    another operation x4, other arithmetic  5.14 us
    dot_general x2, matrix products, shards(): jnp.dot(mine, w_out[layer_idx], preferred_element_type=jnp.float32)  5.09 us
  transfers between devices with their start and end apart: 5, of which 2 were waited for; matrix products, arithmetic and copies ran while one was open for 46% of the time, Pallas kernels for 21%

profile of v8, /device:TPU:8, one launch (start us, length us, event | category | flops | bytes accessed | tf_op | source)
XLA Modules:
  0.0 210.8 jit_solution(3599165373665913169)
XLA Ops:
  7.2 2.4 %fusion.37 = (bf16[1,2,1,384,384]{4,3,2,1,0:T(8,128)(2,1)}, bf16[1,2,1,384,384]{4,3,2,1,0:T(8,128)(2,1)}) fusion(bf16[2,2,1,384,384]{4,3,2,1,0:T(8,128)(2,1)} %param.18), kind=kLoop, calls=%fused_computation.119 | loop fusion | bytes 2359296 | tf_op jit(solution)/shard_map/slice | solution.py:350
  11.2 6.1 %slice_bitcast_fusion = (bf16[3072,3,384]{2,0,1:T(8,128)(2,1)S(1)}, bf16[3072,3,384]{2,0,1:T(8,128)(2,1)S(1)}) fusion(bf16[2,3072,3,384]{3,1,2,0:T(8,128)(2,1)} %param.13), kind=kLoop, calls=%fused_computation | loop fusion | bytes 28311552 | tf_op jit(solution)/shard_map/squeeze | solution.py:361
  17.3 5.2 %slice_bitcast_fusion.4 = (bf16[384,3072]{0,1:T(8,128)(2,1)}, bf16[384,3072]{0,1:T(8,128)(2,1)}, bf16[384,3072]{0,1:T(8,128)(2,1)}, bf16[384,3072]{0,1:T(8,128)(...) fusion(bf16[3072,3,384]{2,0,1:T(8,128)(2,1)S(1)} %get-tuple-element.23, ...), kind=kLoop, calls=%fused_computation.26 | loop fusion | bytes 28311552 | tf_op jit(solution)/shard_map/dot_general | solution.py:63
  22.5 4.4 %copy.65 = bf16[384,3072]{1,0:T(8,128)(2,1)} copy(bf16[384,3072]{0,1:T(8,128)(2,1)} %get-tuple-element.68) | data formatting | bytes 4718592 | tf_op jit(solution)/shard_map/dot_general | solution.py:63
  30.0 1.4 multiply_reduce_fusion.3
  32.3 1.4 reshape.472
  33.8 4.3 %copy.66 = bf16[384,3072]{1,0:T(8,128)(2,1)} copy(bf16[384,3072]{0,1:T(8,128)(2,1)} %get-tuple-element.69) | data formatting | bytes 4718592 | tf_op jit(solution)/shard_map/dot_general | solution.py:63
  38.0 3.8 %multiply_reduce_fusion.2 = (f32[384,3]{0,1:T(4,128)S(1)}, f32[384,3,128]{0,2,1:T(8,128)S(1)}) fusion(bf16[384,3072,1]{1,0,2:T(8,128)(2,1)} %copy-done.6, bf16[3,128,3072]{2,1,0:T(8,128)(2,1)} %bitcast.148), kind=kOutput, calls=%fused_computation.54 | convolution fusion | flops 906263424 | bytes 5313024 | tf_op jit(solution)/shard_map/dot_general | solution.py:63
  42.8 2.2 %reshape.473 = f32[384,3,64,2]{0,3,2,1:T(2,128)} reshape(f32[384,3,128]{0,2,1:T(8,128)} %multiply_multiply_fusion.2) | data formatting | bytes 1179648 | tf_op jit(solution)/shard_map/reshape | solution.py:35
  47.7 3.4 %subtract_convert_fusion.2 = (bf16[384,3,64,1]{0,3,2,1:T(2,128)(2,1)S(1)}, bf16[384,3,64,1]{0,3,2,1:T(2,128)(2,1)S(1)}, bf16[384,3,64,1]{0,3,2,1:T(2,128)(2,1)}, bf16[384,3,64,1]{0,3,2,1:T(2,128)(2,1)}) fusion(f32[384,3,64,2]{0,3,2,1:T(2,128)} %reshape.473, f32[384,64]{0,1:T(8,128)S(1)} %get-tuple-element.55, f32[384,64]{0,1:T(8,128)S(1)} %get-tuple-element.54, ...), kind=kLoop, calls=%fused_computation.70 | loop fusion | flops 1179648 | bytes 1966080 | tf_op jit(solution)/shard_map/convert.4
  52.8 1.7 pad_maximum_fusion
  56.3 4.3 %copy.67 = bf16[384,3072]{1,0:T(8,128)(2,1)} copy(bf16[384,3072]{0,1:T(8,128)(2,1)} %get-tuple-element.70) | data formatting | bytes 4718592 | tf_op jit(solution)/shard_map/dot_general | solution.py:63
  60.6 3.9 %convolution_convert_fusion.1 = bf16[384,3,128]{0,2,1:T(8,128)(2,1)S(1)} fusion(bf16[384,3072,1]{1,0,2:T(8,128)(2,1)} %copy-done.6, bf16[3,128,3072]{2,1,0:T(8,128)(2,1)} %bitcast.149), kind=kOutput, calls=%fused_computation.40 | convolution fusion | flops 906117120 | bytes 5013504 | tf_op jit(solution)/shard_map/dot_general | solution.py:63
  65.4 4.3 %copy.73 = bf16[384,3072]{1,0:T(8,128)(2,1)} copy(bf16[384,3072]{0,1:T(8,128)(2,1)} %get-tuple-element.25) | data formatting | bytes 4718592 | tf_op jit(solution)/shard_map/dot_general | solution.py:63
  69.7 4.4 %copy.71 = bf16[384,3072]{1,0:T(8,128)(2,1)} copy(bf16[384,3072]{0,1:T(8,128)(2,1)} %get-tuple-element.27) | data formatting | bytes 4718592 | tf_op jit(solution)/shard_map/dot_general | solution.py:63
  74.1 4.3 %copy.72 = bf16[384,3072]{1,0:T(8,128)(2,1)} copy(bf16[384,3072]{0,1:T(8,128)(2,1)} %get-tuple-element.26) | data formatting | bytes 4718592 | tf_op jit(solution)/shard_map/dot_general | solution.py:63
  78.4 1.3 convert_reduce_fusion.4
  82.5 1.8 compare_select_fusion.fetch_ref
  84.3 3.9 %all-gather.5.cloned.1.call-done = bf16[16,2,1,384,384]{4,3,2,1,0:T(8,128)(2,1)} async-done(((bf16[1,2,1,384,384]{4,3,2,1,0:T(8,128)(2,1)}), bf16[16,2,1,384,384]{4,3,2,1,0:T(8,128)(2,1)}) %all-gather.5.cloned.1.call-update) | async-done | bytes 9437200 | tf_op jit(solution)/shard_map/all_gather | solution.py:350
  88.2 13.9 %shard_map.130 = bf16[384,384]{1,0:T(8,128)(2,1)} custom-call(s32[7]{0:T(128)} %compare_select_fusion.fetch_ref, s32[7]{0:T(128)} %compare_convert_fusion.allow_ref, bf16[384,384]{1,0:T(8,128)(2,1)} %copy.68.q_ref, bf16[384,384]{1,0:T(8,128)(2,1)} %copy.69.kf_ref, bf16[384,384]{1,0:T(8,128)(2,1)} %copy.70.vf_ref, bf16[16,2,384,384]{3,2,1,0:T(8,128)(2,1)} %bitcast.138, ...), custom_call_target="tpu_custom_call" | custom-call | tf_op jit(solution)/shard_map/pallas_call | solution.py:139
  103.1 2.6 %fusion.18 = f32[192,3072]{1,0:T(8,128)S(1)} fusion(bf16[2,384,3072]{2,1,0:T(8,128)(2,1)} %param.14, bf16[384,384]{1,0:T(8,128)(2,1)} %shard_map.130, s32[]{:T(128)S(6)} %select_n.36), kind=kOutput, calls=%fused_computation.35 | convolution fusion | flops 452984832 | bytes 4866052 | tf_op jit(solution)/shard_map/dot_general | solution.py:374
  105.7 2.6 %fusion.13.part_ref = bf16[192,3072]{1,0:T(8,128)(2,1)S(1)} fusion(f32[192,3072]{1,0:T(8,128)S(1)} %fusion.18, bf16[192,384]{1,0:T(8,128)(2,1)S(1)} %collective-permute-done, bf16[2,384,3072]{2,1,0:T(8,128)(2,1)} %collective-permute-done.1), kind=kOutput, calls=%fused_computation.22 | convolution fusion | flops 454164480 | bytes 6045696 | tf_op jit(solution)/shard_map/dot_general | solution.py:375
  108.2 29.4 %shard_map.131 = (bf16[48,3072]{1,0:T(8,128)(2,1)S(1)}, bf16[2,4,48,3072]{3,2,1,0:T(8,128)(2,1)S(1)}) custom-call(bf16[192,3072]{1,0:T(8,128)(2,1)S(1)} %fusion.13.part_ref, bf16[48,3072]{1,0:T(8,128)(2,1)S(1)} %dynamic-slice_bitcast_fusion.own_ref, f32[1,3072]{1,0:T(1,128)S(1)} %get-tuple-element.47.gate_ref), custom_call_target="tpu_custom_call" | custom-call | tf_op jit(solution)/shard_map/pallas_call | solution.py:292
  140.5 1.4 convolution_convert_fusion
  142.8 3.1 %multiply_reduce_fusion.1 = (f32[384,3]{0,1:T(4,128)S(1)}, f32[384,3,128]{0,2,1:T(8,128)S(1)}) fusion(bf16[384,3072,1]{1,0,2:T(8,128)(2,1)} %bitcast.146, bf16[3,128,3072]{2,1,0:T(8,128)(2,1)S(1)} %bitcast.142), kind=kOutput, calls=%fused_computation.52 | convolution fusion | flops 906263424 | bytes 5313024 | tf_op jit(solution)/shard_map/dot_general | solution.py:63
  146.4 3.9 %multiply_reduce_fusion = (f32[384,3]{0,1:T(4,128)S(1)}, f32[384,3,128]{0,2,1:T(8,128)S(1)}) fusion(bf16[384,3072,1]{1,0,2:T(8,128)(2,1)} %bitcast.147, bf16[3,128,3072]{2,1,0:T(8,128)(2,1)} %bitcast.141), kind=kOutput, calls=%fused_computation.50 | convolution fusion | flops 906263424 | bytes 5313024 | tf_op jit(solution)/shard_map/dot_general | solution.py:63
  151.2 1.6 subtract_convert_fusion
  156.2 9.4 %all-gather.7.cloned.1.call-done = bf16[16,2,1,384,384]{4,3,2,1,0:T(8,128)(2,1)} async-done(((bf16[1,2,1,384,384]{4,3,2,1,0:T(8,128)(2,1)}), bf16[16,2,1,384,384]{4,3,2,1,0:T(8,128)(2,1)}) %all-gather.7.cloned.1.call-update) | async-done | bytes 9437200 | tf_op jit(solution)/shard_map/all_gather | solution.py:350
  165.6 13.9 %shard_map.132 = bf16[384,384]{1,0:T(8,128)(2,1)} custom-call(s32[7]{0:T(128)} %compare_select_fusion.fetch_ref, s32[7]{0:T(128)} %compare_convert_fusion.allow_ref, bf16[384,384]{1,0:T(8,128)(2,1)} %copy.74.q_ref, bf16[384,384]{1,0:T(8,128)(2,1)} %copy.75.kf_ref, bf16[384,384]{1,0:T(8,128)(2,1)} %copy.76.vf_ref, bf16[16,2,384,384]{3,2,1,0:T(8,128)(2,1)} %bitcast.136, ...), custom_call_target="tpu_custom_call" | custom-call | tf_op jit(solution)/shard_map/pallas_call | solution.py:139
  180.5 2.5 %fusion.16 = f32[192,3072]{1,0:T(8,128)S(1)} fusion(bf16[2,384,3072]{2,1,0:T(8,128)(2,1)} %param.14, bf16[384,384]{1,0:T(8,128)(2,1)} %shard_map.132, s32[]{:T(128)S(6)} %select_n.36), kind=kOutput, calls=%fused_computation.33 | convolution fusion | flops 452984832 | bytes 4866052 | tf_op jit(solution)/shard_map/dot_general | solution.py:374
  183.1 2.5 %fusion.14.part_ref = bf16[192,3072]{1,0:T(8,128)(2,1)S(1)} fusion(f32[192,3072]{1,0:T(8,128)S(1)} %fusion.16, bf16[192,384]{1,0:T(8,128)(2,1)S(1)} %collective-permute-done.2, bf16[2,384,3072]{2,1,0:T(8,128)(2,1)} %collective-permute-done.1), kind=kOutput, calls=%fused_computation.23 | convolution fusion | flops 454164480 | bytes 6045696 | tf_op jit(solution)/shard_map/dot_general | solution.py:375
  185.6 16.1 %shard_map.133 = f32[48,3072]{1,0:T(8,128)S(1)} custom-call(bf16[192,3072]{1,0:T(8,128)(2,1)S(1)} %fusion.14.part_ref, bf16[48,3072]{1,0:T(8,128)(2,1)S(1)} %get-tuple-element.5.own_ref, f32[1,3072]{1,0:T(1,128)S(1)} %get-tuple-element.46.gate_ref), custom_call_target="tpu_custom_call" | custom-call | tf_op jit(solution)/shard_map/pallas_call | solution.py:292
  (99 shorter events, 26.9 us)
Async XLA Ops:
  7.2 195.9 %copy-start = (bf16[3072,64]{0,1:T(8,128)(2,1)S(1)}, bf16[3072,64]{0,1:T(8,128)(2,1)}, u32[]{:S(2)}) copy-start(bf16[3072,64]{0,1:T(8,128)(2,1)} %param.15) | copy-start | bytes 1179652
  7.2 81.0 %all-gather.5.cloned.1.call-start = ((), (), s32[]{:S(2)}) async-start(), calls=%async_computation | async-start | bytes 10027008 | tf_op jit(solution)/shard_map/all_gather | solution.py:350
  9.7 155.9 %all-gather.7.cloned.1.call-start = ((), (), s32[]{:S(2)}) async-start(), calls=%async_computation.1 | async-start | bytes 10027008 | tf_op jit(solution)/shard_map/all_gather | solution.py:350
  10.4 95.2 %collective-permute-start.1 = (bf16[2,384,3072]{2,1,0:T(8,128)(2,1)}, bf16[2,384,3072]{2,1,0:T(8,128)(2,1)}, u32[]{:S(2)}, u32[]{:S(2)}) collective-permute-start(bf16[2,384,3072]{2,1,0:T(8,128)(2,1)} %param.14), channel_id=1, source_target_pairs={{0,64},{64,0},{1,65},{65,1},{2,66},{66,2},{3,67},{67,3},{4,68},{68... | collective-permute-start | bytes 14155784 | tf_op jit(solution)/shard_map/ppermute | solution.py:354
  22.5 4.4 %copy-start.10 = (f32[2,2,128]{2,1,0:T(2,128)S(1)}, f32[2,2,128]{2,1,0:T(2,128)}, u32[]{:S(2)}) copy-start(f32[2,2,128]{2,1,0:T(2,128)} %param.16) | copy-start | bytes 6148
  22.5 4.4 %copy-start.1 = (bf16[1,384,3072]{2,1,0:T(8,128)(2,1)S(1)}, bf16[1,384,3072]{2,1,0:T(8,128)(2,1)}, u32[]{:S(2)}) copy-start(bf16[1,384,3072]{2,1,0:T(8,128)(2,1)} %param.11) | copy-start | bytes 7077892
  27.0 1.2 copy-start.9
  28.2 1.7 copy-start.4
  29.5 1.9 copy-start.6
  41.8 3.2 %copy-start.12 = (s32[4]{0:T(128)S(1)}, s32[4]{0:T(128)}, u32[]{:S(2)}) copy-start(s32[4]{0:T(128)} %param.19) | copy-start | bytes 52
  41.9 3.4 %copy-start.13 = (s32[16]{0:T(128)S(1)}, s32[16]{0:T(128)}, u32[]{:S(2)}) copy-start(s32[16]{0:T(128)} %param.20) | copy-start | bytes 196
  47.7 3.4 %copy-start.7 = (f32[384,64]{0,1:T(8,128)}, f32[384,64]{0,1:T(8,128)S(1)}, u32[]{:S(2)}) copy-start(f32[384,64]{0,1:T(8,128)S(1)} %get-tuple-element.55) | copy-start | bytes 294916
  103.0 2.7 %collective-permute-start = (bf16[192,384]{1,0:T(8,128)(2,1)S(1)}, bf16[192,384]{1,0:T(8,128)(2,1)S(1)}, u32[]{:S(2)}, u32[]{:S(2)}) collective-permute-start(bf16[192,384]{1,0:T(8,128)(2,1)S(1)} %constant_dynamic-slice_fusion.1), channel_id=1, source_target_pairs={{0,64},{64,0},{1,65},{65,1},{2,66},{66,2},{3,67},{67,3},{4,68},{68... | collective-permute-start | bytes 442376 | tf_op jit(solution)/shard_map/ppermute | solution.py:372
  138.8 1.7 copy-start.3
  140.1 1.8 copy-start.5
  140.5 2.3 %copy-start.2 = (bf16[384,3072]{1,0:T(8,128)(2,1)S(1)}, bf16[384,3072]{1,0:T(8,128)(2,1)}, u32[]{:S(2)}) copy-start(bf16[384,3072]{1,0:T(8,128)(2,1)} %copy.71) | copy-start | bytes 7077892
  150.3 0.9 copy-start.8
  180.4 2.6 %collective-permute-start.2 = (bf16[192,384]{1,0:T(8,128)(2,1)S(1)}, bf16[192,384]{1,0:T(8,128)(2,1)S(1)}, u32[]{:S(2)}, u32[]{:S(2)}) collective-permute-start(bf16[192,384]{1,0:T(8,128)(2,1)S(1)} %constant_dynamic-slice_fusion), channel_id=1, source_target_pairs={{0,64},{64,0},{1,65},{65,1},{2,66},{66,2},{3,67},{67,3},{4,68},{68... | collective-permute-start | bytes 442376 | tf_op jit(solution)/shard_map/ppermute | solution.py:372
  185.6 17.4 %copy-start.11 = (f32[1,48,64]{2,1,0:T(8,128)S(1)}, f32[1,48,64]{2,1,0:T(8,128)}, u32[]{:S(2)}) copy-start(f32[1,48,64]{2,1,0:T(8,128)} %param.12) | copy-start | bytes 36868
Sparse Core Ops, SparseCore 0:
  10.2 77.9 all-gather.4
  90.3 75.2 all-gather.6

commit v9 on v8

--- a/solution.py
+++ b/solution.py
@@ -155,12 +155,14 @@
     )(fetch, allow, queries, keys_fresh, values_fresh, stale, stale)
 
 
-def exchange_kernel(head_count, own_rows, split, gather, part_ref, own_ref, gate_ref, *rest):
+def exchange_kernel(
+    head_count, own_rows, split, gather, mine_ref, theirs_ref, w_ref, wp_ref, own_ref, gate_ref, *rest
+):
     if gather:
-        (out_ref, full_ref, land_a, land_b, sums_a, sums_b, acc,
+        (out_ref, full_ref, part_ref, land_a, land_b, sums_a, sums_b, acc,
          r_send, r_recv, a_send, a_recv, g2_send, g2_recv) = rest
     else:
-        (out_ref, land_a, land_b, sums_a, sums_b, acc, r_send, r_recv) = rest
+        (out_ref, part_ref, land_a, land_b, sums_a, sums_b, acc, r_send, r_recv) = rest
     mesh_ids = pl.DeviceIdType.MESH
     section = lax.axis_index("section")
     head = lax.axis_index("head")
@@ -181,6 +183,14 @@
         @pl.when(h != head)
         def _greet():
             pl.semaphore_signal(barrier, inc=1, device_id=(section, h, tok), device_id_type=mesh_ids)
+
+    def project_block(block):
+        rows = pl.ds(pl.multiple_of(block * own_rows, 16), own_rows)
+        return jnp.dot(
+            mine_ref[rows, :], w_ref[...], preferred_element_type=jnp.float32
+        ) + jnp.dot(theirs_ref[rows, :], wp_ref[...], preferred_element_type=jnp.float32)
+
+    part_ref[opposite] = project_block(opposite).astype(part_ref.dtype)
     pl.semaphore_wait(barrier, head_count)
 
     def ring(kind, src, dst, target, send_sem, recv_sem):
@@ -195,25 +205,26 @@
 
     low_count = split
     high_count = own_rows - split
-    pass_a = ring(0, part_ref.at[rows_of(opposite, 0, low_count)], land_a.at[0], up, r_send, r_recv)
-    pass_b = ring(1, part_ref.at[rows_of(opposite, split, high_count)], land_b.at[0], down, r_send, r_recv)
-    direct_a = ring(2, part_ref.at[rows_of(down, 0, low_count)], land_a.at[1], down, r_send, r_recv)
-    direct_b = ring(3, part_ref.at[rows_of(up, split, high_count)], land_b.at[1], up, r_send, r_recv)
+    pass_a = ring(0, part_ref.at[opposite, low], land_a.at[0], up, r_send, r_recv)
+    pass_b = ring(1, part_ref.at[opposite, high], land_b.at[0], down, r_send, r_recv)
+    direct_a = ring(2, part_ref.at[down, low], land_a.at[1], down, r_send, r_recv)
+    direct_b = ring(3, part_ref.at[up, high], land_b.at[1], up, r_send, r_recv)
     pass_a.start()
     pass_b.start()
+    part_ref[down] = project_block(down).astype(part_ref.dtype)
     direct_a.start()
+    part_ref[up] = project_block(up).astype(part_ref.dtype)
     direct_b.start()
-    acc[...] = part_ref[rows_of(head, 0, own_rows), :].astype(jnp.float32)
+    acc[...] = project_block(head)
     pass_a.wait()
     sums_a[...] = (
-        part_ref[rows_of(up, 0, low_count), :].astype(jnp.float32) + land_a[0].astype(jnp.float32)
+        part_ref[up, low].astype(jnp.float32) + land_a[0].astype(jnp.float32)
     ).astype(sums_a.dtype)
     joined_a = ring(4, sums_a, land_a.at[2], up, r_send, r_recv)
     joined_a.start()
     pass_b.wait()
     sums_b[...] = (
-        part_ref[rows_of(down, split, high_count), :].astype(jnp.float32)
-        + land_b[0].astype(jnp.float32)
+        part_ref[down, high].astype(jnp.float32) + land_b[0].astype(jnp.float32)
     ).astype(sums_b.dtype)
     joined_b = ring(5, sums_b, land_b.at[2], down, r_send, r_recv)
     joined_b.start()
@@ -266,15 +277,16 @@
     pass_copy(opposite).wait()
 
 
-def exchange(partial, own_input, gate, layer_idx, gather, head_count, own_rows):
-    rows, width = partial.shape
+def exchange(mine, theirs, weight, partner_weight, own_input, gate, layer_idx, gather, head_count, own_rows):
+    width = weight.shape[1]
     split = (own_rows * 2 // 3) // 16 * 16
     vmem = pl.BlockSpec(memory_space=pltpu.VMEM)
     scratch = [
-        pltpu.VMEM((3, split, width), partial.dtype),
-        pltpu.VMEM((3, own_rows - split, width), partial.dtype),
-        pltpu.VMEM((split, width), partial.dtype),
-        pltpu.VMEM((own_rows - split, width), partial.dtype),
+        pltpu.VMEM((head_count, own_rows, width), jnp.bfloat16),
+        pltpu.VMEM((3, split, width), jnp.bfloat16),
+        pltpu.VMEM((3, own_rows - split, width), jnp.bfloat16),
+        pltpu.VMEM((split, width), jnp.bfloat16),
+        pltpu.VMEM((own_rows - split, width), jnp.bfloat16),
         pltpu.VMEM((own_rows, width), jnp.float32),
         pltpu.SemaphoreType.DMA((6,)),
         pltpu.SemaphoreType.DMA((6,)),
@@ -292,13 +304,13 @@
     return pl.pallas_call(
         functools.partial(exchange_kernel, head_count, own_rows, split, gather),
         out_shape=out_shape,
-        in_specs=[vmem, vmem, vmem],
+        in_specs=[vmem] * 6,
         out_specs=out_specs,
         scratch_shapes=scratch,
         compiler_params=pltpu.CompilerParams(
-            collective_id=layer_idx, has_side_effects=True, vmem_limit_bytes=48 * 1024 * 1024
+            collective_id=layer_idx, has_side_effects=True, vmem_limit_bytes=56 * 1024 * 1024
         ),
-    )(partial, own_input, gate.reshape(1, width))
+    )(mine, theirs, weight, partner_weight, own_input, gate.reshape(1, width))
 
 
 def noise_level(position):
@@ -370,18 +382,18 @@
         mine = lax.dynamic_slice_in_dim(attended, section_index * half_rows, half_rows, 0)
         theirs = lax.dynamic_slice_in_dim(attended, (1 - section_index) * half_rows, half_rows, 0)
         swapped = lax.ppermute(theirs, "section", perm=[(0, 1), (1, 0)])
-        partial = (
-            jnp.dot(mine, w_out[layer_idx], preferred_element_type=jnp.float32)
-            + jnp.dot(swapped, w_partner[layer_idx], preferred_element_type=jnp.float32)
-        ).astype(jnp.bfloat16)
         gate = modulation[layer_idx, 2]
         if layer_idx + 1 < layer_count:
             own_out, gathered = exchange(
-                partial, own_input, gate, layer_idx, True, head_count, own_rows
+                mine, swapped, w_out[layer_idx], w_partner[layer_idx], own_input, gate,
+                layer_idx, True, head_count, own_rows,
             )
             current_full = gathered.reshape(patch_len, width)
         else:
-            summed = exchange(partial, own_input, gate, layer_idx, False, head_count, own_rows)
+            summed = exchange(
+                mine, swapped, w_out[layer_idx], w_partner[layer_idx], own_input, gate,
+                layer_idx, False, head_count, own_rows,
+            )
             own_out = (own_input.astype(jnp.float32) + gate * summed).astype(jnp.bfloat16)
         own_input = own_out
         outputs.append(own_out)

time: 212 us -> 214 us (level)
  matrix products: 28.6 us -> 16.8 us
  local copies, waits for them, and re-layouts: 54.4 us -> 65.8 us
  waiting for transfers between devices: 14 us -> 4.57 us
  Pallas kernels: 73.2 us -> 80.2 us
  other arithmetic: 23.7 us -> 28.7 us
    dot_general x4 -> x0, matrix products: 10.1 us -> none  [the longest x2 5.09 us: shards(): jnp.dot(mine, w_out[layer_idx], preferred_element_type=jnp.float32)]
    all_gather x2, waiting for transfers between devices: 13.3 us -> 3.23 us  [shards(): lax.all_gather(jnp.swapaxes(stale_kv[layer], 0, 1), 'tok', axis=0, tiled=...]
    squeeze x0 -> x2, local copies, waits for them, and re-layouts: none -> 9.85 us  [the longest x1 4.99 us: shards(): w_partner[layer_idx]]
    pallas_call x2, Pallas kernels: 45.4 us -> 52.3 us  [exchange(): pl.pallas_call(functools.partial(exchange_kernel, head_count, own_rows, s...]
    reduce_sum x3, other arithmetic: 0.99 us -> 3.86 us  [layer_norm(): average = jnp.mean(inputs, axis=-1, keepdims=True)]
    dot_general x7, local copies, waits for them, and re-layouts: 31.2 us -> 28.9 us  [project(): jnp.dot(normed, weight[:, part, :], preferred_element_type=jnp.float32)]
  transfers between devices with their start and end apart: 5 -> 5, of which waited for: 2 -> 3; matrix products, arithmetic and copies ran while one was open for 46% -> 48% of each run, Pallas kernels for 21% -> 22%
where the time goes in v9:
time: 214 us; the launch traced here: 213 us
  Pallas kernels  80.2 us (37%)
  local copies, waits for them, and re-layouts  65.8 us (31%)
  other arithmetic  28.7 us (13%)
  matrix products  16.8 us (8%)
  between operations  16.4 us (8%)
  waiting for transfers between devices  4.57 us (2%)
    pallas_call x2, Pallas kernels, exchange(): pl.pallas_call(functools.partial(exchange_kernel, head_count, own_rows, s...  52.3 us
    dot_general x7, local copies, waits for them, and re-layouts, project(): jnp.dot(normed, weight[:, part, :], preferred_element_type=jnp.float32)  28.9 us
    pallas_call x2, Pallas kernels, attend(): pl.pallas_call(functools.partial(attention_kernel, head_dim), out_shape=j...  27.8 us
    dot_general x6, matrix products, project(): jnp.dot(normed, weight[:, part, :], preferred_element_type=jnp.float32)  15.9 us
    squeeze x1, local copies, waits for them, and re-layouts, shards(): w_qkv[layer_idx]  6.09 us
    another operation x4, other arithmetic  5.35 us
    squeeze x1, local copies, waits for them, and re-layouts, shards(): w_partner[layer_idx]  4.99 us
    squeeze x1, local copies, waits for them, and re-layouts, shards(): w_out[layer_idx]  4.86 us
  transfers between devices with their start and end apart: 5, of which 3 were waited for; matrix products, arithmetic and copies ran while one was open for 48% of the time, Pallas kernels for 22%

profile of v9, /device:TPU:8, one launch (start us, length us, event | category | flops | bytes accessed | tf_op | source)
XLA Modules:
  0.0 212.6 jit_solution(1940339057617871667)
XLA Ops:
  7.2 2.4 %fusion.25 = (bf16[1,2,1,384,384]{4,3,2,1,0:T(8,128)(2,1)}, bf16[1,2,1,384,384]{4,3,2,1,0:T(8,128)(2,1)}) fusion(bf16[2,2,1,384,384]{4,3,2,1,0:T(8,128)(2,1)} %param.18), kind=kLoop, calls=%fused_computation.109 | loop fusion | bytes 2359296 | tf_op jit(solution)/shard_map/slice | solution.py:362
  10.5 6.1 %slice_bitcast_fusion = (bf16[3072,3,384]{2,0,1:T(8,128)(2,1)S(1)}, bf16[3072,3,384]{2,0,1:T(8,128)(2,1)S(1)}) fusion(bf16[2,3072,3,384]{3,1,2,0:T(8,128)(2,1)} %param.13), kind=kLoop, calls=%fused_computation | loop fusion | bytes 28311552 | tf_op jit(solution)/shard_map/squeeze | solution.py:373
  16.6 4.5 %slice_bitcast_fusion.3 = (bf16[384,3072]{0,1:T(8,128)(2,1)}, bf16[384,3072]{0,1:T(8,128)(2,1)}, bf16[384,3072]{0,1:T(8,128)(2,1)}, bf16[384,3072]{0,1:T(8,128)(...) fusion(bf16[3072,3,384]{2,0,1:T(8,128)(2,1)S(1)} %get-tuple-element.23, ...), kind=kLoop, calls=%fused_computation.22 | loop fusion | bytes 28311552 | tf_op jit(solution)/shard_map/dot_general | solution.py:63
  21.1 2.6 %copy.65 = bf16[384,3072]{1,0:T(8,128)(2,1)} copy(bf16[384,3072]{0,1:T(8,128)(2,1)S(1)} %get-tuple-element.76) | data formatting | bytes 4718592 | tf_op jit(solution)/shard_map/dot_general | solution.py:63
  23.7 4.5 %copy.66 = bf16[384,3072]{1,0:T(8,128)(2,1)} copy(bf16[384,3072]{0,1:T(8,128)(2,1)} %get-tuple-element.77) | data formatting | bytes 4718592 | tf_op jit(solution)/shard_map/dot_general | solution.py:63
  32.2 1.4 multiply_reduce_fusion.3
  34.6 2.2 %multiply_reduce_fusion.2 = (f32[384,3]{0,1:T(4,128)S(1)}, f32[384,3,128]{0,2,1:T(8,128)}) fusion(bf16[384,3072,1]{1,0,2:T(8,128)(2,1)S(1)} %fusion.13, bf16[3,128,3072]{2,1,0:T(8,128)(2,1)S(1)} %bitcast.138), kind=kOutput, calls=%fused_computation.46 | convolution fusion | flops 906263424 | bytes 5313024 | tf_op jit(solution)/shard_map/dot_general | solution.py:63
  36.9 1.4 reshape.472
  38.3 2.0 multiply_multiply_fusion.2
  40.3 2.2 %reshape.473 = f32[384,3,64,2]{0,3,2,1:T(2,128)} reshape(f32[384,3,128]{0,2,1:T(8,128)} %multiply_multiply_fusion.2) | data formatting | bytes 1179648 | tf_op jit(solution)/shard_map/reshape | solution.py:35
  45.1 3.3 %subtract_convert_fusion.2 = (bf16[384,3,64,1]{0,3,2,1:T(2,128)(2,1)S(1)}, bf16[384,3,64,1]{0,3,2,1:T(2,128)(2,1)S(1)}, bf16[384,3,64,1]{0,3,2,1:T(2,128)(2,1)}, bf16[384,3,64,1]{0,3,2,1:T(2,128)(2,1)}) fusion(f32[384,3,64,2]{0,3,2,1:T(2,128)} %reshape.473, f32[384,64]{0,1:T(8,128)S(1)} %get-tuple-element.63, f32[384,64]{0,1:T(8,128)S(1)} %get-tuple-element.62, ...), kind=kLoop, calls=%fused_computation.62 | loop fusion | flops 1179648 | bytes 1966080 | tf_op jit(solution)/shard_map/convert.4
  50.1 1.7 pad_maximum_fusion
  54.2 4.4 %copy.67 = bf16[384,3072]{1,0:T(8,128)(2,1)} copy(bf16[384,3072]{0,1:T(8,128)(2,1)} %get-tuple-element.78) | data formatting | bytes 4718592 | tf_op jit(solution)/shard_map/dot_general | solution.py:63
  58.5 3.8 %convolution_convert_fusion.1 = bf16[384,3,128]{0,2,1:T(8,128)(2,1)S(1)} fusion(bf16[384,3072,1]{1,0,2:T(8,128)(2,1)} %copy-done.9, bf16[3,128,3072]{2,1,0:T(8,128)(2,1)} %bitcast.143), kind=kOutput, calls=%fused_computation.32 | convolution fusion | flops 906117120 | bytes 5013504 | tf_op jit(solution)/shard_map/dot_general | solution.py:63
  63.2 4.3 %copy.73 = bf16[384,3072]{1,0:T(8,128)(2,1)} copy(bf16[384,3072]{0,1:T(8,128)(2,1)} %get-tuple-element.25) | data formatting | bytes 4718592 | tf_op jit(solution)/shard_map/dot_general | solution.py:63
  67.5 4.4 %copy.71 = bf16[384,3072]{1,0:T(8,128)(2,1)} copy(bf16[384,3072]{0,1:T(8,128)(2,1)} %get-tuple-element.27) | data formatting | bytes 4718592 | tf_op jit(solution)/shard_map/dot_general | solution.py:63
  71.9 4.3 %copy.72 = bf16[384,3072]{1,0:T(8,128)(2,1)} copy(bf16[384,3072]{0,1:T(8,128)(2,1)} %get-tuple-element.26) | data formatting | bytes 4718592 | tf_op jit(solution)/shard_map/dot_general | solution.py:63
  80.1 1.8 compare_select_fusion.fetch_ref
  82.6 4.9 %slice_bitcast_fusion.10 = (bf16[384,3072]{1,0:T(8,128)(2,1)}, bf16[384,3072]{1,0:T(8,128)(2,1)}) fusion(bf16[2,384,3072]{2,1,0:T(8,128)(2,1)} %param.14), kind=kLoop, calls=%fused_computation.29 | loop fusion | bytes 9437184 | tf_op jit(solution)/shard_map/squeeze | solution.py:394
  88.3 13.9 %shard_map.130 = bf16[384,384]{1,0:T(8,128)(2,1)} custom-call(s32[7]{0:T(128)} %compare_select_fusion.fetch_ref, s32[7]{0:T(128)} %compare_convert_fusion.allow_ref, bf16[384,384]{1,0:T(8,128)(2,1)} %copy.68.q_ref, bf16[384,384]{1,0:T(8,128)(2,1)} %copy.69.kf_ref, bf16[384,384]{1,0:T(8,128)(2,1)} %copy.70.vf_ref, bf16[16,2,384,384]{3,2,1,0:T(8,128)(2,1)} %bitcast.131, ...), custom_call_target="tpu_custom_call" | custom-call | tf_op jit(solution)/shard_map/pallas_call | solution.py:139
  102.3 1.7 constant_dynamic-slice_fusion.2
  103.9 5.0 %slice_bitcast_fusion.2 = (bf16[384,3072]{1,0:T(8,128)(2,1)}, bf16[384,3072]{1,0:T(8,128)(2,1)}) fusion(bf16[2,384,3072]{2,1,0:T(8,128)(2,1)} %collective-permute-done.1), kind=kLoop, calls=%fused_computation.21 | loop fusion | bytes 9437184 | tf_op jit(solution)/shard_map/squeeze | solution.py:394
  109.6 33.4 %shard_map.131 = (bf16[48,3072]{1,0:T(8,128)(2,1)}, bf16[2,4,48,3072]{3,2,1,0:T(8,128)(2,1)}) custom-call(bf16[192,384]{1,0:T(8,128)(2,1)} %get-tuple-element.48.mine_ref, bf16[192,384]{1,0:T(8,128)(2,1)} %copy-done.11, bf16[384,3072]{1,0:T(8,128)(2,1)} %get-tuple-element.34.w_ref, bf16[384,3072]{1,0:T(8,128)(2,1)} %get-tuple-element.32.wp_ref, ...), custom_call_target="tpu_custom_call" | custom-call | tf_op jit(solution)/shard_map/pallas_call | solution.py:304
  143.0 2.2 %convert_reduce_fusion.1 = f32[2,4,48]{2,1,0:T(4,128)S(1)} fusion(bf16[2,4,48,3072]{3,2,1,0:T(8,128)(2,1)} %get-tuple-element.6), kind=kLoop, calls=%fused_computation.6 | loop fusion | flops 2358912 | bytes 2360832 | tf_op jit(solution)/shard_map/reduce_sum | solution.py:21
  147.9 1.4 convolution_convert_fusion
  150.2 3.2 %multiply_reduce_fusion.1 = (f32[384,3]{0,1:T(4,128)S(1)}, f32[384,3,128]{0,2,1:T(8,128)S(1)}) fusion(bf16[384,3072,1]{1,0,2:T(8,128)(2,1)} %bitcast.141, bf16[3,128,3072]{2,1,0:T(8,128)(2,1)S(1)} %bitcast.136), kind=kOutput, calls=%fused_computation.44 | convolution fusion | flops 906263424 | bytes 5313024 | tf_op jit(solution)/shard_map/dot_general | solution.py:63
  153.9 3.9 %multiply_reduce_fusion = (f32[384,3]{0,1:T(4,128)S(1)}, f32[384,3,128]{0,2,1:T(8,128)S(1)}) fusion(bf16[384,3072,1]{1,0,2:T(8,128)(2,1)} %bitcast.142, bf16[3,128,3072]{2,1,0:T(8,128)(2,1)} %bitcast.135), kind=kOutput, calls=%fused_computation.42 | convolution fusion | flops 906263424 | bytes 5313024 | tf_op jit(solution)/shard_map/dot_general | solution.py:63
  158.3 1.8 subtract_convert_fusion
  163.5 2.3 %all-gather.7.cloned.1.call-done = bf16[16,2,1,384,384]{4,3,2,1,0:T(8,128)(2,1)} async-done(((bf16[1,2,1,384,384]{4,3,2,1,0:T(8,128)(2,1)}), bf16[16,2,1,384,384]{4,3,2,1,0:T(8,128)(2,1)}) %all-gather.7.cloned.1.call-update) | async-done | bytes 9437200 | tf_op jit(solution)/shard_map/all_gather | solution.py:362
  165.8 13.9 %shard_map.132 = bf16[384,384]{1,0:T(8,128)(2,1)} custom-call(s32[7]{0:T(128)} %compare_select_fusion.fetch_ref, s32[7]{0:T(128)} %compare_convert_fusion.allow_ref, bf16[384,384]{1,0:T(8,128)(2,1)} %copy.74.q_ref, bf16[384,384]{1,0:T(8,128)(2,1)} %copy.75.kf_ref, bf16[384,384]{1,0:T(8,128)(2,1)} %copy.76.vf_ref, bf16[16,2,384,384]{3,2,1,0:T(8,128)(2,1)} %bitcast.129, ...), custom_call_target="tpu_custom_call" | custom-call | tf_op jit(solution)/shard_map/pallas_call | solution.py:139
  179.7 1.7 constant_dynamic-slice_fusion
  183.4 18.9 %shard_map.133 = f32[48,3072]{1,0:T(8,128)} custom-call(bf16[192,384]{1,0:T(8,128)(2,1)} %get-tuple-element.46.mine_ref, bf16[192,384]{1,0:T(8,128)(2,1)} %copy-done.10, bf16[384,3072]{1,0:T(8,128)(2,1)} %get-tuple-element.33.w_ref, bf16[384,3072]{1,0:T(8,128)(2,1)} %get-tuple-element.31.wp_ref, bf16[48,3072]{1,0:T(8,128)(2,1)} %get-tuple-element.5.own_ref, ...), custom_call_target="tpu_custom_call" | custom-call | tf_op jit(solution)/shard_map/pallas_call | solution.py:304
  (113 shorter events, 30.7 us)
Async XLA Ops:
  7.2 197.7 %copy-start = (bf16[3072,64]{0,1:T(8,128)(2,1)S(1)}, bf16[3072,64]{0,1:T(8,128)(2,1)}, u32[]{:S(2)}) copy-start(bf16[3072,64]{0,1:T(8,128)(2,1)} %param.15) | copy-start | bytes 1179652
  7.2 81.2 %all-gather.5.cloned.1.call-start = ((), (), s32[]{:S(2)}) async-start(), calls=%async_computation | async-start | bytes 10027008 | tf_op jit(solution)/shard_map/all_gather | solution.py:362
  9.7 156.2 %all-gather.7.cloned.1.call-start = ((), (), s32[]{:S(2)}) async-start(), calls=%async_computation.1 | async-start | bytes 10027008 | tf_op jit(solution)/shard_map/all_gather | solution.py:362
  10.4 93.5 %collective-permute-start.1 = (bf16[2,384,3072]{2,1,0:T(8,128)(2,1)}, bf16[2,384,3072]{2,1,0:T(8,128)(2,1)}, u32[]{:S(2)}, u32[]{:S(2)}) collective-permute-start(bf16[2,384,3072]{2,1,0:T(8,128)(2,1)} %param.14), channel_id=1, source_target_pairs={{0,64},{64,0},{1,65},{65,1},{2,66},{66,2},{3,67},{67,3},{4,68},{68... | collective-permute-start | bytes 14155784 | tf_op jit(solution)/shard_map/ppermute | solution.py:366
  23.7 4.5 %copy-start.16 = (f32[2,2,128]{2,1,0:T(2,128)S(1)}, f32[2,2,128]{2,1,0:T(2,128)}, u32[]{:S(2)}) copy-start(f32[2,2,128]{2,1,0:T(2,128)} %param.16) | copy-start | bytes 6148
  23.7 5.0 %copy-start.1 = (bf16[1,384,3072]{2,1,0:T(8,128)(2,1)S(1)}, bf16[1,384,3072]{2,1,0:T(8,128)(2,1)}, u32[]{:S(2)}) copy-start(bf16[1,384,3072]{2,1,0:T(8,128)(2,1)} %param.11) | copy-start | bytes 7077892
  28.7 1.2 copy-start.12
  30.5 1.7 copy-start.7
  31.7 2.9 %copy-start.9 = (bf16[384,3072,1]{1,0,2:T(8,128)(2,1)}, bf16[384,3072,1]{1,0,2:T(8,128)(2,1)S(1)}, u32[]{:S(2)}) copy-start(bf16[384,3072,1]{1,0,2:T(8,128)(2,1)S(1)} %fusion.13) | copy-start | bytes 7077892
  32.2 2.4 %copy-start.6 = (bf16[384,3072]{1,0:T(8,128)(2,1)S(1)}, bf16[384,3072]{1,0:T(8,128)(2,1)}, u32[]{:S(2)}) copy-start(bf16[384,3072]{1,0:T(8,128)(2,1)} %copy.66) | copy-start | bytes 7077892
  36.8 5.7 %copy-start.20 = (s32[4]{0:T(128)S(1)}, s32[4]{0:T(128)}, u32[]{:S(2)}) copy-start(s32[4]{0:T(128)} %param.19) | copy-start | bytes 52
  36.8 5.8 %copy-start.21 = (s32[16]{0:T(128)S(1)}, s32[16]{0:T(128)}, u32[]{:S(2)}) copy-start(s32[16]{0:T(128)} %param.20) | copy-start | bytes 196
  42.8 1.9 copy-start.17
  71.9 4.3 %copy-start.18 = (s32[16]{0:T(128)S(1)}, s32[16]{0:T(128)}, u32[]{:S(2)}) copy-start(s32[16]{0:T(128)} %copy-done.17) | copy-start | bytes 196
  103.9 5.0 %collective-permute-start = (bf16[192,384]{1,0:T(8,128)(2,1)S(1)}, bf16[192,384]{1,0:T(8,128)(2,1)S(1)}, u32[]{:S(2)}, u32[]{:S(2)}) collective-permute-start(bf16[192,384]{1,0:T(8,128)(2,1)S(1)} %get-tuple-element.47), channel_id=1, source_target_pairs={{0,64},{64,0},{1,65},{65,1},{2,66},{66,2},{3,67},{67,3},{4,68},{68... | collective-permute-start | bytes 442376 | tf_op jit(solution)/shard_map/ppermute | solution.py:384
  108.9 0.7 copy-start.11
  143.0 2.5 %copy-start.2 = (bf16[2,4,48,3072]{3,2,1,0:T(8,128)(2,1)S(1)}, bf16[2,4,48,3072]{3,2,1,0:T(8,128)(2,1)}, u32[]{:S(2)}) copy-start(bf16[2,4,48,3072]{3,2,1,0:T(8,128)(2,1)} %get-tuple-element.6) | copy-start | bytes 7077892
  143.0 3.2 %copy-start.13 = (f32[1,1,3072]{2,0,1:T(1,128)S(1)}, f32[1,1,3072]{2,0,1:T(1,128)}, u32[]{:S(2)}) copy-start(f32[1,1,3072]{2,0,1:T(1,128)} %get-tuple-element.58) | copy-start | bytes 36868
  143.0 3.2 %copy-start.14 = (f32[1,1,3072]{2,0,1:T(1,128)S(1)}, f32[1,1,3072]{2,0,1:T(1,128)}, u32[]{:S(2)}) copy-start(f32[1,1,3072]{2,0,1:T(1,128)} %get-tuple-element.59) | copy-start | bytes 36868
  146.2 1.7 copy-start.5
  147.4 1.9 copy-start.8
  147.9 2.3 %copy-start.4 = (bf16[384,3072]{1,0:T(8,128)(2,1)S(1)}, bf16[384,3072]{1,0:T(8,128)(2,1)}, u32[]{:S(2)}) copy-start(bf16[384,3072]{1,0:T(8,128)(2,1)} %copy.71) | copy-start | bytes 7077892
  150.2 3.2 %copy-start.15 = (f32[128]{0:T(128)S(1)}, f32[128]{0:T(128)}, u32[]{:S(2)}) copy-start(f32[128]{0:T(128)} %get-tuple-element.67) | copy-start | bytes 1540
  181.4 1.4 collective-permute-start.2
  182.8 0.7 copy-start.10
  183.4 19.0 %copy-start.3 = (bf16[48,3072]{1,0:T(8,128)(2,1)S(1)}, bf16[48,3072]{1,0:T(8,128)(2,1)}, u32[]{:S(2)}) copy-start(bf16[48,3072]{1,0:T(8,128)(2,1)} %get-tuple-element.5.own_ref) | copy-start | bytes 884740
  202.4 2.4 %copy-start.19 = (f32[1,48,64]{2,1,0:T(8,128)S(1)}, f32[1,48,64]{2,1,0:T(8,128)}, u32[]{:S(2)}) copy-start(f32[1,48,64]{2,1,0:T(8,128)} %param.12) | copy-start | bytes 36868
Sparse Core Ops, SparseCore 0:
  10.2 78.1 all-gather.4
  90.5 75.3 all-gather.6

commit v10 on v8

--- a/solution.py
+++ b/solution.py
@@ -32,15 +32,12 @@
     half_dim = inputs.shape[-1] // 2
     frequency = rope_base ** (-2.0 * jnp.arange(half_dim, dtype=jnp.float32) / inputs.shape[-1])
     angles = positions[..., None, None] * frequency
+    cosine = jnp.repeat(jnp.cos(angles), 2, axis=-1)
+    sign = jnp.tile(jnp.array([-1.0, 1.0], dtype=jnp.float32), half_dim)
+    sine = jnp.repeat(jnp.sin(angles), 2, axis=-1) * sign
     pairs = inputs.reshape(inputs.shape[:-1] + (half_dim, 2))
-    even_lane = pairs[..., 0]
-    odd_lane = pairs[..., 1]
-    cosine = jnp.cos(angles)
-    sine = jnp.sin(angles)
-    turned = jnp.stack(
-        [even_lane * cosine - odd_lane * sine, even_lane * sine + odd_lane * cosine], axis=-1
-    )
-    return turned.reshape(inputs.shape)
+    swapped = pairs[..., ::-1].reshape(inputs.shape)
+    return inputs * cosine + swapped * sine
 
 
 def slot_layout(request_patches, patch_order):
@@ -203,32 +200,64 @@
     pass_b.start()
     direct_a.start()
     direct_b.start()
-    acc[...] = part_ref[rows_of(head, 0, own_rows), :].astype(jnp.float32)
+    def by_chunks(count, body):
+        @pl.loop(0, count // 16)
+        def _chunk(c):
+            body(pl.multiple_of(c * 16, 16))
+
+    def own_rows_in(r):
+        acc[pl.ds(r, 16), :] = part_ref[rows_of(head, r, 16), :].astype(jnp.float32)
+
+    by_chunks(own_rows, own_rows_in)
     pass_a.wait()
-    sums_a[...] = (
-        part_ref[rows_of(up, 0, low_count), :].astype(jnp.float32) + land_a[0].astype(jnp.float32)
-    ).astype(sums_a.dtype)
+
+    def sum_low(r):
+        sums_a[pl.ds(r, 16), :] = (
+            part_ref[rows_of(up, r, 16), :].astype(jnp.float32)
+            + land_a[0, pl.ds(r, 16), :].astype(jnp.float32)
+        ).astype(sums_a.dtype)
+
+    by_chunks(low_count, sum_low)
     joined_a = ring(4, sums_a, land_a.at[2], up, r_send, r_recv)
     joined_a.start()
     pass_b.wait()
-    sums_b[...] = (
-        part_ref[rows_of(down, split, high_count), :].astype(jnp.float32)
-        + land_b[0].astype(jnp.float32)
-    ).astype(sums_b.dtype)
+    def sum_high(r):
+        sums_b[pl.ds(r, 16), :] = (
+            part_ref[rows_of(down, split + r, 16), :].astype(jnp.float32)
+            + land_b[0, pl.ds(r, 16), :].astype(jnp.float32)
+        ).astype(sums_b.dtype)
+
+    by_chunks(high_count, sum_high)
     joined_b = ring(5, sums_b, land_b.at[2], down, r_send, r_recv)
     joined_b.start()
     direct_a.wait()
     direct_b.wait()
     joined_a.wait()
     joined_b.wait()
-    acc[low, :] += land_a[1].astype(jnp.float32) + land_a[2].astype(jnp.float32)
-    acc[high, :] += land_b[1].astype(jnp.float32) + land_b[2].astype(jnp.float32)
+    def add_low(r):
+        acc[pl.ds(r, 16), :] += (
+            land_a[1, pl.ds(r, 16), :].astype(jnp.float32) + land_a[2, pl.ds(r, 16), :].astype(jnp.float32)
+        )
+
+    def add_high(r):
+        acc[pl.ds(split + r, 16), :] += (
+            land_b[1, pl.ds(r, 16), :].astype(jnp.float32) + land_b[2, pl.ds(r, 16), :].astype(jnp.float32)
+        )
+
+    by_chunks(low_count, add_low)
+    by_chunks(high_count, add_high)
     if not gather:
         out_ref[...] = acc[...]
         return
-    result = (own_ref[...].astype(jnp.float32) + gate_ref[...] * acc[...]).astype(full_ref.dtype)
-    full_ref[section, head] = result
-    out_ref[...] = result
+
+    def finish(r):
+        result = (
+            own_ref[pl.ds(r, 16), :].astype(jnp.float32) + gate_ref[...] * acc[pl.ds(r, 16), :]
+        ).astype(full_ref.dtype)
+        full_ref[section, head, pl.ds(r, 16), :] = result
+        out_ref[pl.ds(r, 16), :] = result
+
+    by_chunks(own_rows, finish)
 
     def pass_copy(h):
         return pltpu.make_async_remote_copy(

time: 212 us -> 222 us (1.047)
  local copies, waits for them, and re-layouts: 54.4 us -> 81 us
  waiting for transfers between devices: 14 us -> 0.74 us
  other arithmetic: 23.7 us -> 19.6 us
    all_gather x2, waiting for transfers between devices: 13.3 us -> 0.02 us  [shards(): lax.all_gather(jnp.swapaxes(stale_kv[layer], 0, 1), 'tok', axis=0, tiled=...]
    rev x0 -> x4, local copies, waits for them, and re-layouts: none -> 13 us  [rotate(): swapped = pairs[..., ::-1].reshape(inputs.shape)]
    reshape x0 -> x8, local copies, waits for them, and re-layouts: none -> 9.89 us  [the longest x4 4.41 us: rotate(): swapped = pairs[..., ::-1].reshape(inputs.shape)]
    another operation x8 -> x2, other arithmetic: 8.88 us -> 0.21 us
    broadcast_in_dim x0 -> x4, local copies, waits for them, and re-layouts: none -> 5 us  [the longest x2 2.51 us: rotate(): cosine = jnp.repeat(jnp.cos(angles), 2, axis=-1)]
    convert_element_type x0 -> x2, other arithmetic: none -> 4.33 us  [project(): rotate(rms_norm(pieces[1], gains[1]), positions).astype(jnp.bfloat16)]
    convert_element_type x8 -> x0, local copies, waits for them, and re-layouts: 4.04 us -> none  [the longest x4 2.02 us: project(): rotate(rms_norm(pieces[1], gains[1]), positions).astype(jnp.bfloat16)]
  transfers between devices with their start and end apart: 5 -> 5, of which waited for: 2 -> 0; matrix products, arithmetic and copies ran while one was open for 46% -> 54% of each run, Pallas kernels for 21% -> 20%
where the time goes in v10:
time: 222 us; the launch traced here: 220 us
  local copies, waits for them, and re-layouts  81 us (36%)
  Pallas kernels  72.1 us (32%)
  matrix products  28.9 us (13%)
  other arithmetic  19.6 us (9%)
  between operations  16.6 us (7%)
    pallas_call x2, Pallas kernels, exchange(): pl.pallas_call(functools.partial(exchange_kernel, head_count, own_rows, s...  44.3 us
    dot_general x7, local copies, waits for them, and re-layouts, project(): jnp.dot(normed, weight[:, part, :], preferred_element_type=jnp.float32)  31.3 us
    pallas_call x2, Pallas kernels, attend(): pl.pallas_call(functools.partial(attention_kernel, head_dim), out_shape=j...  27.8 us
    dot_general x6, matrix products, project(): jnp.dot(normed, weight[:, part, :], preferred_element_type=jnp.float32)  18 us
    rev x4, local copies, waits for them, and re-layouts, rotate(): swapped = pairs[..., ::-1].reshape(inputs.shape)  13 us
    squeeze x1, local copies, waits for them, and re-layouts, shards(): w_qkv[layer_idx]  6.09 us
    dot_general x2, matrix products, shards(): jnp.dot(mine, w_out[layer_idx], preferred_element_type=jnp.float32)  5.06 us
    dot_general x2, matrix products, shards(): jnp.dot(swapped, w_partner[layer_idx], preferred_element_type=jnp.float32)  4.93 us
  transfers between devices with their start and end apart: 5, of which 0 were waited for; matrix products, arithmetic and copies ran while one was open for 54% of the time, Pallas kernels for 20%

profile of v10, /device:TPU:8, one launch (start us, length us, event | category | flops | bytes accessed | tf_op | source)
XLA Modules:
  0.0 220.1 jit_solution(1388314523045675470)
XLA Ops:
  7.2 2.4 %fusion.37 = (bf16[1,2,1,384,384]{4,3,2,1,0:T(8,128)(2,1)}, bf16[1,2,1,384,384]{4,3,2,1,0:T(8,128)(2,1)}) fusion(bf16[2,2,1,384,384]{4,3,2,1,0:T(8,128)(2,1)} %param.22), kind=kLoop, calls=%fused_computation.112 | loop fusion | bytes 2359296 | tf_op jit(solution)/shard_map/slice | solution.py:379
  10.5 6.1 %slice_bitcast_fusion = (bf16[3072,3,384]{2,0,1:T(8,128)(2,1)S(1)}, bf16[3072,3,384]{2,0,1:T(8,128)(2,1)S(1)}) fusion(bf16[2,3072,3,384]{3,1,2,0:T(8,128)(2,1)} %param.17), kind=kLoop, calls=%fused_computation | loop fusion | bytes 28311552 | tf_op jit(solution)/shard_map/squeeze | solution.py:390
  16.6 5.2 %slice_bitcast_fusion.4 = (bf16[384,3072]{0,1:T(8,128)(2,1)}, bf16[384,3072]{0,1:T(8,128)(2,1)}, bf16[384,3072]{0,1:T(8,128)(2,1)}, bf16[384,3072]{0,1:T(8,128)(...) fusion(bf16[3072,3,384]{2,0,1:T(8,128)(2,1)S(1)} %get-tuple-element.23, ...), kind=kLoop, calls=%fused_computation.26 | loop fusion | bytes 28311552 | tf_op jit(solution)/shard_map/dot_general | solution.py:60
  21.9 4.5 %copy.65 = bf16[384,3072]{1,0:T(8,128)(2,1)} copy(bf16[384,3072]{0,1:T(8,128)(2,1)} %get-tuple-element.60) | data formatting | bytes 4718592 | tf_op jit(solution)/shard_map/dot_general | solution.py:60
  34.1 4.1 %rev.12 = f32[384,3,64,2]{0,3,2,1:T(2,128)S(1)} reverse(f32[384,3,64,2]{0,3,2,1:T(2,128)} %reshape.574), dimensions={3} | reverse | bytes 1179648 | tf_op jit(solution)/shard_map/rev | solution.py:39
  39.4 4.3 %copy.66 = bf16[384,3072]{1,0:T(8,128)(2,1)} copy(bf16[384,3072]{0,1:T(8,128)(2,1)} %get-tuple-element.61) | data formatting | bytes 4718592 | tf_op jit(solution)/shard_map/dot_general | solution.py:60
  43.7 3.8 %multiply_reduce_fusion.2 = (f32[384,3]{0,1:T(4,128)S(1)}, f32[384,3,128]{0,2,1:T(8,128)S(1)}) fusion(bf16[384,3072,1]{1,0,2:T(8,128)(2,1)} %copy-done.5, bf16[3,128,3072]{2,1,0:T(8,128)(2,1)} %bitcast.156), kind=kOutput, calls=%fused_computation.57 | convolution fusion | flops 906263424 | bytes 5313024 | tf_op jit(solution)/shard_map/dot_general | solution.py:60
  50.7 3.5 %rev.13 = f32[384,3,64,2]{0,3,2,1:T(2,128)} reverse(f32[384,3,64,2]{0,3,2,1:T(2,128)S(1)} %reshape.577), dimensions={3} | reverse | bytes 1179648 | tf_op jit(solution)/shard_map/rev | solution.py:39
  54.1 2.4 %reshape.578 = f32[384,3,128]{0,2,1:T(8,128)} reshape(f32[384,3,64,2]{0,3,2,1:T(2,128)} %rev.13) | data formatting | bytes 1179648 | tf_op jit(solution)/shard_map/reshape | solution.py:39
  59.9 1.7 broadcast_in_dim.51
  63.7 1.8 broadcast_in_dim.49
  66.5 2.8 %add_convert_fusion.3 = (bf16[384,3,128]{0,2,1:T(8,128)(2,1)}, bf16[384,3,128]{0,2,1:T(8,128)(2,1)}) fusion(f32[384,3,128]{0,2,1:T(8,128)} %reshape.578, f32[384,128]{0,1:T(8,128)S(1)} %broadcast_multiply_fusion, f32[384,128]{0,1:T(8,128)} %broadcast_in_dim.49, f32[384,3,128]{0,2,1:T(8,128)} %reshape.575, f32[128]{0:T(128)} %copy-done.15, ...), kind=kLoop, calls=%fused_computation.55 | loop fusion | flops 1769472 | bytes 3352576 | tf_op jit(solution)/shard_map/convert_element_type | solution.py:66
  69.3 1.9 copy.68.q_ref
  71.2 1.8 copy.69.kf_ref
  73.8 4.4 %copy.67 = bf16[384,3072]{1,0:T(8,128)(2,1)} copy(bf16[384,3072]{0,1:T(8,128)(2,1)} %get-tuple-element.62) | data formatting | bytes 4718592 | tf_op jit(solution)/shard_map/dot_general | solution.py:60
  78.2 3.8 %convolution_convert_fusion.1 = bf16[384,3,128]{0,2,1:T(8,128)(2,1)S(1)} fusion(bf16[384,3072,1]{1,0,2:T(8,128)(2,1)} %copy-done.5, bf16[3,128,3072]{2,1,0:T(8,128)(2,1)} %bitcast.157), kind=kOutput, calls=%fused_computation.40 | convolution fusion | flops 906117120 | bytes 5013504 | tf_op jit(solution)/shard_map/dot_general | solution.py:60
  82.8 4.3 %copy.73 = bf16[384,3072]{1,0:T(8,128)(2,1)} copy(bf16[384,3072]{0,1:T(8,128)(2,1)} %get-tuple-element.25) | data formatting | bytes 4718592 | tf_op jit(solution)/shard_map/dot_general | solution.py:60
  87.1 4.3 %copy.71 = bf16[384,3072]{1,0:T(8,128)(2,1)} copy(bf16[384,3072]{0,1:T(8,128)(2,1)} %get-tuple-element.27) | data formatting | bytes 4718592 | tf_op jit(solution)/shard_map/dot_general | solution.py:60
  91.4 4.3 %copy.72 = bf16[384,3072]{1,0:T(8,128)(2,1)} copy(bf16[384,3072]{0,1:T(8,128)(2,1)} %get-tuple-element.26) | data formatting | bytes 4718592 | tf_op jit(solution)/shard_map/dot_general | solution.py:60
  99.8 1.8 compare_select_fusion.fetch_ref
  101.7 13.9 %shard_map.166 = bf16[384,384]{1,0:T(8,128)(2,1)} custom-call(s32[7]{0:T(128)} %compare_select_fusion.fetch_ref, s32[7]{0:T(128)} %compare_convert_fusion.allow_ref, bf16[384,384]{1,0:T(8,128)(2,1)} %copy.68.q_ref, bf16[384,384]{1,0:T(8,128)(2,1)} %copy.69.kf_ref, bf16[384,384]{1,0:T(8,128)(2,1)} %copy.70.vf_ref, bf16[16,2,384,384]{3,2,1,0:T(8,128)(2,1)} %bitcast.146, ...), custom_call_target="tpu_custom_call" | custom-call | tf_op jit(solution)/shard_map/pallas_call | solution.py:136
  117.0 2.5 %fusion.18 = f32[192,3072]{1,0:T(8,128)S(1)} fusion(bf16[2,384,3072]{2,1,0:T(8,128)(2,1)} %param.18, bf16[384,384]{1,0:T(8,128)(2,1)} %shard_map.166, s32[]{:T(128)S(6)} %select_n.36), kind=kOutput, calls=%fused_computation.35 | convolution fusion | flops 452984832 | bytes 4866052 | tf_op jit(solution)/shard_map/dot_general | solution.py:403
  119.6 2.5 %fusion.13.part_ref = bf16[192,3072]{1,0:T(8,128)(2,1)S(1)} fusion(f32[192,3072]{1,0:T(8,128)S(1)} %fusion.18, bf16[192,384]{1,0:T(8,128)(2,1)S(1)} %collective-permute-done, bf16[2,384,3072]{2,1,0:T(8,128)(2,1)} %collective-permute-done.1), kind=kOutput, calls=%fused_computation.22 | convolution fusion | flops 454164480 | bytes 6045696 | tf_op jit(solution)/shard_map/dot_general | solution.py:404
  122.0 29.1 %shard_map.167 = (bf16[48,3072]{1,0:T(8,128)(2,1)S(1)}, bf16[2,4,48,3072]{3,2,1,0:T(8,128)(2,1)S(1)}) custom-call(bf16[192,3072]{1,0:T(8,128)(2,1)S(1)} %fusion.13.part_ref, bf16[48,3072]{1,0:T(8,128)(2,1)S(1)} %dynamic-slice_bitcast_fusion.own_ref, f32[1,3072]{1,0:T(1,128)S(1)} %get-tuple-element.39.gate_ref), custom_call_target="tpu_custom_call" | custom-call | tf_op jit(solution)/shard_map/pallas_call | solution.py:321
  156.3 3.8 %multiply_reduce_fusion.1 = (f32[384,3]{0,1:T(4,128)S(1)}, f32[384,3,128]{0,2,1:T(8,128)S(1)}) fusion(bf16[384,3072,1]{1,0,2:T(8,128)(2,1)} %bitcast.154, bf16[3,128,3072]{2,1,0:T(8,128)(2,1)} %bitcast.150), kind=kOutput, calls=%fused_computation.54 | convolution fusion | flops 906263424 | bytes 5313024 | tf_op jit(solution)/shard_map/dot_general | solution.py:60
  160.6 2.7 %rev.14 = f32[384,3,64,2]{0,3,2,1:T(2,128)S(1)} reverse(f32[384,3,64,2]{0,3,2,1:T(2,128)S(1)} %reshape.581), dimensions={3} | reverse | bytes 1179648 | tf_op jit(solution)/shard_map/rev | solution.py:39
  163.8 3.8 %multiply_reduce_fusion = (f32[384,3]{0,1:T(4,128)S(1)}, f32[384,3,128]{0,2,1:T(8,128)S(1)}) fusion(bf16[384,3072,1]{1,0,2:T(8,128)(2,1)} %bitcast.155, bf16[3,128,3072]{2,1,0:T(8,128)(2,1)} %bitcast.149), kind=kOutput, calls=%fused_computation.51 | convolution fusion | flops 906263424 | bytes 5313024 | tf_op jit(solution)/shard_map/dot_general | solution.py:60
  168.9 2.7 %rev.15 = f32[384,3,64,2]{0,3,2,1:T(2,128)S(1)} reverse(f32[384,3,64,2]{0,3,2,1:T(2,128)S(1)} %reshape.584), dimensions={3} | reverse | bytes 1179648 | tf_op jit(solution)/shard_map/rev | solution.py:39
  175.3 13.9 %shard_map.168 = bf16[384,384]{1,0:T(8,128)(2,1)} custom-call(s32[7]{0:T(128)} %compare_select_fusion.fetch_ref, s32[7]{0:T(128)} %compare_convert_fusion.allow_ref, bf16[384,384]{1,0:T(8,128)(2,1)} %copy.74.q_ref, bf16[384,384]{1,0:T(8,128)(2,1)} %copy.75.kf_ref, bf16[384,384]{1,0:T(8,128)(2,1)} %copy.76.vf_ref, bf16[16,2,384,384]{3,2,1,0:T(8,128)(2,1)} %bitcast.144, ...), custom_call_target="tpu_custom_call" | custom-call | tf_op jit(solution)/shard_map/pallas_call | solution.py:136
  190.7 2.5 %fusion.16 = f32[192,3072]{1,0:T(8,128)S(1)} fusion(bf16[2,384,3072]{2,1,0:T(8,128)(2,1)} %param.18, bf16[384,384]{1,0:T(8,128)(2,1)} %shard_map.168, s32[]{:T(128)S(6)} %select_n.36), kind=kOutput, calls=%fused_computation.33 | convolution fusion | flops 452984832 | bytes 4866052 | tf_op jit(solution)/shard_map/dot_general | solution.py:403
  193.2 2.5 %fusion.14.part_ref = bf16[192,3072]{1,0:T(8,128)(2,1)S(1)} fusion(f32[192,3072]{1,0:T(8,128)S(1)} %fusion.16, bf16[192,384]{1,0:T(8,128)(2,1)S(1)} %collective-permute-done.2, bf16[2,384,3072]{2,1,0:T(8,128)(2,1)} %collective-permute-done.1), kind=kOutput, calls=%fused_computation.23 | convolution fusion | flops 454164480 | bytes 6045696 | tf_op jit(solution)/shard_map/dot_general | solution.py:404
  195.7 15.2 %shard_map.169 = f32[48,3072]{1,0:T(8,128)S(1)} custom-call(bf16[192,3072]{1,0:T(8,128)(2,1)S(1)} %fusion.14.part_ref, bf16[48,3072]{1,0:T(8,128)(2,1)S(1)} %get-tuple-element.5.own_ref, f32[1,3072]{1,0:T(1,128)S(1)} %get-tuple-element.38.gate_ref), custom_call_target="tpu_custom_call" | custom-call | tf_op jit(solution)/shard_map/pallas_call | solution.py:321
  (122 shorter events, 39.2 us)
Async XLA Ops:
  7.2 205.1 %copy-start = (bf16[3072,64]{0,1:T(8,128)(2,1)S(1)}, bf16[3072,64]{0,1:T(8,128)(2,1)}, u32[]{:S(2)}) copy-start(bf16[3072,64]{0,1:T(8,128)(2,1)} %param.19) | copy-start | bytes 1179652
  7.2 94.5 %all-gather.5.cloned.1.call-start = ((), (), s32[]{:S(2)}) async-start(), calls=%async_computation | async-start | bytes 10027008 | tf_op jit(solution)/shard_map/all_gather | solution.py:379
  9.7 165.7 %all-gather.7.cloned.1.call-start = ((), (), s32[]{:S(2)}) async-start(), calls=%async_computation.1 | async-start | bytes 10027008 | tf_op jit(solution)/shard_map/all_gather | solution.py:379
  10.4 109.1 %collective-permute-start.1 = (bf16[2,384,3072]{2,1,0:T(8,128)(2,1)}, bf16[2,384,3072]{2,1,0:T(8,128)(2,1)}, u32[]{:S(2)}, u32[]{:S(2)}) collective-permute-start(bf16[2,384,3072]{2,1,0:T(8,128)(2,1)} %param.18), channel_id=1, source_target_pairs={{0,64},{64,0},{1,65},{65,1},{2,66},{66,2},{3,67},{67,3},{4,68},{68... | collective-permute-start | bytes 14155784 | tf_op jit(solution)/shard_map/ppermute | solution.py:383
  21.9 4.5 %copy-start.16 = (f32[2,2,128]{2,1,0:T(2,128)S(1)}, f32[2,2,128]{2,1,0:T(2,128)}, u32[]{:S(2)}) copy-start(f32[2,2,128]{2,1,0:T(2,128)} %param.20) | copy-start | bytes 6148
  21.9 5.0 %copy-start.1 = (bf16[1,384,3072]{2,1,0:T(8,128)(2,1)S(1)}, bf16[1,384,3072]{2,1,0:T(8,128)(2,1)}, u32[]{:S(2)}) copy-start(bf16[1,384,3072]{2,1,0:T(8,128)(2,1)} %param.15) | copy-start | bytes 7077892
  26.9 4.4 %copy-start.15 = (f32[128]{0:T(128)}, f32[128]{0:T(128)S(1)}, u32[]{:S(2)}) copy-start(f32[128]{0:T(128)S(1)} %get-tuple-element.50) | copy-start | bytes 1540
  26.9 20.6 %copy-start.14 = (f32[128]{0:T(128)}, f32[128]{0:T(128)S(1)}, u32[]{:S(2)}) copy-start(f32[128]{0:T(128)S(1)} %get-tuple-element.49) | copy-start | bytes 1540
  26.9 1.2 copy-start.12
  28.2 1.7 copy-start.3
  29.5 1.9 copy-start.5
  31.3 0.8 copy-start.6
  47.5 0.8 copy-start.8
  48.3 8.2 %copy-start.20 = (s32[4]{0:T(128)S(1)}, s32[4]{0:T(128)}, u32[]{:S(2)}) copy-start(s32[4]{0:T(128)} %param.23) | copy-start | bytes 52
  48.3 8.3 %copy-start.21 = (s32[16]{0:T(128)S(1)}, s32[16]{0:T(128)}, u32[]{:S(2)}) copy-start(s32[16]{0:T(128)} %param.24) | copy-start | bytes 196
  54.1 12.4 %copy-start.7 = (f32[384,3,128]{0,2,1:T(8,128)S(1)}, f32[384,3,128]{0,2,1:T(8,128)}, u32[]{:S(2)}) copy-start(f32[384,3,128]{0,2,1:T(8,128)} %copy-done.6) | copy-start | bytes 1769476
  56.7 1.9 copy-start.17
  66.5 2.8 %copy-start.11 = (f32[384,128]{0,1:T(8,128)}, f32[384,128]{0,1:T(8,128)S(1)}, u32[]{:S(2)}) copy-start(f32[384,128]{0,1:T(8,128)S(1)} %broadcast_multiply_fusion) | copy-start | bytes 589828
  66.5 6.5 %copy-start.18 = (s32[16]{0:T(128)S(1)}, s32[16]{0:T(128)}, u32[]{:S(2)}) copy-start(s32[16]{0:T(128)} %copy-done.17) | copy-start | bytes 196
  116.5 3.0 %collective-permute-start = (bf16[192,384]{1,0:T(8,128)(2,1)S(1)}, bf16[192,384]{1,0:T(8,128)(2,1)S(1)}, u32[]{:S(2)}, u32[]{:S(2)}) collective-permute-start(bf16[192,384]{1,0:T(8,128)(2,1)S(1)} %constant_dynamic-slice_fusion.1), channel_id=1, source_target_pairs={{0,64},{64,0},{1,65},{65,1},{2,66},{66,2},{3,67},{67,3},{4,68},{68... | collective-permute-start | bytes 442376 | tf_op jit(solution)/shard_map/ppermute | solution.py:401
  152.3 1.7 copy-start.2
  153.6 1.8 copy-start.4
  156.3 3.8 %copy-start.13 = (f32[128]{0:T(128)S(1)}, f32[128]{0:T(128)}, u32[]{:S(2)}) copy-start(f32[128]{0:T(128)} %get-tuple-element.51) | copy-start | bytes 1540
  167.6 0.8 copy-start.9
  168.4 3.6 %copy-start.10 = (f32[384,128]{0,1:T(8,128)S(1)}, f32[384,128]{0,1:T(8,128)}, u32[]{:S(2)}) copy-start(f32[384,128]{0,1:T(8,128)} %broadcast_in_dim.49) | copy-start | bytes 589828
  190.2 3.1 %collective-permute-start.2 = (bf16[192,384]{1,0:T(8,128)(2,1)S(1)}, bf16[192,384]{1,0:T(8,128)(2,1)S(1)}, u32[]{:S(2)}, u32[]{:S(2)}) collective-permute-start(bf16[192,384]{1,0:T(8,128)(2,1)S(1)} %constant_dynamic-slice_fusion), channel_id=1, source_target_pairs={{0,64},{64,0},{1,65},{65,1},{2,66},{66,2},{3,67},{67,3},{4,68},{68... | collective-permute-start | bytes 442376 | tf_op jit(solution)/shard_map/ppermute | solution.py:401
  195.7 16.6 %copy-start.19 = (f32[1,48,64]{2,1,0:T(8,128)S(1)}, f32[1,48,64]{2,1,0:T(8,128)}, u32[]{:S(2)}) copy-start(f32[1,48,64]{2,1,0:T(8,128)} %param.16) | copy-start | bytes 36868
Sparse Core Ops, SparseCore 0:
  10.2 77.9 all-gather.4
  90.3 75.2 all-gather.6

commit v11 on v8

--- a/solution.py
+++ b/solution.py
@@ -75,37 +75,45 @@
     )
 
 
-def attention_kernel(
-    head_dim, fetch_ref, allow_ref, q_ref, kf_ref, vf_ref, ks_ref, vs_ref, o_ref, qt_sc, m_sc, l_sc, acc_sc
-):
-    slot = pl.program_id(0)
+def fresh_kernel(head_dim, q_ref, kf_ref, vf_ref, qt_ref, m_ref, l_ref, acc_ref):
     heads = q_ref.shape[1] // head_dim
     scaling = 1.0 / math.sqrt(head_dim)
     by_key = (((0,), (0,)), ((), ()))
+    for h in range(heads):
+        lanes = slice(h * head_dim, (h + 1) * head_dim)
+        qt_ref[h] = q_ref[:, lanes].T
+        scores = jnp.dot(kf_ref[:, lanes], qt_ref[h], preferred_element_type=jnp.float32) * scaling
+        col_max = jnp.max(scores, axis=0, keepdims=True)
+        weights = jnp.exp(scores - col_max)
+        m_ref[h] = col_max
+        l_ref[h] = jnp.sum(weights, axis=0, keepdims=True)
+        acc_ref[h] = lax.dot_general(
+            vf_ref[:, lanes], weights.astype(jnp.bfloat16), by_key,
+            preferred_element_type=jnp.float32,
+        )
+
+
+def attention_kernel(
+    head_dim, fetch_ref, allow_ref, qt_ref, m0_ref, l0_ref, acc0_ref, ks_ref, vs_ref, o_ref,
+    m_sc, l_sc, acc_sc
+):
+    slot = pl.program_id(0)
+    heads = qt_ref.shape[0]
+    scaling = 1.0 / math.sqrt(head_dim)
+    by_key = (((0,), (0,)), ((), ()))
 
     @pl.when(slot == 0)
-    def _fresh():
-        for h in range(heads):
-            lanes = slice(h * head_dim, (h + 1) * head_dim)
-            qt_sc[h] = q_ref[:, lanes].T
-            scores = (
-                jnp.dot(kf_ref[:, lanes], qt_sc[h], preferred_element_type=jnp.float32) * scaling
-            )
-            col_max = jnp.max(scores, axis=0, keepdims=True)
-            weights = jnp.exp(scores - col_max)
-            m_sc[h] = col_max
-            l_sc[h] = jnp.sum(weights, axis=0, keepdims=True)
-            acc_sc[h] = lax.dot_general(
-                vf_ref[:, lanes], weights.astype(jnp.bfloat16), by_key,
-                preferred_element_type=jnp.float32,
-            )
+    def _start():
+        m_sc[...] = m0_ref[...]
+        l_sc[...] = l0_ref[...]
+        acc_sc[...] = acc0_ref[...]
 
     @pl.when(allow_ref[slot] != 0)
     def _stale():
         for h in range(heads):
             lanes = slice(h * head_dim, (h + 1) * head_dim)
             scores = (
-                jnp.dot(ks_ref[:, lanes], qt_sc[h], preferred_element_type=jnp.float32) * scaling
+                jnp.dot(ks_ref[:, lanes], qt_ref[h], preferred_element_type=jnp.float32) * scaling
             )
             old_max = m_sc[h]
             new_max = jnp.maximum(old_max, jnp.max(scores, axis=0, keepdims=True))
@@ -129,7 +137,21 @@
     rows, features = queries.shape
     slot_total = fetch.shape[0]
     heads = features // head_dim
+    vmem = pl.BlockSpec(memory_space=pltpu.VMEM)
+    state = pl.pallas_call(
+        functools.partial(fresh_kernel, head_dim),
+        out_shape=(
+            jax.ShapeDtypeStruct((heads, head_dim, rows), jnp.bfloat16),
+            jax.ShapeDtypeStruct((heads, 1, rows), jnp.float32),
+            jax.ShapeDtypeStruct((heads, 1, rows), jnp.float32),
+            jax.ShapeDtypeStruct((heads, head_dim, rows), jnp.float32),
+        ),
+        in_specs=[vmem] * 3,
+        out_specs=(vmem,) * 4,
+    )(queries, keys_fresh, values_fresh)
     whole = pl.BlockSpec((rows, features), lambda j, f, a: (0, 0))
+    qt_spec = pl.BlockSpec((heads, head_dim, rows), lambda j, f, a: (0, 0, 0))
+    stat_spec = pl.BlockSpec((heads, 1, rows), lambda j, f, a: (0, 0, 0))
     key_spec = pl.BlockSpec(
         (None, None, rows, features), lambda j, f, a: (f[j], 0, 0, 0)
     )
@@ -142,17 +164,16 @@
         grid_spec=pltpu.PrefetchScalarGridSpec(
             num_scalar_prefetch=2,
             grid=(slot_total,),
-            in_specs=[whole, whole, whole, key_spec, value_spec],
+            in_specs=[qt_spec, stat_spec, stat_spec, qt_spec, key_spec, value_spec],
             out_specs=whole,
             scratch_shapes=[
-                pltpu.VMEM((heads, head_dim, rows), jnp.bfloat16),
                 pltpu.VMEM((heads, 1, rows), jnp.float32),
                 pltpu.VMEM((heads, 1, rows), jnp.float32),
                 pltpu.VMEM((heads, head_dim, rows), jnp.float32),
             ],
         ),
         compiler_params=pltpu.CompilerParams(dimension_semantics=("arbitrary",)),
-    )(fetch, allow, queries, keys_fresh, values_fresh, stale, stale)
+    )(fetch, allow, *state, stale, stale)
 
 
 def exchange_kernel(head_count, own_rows, split, gather, part_ref, own_ref, gate_ref, *rest):

time: 212 us -> 211 us (level)
  waiting for transfers between devices: 14 us -> 8.25 us
  Pallas kernels: 73.2 us -> 77.2 us
    pallas_call x0 -> x2, Pallas kernels: none -> 6.53 us  [attend(): pl.pallas_call(functools.partial(fresh_kernel, head_dim), out_shape=(jax....]
    all_gather x2, waiting for transfers between devices: 13.3 us -> 7.53 us  [shards(): lax.all_gather(jnp.swapaxes(stale_kv[layer], 0, 1), 'tok', axis=0, tiled=...]
    pallas_call x2, Pallas kernels: 27.8 us -> 25.4 us  [attend(): pl.pallas_call(functools.partial(attention_kernel, head_dim), out_shape=j...]
  transfers between devices with their start and end apart: 5 -> 5, of which waited for: 2 -> 2; matrix products, arithmetic and copies ran while one was open for 46% -> 47% of each run, Pallas kernels for 21% -> 23%
where the time goes in v11:
time: 211 us; the launch traced here: 210 us
  Pallas kernels  77.2 us (37%)
  local copies, waits for them, and re-layouts  54.7 us (26%)
  matrix products  28.5 us (14%)
  other arithmetic  23.8 us (11%)
  between operations  16.5 us (8%)
  waiting for transfers between devices  8.25 us (4%)
    pallas_call x2, Pallas kernels, exchange(): pl.pallas_call(functools.partial(exchange_kernel, head_count, own_rows, s...  45.3 us
    dot_general x7, local copies, waits for them, and re-layouts, project(): jnp.dot(normed, weight[:, part, :], preferred_element_type=jnp.float32)  31.4 us
    pallas_call x2, Pallas kernels, attend(): pl.pallas_call(functools.partial(attention_kernel, head_dim), out_shape=j...  25.4 us
    dot_general x6, matrix products, project(): jnp.dot(normed, weight[:, part, :], preferred_element_type=jnp.float32)  17.5 us
    all_gather x2, waiting for transfers between devices, shards(): lax.all_gather(jnp.swapaxes(stale_kv[layer], 0, 1), 'tok', axis=0, tiled=...  7.53 us
    pallas_call x2, Pallas kernels, attend(): pl.pallas_call(functools.partial(fresh_kernel, head_dim), out_shape=(jax....  6.53 us
    squeeze x1, local copies, waits for them, and re-layouts, shards(): w_qkv[layer_idx]  6.09 us
    another operation x4, other arithmetic  5.14 us
  transfers between devices with their start and end apart: 5, of which 2 were waited for; matrix products, arithmetic and copies ran while one was open for 47% of the time, Pallas kernels for 23%

profile of v11, /device:TPU:8, one launch (start us, length us, event | category | flops | bytes accessed | tf_op | source)
XLA Modules:
  0.0 209.6 jit_solution(10576071227113541263)
XLA Ops:
  7.2 2.4 %fusion.37 = (bf16[1,2,1,384,384]{4,3,2,1,0:T(8,128)(2,1)}, bf16[1,2,1,384,384]{4,3,2,1,0:T(8,128)(2,1)}) fusion(bf16[2,2,1,384,384]{4,3,2,1,0:T(8,128)(2,1)} %param.18), kind=kLoop, calls=%fused_computation.119 | loop fusion | bytes 2359296 | tf_op jit(solution)/shard_map/slice | solution.py:371
  11.2 6.1 %slice_bitcast_fusion = (bf16[3072,3,384]{2,0,1:T(8,128)(2,1)S(1)}, bf16[3072,3,384]{2,0,1:T(8,128)(2,1)S(1)}) fusion(bf16[2,3072,3,384]{3,1,2,0:T(8,128)(2,1)} %param.13), kind=kLoop, calls=%fused_computation | loop fusion | bytes 28311552 | tf_op jit(solution)/shard_map/squeeze | solution.py:382
  17.3 5.2 %slice_bitcast_fusion.4 = (bf16[384,3072]{0,1:T(8,128)(2,1)}, bf16[384,3072]{0,1:T(8,128)(2,1)}, bf16[384,3072]{0,1:T(8,128)(2,1)}, bf16[384,3072]{0,1:T(8,128)(...) fusion(bf16[3072,3,384]{2,0,1:T(8,128)(2,1)S(1)} %get-tuple-element.39, ...), kind=kLoop, calls=%fused_computation.26 | loop fusion | bytes 28311552 | tf_op jit(solution)/shard_map/dot_general | solution.py:63
  22.5 4.4 %copy.65 = bf16[384,3072]{1,0:T(8,128)(2,1)} copy(bf16[384,3072]{0,1:T(8,128)(2,1)} %get-tuple-element.84) | data formatting | bytes 4718592 | tf_op jit(solution)/shard_map/dot_general | solution.py:63
  30.0 1.4 multiply_reduce_fusion.3
  32.3 1.4 reshape.472
  33.8 4.3 %copy.66 = bf16[384,3072]{1,0:T(8,128)(2,1)} copy(bf16[384,3072]{0,1:T(8,128)(2,1)} %get-tuple-element.85) | data formatting | bytes 4718592 | tf_op jit(solution)/shard_map/dot_general | solution.py:63
  38.0 3.8 %multiply_reduce_fusion.2 = (f32[384,3]{0,1:T(4,128)S(1)}, f32[384,3,128]{0,2,1:T(8,128)S(1)}) fusion(bf16[384,3072,1]{1,0,2:T(8,128)(2,1)} %copy-done.6, bf16[3,128,3072]{2,1,0:T(8,128)(2,1)} %bitcast.148), kind=kOutput, calls=%fused_computation.54 | convolution fusion | flops 906263424 | bytes 5313024 | tf_op jit(solution)/shard_map/dot_general | solution.py:63
  42.8 2.2 %reshape.473 = f32[384,3,64,2]{0,3,2,1:T(2,128)} reshape(f32[384,3,128]{0,2,1:T(8,128)} %multiply_multiply_fusion.2) | data formatting | bytes 1179648 | tf_op jit(solution)/shard_map/reshape | solution.py:35
  47.7 3.4 %subtract_convert_fusion.2 = (bf16[384,3,64,1]{0,3,2,1:T(2,128)(2,1)S(1)}, bf16[384,3,64,1]{0,3,2,1:T(2,128)(2,1)S(1)}, bf16[384,3,64,1]{0,3,2,1:T(2,128)(2,1)}, bf16[384,3,64,1]{0,3,2,1:T(2,128)(2,1)}) fusion(f32[384,3,64,2]{0,3,2,1:T(2,128)} %reshape.473, f32[384,64]{0,1:T(8,128)S(1)} %get-tuple-element.71, f32[384,64]{0,1:T(8,128)S(1)} %get-tuple-element.70, ...), kind=kLoop, calls=%fused_computation.70 | loop fusion | flops 1179648 | bytes 1966080 | tf_op jit(solution)/shard_map/convert.4
  52.8 1.7 pad_maximum_fusion
  55.5 4.3 %copy.67 = bf16[384,3072]{1,0:T(8,128)(2,1)} copy(bf16[384,3072]{0,1:T(8,128)(2,1)} %get-tuple-element.86) | data formatting | bytes 4718592 | tf_op jit(solution)/shard_map/dot_general | solution.py:63
  59.8 4.0 %convolution_convert_fusion.1 = bf16[384,3,128]{0,2,1:T(8,128)(2,1)S(1)} fusion(bf16[384,3072,1]{1,0,2:T(8,128)(2,1)} %copy-done.6, bf16[3,128,3072]{2,1,0:T(8,128)(2,1)} %bitcast.149), kind=kOutput, calls=%fused_computation.40 | convolution fusion | flops 906117120 | bytes 5013504 | tf_op jit(solution)/shard_map/dot_general | solution.py:63
  65.5 4.5 %copy.73 = bf16[384,3072]{1,0:T(8,128)(2,1)} copy(bf16[384,3072]{0,1:T(8,128)(2,1)} %get-tuple-element.41) | data formatting | bytes 4718592 | tf_op jit(solution)/shard_map/dot_general | solution.py:63
  70.0 4.4 %copy.71 = bf16[384,3072]{1,0:T(8,128)(2,1)} copy(bf16[384,3072]{0,1:T(8,128)(2,1)} %get-tuple-element.43) | data formatting | bytes 4718592 | tf_op jit(solution)/shard_map/dot_general | solution.py:63
  74.3 4.3 %copy.72 = bf16[384,3072]{1,0:T(8,128)(2,1)} copy(bf16[384,3072]{0,1:T(8,128)(2,1)} %get-tuple-element.42) | data formatting | bytes 4718592 | tf_op jit(solution)/shard_map/dot_general | solution.py:63
  80.7 3.3 %shard_map.130 = (bf16[3,128,384]{2,1,0:T(8,128)(2,1)}, f32[3,1,384]{2,1,0:T(1,128)}, f32[3,1,384]{2,1,0:T(1,128)}, f32[3,128,384]{2,1,0:T(8,128)}) custom-call(bf16[384,384]{1,0:T(8,128)(2,1)} %copy.68.q_ref, bf16[384,384]{1,0:T(8,128)(2,1)} %copy.69.kf_ref, bf16[384,384]{1,0:T(8,128)(2,1)} %copy.70.vf_ref), custom_call_target="tpu_custom_call" | custom-call | tf_op jit(solution)/shard_map/pallas_call | solution.py:141
  86.0 1.9 compare_select_fusion.fetch_ref
  88.2 12.7 %shard_map.131 = bf16[384,384]{1,0:T(8,128)(2,1)} custom-call(s32[7]{0:T(128)} %compare_select_fusion.fetch_ref, s32[7]{0:T(128)} %compare_convert_fusion.allow_ref, bf16[3,128,384]{2,1,0:T(8,128)(2,1)} %get-tuple-element.13.qt_ref, f32[3,1,384]{2,1,0:T(1,128)} %get-tuple-element.14.m0_ref, f32[3,1,384]{2,1,0:T(1,128)} %get-tuple-element.15.l0_ref, ...), custom_call_target="tpu_custom_call" | custom-call | tf_op jit(solution)/shard_map/pallas_call | solution.py:161
  102.1 2.5 %fusion.18 = f32[192,3072]{1,0:T(8,128)S(1)} fusion(bf16[2,384,3072]{2,1,0:T(8,128)(2,1)} %param.14, bf16[384,384]{1,0:T(8,128)(2,1)} %shard_map.131, s32[]{:T(128)S(6)} %select_n.36), kind=kOutput, calls=%fused_computation.35 | convolution fusion | flops 452984832 | bytes 4866052 | tf_op jit(solution)/shard_map/dot_general | solution.py:395
  104.7 2.5 %fusion.13.part_ref = bf16[192,3072]{1,0:T(8,128)(2,1)S(1)} fusion(f32[192,3072]{1,0:T(8,128)S(1)} %fusion.18, bf16[192,384]{1,0:T(8,128)(2,1)S(1)} %collective-permute-done, bf16[2,384,3072]{2,1,0:T(8,128)(2,1)} %collective-permute-done.1), kind=kOutput, calls=%fused_computation.22 | convolution fusion | flops 454164480 | bytes 6045696 | tf_op jit(solution)/shard_map/dot_general | solution.py:396
  107.2 29.3 %shard_map.132 = (bf16[48,3072]{1,0:T(8,128)(2,1)S(1)}, bf16[2,4,48,3072]{3,2,1,0:T(8,128)(2,1)S(1)}) custom-call(bf16[192,3072]{1,0:T(8,128)(2,1)S(1)} %fusion.13.part_ref, bf16[48,3072]{1,0:T(8,128)(2,1)S(1)} %dynamic-slice_bitcast_fusion.own_ref, f32[1,3072]{1,0:T(1,128)S(1)} %get-tuple-element.63.gate_ref), custom_call_target="tpu_custom_call" | custom-call | tf_op jit(solution)/shard_map/pallas_call | solution.py:313
  139.5 1.4 convolution_convert_fusion
  141.8 3.1 %multiply_reduce_fusion.1 = (f32[384,3]{0,1:T(4,128)S(1)}, f32[384,3,128]{0,2,1:T(8,128)S(1)}) fusion(bf16[384,3072,1]{1,0,2:T(8,128)(2,1)} %bitcast.146, bf16[3,128,3072]{2,1,0:T(8,128)(2,1)S(1)} %bitcast.142), kind=kOutput, calls=%fused_computation.52 | convolution fusion | flops 906263424 | bytes 5313024 | tf_op jit(solution)/shard_map/dot_general | solution.py:63
  145.4 3.8 %multiply_reduce_fusion = (f32[384,3]{0,1:T(4,128)S(1)}, f32[384,3,128]{0,2,1:T(8,128)S(1)}) fusion(bf16[384,3072,1]{1,0,2:T(8,128)(2,1)} %bitcast.147, bf16[3,128,3072]{2,1,0:T(8,128)(2,1)} %bitcast.141), kind=kOutput, calls=%fused_computation.50 | convolution fusion | flops 906263424 | bytes 5313024 | tf_op jit(solution)/shard_map/dot_general | solution.py:63
  150.1 1.6 subtract_convert_fusion
  155.0 3.3 %shard_map.133 = (bf16[3,128,384]{2,1,0:T(8,128)(2,1)}, f32[3,1,384]{2,1,0:T(1,128)}, f32[3,1,384]{2,1,0:T(1,128)}, f32[3,128,384]{2,1,0:T(8,128)}) custom-call(bf16[384,384]{1,0:T(8,128)(2,1)} %copy.74.q_ref, bf16[384,384]{1,0:T(8,128)(2,1)} %copy.75.kf_ref, bf16[384,384]{1,0:T(8,128)(2,1)} %copy.76.vf_ref), custom_call_target="tpu_custom_call" | custom-call | tf_op jit(solution)/shard_map/pallas_call | solution.py:141
  158.3 7.3 %all-gather.7.cloned.1.call-done = bf16[16,2,1,384,384]{4,3,2,1,0:T(8,128)(2,1)} async-done(((bf16[1,2,1,384,384]{4,3,2,1,0:T(8,128)(2,1)}), bf16[16,2,1,384,384]{4,3,2,1,0:T(8,128)(2,1)}) %all-gather.7.cloned.1.call-update) | async-done | bytes 9437200 | tf_op jit(solution)/shard_map/all_gather | solution.py:371
  165.6 12.7 %shard_map.134 = bf16[384,384]{1,0:T(8,128)(2,1)} custom-call(s32[7]{0:T(128)} %compare_select_fusion.fetch_ref, s32[7]{0:T(128)} %compare_convert_fusion.allow_ref, bf16[3,128,384]{2,1,0:T(8,128)(2,1)} %get-tuple-element.19.qt_ref, f32[3,1,384]{2,1,0:T(1,128)} %get-tuple-element.20.m0_ref, f32[3,1,384]{2,1,0:T(1,128)} %get-tuple-element.21.l0_ref, ...), custom_call_target="tpu_custom_call" | custom-call | tf_op jit(solution)/shard_map/pallas_call | solution.py:161
  179.3 2.5 %fusion.16 = f32[192,3072]{1,0:T(8,128)S(1)} fusion(bf16[2,384,3072]{2,1,0:T(8,128)(2,1)} %param.14, bf16[384,384]{1,0:T(8,128)(2,1)} %shard_map.134, s32[]{:T(128)S(6)} %select_n.36), kind=kOutput, calls=%fused_computation.33 | convolution fusion | flops 452984832 | bytes 4866052 | tf_op jit(solution)/shard_map/dot_general | solution.py:395
  181.9 2.5 %fusion.14.part_ref = bf16[192,3072]{1,0:T(8,128)(2,1)S(1)} fusion(f32[192,3072]{1,0:T(8,128)S(1)} %fusion.16, bf16[192,384]{1,0:T(8,128)(2,1)S(1)} %collective-permute-done.2, bf16[2,384,3072]{2,1,0:T(8,128)(2,1)} %collective-permute-done.1), kind=kOutput, calls=%fused_computation.23 | convolution fusion | flops 454164480 | bytes 6045696 | tf_op jit(solution)/shard_map/dot_general | solution.py:396
  184.4 16.1 %shard_map.135 = f32[48,3072]{1,0:T(8,128)S(1)} custom-call(bf16[192,3072]{1,0:T(8,128)(2,1)S(1)} %fusion.14.part_ref, bf16[48,3072]{1,0:T(8,128)(2,1)S(1)} %get-tuple-element.17.own_ref, f32[1,3072]{1,0:T(1,128)S(1)} %get-tuple-element.62.gate_ref), custom_call_target="tpu_custom_call" | custom-call | tf_op jit(solution)/shard_map/pallas_call | solution.py:313
  (101 shorter events, 28.8 us)
Async XLA Ops:
  7.2 194.6 %copy-start = (bf16[3072,64]{0,1:T(8,128)(2,1)S(1)}, bf16[3072,64]{0,1:T(8,128)(2,1)}, u32[]{:S(2)}) copy-start(bf16[3072,64]{0,1:T(8,128)(2,1)} %param.15) | copy-start | bytes 1179652
  7.2 81.0 %all-gather.5.cloned.1.call-start = ((), (), s32[]{:S(2)}) async-start(), calls=%async_computation | async-start | bytes 10027008 | tf_op jit(solution)/shard_map/all_gather | solution.py:371
  9.7 155.9 %all-gather.7.cloned.1.call-start = ((), (), s32[]{:S(2)}) async-start(), calls=%async_computation.1 | async-start | bytes 10027008 | tf_op jit(solution)/shard_map/all_gather | solution.py:371
  10.4 94.3 %collective-permute-start.1 = (bf16[2,384,3072]{2,1,0:T(8,128)(2,1)}, bf16[2,384,3072]{2,1,0:T(8,128)(2,1)}, u32[]{:S(2)}, u32[]{:S(2)}) collective-permute-start(bf16[2,384,3072]{2,1,0:T(8,128)(2,1)} %param.14), channel_id=1, source_target_pairs={{0,64},{64,0},{1,65},{65,1},{2,66},{66,2},{3,67},{67,3},{4,68},{68... | collective-permute-start | bytes 14155784 | tf_op jit(solution)/shard_map/ppermute | solution.py:375
  22.5 4.4 %copy-start.10 = (f32[2,2,128]{2,1,0:T(2,128)S(1)}, f32[2,2,128]{2,1,0:T(2,128)}, u32[]{:S(2)}) copy-start(f32[2,2,128]{2,1,0:T(2,128)} %param.16) | copy-start | bytes 6148
  22.5 4.4 %copy-start.1 = (bf16[1,384,3072]{2,1,0:T(8,128)(2,1)S(1)}, bf16[1,384,3072]{2,1,0:T(8,128)(2,1)}, u32[]{:S(2)}) copy-start(bf16[1,384,3072]{2,1,0:T(8,128)(2,1)} %param.11) | copy-start | bytes 7077892
  27.0 1.2 copy-start.9
  28.2 1.7 copy-start.4
  29.5 1.9 copy-start.6
  41.8 3.2 %copy-start.12 = (s32[4]{0:T(128)S(1)}, s32[4]{0:T(128)}, u32[]{:S(2)}) copy-start(s32[4]{0:T(128)} %param.19) | copy-start | bytes 52
  41.9 3.4 %copy-start.13 = (s32[16]{0:T(128)S(1)}, s32[16]{0:T(128)}, u32[]{:S(2)}) copy-start(s32[16]{0:T(128)} %param.20) | copy-start | bytes 196
  47.7 3.4 %copy-start.7 = (f32[384,64]{0,1:T(8,128)}, f32[384,64]{0,1:T(8,128)S(1)}, u32[]{:S(2)}) copy-start(f32[384,64]{0,1:T(8,128)S(1)} %get-tuple-element.71) | copy-start | bytes 294916
  101.8 2.9 %collective-permute-start = (bf16[192,384]{1,0:T(8,128)(2,1)S(1)}, bf16[192,384]{1,0:T(8,128)(2,1)S(1)}, u32[]{:S(2)}, u32[]{:S(2)}) collective-permute-start(bf16[192,384]{1,0:T(8,128)(2,1)S(1)} %constant_dynamic-slice_fusion.1), channel_id=1, source_target_pairs={{0,64},{64,0},{1,65},{65,1},{2,66},{66,2},{3,67},{67,3},{4,68},{68... | collective-permute-start | bytes 442376 | tf_op jit(solution)/shard_map/ppermute | solution.py:393
  137.7 1.8 copy-start.3
  138.9 1.9 copy-start.5
  139.5 2.3 %copy-start.2 = (bf16[384,3072]{1,0:T(8,128)(2,1)S(1)}, bf16[384,3072]{1,0:T(8,128)(2,1)}, u32[]{:S(2)}) copy-start(bf16[384,3072]{1,0:T(8,128)(2,1)} %copy.71) | copy-start | bytes 7077892
  149.2 0.9 copy-start.8
  179.2 2.6 %collective-permute-start.2 = (bf16[192,384]{1,0:T(8,128)(2,1)S(1)}, bf16[192,384]{1,0:T(8,128)(2,1)S(1)}, u32[]{:S(2)}, u32[]{:S(2)}) collective-permute-start(bf16[192,384]{1,0:T(8,128)(2,1)S(1)} %constant_dynamic-slice_fusion), channel_id=1, source_target_pairs={{0,64},{64,0},{1,65},{65,1},{2,66},{66,2},{3,67},{67,3},{4,68},{68... | collective-permute-start | bytes 442376 | tf_op jit(solution)/shard_map/ppermute | solution.py:393
  184.4 17.5 %copy-start.11 = (f32[1,48,64]{2,1,0:T(8,128)S(1)}, f32[1,48,64]{2,1,0:T(8,128)}, u32[]{:S(2)}) copy-start(f32[1,48,64]{2,1,0:T(8,128)} %param.12) | copy-start | bytes 36868
Sparse Core Ops, SparseCore 0:
  10.2 77.9 all-gather.4
  90.3 75.2 all-gather.6

commit v12 on v11

--- a/solution.py
+++ b/solution.py
@@ -94,8 +94,8 @@
 
 
 def attention_kernel(
-    head_dim, fetch_ref, allow_ref, qt_ref, m0_ref, l0_ref, acc0_ref, ks_ref, vs_ref, o_ref,
-    m_sc, l_sc, acc_sc
+    head_dim, fetch_ref, allow_ref, qt_ref, m0_ref, l0_ref, acc0_ref, ks_ref, vs_ref, mine_ref,
+    theirs_ref, m_sc, l_sc, acc_sc
 ):
     slot = pl.program_id(0)
     heads = qt_ref.shape[0]
@@ -128,9 +128,15 @@
 
     @pl.when(slot == pl.num_programs(0) - 1)
     def _finish():
+        first = lax.axis_index("section") == 0
+        half_rows = mine_ref.shape[0]
         for h in range(heads):
             lanes = slice(h * head_dim, (h + 1) * head_dim)
-            o_ref[:, lanes] = (acc_sc[h] / l_sc[h]).T.astype(o_ref.dtype)
+            result = (acc_sc[h] / l_sc[h]).T.astype(mine_ref.dtype)
+            top = result[:half_rows]
+            bottom = result[half_rows:]
+            mine_ref[:, lanes] = jnp.where(first, top, bottom)
+            theirs_ref[:, lanes] = jnp.where(first, bottom, top)
 
 
 def attend(queries, keys_fresh, values_fresh, stale, fetch, allow, head_dim):
@@ -149,7 +155,7 @@
         in_specs=[vmem] * 3,
         out_specs=(vmem,) * 4,
     )(queries, keys_fresh, values_fresh)
-    whole = pl.BlockSpec((rows, features), lambda j, f, a: (0, 0))
+    half = pl.BlockSpec((rows // 2, features), lambda j, f, a: (0, 0))
     qt_spec = pl.BlockSpec((heads, head_dim, rows), lambda j, f, a: (0, 0, 0))
     stat_spec = pl.BlockSpec((heads, 1, rows), lambda j, f, a: (0, 0, 0))
     key_spec = pl.BlockSpec(
@@ -160,12 +166,15 @@
     )
     return pl.pallas_call(
         functools.partial(attention_kernel, head_dim),
-        out_shape=jax.ShapeDtypeStruct((rows, features), jnp.bfloat16),
+        out_shape=(
+            jax.ShapeDtypeStruct((rows // 2, features), jnp.bfloat16),
+            jax.ShapeDtypeStruct((rows // 2, features), jnp.bfloat16),
+        ),
         grid_spec=pltpu.PrefetchScalarGridSpec(
             num_scalar_prefetch=2,
             grid=(slot_total,),
             in_specs=[qt_spec, stat_spec, stat_spec, qt_spec, key_spec, value_spec],
-            out_specs=whole,
+            out_specs=(half, half),
             scratch_shapes=[
                 pltpu.VMEM((heads, 1, rows), jnp.float32),
                 pltpu.VMEM((heads, 1, rows), jnp.float32),
@@ -387,9 +396,7 @@
         attended = attend(
             queries, keys_fresh, values_fresh, stale_layers[layer_idx], fetch, allow, head_dim
         )
-        half_rows = patch_len // section_count
-        mine = lax.dynamic_slice_in_dim(attended, section_index * half_rows, half_rows, 0)
-        theirs = lax.dynamic_slice_in_dim(attended, (1 - section_index) * half_rows, half_rows, 0)
+        mine, theirs = attended
         swapped = lax.ppermute(theirs, "section", perm=[(0, 1), (1, 0)])
         partial = (
             jnp.dot(mine, w_out[layer_idx], preferred_element_type=jnp.float32)

time: 211 us -> 210 us (level)
  the two profiles are of different devices: /device:TPU:8 before, /device:TPU:16 now
where the time goes in v12:
time: 210 us; the launch traced here: 209 us
  Pallas kernels  77.3 us (37%)
  local copies, waits for them, and re-layouts  52.9 us (25%)
  matrix products  28.6 us (14%)
  other arithmetic  23.8 us (11%)
  between operations  16.6 us (8%)
  waiting for transfers between devices  8.96 us (4%)
    pallas_call x2, Pallas kernels, exchange(): pl.pallas_call(functools.partial(exchange_kernel, head_count, own_rows, s...  45.2 us
    dot_general x7, local copies, waits for them, and re-layouts, project(): jnp.dot(normed, weight[:, part, :], preferred_element_type=jnp.float32)  31.5 us
    pallas_call x2, Pallas kernels, attend(): pl.pallas_call(functools.partial(attention_kernel, head_dim), out_shape=(...  25.5 us
    dot_general x6, matrix products, project(): jnp.dot(normed, weight[:, part, :], preferred_element_type=jnp.float32)  17.7 us
    all_gather x2, waiting for transfers between devices, shards(): lax.all_gather(jnp.swapaxes(stale_kv[layer], 0, 1), 'tok', axis=0, tiled=...  8.24 us
    pallas_call x2, Pallas kernels, attend(): pl.pallas_call(functools.partial(fresh_kernel, head_dim), out_shape=(jax....  6.56 us
    squeeze x1, local copies, waits for them, and re-layouts, shards(): w_qkv[layer_idx]  6.09 us
    another operation x4, other arithmetic  5.14 us
  transfers between devices with their start and end apart: 5, of which 1 were waited for; matrix products, arithmetic and copies ran while one was open for 46% of the time, Pallas kernels for 23%

profile of v12, /device:TPU:16, one launch (start us, length us, event | category | flops | bytes accessed | tf_op | source)
XLA Modules:
  0.0 208.6 jit_solution(7829030557826185907)
XLA Ops:
  7.2 2.4 %fusion.33 = (bf16[1,2,1,384,384]{4,3,2,1,0:T(8,128)(2,1)}, bf16[1,2,1,384,384]{4,3,2,1,0:T(8,128)(2,1)}) fusion(bf16[2,2,1,384,384]{4,3,2,1,0:T(8,128)(2,1)} %param.18), kind=kLoop, calls=%fused_computation.113 | loop fusion | bytes 2359296 | tf_op jit(solution)/shard_map/slice | solution.py:380
  10.5 6.1 %slice_bitcast_fusion = (bf16[3072,3,384]{2,0,1:T(8,128)(2,1)S(1)}, bf16[3072,3,384]{2,0,1:T(8,128)(2,1)S(1)}) fusion(bf16[2,3072,3,384]{3,1,2,0:T(8,128)(2,1)} %param.13), kind=kLoop, calls=%fused_computation | loop fusion | bytes 28311552 | tf_op jit(solution)/shard_map/squeeze | solution.py:391
  16.6 5.3 %slice_bitcast_fusion.4 = (bf16[384,3072]{0,1:T(8,128)(2,1)}, bf16[384,3072]{0,1:T(8,128)(2,1)}, bf16[384,3072]{0,1:T(8,128)(2,1)}, bf16[384,3072]{0,1:T(8,128)(...) fusion(bf16[3072,3,384]{2,0,1:T(8,128)(2,1)S(1)} %get-tuple-element.47, ...), kind=kLoop, calls=%fused_computation.26 | loop fusion | bytes 28311552 | tf_op jit(solution)/shard_map/dot_general | solution.py:63
  21.9 4.5 %copy.65 = bf16[384,3072]{1,0:T(8,128)(2,1)} copy(bf16[384,3072]{0,1:T(8,128)(2,1)} %get-tuple-element.92) | data formatting | bytes 4718592 | tf_op jit(solution)/shard_map/dot_general | solution.py:63
  29.3 1.4 multiply_reduce_fusion.3
  32.4 1.4 reshape.472
  33.8 4.3 %copy.66 = bf16[384,3072]{1,0:T(8,128)(2,1)} copy(bf16[384,3072]{0,1:T(8,128)(2,1)} %get-tuple-element.93) | data formatting | bytes 4718592 | tf_op jit(solution)/shard_map/dot_general | solution.py:63
  38.1 3.8 %multiply_reduce_fusion.2 = (f32[384,3]{0,1:T(4,128)S(1)}, f32[384,3,128]{0,2,1:T(8,128)S(1)}) fusion(bf16[384,3072,1]{1,0,2:T(8,128)(2,1)} %copy-done.6, bf16[3,128,3072]{2,1,0:T(8,128)(2,1)} %bitcast.150), kind=kOutput, calls=%fused_computation.54 | convolution fusion | flops 906263424 | bytes 5313024 | tf_op jit(solution)/shard_map/dot_general | solution.py:63
  42.8 2.2 %reshape.473 = f32[384,3,64,2]{0,3,2,1:T(2,128)} reshape(f32[384,3,128]{0,2,1:T(8,128)} %multiply_multiply_fusion.2) | data formatting | bytes 1179648 | tf_op jit(solution)/shard_map/reshape | solution.py:35
  47.7 3.4 %subtract_convert_fusion.2 = (bf16[384,3,64,1]{0,3,2,1:T(2,128)(2,1)S(1)}, bf16[384,3,64,1]{0,3,2,1:T(2,128)(2,1)S(1)}, bf16[384,3,64,1]{0,3,2,1:T(2,128)(2,1)}, bf16[384,3,64,1]{0,3,2,1:T(2,128)(2,1)}) fusion(f32[384,3,64,2]{0,3,2,1:T(2,128)} %reshape.473, f32[384,64]{0,1:T(8,128)S(1)} %get-tuple-element.79, f32[384,64]{0,1:T(8,128)S(1)} %get-tuple-element.78, ...), kind=kLoop, calls=%fused_computation.70 | loop fusion | flops 1179648 | bytes 1966080 | tf_op jit(solution)/shard_map/convert.4
  52.8 1.7 pad_maximum_fusion
  55.5 4.3 %copy.67 = bf16[384,3072]{1,0:T(8,128)(2,1)} copy(bf16[384,3072]{0,1:T(8,128)(2,1)} %get-tuple-element.94) | data formatting | bytes 4718592 | tf_op jit(solution)/shard_map/dot_general | solution.py:63
  59.9 4.0 %convolution_convert_fusion.1 = bf16[384,3,128]{0,2,1:T(8,128)(2,1)S(1)} fusion(bf16[384,3072,1]{1,0,2:T(8,128)(2,1)} %copy-done.6, bf16[3,128,3072]{2,1,0:T(8,128)(2,1)} %bitcast.151), kind=kOutput, calls=%fused_computation.40 | convolution fusion | flops 906117120 | bytes 5013504 | tf_op jit(solution)/shard_map/dot_general | solution.py:63
  65.5 4.5 %copy.73 = bf16[384,3072]{1,0:T(8,128)(2,1)} copy(bf16[384,3072]{0,1:T(8,128)(2,1)} %get-tuple-element.49) | data formatting | bytes 4718592 | tf_op jit(solution)/shard_map/dot_general | solution.py:63
  70.0 4.3 %copy.71 = bf16[384,3072]{1,0:T(8,128)(2,1)} copy(bf16[384,3072]{0,1:T(8,128)(2,1)} %get-tuple-element.51) | data formatting | bytes 4718592 | tf_op jit(solution)/shard_map/dot_general | solution.py:63
  74.4 4.3 %copy.72 = bf16[384,3072]{1,0:T(8,128)(2,1)} copy(bf16[384,3072]{0,1:T(8,128)(2,1)} %get-tuple-element.50) | data formatting | bytes 4718592 | tf_op jit(solution)/shard_map/dot_general | solution.py:63
  80.8 3.3 %shard_map.130 = (bf16[3,128,384]{2,1,0:T(8,128)(2,1)}, f32[3,1,384]{2,1,0:T(1,128)}, f32[3,1,384]{2,1,0:T(1,128)}, f32[3,128,384]{2,1,0:T(8,128)}) custom-call(bf16[384,384]{1,0:T(8,128)(2,1)} %copy.68.q_ref, bf16[384,384]{1,0:T(8,128)(2,1)} %copy.69.kf_ref, bf16[384,384]{1,0:T(8,128)(2,1)} %copy.70.vf_ref), custom_call_target="tpu_custom_call" | custom-call | tf_op jit(solution)/shard_map/pallas_call | solution.py:147
  86.2 1.9 compare_select_fusion.fetch_ref
  88.1 12.8 %shard_map.131 = (bf16[192,384]{1,0:T(8,128)(2,1)}, bf16[192,384]{1,0:T(8,128)(2,1)}) custom-call(s32[7]{0:T(128)} %compare_select_fusion.fetch_ref, s32[7]{0:T(128)} %compare_convert_fusion.allow_ref, bf16[3,128,384]{2,1,0:T(8,128)(2,1)} %get-tuple-element.17.qt_ref, f32[3,1,384]{2,1,0:T(1,128)} %get-tuple-element.18.m0_ref, ...), custom_call_target="tpu_custom_call" | custom-call | tf_op jit(solution)/shard_map/pallas_call | solution.py:167
  101.2 2.5 %fusion.18 = f32[192,3072]{1,0:T(8,128)S(1)} fusion(bf16[192,384]{1,0:T(8,128)(2,1)} %get-tuple-element.21, bf16[2,384,3072]{2,1,0:T(8,128)(2,1)} %param.14), kind=kOutput, calls=%fused_computation.35 | convolution fusion | flops 452984832 | bytes 4866048 | tf_op jit(solution)/shard_map/dot_general | solution.py:402
  103.8 2.5 %fusion.13.part_ref = bf16[192,3072]{1,0:T(8,128)(2,1)S(1)} fusion(f32[192,3072]{1,0:T(8,128)S(1)} %fusion.18, bf16[192,384]{1,0:T(8,128)(2,1)S(1)} %collective-permute-done, bf16[2,384,3072]{2,1,0:T(8,128)(2,1)} %collective-permute-done.1), kind=kOutput, calls=%fused_computation.22 | convolution fusion | flops 454164480 | bytes 6045696 | tf_op jit(solution)/shard_map/dot_general | solution.py:403
  106.3 29.1 %shard_map.132 = (bf16[48,3072]{1,0:T(8,128)(2,1)S(1)}, bf16[2,4,48,3072]{3,2,1,0:T(8,128)(2,1)S(1)}) custom-call(bf16[192,3072]{1,0:T(8,128)(2,1)S(1)} %fusion.13.part_ref, bf16[48,3072]{1,0:T(8,128)(2,1)S(1)} %dynamic-slice_bitcast_fusion.own_ref, f32[1,3072]{1,0:T(1,128)S(1)} %get-tuple-element.71.gate_ref), custom_call_target="tpu_custom_call" | custom-call | tf_op jit(solution)/shard_map/pallas_call | solution.py:322
  138.3 1.4 convolution_convert_fusion
  140.6 3.2 %multiply_reduce_fusion.1 = (f32[384,3]{0,1:T(4,128)S(1)}, f32[384,3,128]{0,2,1:T(8,128)S(1)}) fusion(bf16[384,3072,1]{1,0,2:T(8,128)(2,1)} %bitcast.148, bf16[3,128,3072]{2,1,0:T(8,128)(2,1)S(1)} %bitcast.144), kind=kOutput, calls=%fused_computation.52 | convolution fusion | flops 906263424 | bytes 5313024 | tf_op jit(solution)/shard_map/dot_general | solution.py:63
  144.3 3.9 %multiply_reduce_fusion = (f32[384,3]{0,1:T(4,128)S(1)}, f32[384,3,128]{0,2,1:T(8,128)S(1)}) fusion(bf16[384,3072,1]{1,0,2:T(8,128)(2,1)} %bitcast.149, bf16[3,128,3072]{2,1,0:T(8,128)(2,1)} %bitcast.143), kind=kOutput, calls=%fused_computation.50 | convolution fusion | flops 906263424 | bytes 5313024 | tf_op jit(solution)/shard_map/dot_general | solution.py:63
  149.1 1.6 subtract_convert_fusion
  154.1 3.3 %shard_map.133 = (bf16[3,128,384]{2,1,0:T(8,128)(2,1)}, f32[3,1,384]{2,1,0:T(1,128)}, f32[3,1,384]{2,1,0:T(1,128)}, f32[3,128,384]{2,1,0:T(8,128)}) custom-call(bf16[384,384]{1,0:T(8,128)(2,1)} %copy.74.q_ref, bf16[384,384]{1,0:T(8,128)(2,1)} %copy.75.kf_ref, bf16[384,384]{1,0:T(8,128)(2,1)} %copy.76.vf_ref), custom_call_target="tpu_custom_call" | custom-call | tf_op jit(solution)/shard_map/pallas_call | solution.py:147
  157.4 8.2 %all-gather.7.cloned.1.call-done = bf16[16,2,1,384,384]{4,3,2,1,0:T(8,128)(2,1)} async-done(((bf16[1,2,1,384,384]{4,3,2,1,0:T(8,128)(2,1)}), bf16[16,2,1,384,384]{4,3,2,1,0:T(8,128)(2,1)}) %all-gather.7.cloned.1.call-update) | async-done | bytes 9437200 | tf_op jit(solution)/shard_map/all_gather | solution.py:380
  165.6 12.7 %shard_map.134 = (bf16[192,384]{1,0:T(8,128)(2,1)}, bf16[192,384]{1,0:T(8,128)(2,1)}) custom-call(s32[7]{0:T(128)} %compare_select_fusion.fetch_ref, s32[7]{0:T(128)} %compare_convert_fusion.allow_ref, bf16[3,128,384]{2,1,0:T(8,128)(2,1)} %get-tuple-element.25.qt_ref, f32[3,1,384]{2,1,0:T(1,128)} %get-tuple-element.26.m0_ref, ...), custom_call_target="tpu_custom_call" | custom-call | tf_op jit(solution)/shard_map/pallas_call | solution.py:167
  178.3 2.5 %fusion.16 = f32[192,3072]{1,0:T(8,128)S(1)} fusion(bf16[192,384]{1,0:T(8,128)(2,1)} %get-tuple-element.29, bf16[2,384,3072]{2,1,0:T(8,128)(2,1)} %param.14), kind=kOutput, calls=%fused_computation.33 | convolution fusion | flops 452984832 | bytes 4866048 | tf_op jit(solution)/shard_map/dot_general | solution.py:402
  180.9 2.4 %fusion.14.part_ref = bf16[192,3072]{1,0:T(8,128)(2,1)S(1)} fusion(f32[192,3072]{1,0:T(8,128)S(1)} %fusion.16, bf16[192,384]{1,0:T(8,128)(2,1)S(1)} %collective-permute-done.2, bf16[2,384,3072]{2,1,0:T(8,128)(2,1)} %collective-permute-done.1), kind=kOutput, calls=%fused_computation.23 | convolution fusion | flops 454164480 | bytes 6045696 | tf_op jit(solution)/shard_map/dot_general | solution.py:403
  183.3 16.1 %shard_map.135 = f32[48,3072]{1,0:T(8,128)S(1)} custom-call(bf16[192,3072]{1,0:T(8,128)(2,1)S(1)} %fusion.14.part_ref, bf16[48,3072]{1,0:T(8,128)(2,1)S(1)} %get-tuple-element.23.own_ref, f32[1,3072]{1,0:T(1,128)S(1)} %get-tuple-element.70.gate_ref), custom_call_target="tpu_custom_call" | custom-call | tf_op jit(solution)/shard_map/pallas_call | solution.py:322
  (99 shorter events, 26.7 us)
Async XLA Ops:
  7.2 193.6 %copy-start = (bf16[3072,64]{0,1:T(8,128)(2,1)S(1)}, bf16[3072,64]{0,1:T(8,128)(2,1)}, u32[]{:S(2)}) copy-start(bf16[3072,64]{0,1:T(8,128)(2,1)} %param.15) | copy-start | bytes 1179652
  7.2 80.9 %all-gather.5.cloned.1.call-start = ((), (), s32[]{:S(2)}) async-start(), calls=%async_computation | async-start | bytes 10027008 | tf_op jit(solution)/shard_map/all_gather | solution.py:380
  9.7 155.9 %all-gather.7.cloned.1.call-start = ((), (), s32[]{:S(2)}) async-start(), calls=%async_computation.1 | async-start | bytes 10027008 | tf_op jit(solution)/shard_map/all_gather | solution.py:380
  10.4 93.3 %collective-permute-start.1 = (bf16[2,384,3072]{2,1,0:T(8,128)(2,1)}, bf16[2,384,3072]{2,1,0:T(8,128)(2,1)}, u32[]{:S(2)}, u32[]{:S(2)}) collective-permute-start(bf16[2,384,3072]{2,1,0:T(8,128)(2,1)} %param.14), channel_id=1, source_target_pairs={{0,64},{64,0},{1,65},{65,1},{2,66},{66,2},{3,67},{67,3},{4,68},{68... | collective-permute-start | bytes 14155784 | tf_op jit(solution)/shard_map/ppermute | solution.py:384
  21.9 4.5 %copy-start.10 = (f32[2,2,128]{2,1,0:T(2,128)S(1)}, f32[2,2,128]{2,1,0:T(2,128)}, u32[]{:S(2)}) copy-start(f32[2,2,128]{2,1,0:T(2,128)} %param.16) | copy-start | bytes 6148
  21.9 4.5 %copy-start.1 = (bf16[1,384,3072]{2,1,0:T(8,128)(2,1)S(1)}, bf16[1,384,3072]{2,1,0:T(8,128)(2,1)}, u32[]{:S(2)}) copy-start(bf16[1,384,3072]{2,1,0:T(8,128)(2,1)} %param.11) | copy-start | bytes 7077892
  26.4 1.2 copy-start.9
  27.7 1.7 copy-start.4
  29.0 1.8 copy-start.6
  41.9 3.2 %copy-start.12 = (s32[4]{0:T(128)S(1)}, s32[4]{0:T(128)}, u32[]{:S(2)}) copy-start(s32[4]{0:T(128)} %param.19) | copy-start | bytes 52
  41.9 3.4 %copy-start.13 = (s32[16]{0:T(128)S(1)}, s32[16]{0:T(128)}, u32[]{:S(2)}) copy-start(s32[16]{0:T(128)} %param.20) | copy-start | bytes 196
  47.7 3.4 %copy-start.7 = (f32[384,64]{0,1:T(8,128)}, f32[384,64]{0,1:T(8,128)S(1)}, u32[]{:S(2)}) copy-start(f32[384,64]{0,1:T(8,128)S(1)} %get-tuple-element.79) | copy-start | bytes 294916
  100.8 2.9 %collective-permute-start = (bf16[192,384]{1,0:T(8,128)(2,1)}, bf16[192,384]{1,0:T(8,128)(2,1)S(1)}, u32[]{:S(2)}, u32[]{:S(2)}) collective-permute-start(bf16[192,384]{1,0:T(8,128)(2,1)} %get-tuple-element.22), channel_id=1, source_target_pairs={{0,64},{64,0},{1,65},{65,1},{2,66},{66,2},{3,67},{67,3},{4,68},{68... | collective-permute-start | bytes 442376 | tf_op jit(solution)/shard_map/ppermute | solution.py:400
  136.6 1.7 copy-start.3
  137.8 1.9 copy-start.5
  138.3 2.3 %copy-start.2 = (bf16[384,3072]{1,0:T(8,128)(2,1)S(1)}, bf16[384,3072]{1,0:T(8,128)(2,1)}, u32[]{:S(2)}) copy-start(bf16[384,3072]{1,0:T(8,128)(2,1)} %copy.71) | copy-start | bytes 7077892
  148.2 0.9 copy-start.8
  178.3 2.5 %collective-permute-start.2 = (bf16[192,384]{1,0:T(8,128)(2,1)}, bf16[192,384]{1,0:T(8,128)(2,1)S(1)}, u32[]{:S(2)}, u32[]{:S(2)}) collective-permute-start(bf16[192,384]{1,0:T(8,128)(2,1)} %get-tuple-element.30), channel_id=1, source_target_pairs={{0,64},{64,0},{1,65},{65,1},{2,66},{66,2},{3,67},{67,3},{4,68},{68... | collective-permute-start | bytes 442376 | tf_op jit(solution)/shard_map/ppermute | solution.py:400
  183.3 17.5 %copy-start.11 = (f32[1,48,64]{2,1,0:T(8,128)S(1)}, f32[1,48,64]{2,1,0:T(8,128)}, u32[]{:S(2)}) copy-start(f32[1,48,64]{2,1,0:T(8,128)} %param.12) | copy-start | bytes 36868
Sparse Core Ops, SparseCore 0:
  10.2 77.8 all-gather.4
  90.2 75.3 all-gather.6

commit v13 on v12

--- a/solution.py
+++ b/solution.py
@@ -206,12 +206,11 @@
         return pl.ds(pl.multiple_of(block * own_rows + offset, 16), count)
 
     barrier = pltpu.get_barrier_semaphore()
-    pl.semaphore_signal(barrier, inc=1, device_id=(other, head, tok), device_id_type=mesh_ids)
-    for h in range(head_count):
-        @pl.when(h != head)
-        def _greet():
-            pl.semaphore_signal(barrier, inc=1, device_id=(section, h, tok), device_id_type=mesh_ids)
-    pl.semaphore_wait(barrier, head_count)
+    if gather:
+        pl.semaphore_signal(barrier, inc=1, device_id=(other, head, tok), device_id_type=mesh_ids)
+    for neighbour in (up, down):
+        pl.semaphore_signal(barrier, inc=1, device_id=(section, neighbour, tok), device_id_type=mesh_ids)
+    pl.semaphore_wait(barrier, 3 if gather else 2)
 
     def ring(kind, src, dst, target, send_sem, recv_sem):
         return pltpu.make_async_remote_copy(

time: 210 us -> 209 us (level)
  the two profiles are of different devices: /device:TPU:16 before, /device:TPU:8 now
where the time goes in v13:
time: 209 us; the launch traced here: 208 us
  Pallas kernels  75.8 us (36%)
  local copies, waits for them, and re-layouts  52.9 us (25%)
  matrix products  28.5 us (14%)
  other arithmetic  23.8 us (11%)
  between operations  16.6 us (8%)
  waiting for transfers between devices  9.95 us (5%)
    pallas_call x2, Pallas kernels, exchange(): pl.pallas_call(functools.partial(exchange_kernel, head_count, own_rows, s...  43.8 us
    dot_general x7, local copies, waits for them, and re-layouts, project(): jnp.dot(normed, weight[:, part, :], preferred_element_type=jnp.float32)  31.5 us
    pallas_call x2, Pallas kernels, attend(): pl.pallas_call(functools.partial(attention_kernel, head_dim), out_shape=(...  25.5 us
    dot_general x6, matrix products, project(): jnp.dot(normed, weight[:, part, :], preferred_element_type=jnp.float32)  17.6 us
    all_gather x2, waiting for transfers between devices, shards(): lax.all_gather(jnp.swapaxes(stale_kv[layer], 0, 1), 'tok', axis=0, tiled=...  9.23 us
    pallas_call x2, Pallas kernels, attend(): pl.pallas_call(functools.partial(fresh_kernel, head_dim), out_shape=(jax....  6.57 us
    squeeze x1, local copies, waits for them, and re-layouts, shards(): w_qkv[layer_idx]  6.09 us
    another operation x4, other arithmetic  5.14 us
  transfers between devices with their start and end apart: 5, of which 2 were waited for; matrix products, arithmetic and copies ran while one was open for 47% of the time, Pallas kernels for 23%

profile of v13, /device:TPU:8, one launch (start us, length us, event | category | flops | bytes accessed | tf_op | source)
XLA Modules:
  0.0 208.0 jit_solution(4992222287352359962)
XLA Ops:
  7.2 2.4 %fusion.33 = (bf16[1,2,1,384,384]{4,3,2,1,0:T(8,128)(2,1)}, bf16[1,2,1,384,384]{4,3,2,1,0:T(8,128)(2,1)}) fusion(bf16[2,2,1,384,384]{4,3,2,1,0:T(8,128)(2,1)} %param.18), kind=kLoop, calls=%fused_computation.113 | loop fusion | bytes 2359296 | tf_op jit(solution)/shard_map/slice | solution.py:379
  10.5 6.1 %slice_bitcast_fusion = (bf16[3072,3,384]{2,0,1:T(8,128)(2,1)S(1)}, bf16[3072,3,384]{2,0,1:T(8,128)(2,1)S(1)}) fusion(bf16[2,3072,3,384]{3,1,2,0:T(8,128)(2,1)} %param.13), kind=kLoop, calls=%fused_computation | loop fusion | bytes 28311552 | tf_op jit(solution)/shard_map/squeeze | solution.py:390
  16.6 5.3 %slice_bitcast_fusion.4 = (bf16[384,3072]{0,1:T(8,128)(2,1)}, bf16[384,3072]{0,1:T(8,128)(2,1)}, bf16[384,3072]{0,1:T(8,128)(2,1)}, bf16[384,3072]{0,1:T(8,128)(...) fusion(bf16[3072,3,384]{2,0,1:T(8,128)(2,1)S(1)} %get-tuple-element.47, ...), kind=kLoop, calls=%fused_computation.26 | loop fusion | bytes 28311552 | tf_op jit(solution)/shard_map/dot_general | solution.py:63
  21.9 4.5 %copy.65 = bf16[384,3072]{1,0:T(8,128)(2,1)} copy(bf16[384,3072]{0,1:T(8,128)(2,1)} %get-tuple-element.92) | data formatting | bytes 4718592 | tf_op jit(solution)/shard_map/dot_general | solution.py:63
  29.3 1.4 multiply_reduce_fusion.3
  32.4 1.4 reshape.472
  33.8 4.3 %copy.66 = bf16[384,3072]{1,0:T(8,128)(2,1)} copy(bf16[384,3072]{0,1:T(8,128)(2,1)} %get-tuple-element.93) | data formatting | bytes 4718592 | tf_op jit(solution)/shard_map/dot_general | solution.py:63
  38.1 3.8 %multiply_reduce_fusion.2 = (f32[384,3]{0,1:T(4,128)S(1)}, f32[384,3,128]{0,2,1:T(8,128)S(1)}) fusion(bf16[384,3072,1]{1,0,2:T(8,128)(2,1)} %copy-done.6, bf16[3,128,3072]{2,1,0:T(8,128)(2,1)} %bitcast.150), kind=kOutput, calls=%fused_computation.54 | convolution fusion | flops 906263424 | bytes 5313024 | tf_op jit(solution)/shard_map/dot_general | solution.py:63
  42.8 2.2 %reshape.473 = f32[384,3,64,2]{0,3,2,1:T(2,128)} reshape(f32[384,3,128]{0,2,1:T(8,128)} %multiply_multiply_fusion.2) | data formatting | bytes 1179648 | tf_op jit(solution)/shard_map/reshape | solution.py:35
  47.7 3.4 %subtract_convert_fusion.2 = (bf16[384,3,64,1]{0,3,2,1:T(2,128)(2,1)S(1)}, bf16[384,3,64,1]{0,3,2,1:T(2,128)(2,1)S(1)}, bf16[384,3,64,1]{0,3,2,1:T(2,128)(2,1)}, bf16[384,3,64,1]{0,3,2,1:T(2,128)(2,1)}) fusion(f32[384,3,64,2]{0,3,2,1:T(2,128)} %reshape.473, f32[384,64]{0,1:T(8,128)S(1)} %get-tuple-element.79, f32[384,64]{0,1:T(8,128)S(1)} %get-tuple-element.78, ...), kind=kLoop, calls=%fused_computation.70 | loop fusion | flops 1179648 | bytes 1966080 | tf_op jit(solution)/shard_map/convert.4
  52.8 1.7 pad_maximum_fusion
  55.5 4.3 %copy.67 = bf16[384,3072]{1,0:T(8,128)(2,1)} copy(bf16[384,3072]{0,1:T(8,128)(2,1)} %get-tuple-element.94) | data formatting | bytes 4718592 | tf_op jit(solution)/shard_map/dot_general | solution.py:63
  59.9 4.0 %convolution_convert_fusion.1 = bf16[384,3,128]{0,2,1:T(8,128)(2,1)S(1)} fusion(bf16[384,3072,1]{1,0,2:T(8,128)(2,1)} %copy-done.6, bf16[3,128,3072]{2,1,0:T(8,128)(2,1)} %bitcast.151), kind=kOutput, calls=%fused_computation.40 | convolution fusion | flops 906117120 | bytes 5013504 | tf_op jit(solution)/shard_map/dot_general | solution.py:63
  65.6 4.5 %copy.73 = bf16[384,3072]{1,0:T(8,128)(2,1)} copy(bf16[384,3072]{0,1:T(8,128)(2,1)} %get-tuple-element.49) | data formatting | bytes 4718592 | tf_op jit(solution)/shard_map/dot_general | solution.py:63
  70.1 4.3 %copy.71 = bf16[384,3072]{1,0:T(8,128)(2,1)} copy(bf16[384,3072]{0,1:T(8,128)(2,1)} %get-tuple-element.51) | data formatting | bytes 4718592 | tf_op jit(solution)/shard_map/dot_general | solution.py:63
  74.4 4.3 %copy.72 = bf16[384,3072]{1,0:T(8,128)(2,1)} copy(bf16[384,3072]{0,1:T(8,128)(2,1)} %get-tuple-element.50) | data formatting | bytes 4718592 | tf_op jit(solution)/shard_map/dot_general | solution.py:63
  80.8 3.3 %shard_map.130 = (bf16[3,128,384]{2,1,0:T(8,128)(2,1)}, f32[3,1,384]{2,1,0:T(1,128)}, f32[3,1,384]{2,1,0:T(1,128)}, f32[3,128,384]{2,1,0:T(8,128)}) custom-call(bf16[384,384]{1,0:T(8,128)(2,1)} %copy.68.q_ref, bf16[384,384]{1,0:T(8,128)(2,1)} %copy.69.kf_ref, bf16[384,384]{1,0:T(8,128)(2,1)} %copy.70.vf_ref), custom_call_target="tpu_custom_call" | custom-call | tf_op jit(solution)/shard_map/pallas_call | solution.py:147
  86.2 1.9 compare_select_fusion.fetch_ref
  88.2 12.7 %shard_map.131 = (bf16[192,384]{1,0:T(8,128)(2,1)}, bf16[192,384]{1,0:T(8,128)(2,1)}) custom-call(s32[7]{0:T(128)} %compare_select_fusion.fetch_ref, s32[7]{0:T(128)} %compare_convert_fusion.allow_ref, bf16[3,128,384]{2,1,0:T(8,128)(2,1)} %get-tuple-element.17.qt_ref, f32[3,1,384]{2,1,0:T(1,128)} %get-tuple-element.18.m0_ref, ...), custom_call_target="tpu_custom_call" | custom-call | tf_op jit(solution)/shard_map/pallas_call | solution.py:167
  101.2 2.5 %fusion.18 = f32[192,3072]{1,0:T(8,128)S(1)} fusion(bf16[192,384]{1,0:T(8,128)(2,1)} %get-tuple-element.21, bf16[2,384,3072]{2,1,0:T(8,128)(2,1)} %param.14), kind=kOutput, calls=%fused_computation.35 | convolution fusion | flops 452984832 | bytes 4866048 | tf_op jit(solution)/shard_map/dot_general | solution.py:401
  103.8 2.5 %fusion.13.part_ref = bf16[192,3072]{1,0:T(8,128)(2,1)S(1)} fusion(f32[192,3072]{1,0:T(8,128)S(1)} %fusion.18, bf16[192,384]{1,0:T(8,128)(2,1)S(1)} %collective-permute-done, bf16[2,384,3072]{2,1,0:T(8,128)(2,1)} %collective-permute-done.1), kind=kOutput, calls=%fused_computation.22 | convolution fusion | flops 454164480 | bytes 6045696 | tf_op jit(solution)/shard_map/dot_general | solution.py:402
  106.3 28.3 %shard_map.132 = (bf16[48,3072]{1,0:T(8,128)(2,1)S(1)}, bf16[2,4,48,3072]{3,2,1,0:T(8,128)(2,1)S(1)}) custom-call(bf16[192,3072]{1,0:T(8,128)(2,1)S(1)} %fusion.13.part_ref, bf16[48,3072]{1,0:T(8,128)(2,1)S(1)} %dynamic-slice_bitcast_fusion.own_ref, f32[1,3072]{1,0:T(1,128)S(1)} %get-tuple-element.71.gate_ref), custom_call_target="tpu_custom_call" | custom-call | tf_op jit(solution)/shard_map/pallas_call | solution.py:321
  137.5 1.4 convolution_convert_fusion
  139.8 3.1 %multiply_reduce_fusion.1 = (f32[384,3]{0,1:T(4,128)S(1)}, f32[384,3,128]{0,2,1:T(8,128)S(1)}) fusion(bf16[384,3072,1]{1,0,2:T(8,128)(2,1)} %bitcast.148, bf16[3,128,3072]{2,1,0:T(8,128)(2,1)S(1)} %bitcast.144), kind=kOutput, calls=%fused_computation.52 | convolution fusion | flops 906263424 | bytes 5313024 | tf_op jit(solution)/shard_map/dot_general | solution.py:63
  143.4 4.0 %multiply_reduce_fusion = (f32[384,3]{0,1:T(4,128)S(1)}, f32[384,3,128]{0,2,1:T(8,128)S(1)}) fusion(bf16[384,3072,1]{1,0,2:T(8,128)(2,1)} %bitcast.149, bf16[3,128,3072]{2,1,0:T(8,128)(2,1)} %bitcast.143), kind=kOutput, calls=%fused_computation.50 | convolution fusion | flops 906263424 | bytes 5313024 | tf_op jit(solution)/shard_map/dot_general | solution.py:63
  148.2 1.6 subtract_convert_fusion
  153.2 3.3 %shard_map.133 = (bf16[3,128,384]{2,1,0:T(8,128)(2,1)}, f32[3,1,384]{2,1,0:T(1,128)}, f32[3,1,384]{2,1,0:T(1,128)}, f32[3,128,384]{2,1,0:T(8,128)}) custom-call(bf16[384,384]{1,0:T(8,128)(2,1)} %copy.74.q_ref, bf16[384,384]{1,0:T(8,128)(2,1)} %copy.75.kf_ref, bf16[384,384]{1,0:T(8,128)(2,1)} %copy.76.vf_ref), custom_call_target="tpu_custom_call" | custom-call | tf_op jit(solution)/shard_map/pallas_call | solution.py:147
  156.5 9.2 %all-gather.7.cloned.1.call-done = bf16[16,2,1,384,384]{4,3,2,1,0:T(8,128)(2,1)} async-done(((bf16[1,2,1,384,384]{4,3,2,1,0:T(8,128)(2,1)}), bf16[16,2,1,384,384]{4,3,2,1,0:T(8,128)(2,1)}) %all-gather.7.cloned.1.call-update) | async-done | bytes 9437200 | tf_op jit(solution)/shard_map/all_gather | solution.py:379
  165.7 12.7 %shard_map.134 = (bf16[192,384]{1,0:T(8,128)(2,1)}, bf16[192,384]{1,0:T(8,128)(2,1)}) custom-call(s32[7]{0:T(128)} %compare_select_fusion.fetch_ref, s32[7]{0:T(128)} %compare_convert_fusion.allow_ref, bf16[3,128,384]{2,1,0:T(8,128)(2,1)} %get-tuple-element.25.qt_ref, f32[3,1,384]{2,1,0:T(1,128)} %get-tuple-element.26.m0_ref, ...), custom_call_target="tpu_custom_call" | custom-call | tf_op jit(solution)/shard_map/pallas_call | solution.py:167
  178.4 2.5 %fusion.16 = f32[192,3072]{1,0:T(8,128)S(1)} fusion(bf16[192,384]{1,0:T(8,128)(2,1)} %get-tuple-element.29, bf16[2,384,3072]{2,1,0:T(8,128)(2,1)} %param.14), kind=kOutput, calls=%fused_computation.33 | convolution fusion | flops 452984832 | bytes 4866048 | tf_op jit(solution)/shard_map/dot_general | solution.py:401
  181.0 2.4 %fusion.14.part_ref = bf16[192,3072]{1,0:T(8,128)(2,1)S(1)} fusion(f32[192,3072]{1,0:T(8,128)S(1)} %fusion.16, bf16[192,384]{1,0:T(8,128)(2,1)S(1)} %collective-permute-done.2, bf16[2,384,3072]{2,1,0:T(8,128)(2,1)} %collective-permute-done.1), kind=kOutput, calls=%fused_computation.23 | convolution fusion | flops 454164480 | bytes 6045696 | tf_op jit(solution)/shard_map/dot_general | solution.py:402
  183.4 15.4 %shard_map.135 = f32[48,3072]{1,0:T(8,128)S(1)} custom-call(bf16[192,3072]{1,0:T(8,128)(2,1)S(1)} %fusion.14.part_ref, bf16[48,3072]{1,0:T(8,128)(2,1)S(1)} %get-tuple-element.23.own_ref, f32[1,3072]{1,0:T(1,128)S(1)} %get-tuple-element.70.gate_ref), custom_call_target="tpu_custom_call" | custom-call | tf_op jit(solution)/shard_map/pallas_call | solution.py:321
  (99 shorter events, 26.7 us)
Async XLA Ops:
  7.2 193.1 %copy-start = (bf16[3072,64]{0,1:T(8,128)(2,1)S(1)}, bf16[3072,64]{0,1:T(8,128)(2,1)}, u32[]{:S(2)}) copy-start(bf16[3072,64]{0,1:T(8,128)(2,1)} %param.15) | copy-start | bytes 1179652
  7.2 81.0 %all-gather.5.cloned.1.call-start = ((), (), s32[]{:S(2)}) async-start(), calls=%async_computation | async-start | bytes 10027008 | tf_op jit(solution)/shard_map/all_gather | solution.py:379
  9.7 156.0 %all-gather.7.cloned.1.call-start = ((), (), s32[]{:S(2)}) async-start(), calls=%async_computation.1 | async-start | bytes 10027008 | tf_op jit(solution)/shard_map/all_gather | solution.py:379
  10.4 93.3 %collective-permute-start.1 = (bf16[2,384,3072]{2,1,0:T(8,128)(2,1)}, bf16[2,384,3072]{2,1,0:T(8,128)(2,1)}, u32[]{:S(2)}, u32[]{:S(2)}) collective-permute-start(bf16[2,384,3072]{2,1,0:T(8,128)(2,1)} %param.14), channel_id=1, source_target_pairs={{0,64},{64,0},{1,65},{65,1},{2,66},{66,2},{3,67},{67,3},{4,68},{68... | collective-permute-start | bytes 14155784 | tf_op jit(solution)/shard_map/ppermute | solution.py:383
  21.9 4.5 %copy-start.10 = (f32[2,2,128]{2,1,0:T(2,128)S(1)}, f32[2,2,128]{2,1,0:T(2,128)}, u32[]{:S(2)}) copy-start(f32[2,2,128]{2,1,0:T(2,128)} %param.16) | copy-start | bytes 6148
  21.9 4.5 %copy-start.1 = (bf16[1,384,3072]{2,1,0:T(8,128)(2,1)S(1)}, bf16[1,384,3072]{2,1,0:T(8,128)(2,1)}, u32[]{:S(2)}) copy-start(bf16[1,384,3072]{2,1,0:T(8,128)(2,1)} %param.11) | copy-start | bytes 7077892
  26.4 1.2 copy-start.9
  27.7 1.7 copy-start.4
  28.9 1.8 copy-start.6
  41.9 3.2 %copy-start.12 = (s32[4]{0:T(128)S(1)}, s32[4]{0:T(128)}, u32[]{:S(2)}) copy-start(s32[4]{0:T(128)} %param.19) | copy-start | bytes 52
  41.9 3.4 %copy-start.13 = (s32[16]{0:T(128)S(1)}, s32[16]{0:T(128)}, u32[]{:S(2)}) copy-start(s32[16]{0:T(128)} %param.20) | copy-start | bytes 196
  47.7 3.4 %copy-start.7 = (f32[384,64]{0,1:T(8,128)}, f32[384,64]{0,1:T(8,128)S(1)}, u32[]{:S(2)}) copy-start(f32[384,64]{0,1:T(8,128)S(1)} %get-tuple-element.79) | copy-start | bytes 294916
  100.9 2.9 %collective-permute-start = (bf16[192,384]{1,0:T(8,128)(2,1)}, bf16[192,384]{1,0:T(8,128)(2,1)S(1)}, u32[]{:S(2)}, u32[]{:S(2)}) collective-permute-start(bf16[192,384]{1,0:T(8,128)(2,1)} %get-tuple-element.22), channel_id=1, source_target_pairs={{0,64},{64,0},{1,65},{65,1},{2,66},{66,2},{3,67},{67,3},{4,68},{68... | collective-permute-start | bytes 442376 | tf_op jit(solution)/shard_map/ppermute | solution.py:399
  135.8 1.7 copy-start.3
  137.0 1.9 copy-start.5
  137.5 2.3 %copy-start.2 = (bf16[384,3072]{1,0:T(8,128)(2,1)S(1)}, bf16[384,3072]{1,0:T(8,128)(2,1)}, u32[]{:S(2)}) copy-start(bf16[384,3072]{1,0:T(8,128)(2,1)} %copy.71) | copy-start | bytes 7077892
  147.3 0.9 copy-start.8
  178.4 2.5 %collective-permute-start.2 = (bf16[192,384]{1,0:T(8,128)(2,1)}, bf16[192,384]{1,0:T(8,128)(2,1)S(1)}, u32[]{:S(2)}, u32[]{:S(2)}) collective-permute-start(bf16[192,384]{1,0:T(8,128)(2,1)} %get-tuple-element.30), channel_id=1, source_target_pairs={{0,64},{64,0},{1,65},{65,1},{2,66},{66,2},{3,67},{67,3},{4,68},{68... | collective-permute-start | bytes 442376 | tf_op jit(solution)/shard_map/ppermute | solution.py:399
  183.4 16.8 %copy-start.11 = (f32[1,48,64]{2,1,0:T(8,128)S(1)}, f32[1,48,64]{2,1,0:T(8,128)}, u32[]{:S(2)}) copy-start(f32[1,48,64]{2,1,0:T(8,128)} %param.12) | copy-start | bytes 36868
Sparse Core Ops, SparseCore 0:
  10.2 77.9 all-gather.4
  90.3 75.3 all-gather.6

commit v14 on v13

--- a/solution.py
+++ b/solution.py
@@ -190,7 +190,8 @@
         (out_ref, full_ref, land_a, land_b, sums_a, sums_b, acc,
          r_send, r_recv, a_send, a_recv, g2_send, g2_recv) = rest
     else:
-        (out_ref, land_a, land_b, sums_a, sums_b, acc, r_send, r_recv) = rest
+        (wf_ref, latent_ref, levels_ref, out_ref, next_ref, denoised_ref,
+         land_a, land_b, sums_a, sums_b, acc, r_send, r_recv) = rest
     mesh_ids = pl.DeviceIdType.MESH
     section = lax.axis_index("section")
     head = lax.axis_index("head")
@@ -253,7 +254,14 @@
     acc[low, :] += land_a[1].astype(jnp.float32) + land_a[2].astype(jnp.float32)
     acc[high, :] += land_b[1].astype(jnp.float32) + land_b[2].astype(jnp.float32)
     if not gather:
-        out_ref[...] = acc[...]
+        final = (own_ref[...].astype(jnp.float32) + gate_ref[...] * acc[...]).astype(out_ref.dtype)
+        out_ref[...] = final
+        normed = layer_norm(final.astype(jnp.float32)).astype(jnp.bfloat16)
+        velocity = jnp.dot(normed, wf_ref[...], preferred_element_type=jnp.float32)
+        level_now = levels_ref[:, 0:1]
+        level_step = levels_ref[:, 1:2]
+        next_ref[...] = latent_ref[...] + level_step * velocity
+        denoised_ref[...] = latent_ref[...] - level_now * velocity
         return
     result = (own_ref[...].astype(jnp.float32) + gate_ref[...] * acc[...]).astype(full_ref.dtype)
     full_ref[section, head] = result
@@ -295,7 +303,7 @@
     pass_copy(opposite).wait()
 
 
-def exchange(partial, own_input, gate, layer_idx, gather, head_count, own_rows):
+def exchange(partial, own_input, gate, layer_idx, gather, head_count, own_rows, tail=()):
     rows, width = partial.shape
     split = (own_rows * 2 // 3) // 16 * 16
     vmem = pl.BlockSpec(memory_space=pltpu.VMEM)
@@ -316,18 +324,23 @@
         out_specs = (vmem, vmem)
         scratch += [pltpu.SemaphoreType.DMA((head_count,))] * 4
     else:
-        out_shape = jax.ShapeDtypeStruct((own_rows, width), jnp.float32)
-        out_specs = vmem
+        latent_width = tail[1].shape[1]
+        out_shape = (
+            jax.ShapeDtypeStruct((own_rows, width), jnp.bfloat16),
+            jax.ShapeDtypeStruct((own_rows, latent_width), jnp.float32),
+            jax.ShapeDtypeStruct((own_rows, latent_width), jnp.float32),
+        )
+        out_specs = (vmem, vmem, vmem)
     return pl.pallas_call(
         functools.partial(exchange_kernel, head_count, own_rows, split, gather),
         out_shape=out_shape,
-        in_specs=[vmem, vmem, vmem],
+        in_specs=[vmem] * (3 + len(tail)),
         out_specs=out_specs,
         scratch_shapes=scratch,
         compiler_params=pltpu.CompilerParams(
             collective_id=layer_idx, has_side_effects=True, vmem_limit_bytes=48 * 1024 * 1024
         ),
-    )(partial, own_input, gate.reshape(1, width))
+    )(partial, own_input, gate.reshape(1, width), *tail)
 
 
 def noise_level(position):
@@ -408,17 +421,17 @@
             )
             current_full = gathered.reshape(patch_len, width)
         else:
-            summed = exchange(partial, own_input, gate, layer_idx, False, head_count, own_rows)
-            own_out = (own_input.astype(jnp.float32) + gate * summed).astype(jnp.bfloat16)
+            level_now = noise_level(step_index[0])
+            level_next = noise_level(step_index[0] + 1)
+            levels = jnp.stack([level_now, level_next - level_now]).reshape(1, 2)
+            own_out, latent_next, denoised = exchange(
+                partial, own_input, gate, layer_idx, False, head_count, own_rows,
+                tail=(w_final, latent[0], levels),
+            )
         own_input = own_out
         outputs.append(own_out)
-    last_own = outputs[-1]
     layer_out = jnp.stack(outputs)[:, None]
-    normed = layer_norm(last_own.astype(jnp.float32)).astype(jnp.bfloat16)
-    velocity = jnp.dot(normed, w_final, preferred_element_type=jnp.float32)[None]
-    level_now = noise_level(step_index[0])
-    level_next = noise_level(step_index[0] + 1)
-    return (layer_out, latent + (level_next - level_now) * velocity, latent - level_now * velocity)
+    return (layer_out, latent_next[None], denoised[None])
 
 
 def solution(mesh):

time: 209 us -> 209 us (level)
  the two profiles are of different devices: /device:TPU:8 before, /device:TPU:32 now
where the time goes in v14:
time: 209 us; the launch traced here: 208 us
  Pallas kernels  76.6 us (37%)
  local copies, waits for them, and re-layouts  48.6 us (23%)
  matrix products  28.5 us (14%)
  other arithmetic  21.2 us (10%)
  between operations  16.5 us (8%)
  waiting for transfers between devices  16.2 us (8%)
    pallas_call x2, Pallas kernels, exchange(): pl.pallas_call(functools.partial(exchange_kernel, head_count, own_rows, s...  44.6 us
    pallas_call x2, Pallas kernels, attend(): pl.pallas_call(functools.partial(attention_kernel, head_dim), out_shape=(...  25.5 us
    dot_general x7, local copies, waits for them, and re-layouts, project(): jnp.dot(normed, weight[:, part, :], preferred_element_type=jnp.float32)  24.7 us
    dot_general x6, matrix products, project(): jnp.dot(normed, weight[:, part, :], preferred_element_type=jnp.float32)  18.4 us
    all_gather x2, waiting for transfers between devices, shards(): lax.all_gather(jnp.swapaxes(stale_kv[layer], 0, 1), 'tok', axis=0, tiled=...  15.5 us
    pallas_call x2, Pallas kernels, attend(): pl.pallas_call(functools.partial(fresh_kernel, head_dim), out_shape=(jax....  6.54 us
    squeeze x1, local copies, waits for them, and re-layouts, shards(): w_qkv[layer_idx]  6.09 us
    dot_general x2, matrix products, shards(): jnp.dot(mine, w_out[layer_idx], preferred_element_type=jnp.float32)  5.22 us
  transfers between devices with their start and end apart: 5, of which 2 were waited for; matrix products, arithmetic and copies ran while one was open for 43% of the time, Pallas kernels for 23%

profile of v14, /device:TPU:32, one launch (start us, length us, event | category | flops | bytes accessed | tf_op | source)
XLA Modules:
  0.0 207.9 jit_solution(8145493559709208684)
XLA Ops:
  7.2 2.4 %fusion.25 = (bf16[1,2,1,384,384]{4,3,2,1,0:T(8,128)(2,1)}, bf16[1,2,1,384,384]{4,3,2,1,0:T(8,128)(2,1)}) fusion(bf16[2,2,1,384,384]{4,3,2,1,0:T(8,128)(2,1)} %param.18), kind=kLoop, calls=%fused_computation.100 | loop fusion | bytes 2359296 | tf_op jit(solution)/shard_map/slice | solution.py:392
  11.1 6.1 %slice_bitcast_fusion = (bf16[3072,3,384]{2,0,1:T(8,128)(2,1)S(1)}, bf16[3072,3,384]{2,0,1:T(8,128)(2,1)S(1)}) fusion(bf16[2,3072,3,384]{3,1,2,0:T(8,128)(2,1)} %param.13), kind=kLoop, calls=%fused_computation | loop fusion | bytes 28311552 | tf_op jit(solution)/shard_map/squeeze | solution.py:403
  17.2 5.2 %slice_bitcast_fusion.4 = (bf16[384,3072]{0,1:T(8,128)(2,1)}, bf16[384,3072]{0,1:T(8,128)(2,1)}, bf16[384,3072]{0,1:T(8,128)(2,1)}, bf16[384,3072]{0,1:T(8,128)(...) fusion(bf16[3072,3,384]{2,0,1:T(8,128)(2,1)S(1)} %get-tuple-element.51, ...), kind=kLoop, calls=%fused_computation.26 | loop fusion | bytes 28311552 | tf_op jit(solution)/shard_map/dot_general | solution.py:63
  22.5 4.4 %copy.68 = bf16[384,3072]{1,0:T(8,128)(2,1)} copy(bf16[384,3072]{0,1:T(8,128)(2,1)} %get-tuple-element.93) | data formatting | bytes 4718592 | tf_op jit(solution)/shard_map/dot_general | solution.py:63
  32.3 1.5 reshape.460
  33.7 2.7 %copy.69 = bf16[384,3072]{1,0:T(8,128)(2,1)} copy(bf16[384,3072]{0,1:T(8,128)(2,1)S(1)} %copy-done.5) | data formatting | bytes 4718592 | tf_op jit(solution)/shard_map/dot_general | solution.py:63
  36.4 3.8 %multiply_reduce_fusion.2 = (f32[384,3]{0,1:T(4,128)S(1)}, f32[384,3,128]{0,2,1:T(8,128)S(1)}) fusion(bf16[384,3072,1]{1,0,2:T(8,128)(2,1)} %copy-done.10, bf16[3,128,3072]{2,1,0:T(8,128)(2,1)} %bitcast.150), kind=kOutput, calls=%fused_computation.47 | convolution fusion | flops 906263424 | bytes 5313024 | tf_op jit(solution)/shard_map/dot_general | solution.py:63
  44.2 2.2 %subtract_convert_fusion.2 = (bf16[384,3,64,1]{0,3,2,1:T(2,128)(2,1)S(1)}, bf16[384,3,64,1]{0,3,2,1:T(2,128)(2,1)S(1)}, bf16[384,3,64,1]{0,3,2,1:T(2,128)(2,1)S(1)}, bf16[384,3,64,1]{0,3,2,1:T(2,128)(2,1)}) fusion(f32[384,3,64,2]{0,3,2,1:T(2,128)S(1)} %reshape.461, f32[384,64]{0,1:T(8,128)S(1)} %get-tuple-element.80, f32[384,64]{0,1:T(8,128)S(1)} %get-tuple-element.79, ...), kind=kLoop, calls=%fused_computation.60 | loop fusion | flops 1179648 | bytes 1966080 | tf_op jit(solution)/shard_map/convert.4
  48.1 1.6 pad_maximum_fusion
  50.7 2.6 %copy.70 = bf16[384,3072]{1,0:T(8,128)(2,1)} copy(bf16[384,3072]{0,1:T(8,128)(2,1)S(1)} %copy-done.4) | data formatting | bytes 4718592 | tf_op jit(solution)/shard_map/dot_general | solution.py:63
  53.3 4.0 %convolution_convert_fusion.1 = bf16[384,3,128]{0,2,1:T(8,128)(2,1)S(1)} fusion(bf16[384,3072,1]{1,0,2:T(8,128)(2,1)} %copy-done.10, bf16[3,128,3072]{2,1,0:T(8,128)(2,1)} %bitcast.151), kind=kOutput, calls=%fused_computation.40 | convolution fusion | flops 906117120 | bytes 5013504 | tf_op jit(solution)/shard_map/dot_general | solution.py:63
  59.1 2.6 %copy.76 = bf16[384,3072]{1,0:T(8,128)(2,1)} copy(bf16[384,3072]{0,1:T(8,128)(2,1)S(1)} %copy-done.3) | data formatting | bytes 4718592 | tf_op jit(solution)/shard_map/dot_general | solution.py:63
  61.7 4.5 %copy.74 = bf16[384,3072]{1,0:T(8,128)(2,1)} copy(bf16[384,3072]{0,1:T(8,128)(2,1)} %get-tuple-element.55) | data formatting | bytes 4718592 | tf_op jit(solution)/shard_map/dot_general | solution.py:63
  66.2 2.6 %copy.75 = bf16[384,3072]{1,0:T(8,128)(2,1)} copy(bf16[384,3072]{0,1:T(8,128)(2,1)S(1)} %copy-done.2) | data formatting | bytes 4718592 | tf_op jit(solution)/shard_map/dot_general | solution.py:63
  71.3 3.3 %shard_map.130 = (bf16[3,128,384]{2,1,0:T(8,128)(2,1)}, f32[3,1,384]{2,1,0:T(1,128)}, f32[3,1,384]{2,1,0:T(1,128)}, f32[3,128,384]{2,1,0:T(8,128)}) custom-call(bf16[384,384]{1,0:T(8,128)(2,1)} %copy.71.q_ref, bf16[384,384]{1,0:T(8,128)(2,1)} %copy.72.kf_ref, bf16[384,384]{1,0:T(8,128)(2,1)} %copy.73.vf_ref), custom_call_target="tpu_custom_call" | custom-call | tf_op jit(solution)/shard_map/pallas_call | solution.py:147
  76.7 1.8 compare_select_fusion.fetch_ref
  79.5 8.2 %all-gather.5.cloned.1.call-done = bf16[16,2,1,384,384]{4,3,2,1,0:T(8,128)(2,1)} async-done(((bf16[1,2,1,384,384]{4,3,2,1,0:T(8,128)(2,1)}), bf16[16,2,1,384,384]{4,3,2,1,0:T(8,128)(2,1)}) %all-gather.5.cloned.1.call-update) | async-done | bytes 9437200 | tf_op jit(solution)/shard_map/all_gather | solution.py:392
  87.7 12.7 %shard_map.131 = (bf16[192,384]{1,0:T(8,128)(2,1)}, bf16[192,384]{1,0:T(8,128)(2,1)}) custom-call(s32[7]{0:T(128)} %compare_select_fusion.fetch_ref, s32[7]{0:T(128)} %compare_convert_fusion.allow_ref, bf16[3,128,384]{2,1,0:T(8,128)(2,1)} %get-tuple-element.20.qt_ref, f32[3,1,384]{2,1,0:T(1,128)} %get-tuple-element.21.m0_ref, ...), custom_call_target="tpu_custom_call" | custom-call | tf_op jit(solution)/shard_map/pallas_call | solution.py:167
  100.4 2.7 %fusion.18 = f32[192,3072]{1,0:T(8,128)S(1)} fusion(bf16[192,384]{1,0:T(8,128)(2,1)} %get-tuple-element.24, bf16[2,384,3072]{2,1,0:T(8,128)(2,1)} %param.14), kind=kOutput, calls=%fused_computation.35 | convolution fusion | flops 452984832 | bytes 4866048 | tf_op jit(solution)/shard_map/dot_general | solution.py:414
  103.1 2.5 %fusion.13.part_ref = bf16[192,3072]{1,0:T(8,128)(2,1)S(1)} fusion(f32[192,3072]{1,0:T(8,128)S(1)} %fusion.18, bf16[192,384]{1,0:T(8,128)(2,1)S(1)} %collective-permute-done, bf16[2,384,3072]{2,1,0:T(8,128)(2,1)} %collective-permute-done.1), kind=kOutput, calls=%fused_computation.22 | convolution fusion | flops 454164480 | bytes 6045696 | tf_op jit(solution)/shard_map/dot_general | solution.py:415
  105.6 28.6 %shard_map.132 = (bf16[48,3072]{1,0:T(8,128)(2,1)S(1)}, bf16[2,4,48,3072]{3,2,1,0:T(8,128)(2,1)S(1)}) custom-call(bf16[192,3072]{1,0:T(8,128)(2,1)S(1)} %fusion.13.part_ref, bf16[48,3072]{1,0:T(8,128)(2,1)S(1)} %dynamic-slice_bitcast_fusion.own_ref, f32[1,3072]{1,0:T(1,128)S(1)} %get-tuple-element.75.gate_ref), custom_call_target="tpu_custom_call" | custom-call | tf_op jit(solution)/shard_map/pallas_call | solution.py:334
  137.1 2.1 %convolution_convert_fusion = bf16[384,3,128]{0,2,1:T(8,128)(2,1)} fusion(bf16[384,3072,1]{1,0,2:T(8,128)(2,1)S(1)} %bitcast.147, bf16[3,128,3072]{2,1,0:T(8,128)(2,1)S(1)} %bitcast.145), kind=kOutput, calls=%fused_computation.39 | convolution fusion | flops 906117120 | bytes 5013504 | tf_op jit(solution)/shard_map/dot_general | solution.py:63
  139.2 1.9 copy.79.vf_ref
  141.1 3.2 %multiply_reduce_fusion.1 = (f32[384,3]{0,1:T(4,128)S(1)}, f32[384,3,128]{0,2,1:T(8,128)S(1)}) fusion(bf16[384,3072,1]{1,0,2:T(8,128)(2,1)} %bitcast.148, bf16[3,128,3072]{2,1,0:T(8,128)(2,1)S(1)} %bitcast.144), kind=kOutput, calls=%fused_computation.45 | convolution fusion | flops 906263424 | bytes 5313024 | tf_op jit(solution)/shard_map/dot_general | solution.py:63
  144.7 3.9 %multiply_reduce_fusion = (f32[384,3]{0,1:T(4,128)S(1)}, f32[384,3,128]{0,2,1:T(8,128)S(1)}) fusion(bf16[384,3072,1]{1,0,2:T(8,128)(2,1)} %bitcast.149, bf16[3,128,3072]{2,1,0:T(8,128)(2,1)} %bitcast.143), kind=kOutput, calls=%fused_computation.43 | convolution fusion | flops 906263424 | bytes 5313024 | tf_op jit(solution)/shard_map/dot_general | solution.py:63
  149.5 1.6 subtract_convert_fusion
  154.5 3.3 %shard_map.133 = (bf16[3,128,384]{2,1,0:T(8,128)(2,1)}, f32[3,1,384]{2,1,0:T(1,128)}, f32[3,1,384]{2,1,0:T(1,128)}, f32[3,128,384]{2,1,0:T(8,128)}) custom-call(bf16[384,384]{1,0:T(8,128)(2,1)} %copy.77.q_ref, bf16[384,384]{1,0:T(8,128)(2,1)} %copy.78.kf_ref, bf16[384,384]{1,0:T(8,128)(2,1)} %copy.79.vf_ref), custom_call_target="tpu_custom_call" | custom-call | tf_op jit(solution)/shard_map/pallas_call | solution.py:147
  157.8 7.3 %all-gather.7.cloned.1.call-done = bf16[16,2,1,384,384]{4,3,2,1,0:T(8,128)(2,1)} async-done(((bf16[1,2,1,384,384]{4,3,2,1,0:T(8,128)(2,1)}), bf16[16,2,1,384,384]{4,3,2,1,0:T(8,128)(2,1)}) %all-gather.7.cloned.1.call-update) | async-done | bytes 9437200 | tf_op jit(solution)/shard_map/all_gather | solution.py:392
  165.1 12.7 %shard_map.134 = (bf16[192,384]{1,0:T(8,128)(2,1)}, bf16[192,384]{1,0:T(8,128)(2,1)}) custom-call(s32[7]{0:T(128)} %compare_select_fusion.fetch_ref, s32[7]{0:T(128)} %compare_convert_fusion.allow_ref, bf16[3,128,384]{2,1,0:T(8,128)(2,1)} %get-tuple-element.28.qt_ref, f32[3,1,384]{2,1,0:T(1,128)} %get-tuple-element.29.m0_ref, ...), custom_call_target="tpu_custom_call" | custom-call | tf_op jit(solution)/shard_map/pallas_call | solution.py:167
  177.8 2.5 %fusion.16 = f32[192,3072]{1,0:T(8,128)S(1)} fusion(bf16[192,384]{1,0:T(8,128)(2,1)} %get-tuple-element.32, bf16[2,384,3072]{2,1,0:T(8,128)(2,1)} %param.14), kind=kOutput, calls=%fused_computation.33 | convolution fusion | flops 452984832 | bytes 4866048 | tf_op jit(solution)/shard_map/dot_general | solution.py:414
  180.4 2.5 %fusion.14.part_ref = bf16[192,3072]{1,0:T(8,128)(2,1)S(1)} fusion(f32[192,3072]{1,0:T(8,128)S(1)} %fusion.16, bf16[192,384]{1,0:T(8,128)(2,1)S(1)} %collective-permute-done.2, bf16[2,384,3072]{2,1,0:T(8,128)(2,1)} %collective-permute-done.1), kind=kOutput, calls=%fused_computation.23 | convolution fusion | flops 454164480 | bytes 6045696 | tf_op jit(solution)/shard_map/dot_general | solution.py:415
  182.9 16.0 %shard_map.135 = (bf16[48,3072]{1,0:T(8,128)(2,1)S(1)}, f32[48,64]{1,0:T(8,128)S(1)}, f32[48,64]{1,0:T(8,128)S(1)}) custom-call(bf16[192,3072]{1,0:T(8,128)(2,1)S(1)} %fusion.14.part_ref, bf16[48,3072]{1,0:T(8,128)(2,1)S(1)} %get-tuple-element.26.own_ref, f32[1,3072]{1,0:T(1,128)S(1)} %get-tuple-element.73.gate_ref, bf16[3072,64]{1,0:T(8,128)(2,1)S(1)} %copy.80.rest_0_, ...), custom_call_target="tpu_custom_call" | custom-call | tf_op jit(solution)/shard_map/pallas_call | solution.py:334
  (110 shorter events, 28.4 us)
Async XLA Ops:
  7.2 80.5 %all-gather.5.cloned.1.call-start = ((), (), s32[]{:S(2)}) async-start(), calls=%async_computation | async-start | bytes 10027008 | tf_op jit(solution)/shard_map/all_gather | solution.py:392
  9.6 155.5 %all-gather.7.cloned.1.call-start = ((), (), s32[]{:S(2)}) async-start(), calls=%async_computation.1 | async-start | bytes 10027008 | tf_op jit(solution)/shard_map/all_gather | solution.py:392
  10.4 92.7 %collective-permute-start.1 = (bf16[2,384,3072]{2,1,0:T(8,128)(2,1)}, bf16[2,384,3072]{2,1,0:T(8,128)(2,1)}, u32[]{:S(2)}, u32[]{:S(2)}) collective-permute-start(bf16[2,384,3072]{2,1,0:T(8,128)(2,1)} %param.14), channel_id=1, source_target_pairs={{0,64},{64,0},{1,65},{65,1},{2,66},{66,2},{3,67},{67,3},{4,68},{68... | collective-permute-start | bytes 14155784 | tf_op jit(solution)/shard_map/ppermute | solution.py:396
  22.5 4.4 %copy-start.17 = (f32[2,2,128]{2,1,0:T(2,128)S(1)}, f32[2,2,128]{2,1,0:T(2,128)}, u32[]{:S(2)}) copy-start(f32[2,2,128]{2,1,0:T(2,128)} %param.16) | copy-start | bytes 6148
  22.5 4.4 %copy-start.1 = (bf16[1,384,3072]{2,1,0:T(8,128)(2,1)S(1)}, bf16[1,384,3072]{2,1,0:T(8,128)(2,1)}, u32[]{:S(2)}) copy-start(bf16[1,384,3072]{2,1,0:T(8,128)(2,1)} %param.11) | copy-start | bytes 7077892
  26.9 1.2 copy-start.16
  28.2 1.7 copy-start.8
  29.4 1.8 copy-start.10
  31.3 2.4 %copy-start.5 = (bf16[384,3072]{0,1:T(8,128)(2,1)S(1)}, bf16[384,3072]{0,1:T(8,128)(2,1)}, u32[]{:S(2)}) copy-start(bf16[384,3072]{0,1:T(8,128)(2,1)} %get-tuple-element.94) | copy-start | bytes 7077892
  40.2 0.7 copy-start.18
  40.2 0.8 copy-start.19
  43.5 0.6 copy-start.11
  43.5 0.7 copy-start.13
  46.4 4.4 %copy-start.4 = (bf16[384,3072]{0,1:T(8,128)(2,1)S(1)}, bf16[384,3072]{0,1:T(8,128)(2,1)}, u32[]{:S(2)}) copy-start(bf16[384,3072]{0,1:T(8,128)(2,1)} %get-tuple-element.95) | copy-start | bytes 7077892
  53.3 5.7 %copy-start.3 = (bf16[384,3072]{0,1:T(8,128)(2,1)S(1)}, bf16[384,3072]{0,1:T(8,128)(2,1)}, u32[]{:S(2)}) copy-start(bf16[384,3072]{0,1:T(8,128)(2,1)} %get-tuple-element.53) | copy-start | bytes 7077892
  61.7 4.5 %copy-start.2 = (bf16[384,3072]{0,1:T(8,128)(2,1)S(1)}, bf16[384,3072]{0,1:T(8,128)(2,1)}, u32[]{:S(2)}) copy-start(bf16[384,3072]{0,1:T(8,128)(2,1)} %get-tuple-element.54) | copy-start | bytes 7077892
  66.2 2.7 %copy-start.15 = (bf16[3072,64]{0,1:T(8,128)(2,1)S(1)}, bf16[3072,64]{0,1:T(8,128)(2,1)}, u32[]{:S(2)}) copy-start(bf16[3072,64]{0,1:T(8,128)(2,1)} %param.15) | copy-start | bytes 1179652
  100.4 2.7 %collective-permute-start = (bf16[192,384]{1,0:T(8,128)(2,1)}, bf16[192,384]{1,0:T(8,128)(2,1)S(1)}, u32[]{:S(2)}, u32[]{:S(2)}) collective-permute-start(bf16[192,384]{1,0:T(8,128)(2,1)} %get-tuple-element.25), channel_id=1, source_target_pairs={{0,64},{64,0},{1,65},{65,1},{2,66},{66,2},{3,67},{67,3},{4,68},{68... | collective-permute-start | bytes 442376 | tf_op jit(solution)/shard_map/ppermute | solution.py:412
  135.4 1.7 copy-start.7
  136.6 2.6 %copy-start.9 = (bf16[2,4,48,3072]{3,2,1,0:T(8,128)(2,1)}, bf16[2,4,48,3072]{3,2,1,0:T(8,128)(2,1)S(1)}, u32[]{:S(2)}) copy-start(bf16[2,4,48,3072]{3,2,1,0:T(8,128)(2,1)S(1)} %fusion.5) | copy-start | bytes 7077892
  137.1 4.0 %copy-start.6 = (bf16[384,3072]{1,0:T(8,128)(2,1)S(1)}, bf16[384,3072]{1,0:T(8,128)(2,1)}, u32[]{:S(2)}) copy-start(bf16[384,3072]{1,0:T(8,128)(2,1)} %copy.74) | copy-start | bytes 7077892
  148.6 0.9 copy-start.12
  148.6 0.9 copy-start.14
  177.8 2.6 %collective-permute-start.2 = (bf16[192,384]{1,0:T(8,128)(2,1)}, bf16[192,384]{1,0:T(8,128)(2,1)S(1)}, u32[]{:S(2)}, u32[]{:S(2)}) collective-permute-start(bf16[192,384]{1,0:T(8,128)(2,1)} %get-tuple-element.33), channel_id=1, source_target_pairs={{0,64},{64,0},{1,65},{65,1},{2,66},{66,2},{3,67},{67,3},{4,68},{68... | collective-permute-start | bytes 442376 | tf_op jit(solution)/shard_map/ppermute | solution.py:412
  180.4 2.5 %copy-start = (f32[1,48,64]{2,1,0:T(8,128)S(1)}, f32[1,48,64]{2,1,0:T(8,128)}, u32[]{:S(2)}) copy-start(f32[1,48,64]{2,1,0:T(8,128)} %param.12) | copy-start | bytes 36868
Sparse Core Ops, SparseCore 0:
  10.1 77.4 all-gather.4
  89.8 75.2 all-gather.6

commit v15 on v14

--- a/solution.py
+++ b/solution.py
@@ -94,8 +94,8 @@
 
 
 def attention_kernel(
-    head_dim, fetch_ref, allow_ref, qt_ref, m0_ref, l0_ref, acc0_ref, ks_ref, vs_ref, mine_ref,
-    theirs_ref, m_sc, l_sc, acc_sc
+    head_dim, fetch_ref, allow_ref, qt_ref, m0_ref, l0_ref, acc0_ref, ks_ref, vs_ref, ks2_ref, vs2_ref,
+    mine_ref, theirs_ref, m_sc, l_sc, acc_sc
 ):
     slot = pl.program_id(0)
     heads = qt_ref.shape[0]
@@ -108,12 +108,11 @@
         l_sc[...] = l0_ref[...]
         acc_sc[...] = acc0_ref[...]
 
-    @pl.when(allow_ref[slot] != 0)
-    def _stale():
+    def update(key_ref, value_ref):
         for h in range(heads):
             lanes = slice(h * head_dim, (h + 1) * head_dim)
             scores = (
-                jnp.dot(ks_ref[:, lanes], qt_ref[h], preferred_element_type=jnp.float32) * scaling
+                jnp.dot(key_ref[:, lanes], qt_ref[h], preferred_element_type=jnp.float32) * scaling
             )
             old_max = m_sc[h]
             new_max = jnp.maximum(old_max, jnp.max(scores, axis=0, keepdims=True))
@@ -121,10 +120,18 @@
             weights = jnp.exp(scores - new_max)
             l_sc[h] = l_sc[h] * factor + jnp.sum(weights, axis=0, keepdims=True)
             acc_sc[h] = acc_sc[h] * factor + lax.dot_general(
-                vs_ref[:, lanes], weights.astype(jnp.bfloat16), by_key,
+                value_ref[:, lanes], weights.astype(jnp.bfloat16), by_key,
                 preferred_element_type=jnp.float32,
             )
             m_sc[h] = new_max
+
+    @pl.when(allow_ref[2 * slot] != 0)
+    def _first():
+        update(ks_ref, vs_ref)
+
+    @pl.when(allow_ref[2 * slot + 1] != 0)
+    def _second():
+        update(ks2_ref, vs2_ref)
 
     @pl.when(slot == pl.num_programs(0) - 1)
     def _finish():
@@ -141,7 +148,7 @@
 
 def attend(queries, keys_fresh, values_fresh, stale, fetch, allow, head_dim):
     rows, features = queries.shape
-    slot_total = fetch.shape[0]
+    slot_total = fetch.shape[0] // 2
     heads = features // head_dim
     vmem = pl.BlockSpec(memory_space=pltpu.VMEM)
     state = pl.pallas_call(
@@ -159,10 +166,16 @@
     qt_spec = pl.BlockSpec((heads, head_dim, rows), lambda j, f, a: (0, 0, 0))
     stat_spec = pl.BlockSpec((heads, 1, rows), lambda j, f, a: (0, 0, 0))
     key_spec = pl.BlockSpec(
-        (None, None, rows, features), lambda j, f, a: (f[j], 0, 0, 0)
+        (None, None, rows, features), lambda j, f, a: (f[2 * j], 0, 0, 0)
     )
     value_spec = pl.BlockSpec(
-        (None, None, rows, features), lambda j, f, a: (f[j], 1, 0, 0)
+        (None, None, rows, features), lambda j, f, a: (f[2 * j], 1, 0, 0)
+    )
+    key2_spec = pl.BlockSpec(
+        (None, None, rows, features), lambda j, f, a: (f[2 * j + 1], 0, 0, 0)
+    )
+    value2_spec = pl.BlockSpec(
+        (None, None, rows, features), lambda j, f, a: (f[2 * j + 1], 1, 0, 0)
     )
     return pl.pallas_call(
         functools.partial(attention_kernel, head_dim),
@@ -173,7 +186,7 @@
         grid_spec=pltpu.PrefetchScalarGridSpec(
             num_scalar_prefetch=2,
             grid=(slot_total,),
-            in_specs=[qt_spec, stat_spec, stat_spec, qt_spec, key_spec, value_spec],
+            in_specs=[qt_spec, stat_spec, stat_spec, qt_spec, key_spec, value_spec, key2_spec, value2_spec],
             out_specs=(half, half),
             scratch_shapes=[
                 pltpu.VMEM((heads, 1, rows), jnp.float32),
@@ -182,7 +195,7 @@
             ],
         ),
         compiler_params=pltpu.CompilerParams(dimension_semantics=("arbitrary",)),
-    )(fetch, allow, *state, stale, stale)
+    )(fetch, allow, *state, stale, stale, stale, stale)
 
 
 def exchange_kernel(head_count, own_rows, split, gather, part_ref, own_ref, gate_ref, *rest):
@@ -382,7 +395,7 @@
     allowed = (request_of == my_request) & (slot_ids != tok_index)
     rank = jnp.cumsum(allowed.astype(jnp.int32)) - 1
     count = jnp.sum(allowed.astype(jnp.int32))
-    step_ids = jnp.arange(MOST - 1, dtype=jnp.int32)
+    step_ids = jnp.arange(MOST - 1 + (MOST - 1) % 2, dtype=jnp.int32)
     picked = allowed[None, :] & (rank[None, :] == step_ids[:, None])
     compact = jnp.sum(jnp.where(picked, slot_ids[None, :], 0), axis=1)
     last_pick = jnp.sum(jnp.where(allowed & (rank == count - 1), slot_ids, 0))

time: 209 us -> 209 us (level)
  the two profiles are of different devices: /device:TPU:32 before, /device:TPU:8 now
where the time goes in v15:
time: 209 us
  Pallas kernels  77.3 us (37%)
  local copies, waits for them, and re-layouts  48.6 us (23%)
  matrix products  28.4 us (14%)
  other arithmetic  21.2 us (10%)
  between operations  16.5 us (8%)
  waiting for transfers between devices  16.4 us (8%)
    pallas_call x2, Pallas kernels, exchange(): pl.pallas_call(functools.partial(exchange_kernel, head_count, own_rows, s...  44.9 us
    pallas_call x2, Pallas kernels, attend(): pl.pallas_call(functools.partial(attention_kernel, head_dim), out_shape=(...  25.9 us
    dot_general x7, local copies, waits for them, and re-layouts, project(): jnp.dot(normed, weight[:, part, :], preferred_element_type=jnp.float32)  24.7 us
    dot_general x6, matrix products, project(): jnp.dot(normed, weight[:, part, :], preferred_element_type=jnp.float32)  18.4 us
    all_gather x2, waiting for transfers between devices, shards(): lax.all_gather(jnp.swapaxes(stale_kv[layer], 0, 1), 'tok', axis=0, tiled=...  15.7 us
    pallas_call x2, Pallas kernels, attend(): pl.pallas_call(functools.partial(fresh_kernel, head_dim), out_shape=(jax....  6.53 us
    squeeze x1, local copies, waits for them, and re-layouts, shards(): w_qkv[layer_idx]  6.09 us
    dot_general x2, matrix products, shards(): jnp.dot(mine, w_out[layer_idx], preferred_element_type=jnp.float32)  5.08 us
  transfers between devices with their start and end apart: 5, of which 2 were waited for; matrix products, arithmetic and copies ran while one was open for 43% of the time, Pallas kernels for 23%

profile of v15, /device:TPU:8, one launch (start us, length us, event | category | flops | bytes accessed | tf_op | source)
XLA Modules:
  0.0 208.6 jit_solution(18357915992148494196)
XLA Ops:
  7.2 2.4 %fusion.25 = (bf16[1,2,1,384,384]{4,3,2,1,0:T(8,128)(2,1)}, bf16[1,2,1,384,384]{4,3,2,1,0:T(8,128)(2,1)}) fusion(bf16[2,2,1,384,384]{4,3,2,1,0:T(8,128)(2,1)} %param.18), kind=kLoop, calls=%fused_computation.100 | loop fusion | bytes 2359296 | tf_op jit(solution)/shard_map/slice | solution.py:405
  11.1 6.1 %slice_bitcast_fusion = (bf16[3072,3,384]{2,0,1:T(8,128)(2,1)S(1)}, bf16[3072,3,384]{2,0,1:T(8,128)(2,1)S(1)}) fusion(bf16[2,3072,3,384]{3,1,2,0:T(8,128)(2,1)} %param.13), kind=kLoop, calls=%fused_computation | loop fusion | bytes 28311552 | tf_op jit(solution)/shard_map/squeeze | solution.py:416
  17.2 5.2 %slice_bitcast_fusion.4 = (bf16[384,3072]{0,1:T(8,128)(2,1)}, bf16[384,3072]{0,1:T(8,128)(2,1)}, bf16[384,3072]{0,1:T(8,128)(2,1)}, bf16[384,3072]{0,1:T(8,128)(...) fusion(bf16[3072,3,384]{2,0,1:T(8,128)(2,1)S(1)} %get-tuple-element.51, ...), kind=kLoop, calls=%fused_computation.26 | loop fusion | bytes 28311552 | tf_op jit(solution)/shard_map/dot_general | solution.py:63
  22.5 4.4 %copy.68 = bf16[384,3072]{1,0:T(8,128)(2,1)} copy(bf16[384,3072]{0,1:T(8,128)(2,1)} %get-tuple-element.93) | data formatting | bytes 4718592 | tf_op jit(solution)/shard_map/dot_general | solution.py:63
  32.3 1.4 reshape.460
  33.7 2.7 %copy.69 = bf16[384,3072]{1,0:T(8,128)(2,1)} copy(bf16[384,3072]{0,1:T(8,128)(2,1)S(1)} %copy-done.5) | data formatting | bytes 4718592 | tf_op jit(solution)/shard_map/dot_general | solution.py:63
  36.4 3.8 %multiply_reduce_fusion.2 = (f32[384,3]{0,1:T(4,128)S(1)}, f32[384,3,128]{0,2,1:T(8,128)S(1)}) fusion(bf16[384,3072,1]{1,0,2:T(8,128)(2,1)} %copy-done.10, bf16[3,128,3072]{2,1,0:T(8,128)(2,1)} %bitcast.154), kind=kOutput, calls=%fused_computation.47 | convolution fusion | flops 906263424 | bytes 5313024 | tf_op jit(solution)/shard_map/dot_general | solution.py:63
  44.2 2.2 %subtract_convert_fusion.2 = (bf16[384,3,64,1]{0,3,2,1:T(2,128)(2,1)S(1)}, bf16[384,3,64,1]{0,3,2,1:T(2,128)(2,1)S(1)}, bf16[384,3,64,1]{0,3,2,1:T(2,128)(2,1)S(1)}, bf16[384,3,64,1]{0,3,2,1:T(2,128)(2,1)}) fusion(f32[384,3,64,2]{0,3,2,1:T(2,128)S(1)} %reshape.461, f32[384,64]{0,1:T(8,128)S(1)} %get-tuple-element.80, f32[384,64]{0,1:T(8,128)S(1)} %get-tuple-element.79, ...), kind=kLoop, calls=%fused_computation.60 | loop fusion | flops 1179648 | bytes 1966080 | tf_op jit(solution)/shard_map/convert.4
  48.1 1.6 pad_maximum_fusion
  50.7 2.6 %copy.70 = bf16[384,3072]{1,0:T(8,128)(2,1)} copy(bf16[384,3072]{0,1:T(8,128)(2,1)S(1)} %copy-done.4) | data formatting | bytes 4718592 | tf_op jit(solution)/shard_map/dot_general | solution.py:63
  53.3 4.1 %convolution_convert_fusion.1 = bf16[384,3,128]{0,2,1:T(8,128)(2,1)S(1)} fusion(bf16[384,3072,1]{1,0,2:T(8,128)(2,1)} %copy-done.10, bf16[3,128,3072]{2,1,0:T(8,128)(2,1)} %bitcast.155), kind=kOutput, calls=%fused_computation.40 | convolution fusion | flops 906117120 | bytes 5013504 | tf_op jit(solution)/shard_map/dot_general | solution.py:63
  59.2 2.6 %copy.76 = bf16[384,3072]{1,0:T(8,128)(2,1)} copy(bf16[384,3072]{0,1:T(8,128)(2,1)S(1)} %copy-done.3) | data formatting | bytes 4718592 | tf_op jit(solution)/shard_map/dot_general | solution.py:63
  61.8 4.5 %copy.74 = bf16[384,3072]{1,0:T(8,128)(2,1)} copy(bf16[384,3072]{0,1:T(8,128)(2,1)} %get-tuple-element.55) | data formatting | bytes 4718592 | tf_op jit(solution)/shard_map/dot_general | solution.py:63
  66.3 2.6 %copy.75 = bf16[384,3072]{1,0:T(8,128)(2,1)} copy(bf16[384,3072]{0,1:T(8,128)(2,1)S(1)} %copy-done.2) | data formatting | bytes 4718592 | tf_op jit(solution)/shard_map/dot_general | solution.py:63
  71.3 3.3 %shard_map.130 = (bf16[3,128,384]{2,1,0:T(8,128)(2,1)}, f32[3,1,384]{2,1,0:T(1,128)}, f32[3,1,384]{2,1,0:T(1,128)}, f32[3,128,384]{2,1,0:T(8,128)}) custom-call(bf16[384,384]{1,0:T(8,128)(2,1)} %copy.71.q_ref, bf16[384,384]{1,0:T(8,128)(2,1)} %copy.72.kf_ref, bf16[384,384]{1,0:T(8,128)(2,1)} %copy.73.vf_ref), custom_call_target="tpu_custom_call" | custom-call | tf_op jit(solution)/shard_map/pallas_call | solution.py:154
  76.8 1.8 compare_select_fusion.fetch_ref
  79.6 8.6 %all-gather.5.cloned.1.call-done = bf16[16,2,1,384,384]{4,3,2,1,0:T(8,128)(2,1)} async-done(((bf16[1,2,1,384,384]{4,3,2,1,0:T(8,128)(2,1)}), bf16[16,2,1,384,384]{4,3,2,1,0:T(8,128)(2,1)}) %all-gather.5.cloned.1.call-update) | async-done | bytes 9437200 | tf_op jit(solution)/shard_map/all_gather | solution.py:405
  88.2 12.9 %shard_map.131 = (bf16[192,384]{1,0:T(8,128)(2,1)}, bf16[192,384]{1,0:T(8,128)(2,1)}) custom-call(s32[8]{0:T(128)} %compare_select_fusion.fetch_ref, s32[8]{0:T(128)} %compare_convert_fusion.allow_ref, bf16[3,128,384]{2,1,0:T(8,128)(2,1)} %get-tuple-element.20.qt_ref, f32[3,1,384]{2,1,0:T(1,128)} %get-tuple-element.21.m0_ref, ...), custom_call_target="tpu_custom_call" | custom-call | tf_op jit(solution)/shard_map/pallas_call | solution.py:180
  101.1 2.5 %fusion.18 = f32[192,3072]{1,0:T(8,128)S(1)} fusion(bf16[192,384]{1,0:T(8,128)(2,1)} %get-tuple-element.24, bf16[2,384,3072]{2,1,0:T(8,128)(2,1)} %param.14), kind=kOutput, calls=%fused_computation.35 | convolution fusion | flops 452984832 | bytes 4866048 | tf_op jit(solution)/shard_map/dot_general | solution.py:427
  103.7 2.5 %fusion.13.part_ref = bf16[192,3072]{1,0:T(8,128)(2,1)S(1)} fusion(f32[192,3072]{1,0:T(8,128)S(1)} %fusion.18, bf16[192,384]{1,0:T(8,128)(2,1)S(1)} %collective-permute-done, bf16[2,384,3072]{2,1,0:T(8,128)(2,1)} %collective-permute-done.1), kind=kOutput, calls=%fused_computation.22 | convolution fusion | flops 454164480 | bytes 6045696 | tf_op jit(solution)/shard_map/dot_general | solution.py:428
  106.1 28.9 %shard_map.132 = (bf16[48,3072]{1,0:T(8,128)(2,1)S(1)}, bf16[2,4,48,3072]{3,2,1,0:T(8,128)(2,1)S(1)}) custom-call(bf16[192,3072]{1,0:T(8,128)(2,1)S(1)} %fusion.13.part_ref, bf16[48,3072]{1,0:T(8,128)(2,1)S(1)} %dynamic-slice_bitcast_fusion.own_ref, f32[1,3072]{1,0:T(1,128)S(1)} %get-tuple-element.75.gate_ref), custom_call_target="tpu_custom_call" | custom-call | tf_op jit(solution)/shard_map/pallas_call | solution.py:347
  137.9 2.1 %convolution_convert_fusion = bf16[384,3,128]{0,2,1:T(8,128)(2,1)} fusion(bf16[384,3072,1]{1,0,2:T(8,128)(2,1)S(1)} %bitcast.151, bf16[3,128,3072]{2,1,0:T(8,128)(2,1)S(1)} %bitcast.149), kind=kOutput, calls=%fused_computation.39 | convolution fusion | flops 906117120 | bytes 5013504 | tf_op jit(solution)/shard_map/dot_general | solution.py:63
  140.0 1.9 copy.79.vf_ref
  141.9 3.1 %multiply_reduce_fusion.1 = (f32[384,3]{0,1:T(4,128)S(1)}, f32[384,3,128]{0,2,1:T(8,128)S(1)}) fusion(bf16[384,3072,1]{1,0,2:T(8,128)(2,1)} %bitcast.152, bf16[3,128,3072]{2,1,0:T(8,128)(2,1)S(1)} %bitcast.148), kind=kOutput, calls=%fused_computation.45 | convolution fusion | flops 906263424 | bytes 5313024 | tf_op jit(solution)/shard_map/dot_general | solution.py:63
  145.5 3.8 %multiply_reduce_fusion = (f32[384,3]{0,1:T(4,128)S(1)}, f32[384,3,128]{0,2,1:T(8,128)S(1)}) fusion(bf16[384,3072,1]{1,0,2:T(8,128)(2,1)} %bitcast.153, bf16[3,128,3072]{2,1,0:T(8,128)(2,1)} %bitcast.147), kind=kOutput, calls=%fused_computation.43 | convolution fusion | flops 906263424 | bytes 5313024 | tf_op jit(solution)/shard_map/dot_general | solution.py:63
  150.3 1.6 subtract_convert_fusion
  155.3 3.3 %shard_map.133 = (bf16[3,128,384]{2,1,0:T(8,128)(2,1)}, f32[3,1,384]{2,1,0:T(1,128)}, f32[3,1,384]{2,1,0:T(1,128)}, f32[3,128,384]{2,1,0:T(8,128)}) custom-call(bf16[384,384]{1,0:T(8,128)(2,1)} %copy.77.q_ref, bf16[384,384]{1,0:T(8,128)(2,1)} %copy.78.kf_ref, bf16[384,384]{1,0:T(8,128)(2,1)} %copy.79.vf_ref), custom_call_target="tpu_custom_call" | custom-call | tf_op jit(solution)/shard_map/pallas_call | solution.py:154
  158.5 7.1 %all-gather.7.cloned.1.call-done = bf16[16,2,1,384,384]{4,3,2,1,0:T(8,128)(2,1)} async-done(((bf16[1,2,1,384,384]{4,3,2,1,0:T(8,128)(2,1)}), bf16[16,2,1,384,384]{4,3,2,1,0:T(8,128)(2,1)}) %all-gather.7.cloned.1.call-update) | async-done | bytes 9437200 | tf_op jit(solution)/shard_map/all_gather | solution.py:405
  165.6 12.9 %shard_map.134 = (bf16[192,384]{1,0:T(8,128)(2,1)}, bf16[192,384]{1,0:T(8,128)(2,1)}) custom-call(s32[8]{0:T(128)} %compare_select_fusion.fetch_ref, s32[8]{0:T(128)} %compare_convert_fusion.allow_ref, bf16[3,128,384]{2,1,0:T(8,128)(2,1)} %get-tuple-element.28.qt_ref, f32[3,1,384]{2,1,0:T(1,128)} %get-tuple-element.29.m0_ref, ...), custom_call_target="tpu_custom_call" | custom-call | tf_op jit(solution)/shard_map/pallas_call | solution.py:180
  178.5 2.5 %fusion.16 = f32[192,3072]{1,0:T(8,128)S(1)} fusion(bf16[192,384]{1,0:T(8,128)(2,1)} %get-tuple-element.32, bf16[2,384,3072]{2,1,0:T(8,128)(2,1)} %param.14), kind=kOutput, calls=%fused_computation.33 | convolution fusion | flops 452984832 | bytes 4866048 | tf_op jit(solution)/shard_map/dot_general | solution.py:427
  181.1 2.5 %fusion.14.part_ref = bf16[192,3072]{1,0:T(8,128)(2,1)S(1)} fusion(f32[192,3072]{1,0:T(8,128)S(1)} %fusion.16, bf16[192,384]{1,0:T(8,128)(2,1)S(1)} %collective-permute-done.2, bf16[2,384,3072]{2,1,0:T(8,128)(2,1)} %collective-permute-done.1), kind=kOutput, calls=%fused_computation.23 | convolution fusion | flops 454164480 | bytes 6045696 | tf_op jit(solution)/shard_map/dot_general | solution.py:428
  183.6 16.0 %shard_map.135 = (bf16[48,3072]{1,0:T(8,128)(2,1)S(1)}, f32[48,64]{1,0:T(8,128)S(1)}, f32[48,64]{1,0:T(8,128)S(1)}) custom-call(bf16[192,3072]{1,0:T(8,128)(2,1)S(1)} %fusion.14.part_ref, bf16[48,3072]{1,0:T(8,128)(2,1)S(1)} %get-tuple-element.26.own_ref, f32[1,3072]{1,0:T(1,128)S(1)} %get-tuple-element.73.gate_ref, bf16[3072,64]{1,0:T(8,128)(2,1)S(1)} %copy.80.rest_0_, ...), custom_call_target="tpu_custom_call" | custom-call | tf_op jit(solution)/shard_map/pallas_call | solution.py:347
  (110 shorter events, 28.4 us)
Async XLA Ops:
  7.2 81.0 %all-gather.5.cloned.1.call-start = ((), (), s32[]{:S(2)}) async-start(), calls=%async_computation | async-start | bytes 10027008 | tf_op jit(solution)/shard_map/all_gather | solution.py:405
  9.6 156.0 %all-gather.7.cloned.1.call-start = ((), (), s32[]{:S(2)}) async-start(), calls=%async_computation.1 | async-start | bytes 10027008 | tf_op jit(solution)/shard_map/all_gather | solution.py:405
  10.4 93.3 %collective-permute-start.1 = (bf16[2,384,3072]{2,1,0:T(8,128)(2,1)}, bf16[2,384,3072]{2,1,0:T(8,128)(2,1)}, u32[]{:S(2)}, u32[]{:S(2)}) collective-permute-start(bf16[2,384,3072]{2,1,0:T(8,128)(2,1)} %param.14), channel_id=1, source_target_pairs={{0,64},{64,0},{1,65},{65,1},{2,66},{66,2},{3,67},{67,3},{4,68},{68... | collective-permute-start | bytes 14155784 | tf_op jit(solution)/shard_map/ppermute | solution.py:409
  22.5 4.4 %copy-start.17 = (f32[2,2,128]{2,1,0:T(2,128)S(1)}, f32[2,2,128]{2,1,0:T(2,128)}, u32[]{:S(2)}) copy-start(f32[2,2,128]{2,1,0:T(2,128)} %param.16) | copy-start | bytes 6148
  22.5 4.4 %copy-start.1 = (bf16[1,384,3072]{2,1,0:T(8,128)(2,1)S(1)}, bf16[1,384,3072]{2,1,0:T(8,128)(2,1)}, u32[]{:S(2)}) copy-start(bf16[1,384,3072]{2,1,0:T(8,128)(2,1)} %param.11) | copy-start | bytes 7077892
  26.9 1.2 copy-start.16
  28.2 1.7 copy-start.8
  29.5 1.9 copy-start.10
  31.3 2.4 %copy-start.5 = (bf16[384,3072]{0,1:T(8,128)(2,1)S(1)}, bf16[384,3072]{0,1:T(8,128)(2,1)}, u32[]{:S(2)}) copy-start(bf16[384,3072]{0,1:T(8,128)(2,1)} %get-tuple-element.94) | copy-start | bytes 7077892
  40.2 0.7 copy-start.18
  40.2 0.8 copy-start.19
  43.5 0.6 copy-start.11
  43.5 0.7 copy-start.13
  46.4 4.4 %copy-start.4 = (bf16[384,3072]{0,1:T(8,128)(2,1)S(1)}, bf16[384,3072]{0,1:T(8,128)(2,1)}, u32[]{:S(2)}) copy-start(bf16[384,3072]{0,1:T(8,128)(2,1)} %get-tuple-element.95) | copy-start | bytes 7077892
  53.3 5.8 %copy-start.3 = (bf16[384,3072]{0,1:T(8,128)(2,1)S(1)}, bf16[384,3072]{0,1:T(8,128)(2,1)}, u32[]{:S(2)}) copy-start(bf16[384,3072]{0,1:T(8,128)(2,1)} %get-tuple-element.53) | copy-start | bytes 7077892
  61.8 4.5 %copy-start.2 = (bf16[384,3072]{0,1:T(8,128)(2,1)S(1)}, bf16[384,3072]{0,1:T(8,128)(2,1)}, u32[]{:S(2)}) copy-start(bf16[384,3072]{0,1:T(8,128)(2,1)} %get-tuple-element.54) | copy-start | bytes 7077892
  66.3 2.7 %copy-start.15 = (bf16[3072,64]{0,1:T(8,128)(2,1)S(1)}, bf16[3072,64]{0,1:T(8,128)(2,1)}, u32[]{:S(2)}) copy-start(bf16[3072,64]{0,1:T(8,128)(2,1)} %param.15) | copy-start | bytes 1179652
  101.1 2.6 %collective-permute-start = (bf16[192,384]{1,0:T(8,128)(2,1)}, bf16[192,384]{1,0:T(8,128)(2,1)S(1)}, u32[]{:S(2)}, u32[]{:S(2)}) collective-permute-start(bf16[192,384]{1,0:T(8,128)(2,1)} %get-tuple-element.25), channel_id=1, source_target_pairs={{0,64},{64,0},{1,65},{65,1},{2,66},{66,2},{3,67},{67,3},{4,68},{68... | collective-permute-start | bytes 442376 | tf_op jit(solution)/shard_map/ppermute | solution.py:425
  136.2 1.7 copy-start.7
  137.4 2.6 %copy-start.9 = (bf16[2,4,48,3072]{3,2,1,0:T(8,128)(2,1)}, bf16[2,4,48,3072]{3,2,1,0:T(8,128)(2,1)S(1)}, u32[]{:S(2)}) copy-start(bf16[2,4,48,3072]{3,2,1,0:T(8,128)(2,1)S(1)} %fusion.5) | copy-start | bytes 7077892
  137.9 4.0 %copy-start.6 = (bf16[384,3072]{1,0:T(8,128)(2,1)S(1)}, bf16[384,3072]{1,0:T(8,128)(2,1)}, u32[]{:S(2)}) copy-start(bf16[384,3072]{1,0:T(8,128)(2,1)} %copy.74) | copy-start | bytes 7077892
  149.3 0.9 copy-start.12
  149.3 0.9 copy-start.14
  178.5 2.6 %collective-permute-start.2 = (bf16[192,384]{1,0:T(8,128)(2,1)}, bf16[192,384]{1,0:T(8,128)(2,1)S(1)}, u32[]{:S(2)}, u32[]{:S(2)}) collective-permute-start(bf16[192,384]{1,0:T(8,128)(2,1)} %get-tuple-element.33), channel_id=1, source_target_pairs={{0,64},{64,0},{1,65},{65,1},{2,66},{66,2},{3,67},{67,3},{4,68},{68... | collective-permute-start | bytes 442376 | tf_op jit(solution)/shard_map/ppermute | solution.py:425
  181.1 2.5 %copy-start = (f32[1,48,64]{2,1,0:T(8,128)S(1)}, f32[1,48,64]{2,1,0:T(8,128)}, u32[]{:S(2)}) copy-start(f32[1,48,64]{2,1,0:T(8,128)} %param.12) | copy-start | bytes 36868
Sparse Core Ops, SparseCore 0:
  10.1 77.9 all-gather.4
  90.3 75.2 all-gather.6

commit v16 on v14

--- a/solution.py
+++ b/solution.py
@@ -394,6 +394,7 @@
     ]
     current_full = hidden[0]
     w_partner = lax.ppermute(w_out, "section", perm=[(0, 1), (1, 0)])
+    w_joined = jnp.concatenate([w_out, w_partner], axis=1)
     own_input = lax.dynamic_slice_in_dim(current_full, group_index * own_rows, own_rows, 0)
     outputs = []
     for layer_idx in range(layer_count):
@@ -410,9 +411,10 @@
         )
         mine, theirs = attended
         swapped = lax.ppermute(theirs, "section", perm=[(0, 1), (1, 0)])
-        partial = (
-            jnp.dot(mine, w_out[layer_idx], preferred_element_type=jnp.float32)
-            + jnp.dot(swapped, w_partner[layer_idx], preferred_element_type=jnp.float32)
+        partial = jnp.dot(
+            jnp.concatenate([mine, swapped], axis=1),
+            w_joined[layer_idx],
+            preferred_element_type=jnp.float32,
         ).astype(jnp.bfloat16)
         gate = modulation[layer_idx, 2]
         if layer_idx + 1 < layer_count:

time: 209 us -> 209 us (level)
  the two profiles are of different devices: /device:TPU:32 before, /device:TPU:8 now
where the time goes in v16:
time: 209 us; the launch traced here: 208 us
  Pallas kernels  76.1 us (36%)
  local copies, waits for them, and re-layouts  64.7 us (31%)
  other arithmetic  24.4 us (12%)
  matrix products  23.9 us (11%)
  between operations  16.5 us (8%)
    pallas_call x2, Pallas kernels, exchange(): pl.pallas_call(functools.partial(exchange_kernel, head_count, own_rows, s...  44 us
    dot_general x7, local copies, waits for them, and re-layouts, project(): jnp.dot(normed, weight[:, part, :], preferred_element_type=jnp.float32)  31.5 us
    pallas_call x2, Pallas kernels, attend(): pl.pallas_call(functools.partial(attention_kernel, head_dim), out_shape=(...  25.6 us
    dot_general x6, matrix products, project(): jnp.dot(normed, weight[:, part, :], preferred_element_type=jnp.float32)  16.8 us
    unnamed x32, local copies, waits for them, and re-layouts  7.28 us
    dot_general x2, matrix products, shards(): jnp.dot(jnp.concatenate([mine, swapped], axis=1), w_joined[layer_idx], pr...  7.15 us
    pallas_call x2, Pallas kernels, attend(): pl.pallas_call(functools.partial(fresh_kernel, head_dim), out_shape=(jax....  6.53 us
    squeeze x1, local copies, waits for them, and re-layouts, shards(): w_qkv[layer_idx]  6.09 us
  transfers between devices with their start and end apart: 5, of which 2 were waited for; matrix products, arithmetic and copies ran while one was open for 50% of the time, Pallas kernels for 23%

profile of v16, /device:TPU:8, one launch (start us, length us, event | category | flops | bytes accessed | tf_op | source)
XLA Modules:
  0.0 208.3 jit_solution(504992915585038681)
XLA Ops:
  7.2 2.4 %fusion.29 = (bf16[1,2,1,384,384]{4,3,2,1,0:T(8,128)(2,1)}, bf16[1,2,1,384,384]{4,3,2,1,0:T(8,128)(2,1)}) fusion(bf16[2,2,1,384,384]{4,3,2,1,0:T(8,128)(2,1)} %param.18), kind=kLoop, calls=%fused_computation.104 | loop fusion | bytes 2359296 | tf_op jit(solution)/shard_map/slice | solution.py:392
  10.5 6.1 %slice_bitcast_fusion = (bf16[3072,3,384]{2,0,1:T(8,128)(2,1)S(1)}, bf16[3072,3,384]{2,0,1:T(8,128)(2,1)S(1)}) fusion(bf16[2,3072,3,384]{3,1,2,0:T(8,128)(2,1)} %param.13), kind=kLoop, calls=%fused_computation | loop fusion | bytes 28311552 | tf_op jit(solution)/shard_map/squeeze | solution.py:404
  16.6 5.4 %slice_bitcast_fusion.10 = (bf16[384,3072]{0,1:T(8,128)(2,1)}, bf16[384,3072]{0,1:T(8,128)(2,1)}, bf16[384,3072]{0,1:T(8,128)(2,1)}, bf16[384,3072]{0,1:T(8,128)...) fusion(bf16[3072,3,384]{2,0,1:T(8,128)(2,1)S(1)} %get-tuple-element.51, ...), kind=kLoop, calls=%fused_computation.27 | loop fusion | bytes 28311552 | tf_op jit(solution)/shard_map/dot_general | solution.py:63
  22.0 4.5 %copy.68 = bf16[384,3072]{1,0:T(8,128)(2,1)} copy(bf16[384,3072]{0,1:T(8,128)(2,1)} %get-tuple-element.93) | data formatting | bytes 4718592 | tf_op jit(solution)/shard_map/dot_general | solution.py:63
  29.4 1.4 multiply_reduce_fusion.3
  31.8 1.4 reshape.460
  33.2 4.3 %copy.69 = bf16[384,3072]{1,0:T(8,128)(2,1)} copy(bf16[384,3072]{0,1:T(8,128)(2,1)} %get-tuple-element.94) | data formatting | bytes 4718592 | tf_op jit(solution)/shard_map/dot_general | solution.py:63
  37.5 3.8 %multiply_reduce_fusion.2 = (f32[384,3]{0,1:T(4,128)S(1)}, f32[384,3,128]{0,2,1:T(8,128)S(1)}) fusion(bf16[384,3072,1]{1,0,2:T(8,128)(2,1)} %copy-done.7, bf16[3,128,3072]{2,1,0:T(8,128)(2,1)} %bitcast.144), kind=kOutput, calls=%fused_computation.41 | convolution fusion | flops 906263424 | bytes 5313024 | tf_op jit(solution)/shard_map/dot_general | solution.py:63
  42.2 2.2 %reshape.461 = f32[384,3,64,2]{0,3,2,1:T(2,128)} reshape(f32[384,3,128]{0,2,1:T(8,128)} %multiply_multiply_fusion.2) | data formatting | bytes 1179648 | tf_op jit(solution)/shard_map/reshape | solution.py:35
  47.1 3.4 %subtract_convert_fusion.2 = (bf16[384,3,64,1]{0,3,2,1:T(2,128)(2,1)S(1)}, bf16[384,3,64,1]{0,3,2,1:T(2,128)(2,1)S(1)}, bf16[384,3,64,1]{0,3,2,1:T(2,128)(2,1)S(1)}, bf16[384,3,64,1]{0,3,2,1:T(2,128)(2,1)}) fusion(f32[384,3,64,2]{0,3,2,1:T(2,128)} %reshape.461, f32[384,64]{0,1:T(8,128)S(1)} %get-tuple-element.80, f32[384,64]{0,1:T(8,128)S(1)} %get-tuple-element.79, ...), kind=kLoop, calls=%fused_computation.60 | loop fusion | flops 1179648 | bytes 1966080 | tf_op jit(solution)/shard_map/convert.4
  52.2 1.6 pad_maximum_fusion
  54.8 4.4 %copy.70 = bf16[384,3072]{1,0:T(8,128)(2,1)} copy(bf16[384,3072]{0,1:T(8,128)(2,1)} %get-tuple-element.95) | data formatting | bytes 4718592 | tf_op jit(solution)/shard_map/dot_general | solution.py:63
  59.2 3.9 %convolution_convert_fusion.1 = bf16[384,3,128]{0,2,1:T(8,128)(2,1)S(1)} fusion(bf16[384,3072,1]{1,0,2:T(8,128)(2,1)} %copy-done.7, bf16[3,128,3072]{2,1,0:T(8,128)(2,1)} %bitcast.145), kind=kOutput, calls=%fused_computation.34 | convolution fusion | flops 906117120 | bytes 5013504 | tf_op jit(solution)/shard_map/dot_general | solution.py:63
  64.7 4.3 %copy.76 = bf16[384,3072]{1,0:T(8,128)(2,1)} copy(bf16[384,3072]{0,1:T(8,128)(2,1)} %get-tuple-element.53) | data formatting | bytes 4718592 | tf_op jit(solution)/shard_map/dot_general | solution.py:63
  69.1 4.3 %copy.74 = bf16[384,3072]{1,0:T(8,128)(2,1)} copy(bf16[384,3072]{0,1:T(8,128)(2,1)} %get-tuple-element.55) | data formatting | bytes 4718592 | tf_op jit(solution)/shard_map/dot_general | solution.py:63
  73.4 4.3 %copy.75 = bf16[384,3072]{1,0:T(8,128)(2,1)} copy(bf16[384,3072]{0,1:T(8,128)(2,1)} %get-tuple-element.54) | data formatting | bytes 4718592 | tf_op jit(solution)/shard_map/dot_general | solution.py:63
  79.7 3.3 %shard_map.130 = (bf16[3,128,384]{2,1,0:T(8,128)(2,1)}, f32[3,1,384]{2,1,0:T(1,128)}, f32[3,1,384]{2,1,0:T(1,128)}, f32[3,128,384]{2,1,0:T(8,128)}) custom-call(bf16[384,384]{1,0:T(8,128)(2,1)} %copy.71.q_ref, bf16[384,384]{1,0:T(8,128)(2,1)} %copy.72.kf_ref, bf16[384,384]{1,0:T(8,128)(2,1)} %copy.73.vf_ref), custom_call_target="tpu_custom_call" | custom-call | tf_op jit(solution)/shard_map/pallas_call | solution.py:147
  85.1 1.8 compare_select_fusion.fetch_ref
  87.0 4.8 %constant_dynamic-update-slice_fusion.1 = bf16[2,768,3072]{2,1,0:T(8,128)(2,1)} fusion(bf16[2,384,3072]{2,1,0:T(8,128)(2,1)} %param.14), kind=kLoop, calls=%fused_computation.71 | loop fusion | bytes 9437184
  91.8 12.7 %shard_map.131 = (bf16[192,384]{1,0:T(8,128)(2,1)}, bf16[192,384]{1,0:T(8,128)(2,1)}) custom-call(s32[7]{0:T(128)} %compare_select_fusion.fetch_ref, s32[7]{0:T(128)} %compare_convert_fusion.allow_ref, bf16[3,128,384]{2,1,0:T(8,128)(2,1)} %get-tuple-element.20.qt_ref, f32[3,1,384]{2,1,0:T(1,128)} %get-tuple-element.21.m0_ref, ...), custom_call_target="tpu_custom_call" | custom-call | tf_op jit(solution)/shard_map/pallas_call | solution.py:167
  105.0 4.9 %constant_dynamic-update-slice_fusion = bf16[2,768,3072]{2,1,0:T(8,128)(2,1)} fusion(bf16[2,768,3072]{2,1,0:T(8,128)(2,1)} %constant_dynamic-update-slice_fusion.1, bf16[2,384,3072]{2,1,0:T(8,128)(2,1)} %collective-permute-done.1), kind=kLoop, calls=%fused_computation.70 | loop fusion | bytes 9437184 | tf_op jit(solution)/shard_map/concatenate | solution.py:397
  109.9 3.6 %fusion.15.part_ref = bf16[192,3072]{1,0:T(8,128)(2,1)S(1)} fusion(bf16[2,768,3072]{2,1,0:T(8,128)(2,1)} %constant_dynamic-update-slice_fusion, bf16[192,384]{1,0:T(8,128)(2,1)S(1)} %collective-permute-done, bf16[192,384]{1,0:T(8,128)(2,1)S(1)} %copy-done.11), kind=kOutput, calls=%fused_computation.24 | convolution fusion | flops 907149312 | bytes 6193152 | tf_op jit(solution)/shard_map/dot_general | solution.py:414
  113.5 28.3 %shard_map.132 = (bf16[48,3072]{1,0:T(8,128)(2,1)S(1)}, bf16[2,4,48,3072]{3,2,1,0:T(8,128)(2,1)S(1)}) custom-call(bf16[192,3072]{1,0:T(8,128)(2,1)S(1)} %fusion.15.part_ref, bf16[48,3072]{1,0:T(8,128)(2,1)S(1)} %dynamic-slice_bitcast_fusion.own_ref, f32[1,3072]{1,0:T(1,128)S(1)} %get-tuple-element.75.gate_ref), custom_call_target="tpu_custom_call" | custom-call | tf_op jit(solution)/shard_map/pallas_call | solution.py:334
  144.7 1.4 convolution_convert_fusion
  147.0 3.2 %multiply_reduce_fusion.1 = (f32[384,3]{0,1:T(4,128)S(1)}, f32[384,3,128]{0,2,1:T(8,128)S(1)}) fusion(bf16[384,3072,1]{1,0,2:T(8,128)(2,1)} %bitcast.142, bf16[3,128,3072]{2,1,0:T(8,128)(2,1)S(1)} %bitcast.138), kind=kOutput, calls=%fused_computation.39 | convolution fusion | flops 906263424 | bytes 5313024 | tf_op jit(solution)/shard_map/dot_general | solution.py:63
  151.1 1.5 reshape.463
  152.6 3.1 %multiply_reduce_fusion = (f32[384,3]{0,1:T(4,128)S(1)}, f32[384,3,128]{0,2,1:T(8,128)S(1)}) fusion(bf16[384,3072,1]{1,0,2:T(8,128)(2,1)} %bitcast.143, bf16[3,128,3072]{2,1,0:T(8,128)(2,1)S(1)} %bitcast.137), kind=kOutput, calls=%fused_computation.37 | convolution fusion | flops 906263424 | bytes 5313024 | tf_op jit(solution)/shard_map/dot_general | solution.py:63
  156.2 1.8 subtract_convert_fusion
  161.4 3.3 %shard_map.133 = (bf16[3,128,384]{2,1,0:T(8,128)(2,1)}, f32[3,1,384]{2,1,0:T(1,128)}, f32[3,1,384]{2,1,0:T(1,128)}, f32[3,128,384]{2,1,0:T(8,128)}) custom-call(bf16[384,384]{1,0:T(8,128)(2,1)} %copy.77.q_ref, bf16[384,384]{1,0:T(8,128)(2,1)} %copy.78.kf_ref, bf16[384,384]{1,0:T(8,128)(2,1)} %copy.79.vf_ref), custom_call_target="tpu_custom_call" | custom-call | tf_op jit(solution)/shard_map/pallas_call | solution.py:147
  165.7 12.9 %shard_map.134 = (bf16[192,384]{1,0:T(8,128)(2,1)}, bf16[192,384]{1,0:T(8,128)(2,1)}) custom-call(s32[7]{0:T(128)} %compare_select_fusion.fetch_ref, s32[7]{0:T(128)} %compare_convert_fusion.allow_ref, bf16[3,128,384]{2,1,0:T(8,128)(2,1)} %get-tuple-element.28.qt_ref, f32[3,1,384]{2,1,0:T(1,128)} %get-tuple-element.29.m0_ref, ...), custom_call_target="tpu_custom_call" | custom-call | tf_op jit(solution)/shard_map/pallas_call | solution.py:167
  180.1 3.6 %fusion.16.part_ref = bf16[192,3072]{1,0:T(8,128)(2,1)S(1)} fusion(bf16[2,768,3072]{2,1,0:T(8,128)(2,1)} %constant_dynamic-update-slice_fusion, bf16[192,384]{1,0:T(8,128)(2,1)S(1)} %collective-permute-done.2, bf16[192,384]{1,0:T(8,128)(2,1)} %get-tuple-element.32), kind=kOutput, calls=%fused_computation.25 | convolution fusion | flops 907149312 | bytes 6193152 | tf_op jit(solution)/shard_map/dot_general | solution.py:414
  183.7 15.7 %shard_map.135 = (bf16[48,3072]{1,0:T(8,128)(2,1)S(1)}, f32[48,64]{1,0:T(8,128)S(1)}, f32[48,64]{1,0:T(8,128)S(1)}) custom-call(bf16[192,3072]{1,0:T(8,128)(2,1)S(1)} %fusion.16.part_ref, bf16[48,3072]{1,0:T(8,128)(2,1)S(1)} %get-tuple-element.26.own_ref, f32[1,3072]{1,0:T(1,128)S(1)} %get-tuple-element.73.gate_ref, bf16[3072,64]{1,0:T(8,128)(2,1)S(1)} %copy.80.rest_0_, ...), custom_call_target="tpu_custom_call" | custom-call | tf_op jit(solution)/shard_map/pallas_call | solution.py:334
  (98 shorter events, 28.2 us)
Async XLA Ops:
  7.2 84.7 %all-gather.5.cloned.1.call-start = ((), (), s32[]{:S(2)}) async-start(), calls=%async_computation | async-start | bytes 10027008 | tf_op jit(solution)/shard_map/all_gather | solution.py:392
  9.6 156.0 %all-gather.7.cloned.1.call-start = ((), (), s32[]{:S(2)}) async-start(), calls=%async_computation.1 | async-start | bytes 10027008 | tf_op jit(solution)/shard_map/all_gather | solution.py:392
  10.4 94.6 %collective-permute-start.1 = (bf16[2,384,3072]{2,1,0:T(8,128)(2,1)}, bf16[2,384,3072]{2,1,0:T(8,128)(2,1)}, u32[]{:S(2)}, u32[]{:S(2)}) collective-permute-start(bf16[2,384,3072]{2,1,0:T(8,128)(2,1)} %param.14), channel_id=1, source_target_pairs={{0,64},{64,0},{1,65},{65,1},{2,66},{66,2},{3,67},{67,3},{4,68},{68... | collective-permute-start | bytes 14155784 | tf_op jit(solution)/shard_map/ppermute | solution.py:396
  22.0 4.5 %copy-start.10 = (f32[2,2,128]{2,1,0:T(2,128)S(1)}, f32[2,2,128]{2,1,0:T(2,128)}, u32[]{:S(2)}) copy-start(f32[2,2,128]{2,1,0:T(2,128)} %param.16) | copy-start | bytes 6148
  22.0 4.5 %copy-start.1 = (bf16[1,384,3072]{2,1,0:T(8,128)(2,1)S(1)}, bf16[1,384,3072]{2,1,0:T(8,128)(2,1)}, u32[]{:S(2)}) copy-start(bf16[1,384,3072]{2,1,0:T(8,128)(2,1)} %param.11) | copy-start | bytes 7077892
  26.5 1.2 copy-start.9
  27.7 1.7 copy-start.5
  29.0 1.8 copy-start.7
  41.3 3.2 %copy-start.12 = (s32[4]{0:T(128)S(1)}, s32[4]{0:T(128)}, u32[]{:S(2)}) copy-start(s32[4]{0:T(128)} %param.19) | copy-start | bytes 52
  41.3 3.4 %copy-start.13 = (s32[16]{0:T(128)S(1)}, s32[16]{0:T(128)}, u32[]{:S(2)}) copy-start(s32[16]{0:T(128)} %param.20) | copy-start | bytes 196
  104.6 5.3 %copy-start.11 = (bf16[192,384]{1,0:T(8,128)(2,1)S(1)}, bf16[192,384]{1,0:T(8,128)(2,1)}, u32[]{:S(2)}) copy-start(bf16[192,384]{1,0:T(8,128)(2,1)} %get-tuple-element.24) | copy-start | bytes 442372
  104.6 5.3 %collective-permute-start = (bf16[192,384]{1,0:T(8,128)(2,1)}, bf16[192,384]{1,0:T(8,128)(2,1)S(1)}, u32[]{:S(2)}, u32[]{:S(2)}) collective-permute-start(bf16[192,384]{1,0:T(8,128)(2,1)} %get-tuple-element.25), channel_id=1, source_target_pairs={{0,64},{64,0},{1,65},{65,1},{2,66},{66,2},{3,67},{67,3},{4,68},{68... | collective-permute-start | bytes 442376 | tf_op jit(solution)/shard_map/ppermute | solution.py:413
  143.0 1.7 copy-start.4
  144.3 1.8 copy-start.6
  144.7 2.3 %copy-start.3 = (bf16[384,3072]{1,0:T(8,128)(2,1)S(1)}, bf16[384,3072]{1,0:T(8,128)(2,1)}, u32[]{:S(2)}) copy-start(bf16[384,3072]{1,0:T(8,128)(2,1)} %copy.74) | copy-start | bytes 7077892
  150.2 2.5 %copy-start.2 = (bf16[384,3072]{1,0:T(8,128)(2,1)S(1)}, bf16[384,3072]{1,0:T(8,128)(2,1)}, u32[]{:S(2)}) copy-start(bf16[384,3072]{1,0:T(8,128)(2,1)} %copy.75) | copy-start | bytes 7077892
  165.7 13.5 %copy-start.8 = (bf16[3072,64]{0,1:T(8,128)(2,1)S(1)}, bf16[3072,64]{0,1:T(8,128)(2,1)}, u32[]{:S(2)}) copy-start(bf16[3072,64]{0,1:T(8,128)(2,1)} %param.15) | copy-start | bytes 1179652
  178.5 1.6 collective-permute-start.2
  180.1 3.6 %copy-start = (f32[1,48,64]{2,1,0:T(8,128)S(1)}, f32[1,48,64]{2,1,0:T(8,128)}, u32[]{:S(2)}) copy-start(f32[1,48,64]{2,1,0:T(8,128)} %param.12) | copy-start | bytes 36868
Sparse Core Ops, SparseCore 0:
  10.1 77.9 all-gather.4
  90.3 75.3 all-gather.6
